TPU v7x, 128 devices: a whole 4x4x4 slice. The times are simulated.
128 devices in a mesh: atm: 16 (over y, x), ocn: 8 (over z, core).
Axes of the slice: x: 4, y: 4, z: 4, core: 2. Of those that a mesh axis runs over, the one named last changes fastest.
Arguments:
- atm_state: float32 [13824, 3, 1024], P('atm', None, 'ocn'), may hold values from -6 to 6
- diffusivity: float32 [13824, 3, 1024], P('atm', None, 'ocn'), may hold values from 0.1 to 0.24
- ocean_state: float32 [32768, 3, 128], P(('atm', 'ocn')), may hold values from -6 to 6
- land_mask: int32 [32768, 128], P(('atm', 'ocn')), may hold values 0 or 1
- intersection_area: float32 [65536, 128], P(('atm', 'ocn')), may hold values from 0.2 to 1
- intersection_seg: int32 [65536], P(('atm', 'ocn')), may hold values from 0 to 255
- intersection_dest: int32 [65536, 1], P(('atm', 'ocn')), may hold values from 0 to 127; in each aligned block of 512 rows (0 to 511, 512 to 1023, ...) at most 8 rows name the same one
- intersection_row: int32 [65536], P(('atm', 'ocn')), may hold values from 0 to 863
Outputs:
- atm_next: float32 [13824, 3, 1024], P('atm', None, 'ocn')
- ocean_flux: float32 [32768, 3, 128], P(('atm', 'ocn'))
Inputs may be any that keep to these rules, and one draw needn't show every extreme that they name: intersection_seg indexes the segments owned by the same device as the intersection row. `intersection_dest`: among the 512 intersection rows of one device, no device is named by more than 8 rows, and some device is named by exactly 8.
All inputs are finite; a program needn't handle non-finite values. No bound on the sum of `land_mask` on one device may be relied on, other than what follows from the above.
Results may differ from a plain program's by a relative error of at most 0.00002.
Values sent between devices are 32-bit elements; how exact they have to be, the bound alone decides.
A program may use at most 64 MiB of HBM per device.

v0:
```python
import functools

import jax
import jax.numpy as jnp
from jax import lax
from jax.experimental import pallas as pl
from jax.experimental.pallas import tpu as pltpu
from jax.sharding import PartitionSpec as P

ITERS = 3
HIGHEST = lax.Precision.HIGHEST
HALO = ITERS


def with_halo(block, sides, width):
    for axis, dim in sides:
        count = lax.axis_size(axis)
        forward = [(i, i + 1) for i in range(count - 1)]
        backward = [(target, source) for source, target in forward]
        low = lax.ppermute(
            lax.slice_in_dim(block, block.shape[dim] - width, None, axis=dim), axis, forward
        )
        high = lax.ppermute(lax.slice_in_dim(block, 0, width, axis=dim), axis, backward)
        block = jnp.concatenate([low, block, high], axis=dim)
    return block


def beside_all(padded):
    return padded[2:, :, 1:-1] + padded[:-2, :, 1:-1] + padded[1:-1, :, 2:] + padded[1:-1, :, :-2]


def fluxes(ocean_part, air_part):
    wind_east = air_part[:, 1] - ocean_part[:, 1]
    wind_north = air_part[:, 2] - ocean_part[:, 2]
    wind_speed = jnp.sqrt(wind_east * wind_east + wind_north * wind_north + 0.5)
    temp_gap = ocean_part[:, 0] - air_part[:, 0]
    factor = 1.0 + 0.5 * jnp.tanh(temp_gap / wind_speed)
    return jnp.stack(
        [
            0.8 * factor * wind_speed * temp_gap,
            0.6 * factor * wind_speed * wind_east,
            0.6 * factor * wind_speed * wind_north,
        ],
        axis=1,
    )


def select_rows(chosen, values, precision=HIGHEST):
    flat = values.reshape(values.shape[0], -1)
    total = jnp.dot(chosen, flat, precision=precision, preferred_element_type=jnp.float32)
    return total.reshape((chosen.shape[0],) + values.shape[1:])


def planes_with_halo(block, rows_padded, lanes):
    chans, rows, width = block.shape
    atm_n = lax.axis_size("atm")
    ocn_n = lax.axis_size("ocn")
    fwd = [(i, i + 1) for i in range(atm_n - 1)]
    bwd = [(t, s) for s, t in fwd]
    up = lax.ppermute(block[:, rows - HALO :, :], "atm", fwd)
    down = lax.ppermute(block[:, :HALO, :], "atm", bwd)
    extra = rows_padded - rows - 2 * HALO
    tall = jnp.concatenate(
        [up, block, down, jnp.zeros((chans, extra, width), block.dtype)], axis=1
    )
    fwd = [(i, i + 1) for i in range(ocn_n - 1)]
    bwd = [(t, s) for s, t in fwd]
    left = lax.ppermute(tall[:, :, width - HALO :], "ocn", fwd)
    right = lax.ppermute(tall[:, :, :HALO], "ocn", bwd)
    gap = lanes - width - 2 * HALO
    return jnp.concatenate(
        [tall, right, jnp.zeros((chans, rows_padded, gap), block.dtype), left], axis=2
    )


def diffuse_kernel(rows, width, state_ref, diff_ref, out_ref):
    rows_padded, lanes = state_ref.shape[1], state_ref.shape[2]
    for chan in range(state_ref.shape[0]):
        state = state_ref[chan]
        diff = diff_ref[chan]
        for iteration in range(ITERS):
            around = (
                pltpu.roll(state, rows_padded - 1, 0)
                + pltpu.roll(state, 1, 0)
                + pltpu.roll(state, lanes - 1, 1)
                + pltpu.roll(state, 1, 1)
            )
            state = state + diff * (around - 4.0 * state)
        out_ref[chan] = state[HALO : HALO + rows, :width]


def diffuse(state_ext, diff_ext, rows, width):
    chans = state_ext.shape[0]
    return pl.pallas_call(
        functools.partial(diffuse_kernel, rows, width),
        out_shape=jax.ShapeDtypeStruct((chans, rows, width), jnp.float32),
        in_specs=[pl.BlockSpec(memory_space=pltpu.VMEM)] * 2,
        out_specs=pl.BlockSpec(memory_space=pltpu.VMEM),
    )(state_ext, diff_ext)


def per_device(
    atm_state,
    diffusivity,
    ocean_state,
    land_mask,
    intersection_area,
    intersection_seg,
    intersection_dest,
    intersection_row,
):
    atm_count = lax.axis_size("atm")
    ocn_count = lax.axis_size("ocn")
    devices = atm_count * ocn_count
    row_count, chan_count, seg_width = atm_state.shape
    seg_count = ocean_state.shape[0]
    ov_rows = intersection_seg.shape[0]
    capacity = max(2, 2 * ov_rows // devices)
    slots = devices * capacity
    rows_padded = -(-(row_count + 2 * HALO) // 8) * 8
    lanes = 2 * seg_width

    diff_ext = planes_with_halo(jnp.transpose(diffusivity, (1, 0, 2)), rows_padded, lanes)

    padded = with_halo(atm_state, (("atm", 0), ("ocn", 2)), 1)
    smoothed = 0.5 * atm_state + 0.125 * beside_all(padded)

    target = intersection_dest[:, 0]
    matches = (target[:, None] == jnp.arange(devices, dtype=jnp.int32)[None, :]).astype(jnp.int32)
    position = jnp.sum((jnp.cumsum(matches, axis=0) - matches) * matches, axis=1)
    slot_index = target * capacity + position
    slot_pick = (
        jnp.arange(slots, dtype=jnp.int32)[:, None] == slot_index[None, :]
    ).astype(jnp.bfloat16)
    seg_pick = (
        intersection_seg[:, None] == jnp.arange(seg_count, dtype=jnp.int32)[None, :]
    ).astype(jnp.bfloat16)
    slot_seg = jnp.dot(slot_pick, seg_pick, preferred_element_type=jnp.float32)
    out_ocean = select_rows(slot_seg, ocean_state)
    out_mask = select_rows(slot_seg, land_mask.astype(jnp.float32), None)
    row_high = (intersection_row // 32).astype(jnp.bfloat16)
    row_low = (intersection_row % 32).astype(jnp.bfloat16)
    row_parts = jnp.concatenate(
        [jnp.broadcast_to(row_high[:, None], (ov_rows, seg_width)),
         jnp.broadcast_to(row_low[:, None], (ov_rows, seg_width))], axis=1
    )
    out_rows = jnp.dot(slot_pick, row_parts, preferred_element_type=jnp.float32)
    out_label = 32.0 * out_rows[:, :seg_width] + out_rows[:, seg_width:]
    out_area = select_rows(slot_pick.astype(jnp.float32), intersection_area)
    out_weight = out_area * out_mask
    outgoing = jnp.concatenate(
        [out_ocean, out_weight[:, None, :], out_label[:, None, :]], axis=1
    )
    incoming = lax.all_to_all(outgoing, ("atm", "ocn"), split_axis=0, concat_axis=0, tiled=True)
    in_labels = jnp.max(incoming[:, chan_count + 1, :], axis=1).astype(jnp.int32)
    row_pick = (
        jnp.arange(row_count, dtype=jnp.int32)[:, None] == in_labels[None, :]
    ).astype(jnp.float32)
    air_rows = select_rows(row_pick.T, smoothed)
    weighted = incoming[:, chan_count : chan_count + 1, :] * fluxes(
        incoming[:, :chan_count, :], air_rows
    )
    air_sum = select_rows(row_pick, weighted)
    returned = lax.all_to_all(weighted, ("atm", "ocn"), split_axis=0, concat_axis=0, tiled=True)
    ocean_flux = select_rows(slot_seg.T, returned)
    direction_sign = jnp.array([1.0, -1.0, -1.0], dtype=jnp.float32)[None, :, None]
    forced = atm_state + direction_sign * air_sum
    state_ext = planes_with_halo(jnp.transpose(forced, (1, 0, 2)), rows_padded, lanes)
    current = diffuse(state_ext, diff_ext, row_count, seg_width)
    return (jnp.transpose(current, (1, 0, 2)), ocean_flux)


def solution(mesh):
    placed = (
        P("atm", None, "ocn"),
        P("atm", None, "ocn"),
        P(("atm", "ocn"), None, None),
        P(("atm", "ocn"), None),
        P(("atm", "ocn"), None),
        P(("atm", "ocn")),
        P(("atm", "ocn"), None),
        P(("atm", "ocn")),
    )
    return jax.shard_map(
        per_device,
        mesh=mesh,
        in_specs=placed,
        out_specs=(P("atm", None, "ocn"), P(("atm", "ocn"), None, None)),
        check_vma=False,
    )
```

profile of v0, /device:TPU:1, one launch (start us, length us, event | category | flops | bytes accessed | tf_op | source)
XLA Modules:
  0.0 209.2 jit_solution(261654004749550049)
XLA Ops:
  5.6 1.8 fusion.50
  7.9 3.6 %copy.86 = f32[1024,5,128]{2,1,0:T(8,128)} copy(f32[1024,5,128]{2,0,1:T(8,128)S(1)} %pad_maximum_fusion.2) | data formatting | bytes 5242880 | tf_op jit(solution)/shard_map/concatenate | solution.py:151
  11.5 12.0 %all-to-all-start = ((f32[1024,5,128]{2,1,0:T(8,128)}), f32[1024,5,128]{2,1,0:T(8,128)}, u32[]{:S(2)}, u32[]{:S(2)}) async-start(f32[1024,5,128]{2,1,0:T(8,128)} %copy.86), calls=%async_computation | async-start | bytes 8388608 | tf_op jit(solution)/shard_map/all_to_all | solution.py:154
  23.5 3.3 %collective-permute-start.1 = (f32[1,3,128]{2,0,1:T(1,128)S(1)}, f32[1,3,128]{2,0,1:T(1,128)S(1)}, u32[]{:S(2)}, u32[]{:S(2)}) collective-permute-start(f32[1,3,128]{2,0,1:T(1,128)S(1)} %get-tuple-element.21), channel_id=1, source_target_pairs={{0,8},{8,16},{16,24},{24,32},{32,40},{40,48},{48,56},{56,64},{64,7... | collective-permute-start | bytes 4616 | tf_op jit(solution)/shard_map/ppermute | solution.py:20
  28.1 38.7 %collective-permute-done.1 = f32[1,3,128]{2,0,1:T(1,128)S(1)} collective-permute-done((f32[1,3,128]{2,0,1:T(1,128)S(1)}, f32[1,3,128]{2,0,1:T(1,128)S(1)}, u32[]{:S(2)}, u32[]{:S(2)}) %collective-permute-start.1) | collective-permute-done | bytes 1568 | tf_op jit(solution)/shard_map/ppermute | solution.py:20
  66.8 2.8 %collective-permute-done = f32[1,3,128]{2,0,1:T(1,128)S(1)} collective-permute-done((f32[1,3,128]{2,0,1:T(1,128)S(1)}, f32[1,3,128]{2,0,1:T(1,128)S(1)}, u32[]{:S(2)}, u32[]{:S(2)}) %collective-permute-start) | collective-permute-done | bytes 1568 | tf_op jit(solution)/shard_map/ppermute | solution.py:23
  71.2 1.9 copy.114
  73.7 3.9 %collective-permute-start.3 = (f32[866,3,1]{0,1,2:T(4,128)S(1)}, f32[866,3,1]{0,1,2:T(4,128)S(1)}, u32[]{:S(2)}, u32[]{:S(2)}) collective-permute-start(f32[866,3,1]{0,1,2:T(4,128)S(1)} %copy.115), channel_id=1, source_target_pairs={{0,1},{1,2},{2,3},{3,4},{4,5},{5,6},{6,7},{8,9},{9,10},{10,11},{11... | collective-permute-start | bytes 31184 | tf_op jit(solution)/shard_map/ppermute | solution.py:20
  77.6 1.9 collective-permute-start.2
  80.2 2.4 %collective-permute-start.8 = (f32[3,3,128]{2,1,0:T(4,128)S(1)}, f32[3,3,128]{2,1,0:T(4,128)S(1)}, u32[]{:S(2)}, u32[]{:S(2)}) collective-permute-start(f32[3,3,128]{2,1,0:T(4,128)S(1)} %get-tuple-element.17), channel_id=1, source_target_pairs={{0,8},{8,16},{16,24},{24,32},{32,40},{40,48},{48,56},{56,64},{64,7... | collective-permute-start | bytes 13832 | tf_op jit(solution)/shard_map/ppermute | solution.py:60
  87.2 17.9 %fusion.78 = (f32[1024,1,128]{2,1,0:T(1,128)S(1)}, f32[1024,1,128]{2,1,0:T(1,128)S(1)}, f32[1024,1,128]{2,1,0:T(1,128)S(1)}, f32[1024,1,128]{2,1,0:T(1,128)}, f32[1024]{0:T(1024)S(1)}) fusion(f32[1024,5,128]{2,1,0:T(8,128)} %all-to-all-done), kind=kLoop, calls=%fused_computation.103 | loop fusion | flops 130048 | bytes 4722688 | tf_op jit(solution)/shard_map/slice | solution.py:160
  107.3 8.5 %fusion.3 = f32[1024,3,128]{0,2,1:T(8,128)S(1)} fusion(s32[1024]{0:T(1024)S(1)} %convert_element_type.32, f32[866,3,1]{2,0,1:T(8,128)} %copy.92, f32[1,3,128]{2,0,1:T(1,128)S(1)} %collective-permute-done, f32[864,3,128]{2,0,1:T(8,128)} %param.9, f32[1,3,128]{2,0,1:T(1,128)S(1)} %collective-permute-done.1, f32[866,3,1]{2,0,1:T(8,128)} %copy.90), kind=kOutput, calls=%fused_computation.5 | convolution fusion | flops 4082393088 | bytes 2927920 | tf_op jit(solution)/shard_map/dot_general | solution.py:50
  117.0 1.8 copy.105
  118.8 12.8 %all-to-all-start.1 = ((f32[1024,3,128]{2,1,0:T(4,128)}), f32[1024,3,128]{2,1,0:T(4,128)S(1)}, u32[]{:S(2)}, u32[]{:S(2)}) async-start(f32[1024,3,128]{2,1,0:T(4,128)} %copy.105), calls=%async_computation.1 | async-start | bytes 4194304 | tf_op jit(solution)/shard_map/all_to_all | solution.py:164
  131.7 4.9 %fusion.29 = f32[3,864,128]{2,1,0:T(8,128)S(1)} fusion(f32[864,3,128]{2,0,1:T(8,128)} %param.9, f32[1024,3,128]{0,2,1:T(8,128)} %copy-done.1, s32[1024]{0:T(1024)S(1)} %convert_element_type.32, f32[3]{0:T(128)S(1)} %copy-done.16), kind=kOutput, calls=%fused_computation.27 | convolution fusion | flops 4078411776 | bytes 4231180 | tf_op jit(solution)/shard_map/dot_general | solution.py:50
  136.6 3.3 %collective-permute-start.4 = (f32[3,3,128]{2,1,0:T(4,128)S(1)}, f32[3,3,128]{2,1,0:T(4,128)S(1)}, u32[]{:S(2)}, u32[]{:S(2)}) collective-permute-start(f32[3,3,128]{2,1,0:T(4,128)S(1)} %get-tuple-element.19), channel_id=1, source_target_pairs={{0,8},{8,16},{16,24},{24,32},{32,40},{40,48},{48,56},{56,64},{64,7... | collective-permute-start | bytes 13832 | tf_op jit(solution)/shard_map/ppermute | solution.py:60
  141.2 11.5 %collective-permute-done.4 = f32[3,3,128]{2,1,0:T(4,128)S(1)} collective-permute-done((f32[3,3,128]{2,1,0:T(4,128)S(1)}, f32[3,3,128]{2,1,0:T(4,128)S(1)}, u32[]{:S(2)}, u32[]{:S(2)}) %collective-permute-start.4) | collective-permute-done | bytes 4640 | tf_op jit(solution)/shard_map/ppermute | solution.py:60
  152.7 3.0 %collective-permute-done.5 = f32[3,3,128]{2,1,0:T(4,128)S(1)} collective-permute-done((f32[3,3,128]{2,1,0:T(4,128)S(1)}, f32[3,3,128]{2,1,0:T(4,128)S(1)}, u32[]{:S(2)}, u32[]{:S(2)}) %collective-permute-start.5) | collective-permute-done | bytes 4640 | tf_op jit(solution)/shard_map/ppermute | solution.py:61
  156.3 3.2 %fusion.79 = (f32[3,872,3]{2,1,0:T(8,128)}, f32[3,872,3]{2,1,0:T(8,128)}, f32[3,872,3]{2,1,0:T(8,128)}, f32[3,872,3]{2,1,0:T(8,128)}) fusion(f32[3,872,128]{2,1,0:T(8,128)S(1)} %get-tuple-element.25, f32[3,872,128]{2,1,0:T(8,128)S(1)} %get-tuple-element.26), kind=kLoop, calls=%fused_computation.104 | loop fusion | bytes 251136 | tf_op jit(solution)/shard_map/slice | solution.py:69
  161.2 1.8 copy.102
  163.0 2.8 %collective-permute-start.10 = (f32[3,872,3]{1,2,0:T(4,128)S(1)}, f32[3,872,3]{1,2,0:T(4,128)}, u32[]{:S(2)}, u32[]{:S(2)}) collective-permute-start(f32[3,872,3]{1,2,0:T(4,128)S(1)} %copy.101), channel_id=1, source_target_pairs={{1,0},{2,1},{3,2},{4,3},{5,4},{6,5},{7,6},{9,8},{10,9},{11,10},{12... | collective-permute-start | bytes 94184 | tf_op jit(solution)/shard_map/ppermute | solution.py:69
  167.5 3.1 %collective-permute-start.11 = (f32[3,872,3]{1,2,0:T(4,128)S(1)}, f32[3,872,3]{1,2,0:T(4,128)}, u32[]{:S(2)}, u32[]{:S(2)}) collective-permute-start(f32[3,872,3]{1,2,0:T(4,128)S(1)} %copy.102), channel_id=1, source_target_pairs={{0,1},{1,2},{2,3},{3,4},{4,5},{5,6},{6,7},{8,9},{9,10},{10,11},{11... | collective-permute-start | bytes 94184 | tf_op jit(solution)/shard_map/ppermute | solution.py:68
  170.7 2.4 %collective-permute-start.7 = (f32[3,872,3]{1,2,0:T(4,128)S(1)}, f32[3,872,3]{1,2,0:T(4,128)}, u32[]{:S(2)}, u32[]{:S(2)}) collective-permute-start(f32[3,872,3]{1,2,0:T(4,128)S(1)} %copy.98), channel_id=1, source_target_pairs={{0,1},{1,2},{2,3},{3,4},{4,5},{5,6},{6,7},{8,9},{9,10},{10,11},{11... | collective-permute-start | bytes 94184 | tf_op jit(solution)/shard_map/ppermute | solution.py:68
  173.1 2.4 %copy.97 = f32[3,872,3]{1,2,0:T(4,128)} copy(f32[3,872,3]{2,1,0:T(8,128)} %get-tuple-element.30) | data formatting | bytes 62784 | tf_op jit(solution)/shard_map/slice | solution.py:69
  175.5 2.5 %collective-permute-start.6 = (f32[3,872,3]{1,2,0:T(4,128)}, f32[3,872,3]{1,2,0:T(4,128)}, u32[]{:S(2)}, u32[]{:S(2)}) collective-permute-start(f32[3,872,3]{1,2,0:T(4,128)} %copy.97), channel_id=1, source_target_pairs={{1,0},{2,1},{3,2},{4,3},{5,4},{6,5},{7,6},{9,8},{10,9},{11,10},{12... | collective-permute-start | bytes 94184 | tf_op jit(solution)/shard_map/ppermute | solution.py:69
  178.6 2.4 %copy.103 = f32[3,872,3]{2,1,0:T(8,128)} copy(f32[3,872,3]{1,2,0:T(4,128)} %collective-permute-done.10) | data formatting | bytes 62784 | tf_op jit(solution)/shard_map/ppermute | solution.py:69
  181.0 2.3 %copy.104 = f32[3,872,3]{2,1,0:T(8,128)} copy(f32[3,872,3]{1,2,0:T(4,128)} %collective-permute-done.11) | data formatting | bytes 62784 | tf_op jit(solution)/shard_map/ppermute | solution.py:68
  183.3 2.3 %copy.100 = f32[3,872,3]{2,1,0:T(8,128)} copy(f32[3,872,3]{1,2,0:T(4,128)} %collective-permute-done.7) | data formatting | bytes 62784 | tf_op jit(solution)/shard_map/ppermute | solution.py:68
  185.7 2.4 %copy.99 = f32[3,872,3]{2,1,0:T(8,128)} copy(f32[3,872,3]{1,2,0:T(4,128)} %collective-permute-done.6) | data formatting | bytes 62784 | tf_op jit(solution)/shard_map/ppermute | solution.py:69
  188.1 5.9 %fusion.10 = (f32[3,872,256]{2,1,0:T(8,128)}, f32[3,872,256]{2,1,0:T(8,128)}) fusion(f32[3,2,128]{2,1,0:T(2,128)S(1)} %broadcast.63, f32[3,872,3]{2,1,0:T(8,128)} %copy.104, f32[3,872,3]{2,1,0:T(8,128)} %copy.103, f32[3,3,128]{2,1,0:T(4,128)S(1)} %copy-done.8, f32[3,864,128]{2,1,0:T(8,128)} %bitcast.76, f32[3,3,128]{2,1,0:T(4,128)S(1)} %collective-permute-done.8, ...), kind=kLoop, calls=%fused_computation.11 | loop fusion | flops 8036352 | bytes 8159872 | tf_op jit(solution)/shard_map/concatenate | solution.py:71
  193.9 8.1 %shard_map.104 = f32[3,864,128]{2,1,0:T(8,128)} custom-call(f32[3,872,256]{2,1,0:T(8,128)} %get-tuple-element.24.state_ref, f32[3,872,256]{2,1,0:T(8,128)} %get-tuple-element.23.diff_ref), custom_call_target="tpu_custom_call" | custom-call | tf_op jit(solution)/shard_map/pallas_call | solution.py:94
  203.7 5.6 %fusion.16 = f32[256,3,128]{2,0,1:T(8,128)} fusion(f32[1024,3,128]{0,2,1:T(8,128)} %copy.106, f32[1024,256]{1,0:T(8,128)S(1)} %fusion.13), kind=kOutput, calls=%fused_computation.22 | convolution fusion | flops 1207959552 | bytes 3014656 | tf_op jit(solution)/shard_map/dot_general | solution.py:50
  (90 shorter events, 25.0 us)
Async XLA Ops:
  0.6 2.3 %copy-start = (f32[512,128]{1,0:T(8,128)S(1)}, f32[512,128]{1,0:T(8,128)}, u32[]{:S(2)}) copy-start(f32[512,128]{1,0:T(8,128)} %param.13) | copy-start | bytes 786436
  0.6 1.9 copy-start.13
  0.7 2.1 %copy-start.5 = (f32[256,3,128]{2,0,1:T(8,128)S(1)}, f32[256,3,128]{2,0,1:T(8,128)}, u32[]{:S(2)}) copy-start(f32[256,3,128]{2,0,1:T(8,128)} %param.11) | copy-start | bytes 1179652
  4.3 0.7 copy-start.15
  5.6 1.8 copy-start.6
  11.5 12.0 %copy-start.4 = (f32[864,3,128]{2,0,1:T(8,128)S(1)}, f32[864,3,128]{2,0,1:T(8,128)}, u32[]{:S(2)}) copy-start(f32[864,3,128]{2,0,1:T(8,128)} %param.9) | copy-start | bytes 3981316
  11.5 75.7 %all-to-all-start = ((f32[1024,5,128]{2,1,0:T(8,128)}), f32[1024,5,128]{2,1,0:T(8,128)}, u32[]{:S(2)}, u32[]{:S(2)}) async-start(f32[1024,5,128]{2,1,0:T(8,128)} %copy.86), calls=%async_computation | async-start | bytes 8388608 | tf_op jit(solution)/shard_map/all_to_all | solution.py:154
  23.5 43.3 %collective-permute-start.1 = (f32[1,3,128]{2,0,1:T(1,128)S(1)}, f32[1,3,128]{2,0,1:T(1,128)S(1)}, u32[]{:S(2)}, u32[]{:S(2)}) collective-permute-start(f32[1,3,128]{2,0,1:T(1,128)S(1)} %get-tuple-element.21), channel_id=1, source_target_pairs={{0,8},{8,16},{16,24},{24,32},{32,40},{40,48},{48,56},{56,64},{64,7... | collective-permute-start | bytes 4616 | tf_op jit(solution)/shard_map/ppermute | solution.py:20
  26.8 42.8 %collective-permute-start = (f32[1,3,128]{2,0,1:T(1,128)S(1)}, f32[1,3,128]{2,0,1:T(1,128)S(1)}, u32[]{:S(2)}, u32[]{:S(2)}) collective-permute-start(f32[1,3,128]{2,0,1:T(1,128)S(1)} %get-tuple-element.22), channel_id=1, source_target_pairs={{8,0},{16,8},{24,16},{32,24},{40,32},{48,40},{56,48},{64,56},{72,6... | collective-permute-start | bytes 4616 | tf_op jit(solution)/shard_map/ppermute | solution.py:23
  73.7 12.0 %collective-permute-start.3 = (f32[866,3,1]{0,1,2:T(4,128)S(1)}, f32[866,3,1]{0,1,2:T(4,128)S(1)}, u32[]{:S(2)}, u32[]{:S(2)}) collective-permute-start(f32[866,3,1]{0,1,2:T(4,128)S(1)} %copy.115), channel_id=1, source_target_pairs={{0,1},{1,2},{2,3},{3,4},{4,5},{5,6},{6,7},{8,9},{9,10},{10,11},{11... | collective-permute-start | bytes 31184 | tf_op jit(solution)/shard_map/ppermute | solution.py:20
  77.6 6.5 %collective-permute-start.2 = (f32[866,3,1]{0,1,2:T(4,128)S(1)}, f32[866,3,1]{0,1,2:T(4,128)S(1)}, u32[]{:S(2)}, u32[]{:S(2)}) collective-permute-start(f32[866,3,1]{0,1,2:T(4,128)S(1)} %copy.114), channel_id=1, source_target_pairs={{1,0},{2,1},{3,2},{4,3},{5,4},{6,5},{7,6},{9,8},{10,9},{11,10},{12... | collective-permute-start | bytes 31184 | tf_op jit(solution)/shard_map/ppermute | solution.py:23
  80.2 60.9 %collective-permute-start.8 = (f32[3,3,128]{2,1,0:T(4,128)S(1)}, f32[3,3,128]{2,1,0:T(4,128)S(1)}, u32[]{:S(2)}, u32[]{:S(2)}) collective-permute-start(f32[3,3,128]{2,1,0:T(4,128)S(1)} %get-tuple-element.17), channel_id=1, source_target_pairs={{0,8},{8,16},{16,24},{24,32},{32,40},{40,48},{48,56},{56,64},{64,7... | collective-permute-start | bytes 13832 | tf_op jit(solution)/shard_map/ppermute | solution.py:60
  82.6 58.6 %collective-permute-start.9 = (f32[3,3,128]{2,1,0:T(4,128)S(1)}, f32[3,3,128]{2,1,0:T(4,128)S(1)}, u32[]{:S(2)}, u32[]{:S(2)}) collective-permute-start(f32[3,3,128]{2,1,0:T(4,128)S(1)} %get-tuple-element.18), channel_id=1, source_target_pairs={{8,0},{16,8},{24,16},{32,24},{40,32},{48,40},{56,48},{64,56},{72,6... | collective-permute-start | bytes 13832 | tf_op jit(solution)/shard_map/ppermute | solution.py:61
  117.0 1.8 copy-start.1
  118.8 12.8 %copy-start.16 = (f32[3]{0:T(128)S(1)}, f32[3]{0:T(128)}, u32[]{:S(2)}) copy-start(f32[3]{0:T(128)} %constant.55.clone) | copy-start | bytes 40
  118.8 83.2 %all-to-all-start.1 = ((f32[1024,3,128]{2,1,0:T(4,128)}), f32[1024,3,128]{2,1,0:T(4,128)S(1)}, u32[]{:S(2)}, u32[]{:S(2)}) async-start(f32[1024,3,128]{2,1,0:T(4,128)} %copy.105), calls=%async_computation.1 | async-start | bytes 4194304 | tf_op jit(solution)/shard_map/all_to_all | solution.py:164
  131.6 24.1 %copy-start.2 = (f32[864,3,128]{2,0,1:T(8,128)S(1)}, f32[864,3,128]{2,0,1:T(8,128)}, u32[]{:S(2)}) copy-start(f32[864,3,128]{2,0,1:T(8,128)} %param.10) | copy-start | bytes 3981316
  136.5 19.4 %copy-start.3 = (f32[3,864,128]{2,1,0:T(8,128)}, f32[3,864,128]{2,1,0:T(8,128)S(1)}, u32[]{:S(2)}) copy-start(f32[3,864,128]{2,1,0:T(8,128)S(1)} %fusion.29) | copy-start | bytes 3981316
  136.6 16.1 %collective-permute-start.4 = (f32[3,3,128]{2,1,0:T(4,128)S(1)}, f32[3,3,128]{2,1,0:T(4,128)S(1)}, u32[]{:S(2)}, u32[]{:S(2)}) collective-permute-start(f32[3,3,128]{2,1,0:T(4,128)S(1)} %get-tuple-element.19), channel_id=1, source_target_pairs={{0,8},{8,16},{16,24},{24,32},{32,40},{40,48},{48,56},{56,64},{64,7... | collective-permute-start | bytes 13832 | tf_op jit(solution)/shard_map/ppermute | solution.py:60
  139.9 15.8 %collective-permute-start.5 = (f32[3,3,128]{2,1,0:T(4,128)S(1)}, f32[3,3,128]{2,1,0:T(4,128)S(1)}, u32[]{:S(2)}, u32[]{:S(2)}) collective-permute-start(f32[3,3,128]{2,1,0:T(4,128)S(1)} %get-tuple-element.20), channel_id=1, source_target_pairs={{8,0},{16,8},{24,16},{32,24},{40,32},{48,40},{56,48},{64,56},{72,6... | collective-permute-start | bytes 13832 | tf_op jit(solution)/shard_map/ppermute | solution.py:61
  141.2 14.7 %copy-start.7 = (f32[3,3,128]{2,1,0:T(4,128)}, f32[3,3,128]{2,1,0:T(4,128)S(1)}, u32[]{:S(2)}) copy-start(f32[3,3,128]{2,1,0:T(4,128)S(1)} %collective-permute-done.9) | copy-start | bytes 13828
  152.7 3.3 %copy-start.9 = (f32[3,3,128]{2,1,0:T(4,128)}, f32[3,3,128]{2,1,0:T(4,128)S(1)}, u32[]{:S(2)}) copy-start(f32[3,3,128]{2,1,0:T(4,128)S(1)} %collective-permute-done.4) | copy-start | bytes 13828
  155.7 0.6 copy-start.11
  163.0 15.7 %collective-permute-start.10 = (f32[3,872,3]{1,2,0:T(4,128)S(1)}, f32[3,872,3]{1,2,0:T(4,128)}, u32[]{:S(2)}, u32[]{:S(2)}) collective-permute-start(f32[3,872,3]{1,2,0:T(4,128)S(1)} %copy.101), channel_id=1, source_target_pairs={{1,0},{2,1},{3,2},{4,3},{5,4},{6,5},{7,6},{9,8},{10,9},{11,10},{12... | collective-permute-start | bytes 94184 | tf_op jit(solution)/shard_map/ppermute | solution.py:69
  167.5 13.5 %collective-permute-start.11 = (f32[3,872,3]{1,2,0:T(4,128)S(1)}, f32[3,872,3]{1,2,0:T(4,128)}, u32[]{:S(2)}, u32[]{:S(2)}) collective-permute-start(f32[3,872,3]{1,2,0:T(4,128)S(1)} %copy.102), channel_id=1, source_target_pairs={{0,1},{1,2},{2,3},{3,4},{4,5},{5,6},{6,7},{8,9},{9,10},{10,11},{11... | collective-permute-start | bytes 94184 | tf_op jit(solution)/shard_map/ppermute | solution.py:68
  170.7 12.6 %collective-permute-start.7 = (f32[3,872,3]{1,2,0:T(4,128)S(1)}, f32[3,872,3]{1,2,0:T(4,128)}, u32[]{:S(2)}, u32[]{:S(2)}) collective-permute-start(f32[3,872,3]{1,2,0:T(4,128)S(1)} %copy.98), channel_id=1, source_target_pairs={{0,1},{1,2},{2,3},{3,4},{4,5},{5,6},{6,7},{8,9},{9,10},{10,11},{11... | collective-permute-start | bytes 94184 | tf_op jit(solution)/shard_map/ppermute | solution.py:68
  175.5 10.2 %collective-permute-start.6 = (f32[3,872,3]{1,2,0:T(4,128)}, f32[3,872,3]{1,2,0:T(4,128)}, u32[]{:S(2)}, u32[]{:S(2)}) collective-permute-start(f32[3,872,3]{1,2,0:T(4,128)} %copy.97), channel_id=1, source_target_pairs={{1,0},{2,1},{3,2},{4,3},{5,4},{6,5},{7,6},{9,8},{10,9},{11,10},{12... | collective-permute-start | bytes 94184 | tf_op jit(solution)/shard_map/ppermute | solution.py:69
  183.3 4.8 %copy-start.8 = (f32[3,3,128]{2,1,0:T(4,128)S(1)}, f32[3,3,128]{2,1,0:T(4,128)}, u32[]{:S(2)}) copy-start(f32[3,3,128]{2,1,0:T(4,128)} %copy-done.7) | copy-start | bytes 13828
  183.3 4.8 %copy-start.10 = (f32[3,3,128]{2,1,0:T(4,128)S(1)}, f32[3,3,128]{2,1,0:T(4,128)}, u32[]{:S(2)}) copy-start(f32[3,3,128]{2,1,0:T(4,128)} %copy-done.9) | copy-start | bytes 13828
  183.3 4.8 %copy-start.12 = (f32[3,3,128]{2,1,0:T(4,128)S(1)}, f32[3,3,128]{2,1,0:T(4,128)}, u32[]{:S(2)}) copy-start(f32[3,3,128]{2,1,0:T(4,128)} %copy-done.11) | copy-start | bytes 13828
  183.3 4.8 %copy-start.14 = (f32[256]{0:T(256)S(1)}, f32[256]{0:T(256)}, u32[]{:S(2)}) copy-start(f32[256]{0:T(256)} %pad.16.clone) | copy-start | bytes 3076
where the time goes:
time: 211 us; the launch traced here: 209 us
  waiting for transfers between devices  56 us (27%)
  starting transfers between devices  54.5 us (26%)
  local copies, waits for them, and re-layouts  39.6 us (19%)
  other arithmetic  26.7 us (13%)
  matrix products  23.2 us (11%)
  Pallas kernels  8.1 us (4%)
    ppermute x2, waiting for transfers between devices, with_halo(): lax.ppermute(lax.slice_in_dim(block, block.shape[dim] - width, None, axis...  38.7 us
    dot_general x6, matrix products, select_rows(): jnp.dot(chosen, flat, precision=precision, preferred_element_type=jnp.flo...  22.1 us
    slice x1, other arithmetic, per_device(): incoming[:, chan_count:chan_count + 1, :]  17.9 us
    all_to_all x1, starting transfers between devices, per_device(): lax.all_to_all(weighted, ('atm', 'ocn'), split_axis=0, concat_axis=0, til...  12.8 us
    all_to_all x1, starting transfers between devices, per_device(): lax.all_to_all(outgoing, ('atm', 'ocn'), split_axis=0, concat_axis=0, til...  12 us
    ppermute x2, waiting for transfers between devices, planes_with_halo(): up = lax.ppermute(block[:, rows - HALO:, :], 'atm', fwd)  11.5 us
    pallas_call x1, Pallas kernels, diffuse(): pl.pallas_call(functools.partial(diffuse_kernel, rows, width), out_shape=...  8.1 us
    slice x3, local copies, waits for them, and re-layouts, planes_with_halo(): right = lax.ppermute(tall[:, :, :HALO], 'ocn', bwd)  7.27 us
  transfers between devices with their start and end apart: 14, of which 4 were waited for; matrix products, arithmetic and copies ran while one was open for 34% of the time, Pallas kernels for 4%

commit v1 on v0

--- a/solution.py
+++ b/solution.py
@@ -121,9 +121,7 @@
     lanes = 2 * seg_width
 
     diff_ext = planes_with_halo(jnp.transpose(diffusivity, (1, 0, 2)), rows_padded, lanes)
-
     padded = with_halo(atm_state, (("atm", 0), ("ocn", 2)), 1)
-    smoothed = 0.5 * atm_state + 0.125 * beside_all(padded)
 
     target = intersection_dest[:, 0]
     matches = (target[:, None] == jnp.arange(devices, dtype=jnp.int32)[None, :]).astype(jnp.int32)
@@ -136,7 +134,8 @@
         intersection_seg[:, None] == jnp.arange(seg_count, dtype=jnp.int32)[None, :]
     ).astype(jnp.bfloat16)
     slot_seg = jnp.dot(slot_pick, seg_pick, preferred_element_type=jnp.float32)
-    out_ocean = select_rows(slot_seg, ocean_state)
+    plane = chan_count * seg_width
+    out_ocean = select_rows(slot_seg, ocean_state.reshape(seg_count, plane))
     out_mask = select_rows(slot_seg, land_mask.astype(jnp.float32), None)
     row_high = (intersection_row // 32).astype(jnp.bfloat16)
     row_low = (intersection_row % 32).astype(jnp.bfloat16)
@@ -148,21 +147,24 @@
     out_label = 32.0 * out_rows[:, :seg_width] + out_rows[:, seg_width:]
     out_area = select_rows(slot_pick.astype(jnp.float32), intersection_area)
     out_weight = out_area * out_mask
-    outgoing = jnp.concatenate(
-        [out_ocean, out_weight[:, None, :], out_label[:, None, :]], axis=1
-    )
+    outgoing = jnp.concatenate([out_ocean, out_weight, out_label], axis=1)
+    outgoing, padded, diff_ext = lax.optimization_barrier((outgoing, padded, diff_ext))
+    smoothed = 0.5 * atm_state + 0.125 * beside_all(padded)
     incoming = lax.all_to_all(outgoing, ("atm", "ocn"), split_axis=0, concat_axis=0, tiled=True)
-    in_labels = jnp.max(incoming[:, chan_count + 1, :], axis=1).astype(jnp.int32)
+    in_labels = jnp.max(incoming[:, plane + seg_width :], axis=1).astype(jnp.int32)
     row_pick = (
         jnp.arange(row_count, dtype=jnp.int32)[:, None] == in_labels[None, :]
     ).astype(jnp.float32)
-    air_rows = select_rows(row_pick.T, smoothed)
-    weighted = incoming[:, chan_count : chan_count + 1, :] * fluxes(
-        incoming[:, :chan_count, :], air_rows
+    air_rows = select_rows(row_pick.T, smoothed.reshape(row_count, plane))
+    in_ocean = incoming[:, :plane].reshape(slots, chan_count, seg_width)
+    in_weight = incoming[:, plane : plane + seg_width]
+    weighted = in_weight[:, None, :] * fluxes(
+        in_ocean, air_rows.reshape(slots, chan_count, seg_width)
     )
-    air_sum = select_rows(row_pick, weighted)
+    weighted = weighted.reshape(slots, plane)
+    air_sum = select_rows(row_pick, weighted).reshape(row_count, chan_count, seg_width)
     returned = lax.all_to_all(weighted, ("atm", "ocn"), split_axis=0, concat_axis=0, tiled=True)
-    ocean_flux = select_rows(slot_seg.T, returned)
+    ocean_flux = select_rows(slot_seg.T, returned).reshape(seg_count, chan_count, seg_width)
     direction_sign = jnp.array([1.0, -1.0, -1.0], dtype=jnp.float32)[None, :, None]
     forced = atm_state + direction_sign * air_sum
     state_ext = planes_with_halo(jnp.transpose(forced, (1, 0, 2)), rows_padded, lanes)

time: 211 us -> 178 us (0.84)
  other arithmetic: 26.7 us -> 15.1 us
  waiting for transfers between devices: 56 us -> 44.5 us
  starting transfers between devices: 54.5 us -> 50.2 us
  local copies, waits for them, and re-layouts: 39.6 us -> 36.5 us
    ppermute x2, waiting for transfers between devices: 38.7 us -> 0.01 us  [with_halo(): lax.ppermute(lax.slice_in_dim(block, block.shape[dim] - width, None, axis...]
    all_to_all x1, waiting for transfers between devices: 0.01 us -> 32.9 us  [per_device(): lax.all_to_all(outgoing, ('atm', 'ocn'), split_axis=0, concat_axis=0, til...]
    slice x1, other arithmetic: 17.9 us -> 0.21 us  [per_device(): in_weight = incoming[:, plane:plane + seg_width]]
    all_to_all x1, starting transfers between devices: 12.8 us -> 4.9 us  [per_device(): lax.all_to_all(weighted, ('atm', 'ocn'), split_axis=0, concat_axis=0, til...]
    ppermute x2, waiting for transfers between devices: 11.5 us -> 6.56 us  [planes_with_halo(): up = lax.ppermute(block[:, rows - HALO:, :], 'atm', fwd)]
    concatenate x1, local copies, waits for them, and re-layouts: 3.63 us -> 0.43 us  [with_halo(): block = jnp.concatenate([low, block, high], axis=dim)]
    ppermute x2, waiting for transfers between devices: 2.78 us -> 0.01 us  [with_halo(): lax.ppermute(lax.slice_in_dim(block, 0, width, axis=dim), axis, backward)]
    slice x1 -> x2, local copies, waits for them, and re-layouts: 0.01 us -> 2.7 us  [with_halo(): lax.slice_in_dim(block, block.shape[dim] - width, None, axis=dim)]
  transfers between devices with their start and end apart: 14 -> 14, of which waited for: 4 -> 4; matrix products, arithmetic and copies ran while one was open for 34% -> 23% of each run, Pallas kernels for 4% -> 5%
where the time goes in v1:
time: 178 us; the launch traced here: 177 us
  starting transfers between devices  50.2 us (28%)
  waiting for transfers between devices  44.5 us (25%)
  local copies, waits for them, and re-layouts  36.5 us (21%)
  matrix products  21.1 us (12%)
  other arithmetic  15.1 us (8%)
  Pallas kernels  8.1 us (5%)
    all_to_all x1, waiting for transfers between devices, per_device(): lax.all_to_all(outgoing, ('atm', 'ocn'), split_axis=0, concat_axis=0, til...  32.9 us
    dot_general x6, matrix products, select_rows(): jnp.dot(chosen, flat, precision=precision, preferred_element_type=jnp.flo...  19.9 us
    all_to_all x1, starting transfers between devices, per_device(): lax.all_to_all(outgoing, ('atm', 'ocn'), split_axis=0, concat_axis=0, til...  12.6 us
    pallas_call x1, Pallas kernels, diffuse(): pl.pallas_call(functools.partial(diffuse_kernel, rows, width), out_shape=...  8.1 us
    concatenate x2, other arithmetic, planes_with_halo(): jnp.concatenate([tall, right, jnp.zeros((chans, rows_padded, gap), block....  8 us
    ppermute x2, starting transfers between devices, with_halo(): lax.ppermute(lax.slice_in_dim(block, block.shape[dim] - width, None, axis...  7.37 us
    ppermute x2, starting transfers between devices, planes_with_halo(): up = lax.ppermute(block[:, rows - HALO:, :], 'atm', fwd)  7.27 us
    unnamed x33, local copies, waits for them, and re-layouts  6.92 us
  transfers between devices with their start and end apart: 14, of which 4 were waited for; matrix products, arithmetic and copies ran while one was open for 23% of the time, Pallas kernels for 5%

profile of v1, /device:TPU:1, one launch (start us, length us, event | category | flops | bytes accessed | tf_op | source)
XLA Modules:
  0.0 176.8 jit_solution(8077342095012760200)
XLA Ops:
  1.5 3.9 %collective-permute-start = (f32[1,3,128]{2,0,1:T(1,128)S(1)}, f32[1,3,128]{2,0,1:T(1,128)S(1)}, u32[]{:S(2)}, u32[]{:S(2)}) collective-permute-start(f32[1,3,128]{2,0,1:T(1,128)S(1)} %get-tuple-element.24), channel_id=1, source_target_pairs={{0,8},{8,16},{16,24},{24,32},{32,40},{40,48},{48,56},{56,64},{64,7... | collective-permute-start | bytes 4616 | tf_op jit(solution)/shard_map/ppermute | solution.py:20
  7.4 4.0 %collective-permute-start.4 = (f32[3,3,128]{2,1,0:T(4,128)S(1)}, f32[3,3,128]{2,1,0:T(4,128)S(1)}, u32[]{:S(2)}, u32[]{:S(2)}) collective-permute-start(f32[3,3,128]{2,1,0:T(4,128)S(1)} %get-tuple-element.22), channel_id=1, source_target_pairs={{0,8},{8,16},{16,24},{24,32},{32,40},{40,48},{48,56},{56,64},{64,7... | collective-permute-start | bytes 13832 | tf_op jit(solution)/shard_map/ppermute | solution.py:60
  19.7 1.8 %pad_maximum_fusion.2 = f32[1024,640]{0,1:T(8,128)} fusion(f32[1024,128]{0,1:T(8,128)S(1)} %slice_add_fusion, f32[1024,128]{0,1:T(8,128)S(1)} %convolution_multiply_fusion, f32[1024,384]{0,1:T(8,128)S(1)} %fusion.75), kind=kLoop, calls=%fused_computation.12 | loop fusion | flops 1310720 | bytes 5242880 | tf_op jit(solution)/shard_map/concatenate | solution.py:150
  21.7 1.9 %fusion.71 = (f32[866,3,1]{2,0,1:T(8,128)}, f32[866,3,1]{2,0,1:T(8,128)}) fusion(f32[866,3,128]{2,0,1:T(8,128)S(1)} %pad_maximum_fusion.6), kind=kLoop, calls=%fused_computation.92 | loop fusion | bytes 41568 | tf_op jit(solution)/shard_map/slice | solution.py:21
  24.0 2.0 %copy.74 = f32[866,3,1]{0,1,2:T(4,128)S(1)} copy(f32[866,3,1]{2,0,1:T(8,128)} %get-tuple-element.18) | data formatting | bytes 20784
  26.0 1.9 %copy.75 = f32[866,3,1]{0,1,2:T(4,128)S(1)} copy(f32[866,3,1]{2,0,1:T(8,128)} %get-tuple-element.19) | data formatting | bytes 20784
  27.9 3.4 %collective-permute-start.3 = (f32[866,3,1]{0,1,2:T(4,128)S(1)}, f32[866,3,1]{0,1,2:T(4,128)S(1)}, u32[]{:S(2)}, u32[]{:S(2)}) collective-permute-start(f32[866,3,1]{0,1,2:T(4,128)S(1)} %copy.75), channel_id=1, source_target_pairs={{1,0},{2,1},{3,2},{4,3},{5,4},{6,5},{7,6},{9,8},{10,9},{11,10},{12... | collective-permute-start | bytes 31184 | tf_op jit(solution)/shard_map/ppermute | solution.py:23
  31.3 3.4 %collective-permute-start.2 = (f32[866,3,1]{0,1,2:T(4,128)S(1)}, f32[866,3,1]{0,1,2:T(4,128)S(1)}, u32[]{:S(2)}, u32[]{:S(2)}) collective-permute-start(f32[866,3,1]{0,1,2:T(4,128)S(1)} %copy.74), channel_id=1, source_target_pairs={{0,1},{1,2},{2,3},{3,4},{4,5},{5,6},{6,7},{8,9},{9,10},{10,11},{11... | collective-permute-start | bytes 31184 | tf_op jit(solution)/shard_map/ppermute | solution.py:20
  36.4 1.7 copy.55
  38.6 2.4 %collective-permute-start.7 = (f32[3,872,3]{1,2,0:T(4,128)S(1)}, f32[3,872,3]{1,2,0:T(4,128)S(1)}, u32[]{:S(2)}, u32[]{:S(2)}) collective-permute-start(f32[3,872,3]{1,2,0:T(4,128)S(1)} %copy.56), channel_id=1, source_target_pairs={{0,1},{1,2},{2,3},{3,4},{4,5},{5,6},{6,7},{8,9},{9,10},{10,11},{11... | collective-permute-start | bytes 94184 | tf_op jit(solution)/shard_map/ppermute | solution.py:68
  41.0 1.9 %collective-permute-start.6 = (f32[3,872,3]{1,2,0:T(4,128)S(1)}, f32[3,872,3]{1,2,0:T(4,128)S(1)}, u32[]{:S(2)}, u32[]{:S(2)}) collective-permute-start(f32[3,872,3]{1,2,0:T(4,128)S(1)} %copy.55), channel_id=1, source_target_pairs={{1,0},{2,1},{3,2},{4,3},{5,4},{6,5},{7,6},{9,8},{10,9},{11,10},{12... | collective-permute-start | bytes 94184 | tf_op jit(solution)/shard_map/ppermute | solution.py:69
  44.2 2.1 %collective-permute-done.6 = f32[3,872,3]{1,2,0:T(4,128)S(1)} collective-permute-done((f32[3,872,3]{1,2,0:T(4,128)S(1)}, f32[3,872,3]{1,2,0:T(4,128)S(1)}, u32[]{:S(2)}, u32[]{:S(2)}) %collective-permute-start.6) | collective-permute-done | bytes 31424 | tf_op jit(solution)/shard_map/ppermute | solution.py:69
  49.5 4.3 %fusion.7.diff_ref = f32[3,872,256]{2,1,0:T(8,128)} fusion(f32[3,2,128]{2,1,0:T(2,128)S(1)} %broadcast.62, f32[3,872,3]{2,1,0:T(8,128)} %copy.58, f32[3,872,3]{2,1,0:T(8,128)} %copy.57, f32[3,3,128]{2,1,0:T(4,128)S(1)} %collective-permute-done.5, f32[3,864,128]{2,1,0:T(8,128)} %bitcast.73, f32[3,3,128]{2,1,0:T(4,128)S(1)} %collective-permute-done.4, ...), kind=kLoop, calls=%fused_computation.8 | loop fusion | flops 4018176 | bytes 4081984 | tf_op jit(solution)/shard_map/concatenate | solution.py:71
  53.8 2.2 %copy.59 = f32[1024,640]{1,0:T(8,128)} copy(f32[1024,640]{0,1:T(8,128)S(1)} %copy-done.1) | data formatting | bytes 5242880 | tf_op jit(solution)/shard_map/optimization_barrier | solution.py:151
  56.0 12.6 %all-to-all-start = ((f32[128,8,640]{2,1,0:T(8,128)}), f32[128,8,640]{2,1,0:T(8,128)S(1)}, u32[]{:S(2)}, u32[]{:S(2)}) async-start(f32[128,8,640]{2,1,0:T(8,128)} %bitcast.69), calls=%async_computation | async-start | bytes 5242880 | tf_op jit(solution)/shard_map/all_to_all | solution.py:153
  68.6 2.8 %copy.62 = f32[864,3,128]{0,2,1:T(8,128)} copy(f32[864,3,128]{2,0,1:T(8,128)} %param.9) | data formatting | bytes 2654208 | tf_op args[0]
  71.4 32.9 %all-to-all-done = f32[128,8,640]{2,1,0:T(8,128)S(1)} async-done(((f32[128,8,640]{2,1,0:T(8,128)}), f32[128,8,640]{2,1,0:T(8,128)S(1)}, u32[]{:S(2)}, u32[]{:S(2)}) %all-to-all-start) | async-done | bytes 2621472 | tf_op jit(solution)/shard_map/all_to_all | solution.py:153
  105.9 1.9 %copy.61 = f32[1024,384]{0,1:T(8,128)S(1)} copy(f32[1024,384]{1,0:T(8,128)} %slice.127) | data formatting | bytes 3145728 | tf_op jit(solution)/shard_map/slice | solution.py:159
  108.0 7.0 %fusion.3 = f32[1024,3,128]{0,2,1:T(8,128)S(1)} fusion(s32[1024]{0:T(1024)S(1)} %convert_element_type.32, f32[866,3,130]{0,2,1:T(8,128)} %pad_maximum_fusion.5, f32[864,3,128]{0,2,1:T(8,128)} %copy.62), kind=kOutput, calls=%fused_computation.5 | convolution fusion | flops 4079738880 | bytes 8458240 | tf_op jit(solution)/shard_map/dot_general | solution.py:50
  117.2 1.9 %copy.68 = f32[1024,3,128]{2,1,0:T(4,128)S(1)} copy(f32[1024,3,128]{0,2,1:T(8,128)} %maximum_multiply_fusion) | data formatting | bytes 3145728 | tf_op jit(solution)/shard_map/mul | solution.py:161
  119.2 1.8 %mul.137 = f32[128,8,384]{2,1,0:T(8,128)} reshape(f32[1024,3,128]{2,1,0:T(4,128)S(1)} %copy.68) | data formatting | bytes 3145728 | tf_op jit(solution)/shard_map/mul | solution.py:161
  120.9 4.9 %all-to-all-start.1 = ((f32[128,8,384]{2,1,0:T(8,128)}), f32[128,8,384]{2,1,0:T(8,128)S(1)}, u32[]{:S(2)}, u32[]{:S(2)}) async-start(f32[128,8,384]{2,1,0:T(8,128)} %mul.137), calls=%async_computation.1 | async-start | bytes 3145728 | tf_op jit(solution)/shard_map/all_to_all | solution.py:166
  125.9 4.3 %fusion.27 = f32[3,864,128]{2,1,0:T(8,128)S(1)} fusion(f32[864,3,128]{2,0,1:T(8,128)} %param.9, f32[1024,3,128]{0,2,1:T(8,128)S(1)} %copy-done.4, s32[1024]{0:T(1024)S(1)} %convert_element_type.32, f32[3]{0:T(128)S(1)} %copy-done.13), kind=kOutput, calls=%fused_computation.26 | convolution fusion | flops 4078411776 | bytes 4231180 | tf_op jit(solution)/shard_map/dot_general | solution.py:50
  130.2 3.3 %collective-permute-start.8 = (f32[3,3,128]{2,1,0:T(4,128)S(1)}, f32[3,3,128]{2,1,0:T(4,128)S(1)}, u32[]{:S(2)}, u32[]{:S(2)}) collective-permute-start(f32[3,3,128]{2,1,0:T(4,128)S(1)} %get-tuple-element.20), channel_id=1, source_target_pairs={{0,8},{8,16},{16,24},{24,32},{32,40},{40,48},{48,56},{56,64},{64,7... | collective-permute-start | bytes 13832 | tf_op jit(solution)/shard_map/ppermute | solution.py:60
  134.8 6.6 %collective-permute-done.8 = f32[3,3,128]{2,1,0:T(4,128)S(1)} collective-permute-done((f32[3,3,128]{2,1,0:T(4,128)S(1)}, f32[3,3,128]{2,1,0:T(4,128)S(1)}, u32[]{:S(2)}, u32[]{:S(2)}) %collective-permute-start.8) | collective-permute-done | bytes 4640 | tf_op jit(solution)/shard_map/ppermute | solution.py:60
  141.4 2.9 %collective-permute-done.9 = f32[3,3,128]{2,1,0:T(4,128)S(1)} collective-permute-done((f32[3,3,128]{2,1,0:T(4,128)S(1)}, f32[3,3,128]{2,1,0:T(4,128)S(1)}, u32[]{:S(2)}, u32[]{:S(2)}) %collective-permute-start.9) | collective-permute-done | bytes 4640 | tf_op jit(solution)/shard_map/ppermute | solution.py:61
  145.9 1.7 copy.64
  147.7 2.8 %collective-permute-start.10 = (f32[3,872,3]{1,2,0:T(4,128)S(1)}, f32[3,872,3]{1,2,0:T(4,128)S(1)}, u32[]{:S(2)}, u32[]{:S(2)}) collective-permute-start(f32[3,872,3]{1,2,0:T(4,128)S(1)} %copy.64), channel_id=1, source_target_pairs={{1,0},{2,1},{3,2},{4,3},{5,4},{6,5},{7,6},{9,8},{10,9},{11,10},{12... | collective-permute-start | bytes 94184 | tf_op jit(solution)/shard_map/ppermute | solution.py:69
  150.9 3.6 %collective-permute-start.11 = (f32[3,872,3]{1,2,0:T(4,128)S(1)}, f32[3,872,3]{1,2,0:T(4,128)S(1)}, u32[]{:S(2)}, u32[]{:S(2)}) collective-permute-start(f32[3,872,3]{1,2,0:T(4,128)S(1)} %copy.65), channel_id=1, source_target_pairs={{0,1},{1,2},{2,3},{3,4},{4,5},{5,6},{6,7},{8,9},{9,10},{10,11},{11... | collective-permute-start | bytes 94184 | tf_op jit(solution)/shard_map/ppermute | solution.py:68
  157.7 3.7 %fusion.10.state_ref = f32[3,872,256]{2,1,0:T(8,128)} fusion(f32[3,2,128]{2,1,0:T(2,128)S(1)} %broadcast.62, f32[3,872,3]{2,1,0:T(8,128)} %copy.67, f32[3,872,3]{2,1,0:T(8,128)} %copy.66, f32[3,3,128]{2,1,0:T(4,128)S(1)} %collective-permute-done.9, f32[3,864,128]{2,1,0:T(8,128)S(1)} %copy-done.7, f32[3,3,128]{2,1,0:T(4,128)S(1)} %collective-permute-done.8, ...), kind=kLoop, calls=%fused_computation.11 | loop fusion | flops 4018176 | bytes 4081984 | tf_op jit(solution)/shard_map/concatenate | solution.py:71
  161.4 8.1 %shard_map.104 = f32[3,864,128]{2,1,0:T(8,128)} custom-call(f32[3,872,256]{2,1,0:T(8,128)} %fusion.10.state_ref, f32[3,872,256]{2,1,0:T(8,128)} %fusion.7.diff_ref), custom_call_target="tpu_custom_call" | custom-call | tf_op jit(solution)/shard_map/pallas_call | solution.py:94
  171.2 5.6 %fusion.43 = f32[256,3,128]{2,0,1:T(8,128)} fusion(f32[3,128,1024]{2,1,0:T(8,128)} %bitcast.71, f32[1024,256]{1,0:T(8,128)S(1)} %copy-done.3), kind=kOutput, calls=%fused_computation.40 | convolution fusion | flops 1207959552 | bytes 3014656 | tf_op jit(solution)/shard_map/dot_general | solution.py:50
  (90 shorter events, 30.1 us)
Async XLA Ops:
  0.6 14.3 %copy-start = (f32[512,128]{1,0:T(8,128)S(1)}, f32[512,128]{1,0:T(8,128)}, u32[]{:S(2)}) copy-start(f32[512,128]{1,0:T(8,128)} %param.13) | copy-start | bytes 786436
  0.6 13.9 %copy-start.11 = (s32[512,1]{0,1:T(1,128)S(1)}, s32[512,1]{0,1:T(1,128)}, u32[]{:S(2)}) copy-start(s32[512,1]{0,1:T(1,128)} %param.15) | copy-start | bytes 6148
  0.7 14.1 %copy-start.9 = (f32[256,3,128]{2,0,1:T(8,128)S(1)}, f32[256,3,128]{2,0,1:T(8,128)}, u32[]{:S(2)}) copy-start(f32[256,3,128]{2,0,1:T(8,128)} %param.11) | copy-start | bytes 1179652
  1.5 20.1 %collective-permute-start = (f32[1,3,128]{2,0,1:T(1,128)S(1)}, f32[1,3,128]{2,0,1:T(1,128)S(1)}, u32[]{:S(2)}, u32[]{:S(2)}) collective-permute-start(f32[1,3,128]{2,0,1:T(1,128)S(1)} %get-tuple-element.24), channel_id=1, source_target_pairs={{0,8},{8,16},{16,24},{24,32},{32,40},{40,48},{48,56},{56,64},{64,7... | collective-permute-start | bytes 4616 | tf_op jit(solution)/shard_map/ppermute | solution.py:20
  5.4 16.2 %collective-permute-start.1 = (f32[1,3,128]{2,0,1:T(1,128)S(1)}, f32[1,3,128]{2,0,1:T(1,128)S(1)}, u32[]{:S(2)}, u32[]{:S(2)}) collective-permute-start(f32[1,3,128]{2,0,1:T(1,128)S(1)} %get-tuple-element.25), channel_id=1, source_target_pairs={{8,0},{16,8},{24,16},{32,24},{40,32},{48,40},{56,48},{64,56},{72,6... | collective-permute-start | bytes 4616 | tf_op jit(solution)/shard_map/ppermute | solution.py:23
  7.4 27.3 %collective-permute-start.4 = (f32[3,3,128]{2,1,0:T(4,128)S(1)}, f32[3,3,128]{2,1,0:T(4,128)S(1)}, u32[]{:S(2)}, u32[]{:S(2)}) collective-permute-start(f32[3,3,128]{2,1,0:T(4,128)S(1)} %get-tuple-element.22), channel_id=1, source_target_pairs={{0,8},{8,16},{16,24},{24,32},{32,40},{40,48},{48,56},{56,64},{64,7... | collective-permute-start | bytes 13832 | tf_op jit(solution)/shard_map/ppermute | solution.py:60
  11.4 23.4 %collective-permute-start.5 = (f32[3,3,128]{2,1,0:T(4,128)S(1)}, f32[3,3,128]{2,1,0:T(4,128)S(1)}, u32[]{:S(2)}, u32[]{:S(2)}) collective-permute-start(f32[3,3,128]{2,1,0:T(4,128)S(1)} %get-tuple-element.23), channel_id=1, source_target_pairs={{8,0},{16,8},{24,16},{32,24},{40,32},{48,40},{56,48},{64,56},{72,6... | collective-permute-start | bytes 13832 | tf_op jit(solution)/shard_map/ppermute | solution.py:61
  16.5 0.7 copy-start.12
  17.8 1.5 copy-start.2
  17.8 1.5 copy-start.10
  19.7 1.9 %copy-start.8 = (f32[864,3,128]{2,0,1:T(8,128)S(1)}, f32[864,3,128]{2,0,1:T(8,128)}, u32[]{:S(2)}) copy-start(f32[864,3,128]{2,0,1:T(8,128)} %param.9) | copy-start | bytes 3981316
  24.0 10.8 %copy-start.5 = (f32[864,3,128]{2,0,1:T(8,128)S(1)}, f32[864,3,128]{2,0,1:T(8,128)}, u32[]{:S(2)}) copy-start(f32[864,3,128]{2,0,1:T(8,128)} %param.10) | copy-start | bytes 3981316
  27.9 15.1 %collective-permute-start.3 = (f32[866,3,1]{0,1,2:T(4,128)S(1)}, f32[866,3,1]{0,1,2:T(4,128)S(1)}, u32[]{:S(2)}, u32[]{:S(2)}) collective-permute-start(f32[866,3,1]{0,1,2:T(4,128)S(1)} %copy.75), channel_id=1, source_target_pairs={{1,0},{2,1},{3,2},{4,3},{5,4},{6,5},{7,6},{9,8},{10,9},{11,10},{12... | collective-permute-start | bytes 31184 | tf_op jit(solution)/shard_map/ppermute | solution.py:23
  31.3 11.7 %collective-permute-start.2 = (f32[866,3,1]{0,1,2:T(4,128)S(1)}, f32[866,3,1]{0,1,2:T(4,128)S(1)}, u32[]{:S(2)}, u32[]{:S(2)}) collective-permute-start(f32[866,3,1]{0,1,2:T(4,128)S(1)} %copy.74), channel_id=1, source_target_pairs={{0,1},{1,2},{2,3},{3,4},{4,5},{5,6},{6,7},{8,9},{9,10},{10,11},{11... | collective-permute-start | bytes 31184 | tf_op jit(solution)/shard_map/ppermute | solution.py:20
  38.6 9.3 %collective-permute-start.7 = (f32[3,872,3]{1,2,0:T(4,128)S(1)}, f32[3,872,3]{1,2,0:T(4,128)S(1)}, u32[]{:S(2)}, u32[]{:S(2)}) collective-permute-start(f32[3,872,3]{1,2,0:T(4,128)S(1)} %copy.56), channel_id=1, source_target_pairs={{0,1},{1,2},{2,3},{3,4},{4,5},{5,6},{6,7},{8,9},{9,10},{10,11},{11... | collective-permute-start | bytes 94184 | tf_op jit(solution)/shard_map/ppermute | solution.py:68
  41.0 5.3 %collective-permute-start.6 = (f32[3,872,3]{1,2,0:T(4,128)S(1)}, f32[3,872,3]{1,2,0:T(4,128)S(1)}, u32[]{:S(2)}, u32[]{:S(2)}) collective-permute-start(f32[3,872,3]{1,2,0:T(4,128)S(1)} %copy.55), channel_id=1, source_target_pairs={{1,0},{2,1},{3,2},{4,3},{5,4},{6,5},{7,6},{9,8},{10,9},{11,10},{12... | collective-permute-start | bytes 94184 | tf_op jit(solution)/shard_map/ppermute | solution.py:69
  49.5 4.3 %copy-start.1 = (f32[1024,640]{0,1:T(8,128)S(1)}, f32[1024,640]{0,1:T(8,128)}, u32[]{:S(2)}) copy-start(f32[1024,640]{0,1:T(8,128)} %pad_maximum_fusion.2) | copy-start | bytes 7864324
  56.0 48.3 %all-to-all-start = ((f32[128,8,640]{2,1,0:T(8,128)}), f32[128,8,640]{2,1,0:T(8,128)S(1)}, u32[]{:S(2)}, u32[]{:S(2)}) async-start(f32[128,8,640]{2,1,0:T(8,128)} %bitcast.69), calls=%async_computation | async-start | bytes 5242880 | tf_op jit(solution)/shard_map/all_to_all | solution.py:153
  120.9 4.9 %copy-start.4 = (f32[1024,3,128]{0,2,1:T(8,128)S(1)}, f32[1024,3,128]{0,2,1:T(8,128)}, u32[]{:S(2)}) copy-start(f32[1024,3,128]{0,2,1:T(8,128)} %maximum_multiply_fusion) | copy-start | bytes 4718596
  120.9 4.9 %copy-start.13 = (f32[3]{0:T(128)S(1)}, f32[3]{0:T(128)}, u32[]{:S(2)}) copy-start(f32[3]{0:T(128)} %constant.55.clone) | copy-start | bytes 40
  120.9 48.6 %all-to-all-start.1 = ((f32[128,8,384]{2,1,0:T(8,128)}), f32[128,8,384]{2,1,0:T(8,128)S(1)}, u32[]{:S(2)}, u32[]{:S(2)}) async-start(f32[128,8,384]{2,1,0:T(8,128)} %mul.137), calls=%async_computation.1 | async-start | bytes 3145728 | tf_op jit(solution)/shard_map/all_to_all | solution.py:166
  130.2 14.1 %copy-start.6 = (f32[3,864,128]{2,1,0:T(8,128)}, f32[3,864,128]{2,1,0:T(8,128)S(1)}, u32[]{:S(2)}) copy-start(f32[3,864,128]{2,1,0:T(8,128)S(1)} %fusion.27) | copy-start | bytes 3981316
  130.2 11.2 %collective-permute-start.8 = (f32[3,3,128]{2,1,0:T(4,128)S(1)}, f32[3,3,128]{2,1,0:T(4,128)S(1)}, u32[]{:S(2)}, u32[]{:S(2)}) collective-permute-start(f32[3,3,128]{2,1,0:T(4,128)S(1)} %get-tuple-element.20), channel_id=1, source_target_pairs={{0,8},{8,16},{16,24},{24,32},{32,40},{40,48},{48,56},{56,64},{64,7... | collective-permute-start | bytes 13832 | tf_op jit(solution)/shard_map/ppermute | solution.py:60
  133.5 10.8 %collective-permute-start.9 = (f32[3,3,128]{2,1,0:T(4,128)S(1)}, f32[3,3,128]{2,1,0:T(4,128)S(1)}, u32[]{:S(2)}, u32[]{:S(2)}) collective-permute-start(f32[3,3,128]{2,1,0:T(4,128)S(1)} %get-tuple-element.21), channel_id=1, source_target_pairs={{8,0},{16,8},{24,16},{32,24},{40,32},{48,40},{56,48},{64,56},{72,6... | collective-permute-start | bytes 13832 | tf_op jit(solution)/shard_map/ppermute | solution.py:61
  147.7 6.9 %collective-permute-start.10 = (f32[3,872,3]{1,2,0:T(4,128)S(1)}, f32[3,872,3]{1,2,0:T(4,128)S(1)}, u32[]{:S(2)}, u32[]{:S(2)}) collective-permute-start(f32[3,872,3]{1,2,0:T(4,128)S(1)} %copy.64), channel_id=1, source_target_pairs={{1,0},{2,1},{3,2},{4,3},{5,4},{6,5},{7,6},{9,8},{10,9},{11,10},{12... | collective-permute-start | bytes 94184 | tf_op jit(solution)/shard_map/ppermute | solution.py:69
  150.9 6.8 %copy-start.7 = (f32[3,864,128]{2,1,0:T(8,128)S(1)}, f32[3,864,128]{2,1,0:T(8,128)}, u32[]{:S(2)}) copy-start(f32[3,864,128]{2,1,0:T(8,128)} %copy-done.6) | copy-start | bytes 3981316
  150.9 5.2 %collective-permute-start.11 = (f32[3,872,3]{1,2,0:T(4,128)S(1)}, f32[3,872,3]{1,2,0:T(4,128)S(1)}, u32[]{:S(2)}, u32[]{:S(2)}) collective-permute-start(f32[3,872,3]{1,2,0:T(4,128)S(1)} %copy.65), channel_id=1, source_target_pairs={{0,1},{1,2},{2,3},{3,4},{4,5},{5,6},{6,7},{8,9},{9,10},{10,11},{11... | collective-permute-start | bytes 94184 | tf_op jit(solution)/shard_map/ppermute | solution.py:68
  169.5 1.6 copy-start.3

commit v2 on v1

--- a/solution.py
+++ b/solution.py
@@ -87,6 +87,28 @@
             )
             state = state + diff * (around - 4.0 * state)
         out_ref[chan] = state[HALO : HALO + rows, :width]
+
+
+def smooth_kernel(rows, width, state_ref, out_ref):
+    rows_padded, lanes = state_ref.shape[1], state_ref.shape[2]
+    for chan in range(out_ref.shape[0]):
+        state = state_ref[chan]
+        around = (
+            pltpu.roll(state, rows_padded - 1, 0)
+            + pltpu.roll(state, 1, 0)
+            + pltpu.roll(state, lanes - 1, 1)
+            + pltpu.roll(state, 1, 1)
+        )
+        out_ref[chan] = (0.5 * state + 0.125 * around)[HALO : HALO + rows, :width]
+
+
+def smooth(state_ext, chans, rows, width):
+    return pl.pallas_call(
+        functools.partial(smooth_kernel, rows, width),
+        out_shape=jax.ShapeDtypeStruct((chans, rows, width), jnp.float32),
+        in_specs=[pl.BlockSpec(memory_space=pltpu.VMEM)],
+        out_specs=pl.BlockSpec(memory_space=pltpu.VMEM),
+    )(state_ext)
 
 
 def diffuse(state_ext, diff_ext, rows, width):
@@ -120,9 +142,6 @@
     rows_padded = -(-(row_count + 2 * HALO) // 8) * 8
     lanes = 2 * seg_width
 
-    diff_ext = planes_with_halo(jnp.transpose(diffusivity, (1, 0, 2)), rows_padded, lanes)
-    padded = with_halo(atm_state, (("atm", 0), ("ocn", 2)), 1)
-
     target = intersection_dest[:, 0]
     matches = (target[:, None] == jnp.arange(devices, dtype=jnp.int32)[None, :]).astype(jnp.int32)
     position = jnp.sum((jnp.cumsum(matches, axis=0) - matches) * matches, axis=1)
@@ -148,26 +167,44 @@
     out_area = select_rows(slot_pick.astype(jnp.float32), intersection_area)
     out_weight = out_area * out_mask
     outgoing = jnp.concatenate([out_ocean, out_weight, out_label], axis=1)
-    outgoing, padded, diff_ext = lax.optimization_barrier((outgoing, padded, diff_ext))
-    smoothed = 0.5 * atm_state + 0.125 * beside_all(padded)
     incoming = lax.all_to_all(outgoing, ("atm", "ocn"), split_axis=0, concat_axis=0, tiled=True)
+
+    atm_planes = jnp.transpose(atm_state, (1, 0, 2))
+    both = jnp.concatenate([atm_planes, jnp.transpose(diffusivity, (1, 0, 2))], axis=0)
+    both_ext = planes_with_halo(both, rows_padded, lanes)
+    diff_ext = both_ext[chan_count:]
+    smoothed = smooth(both_ext, chan_count, row_count, seg_width)
+
     in_labels = jnp.max(incoming[:, plane + seg_width :], axis=1).astype(jnp.int32)
     row_pick = (
         jnp.arange(row_count, dtype=jnp.int32)[:, None] == in_labels[None, :]
     ).astype(jnp.float32)
-    air_rows = select_rows(row_pick.T, smoothed.reshape(row_count, plane))
-    in_ocean = incoming[:, :plane].reshape(slots, chan_count, seg_width)
+    pick_rows = row_pick.T
+    air = [jnp.dot(pick_rows, smoothed[c], precision=HIGHEST, preferred_element_type=jnp.float32)
+           for c in range(chan_count)]
+    ocean = [incoming[:, c * seg_width : (c + 1) * seg_width] for c in range(chan_count)]
     in_weight = incoming[:, plane : plane + seg_width]
-    weighted = in_weight[:, None, :] * fluxes(
-        in_ocean, air_rows.reshape(slots, chan_count, seg_width)
-    )
-    weighted = weighted.reshape(slots, plane)
-    air_sum = select_rows(row_pick, weighted).reshape(row_count, chan_count, seg_width)
-    returned = lax.all_to_all(weighted, ("atm", "ocn"), split_axis=0, concat_axis=0, tiled=True)
+    wind_east = air[1] - ocean[1]
+    wind_north = air[2] - ocean[2]
+    wind_speed = jnp.sqrt(wind_east * wind_east + wind_north * wind_north + 0.5)
+    temp_gap = ocean[0] - air[0]
+    factor = 1.0 + 0.5 * jnp.tanh(temp_gap / wind_speed)
+    weighted = [
+        in_weight * (0.8 * factor * wind_speed * temp_gap),
+        in_weight * (0.6 * factor * wind_speed * wind_east),
+        in_weight * (0.6 * factor * wind_speed * wind_north),
+    ]
+    returned = lax.all_to_all(
+        jnp.concatenate(weighted, axis=1), ("atm", "ocn"), split_axis=0, concat_axis=0, tiled=True
+    )
     ocean_flux = select_rows(slot_seg.T, returned).reshape(seg_count, chan_count, seg_width)
-    direction_sign = jnp.array([1.0, -1.0, -1.0], dtype=jnp.float32)[None, :, None]
-    forced = atm_state + direction_sign * air_sum
-    state_ext = planes_with_halo(jnp.transpose(forced, (1, 0, 2)), rows_padded, lanes)
+    signs = (1.0, -1.0, -1.0)
+    forced = jnp.stack(
+        [atm_planes[c] + signs[c] * jnp.dot(row_pick, weighted[c], precision=HIGHEST,
+                                             preferred_element_type=jnp.float32)
+         for c in range(chan_count)]
+    )
+    state_ext = planes_with_halo(forced, rows_padded, lanes)
     current = diffuse(state_ext, diff_ext, row_count, seg_width)
     return (jnp.transpose(current, (1, 0, 2)), ocean_flux)
 

time: 178 us -> 168 us (0.944)
  waiting for transfers between devices: 44.5 us -> 31.2 us
  starting transfers between devices: 50.2 us -> 42.3 us
  matrix products: 21.1 us -> 28 us
  Pallas kernels: 8.1 us -> 13.1 us
    all_to_all x1, waiting for transfers between devices: 32.9 us -> 0.01 us  [per_device(): lax.all_to_all(outgoing, ('atm', 'ocn'), split_axis=0, concat_axis=0, til...]
    ppermute x2, waiting for transfers between devices: 6.56 us -> 25.3 us  [planes_with_halo(): up = lax.ppermute(block[:, rows - HALO:, :], 'atm', fwd)]
    dot_general x0 -> x6, matrix products: none -> 17.5 us  [the longest x3 10 us: per_device(): jnp.dot(pick_rows, smoothed[c], precision=HIGHEST, preferred_element_type...]
    ppermute x4 -> x0, starting transfers between devices: 12.1 us -> none  [the longest x2 7.37 us: with_halo(): lax.ppermute(lax.slice_in_dim(block, block.shape[dim] - width, None, axis...]
    dot_general x6 -> x4, matrix products: 19.9 us -> 8.64 us  [select_rows(): jnp.dot(chosen, flat, precision=precision, preferred_element_type=jnp.flo...]
    pallas_call x0 -> x1, Pallas kernels: none -> 5.04 us  [smooth(): pl.pallas_call(functools.partial(smooth_kernel, rows, width), out_shape=j...]
    all_to_all x1, starting transfers between devices: 4.9 us -> 9.03 us  [per_device(): lax.all_to_all(jnp.concatenate(weighted, axis=1), ('atm', 'ocn'), split_a...]
    mul x2 -> x0, local copies, waits for them, and re-layouts: 3.71 us -> none  [per_device(): in_weight[:, None, :]]
  transfers between devices with their start and end apart: 14 -> 10, of which waited for: 4 -> 4; matrix products, arithmetic and copies ran while one was open for 23% -> 25% of each run, Pallas kernels for 5% -> 8%
where the time goes in v2:
time: 168 us; the launch traced here: 167 us
  starting transfers between devices  42.3 us (25%)
  local copies, waits for them, and re-layouts  36.7 us (22%)
  waiting for transfers between devices  31.2 us (19%)
  matrix products  28 us (17%)
  other arithmetic  14.6 us (9%)
  Pallas kernels  13.1 us (8%)
    ppermute x2, waiting for transfers between devices, planes_with_halo(): up = lax.ppermute(block[:, rows - HALO:, :], 'atm', fwd)  25.3 us
    all_to_all x1, starting transfers between devices, per_device(): lax.all_to_all(outgoing, ('atm', 'ocn'), split_axis=0, concat_axis=0, til...  11.9 us
    dot_general x3, matrix products, per_device(): jnp.dot(pick_rows, smoothed[c], precision=HIGHEST, preferred_element_type...  10 us
    slice x4, local copies, waits for them, and re-layouts, planes_with_halo(): right = lax.ppermute(tall[:, :, :HALO], 'ocn', bwd)  9.61 us
    concatenate x2, other arithmetic, planes_with_halo(): jnp.concatenate([tall, right, jnp.zeros((chans, rows_padded, gap), block....  9.35 us
    all_to_all x1, starting transfers between devices, per_device(): lax.all_to_all(jnp.concatenate(weighted, axis=1), ('atm', 'ocn'), split_a...  9.03 us
    dot_general x4, matrix products, select_rows(): jnp.dot(chosen, flat, precision=precision, preferred_element_type=jnp.flo...  8.64 us
    pallas_call x1, Pallas kernels, diffuse(): pl.pallas_call(functools.partial(diffuse_kernel, rows, width), out_shape=...  8.1 us
  transfers between devices with their start and end apart: 10, of which 4 were waited for; matrix products, arithmetic and copies ran while one was open for 25% of the time, Pallas kernels for 8%

profile of v2, /device:TPU:1, one launch (start us, length us, event | category | flops | bytes accessed | tf_op | source)
XLA Modules:
  0.0 167.1 jit_solution(5253201037639995517)
XLA Ops:
  9.2 2.1 %copy.26 = f32[1024,640]{1,0:T(8,128)} copy(f32[1024,640]{0,1:T(8,128)S(1)} %pad_maximum_fusion.3) | data formatting | bytes 5242880 | tf_op jit(solution)/shard_map/concatenate | solution.py:169
  11.3 11.9 %all-to-all-start = ((f32[128,8,640]{2,1,0:T(8,128)}), f32[128,8,640]{2,1,0:T(8,128)}, u32[]{:S(2)}, u32[]{:S(2)}) async-start(f32[128,8,640]{2,1,0:T(8,128)} %bitcast.75), calls=%async_computation | async-start | bytes 5242880 | tf_op jit(solution)/shard_map/all_to_all | solution.py:170
  23.2 3.3 %collective-permute-start = (f32[6,3,128]{2,1,0:T(4,128)S(1)}, f32[6,3,128]{2,1,0:T(4,128)S(1)}, u32[]{:S(2)}, u32[]{:S(2)}) collective-permute-start(f32[6,3,128]{2,1,0:T(4,128)S(1)} %get-tuple-element.4), channel_id=1, source_target_pairs={{0,8},{8,16},{16,24},{24,32},{32,40},{40,48},{48,56},{56,64},{64,7... | collective-permute-start | bytes 27656 | tf_op jit(solution)/shard_map/ppermute | solution.py:60
  27.8 22.0 %collective-permute-done = f32[6,3,128]{2,1,0:T(4,128)S(1)} collective-permute-done((f32[6,3,128]{2,1,0:T(4,128)S(1)}, f32[6,3,128]{2,1,0:T(4,128)S(1)}, u32[]{:S(2)}, u32[]{:S(2)}) %collective-permute-start) | collective-permute-done | bytes 9248 | tf_op jit(solution)/shard_map/ppermute | solution.py:60
  49.8 2.9 %collective-permute-done.1 = f32[6,3,128]{2,1,0:T(4,128)S(1)} collective-permute-done((f32[6,3,128]{2,1,0:T(4,128)S(1)}, f32[6,3,128]{2,1,0:T(4,128)S(1)}, u32[]{:S(2)}, u32[]{:S(2)}) %collective-permute-start.1) | collective-permute-done | bytes 9248 | tf_op jit(solution)/shard_map/ppermute | solution.py:61
  52.9 3.1 %fusion.45 = (f32[6,872,3]{2,1,0:T(8,128)}, f32[6,872,3]{2,1,0:T(8,128)}) fusion(f32[6,872,128]{2,1,0:T(8,128)S(1)} %pad_maximum_fusion.1), kind=kLoop, calls=%fused_computation.88 | loop fusion | bytes 251136 | tf_op jit(solution)/shard_map/slice | solution.py:69
  56.1 2.8 %copy.29 = f32[6,872,3]{1,0,2:T(8,128)S(1)} copy(f32[6,872,3]{2,1,0:T(8,128)} %get-tuple-element.2) | data formatting | bytes 125568 | tf_op jit(solution)/shard_map/slice | solution.py:69
  58.9 2.7 %collective-permute-start.2 = (f32[6,872,3]{1,0,2:T(8,128)S(1)}, f32[6,872,3]{1,0,2:T(8,128)S(1)}, u32[]{:S(2)}, u32[]{:S(2)}) collective-permute-start(f32[6,872,3]{1,0,2:T(8,128)S(1)} %copy.29), channel_id=1, source_target_pairs={{1,0},{2,1},{3,2},{4,3},{5,4},{6,5},{7,6},{9,8},{10,9},{11,10},{12... | collective-permute-start | bytes 188360 | tf_op jit(solution)/shard_map/ppermute | solution.py:69
  61.6 2.8 %copy.30 = f32[6,872,3]{1,0,2:T(8,128)S(1)} copy(f32[6,872,3]{2,1,0:T(8,128)} %get-tuple-element.3) | data formatting | bytes 125568 | tf_op jit(solution)/shard_map/slice | solution.py:68
  64.4 3.3 %collective-permute-start.3 = (f32[6,872,3]{1,0,2:T(8,128)S(1)}, f32[6,872,3]{1,0,2:T(8,128)S(1)}, u32[]{:S(2)}, u32[]{:S(2)}) collective-permute-start(f32[6,872,3]{1,0,2:T(8,128)S(1)} %copy.30), channel_id=1, source_target_pairs={{0,1},{1,2},{2,3},{3,4},{4,5},{5,6},{6,7},{8,9},{9,10},{10,11},{11... | collective-permute-start | bytes 188360 | tf_op jit(solution)/shard_map/ppermute | solution.py:68
  67.8 2.3 %copy.31 = f32[6,872,3]{2,1,0:T(8,128)} copy(f32[6,872,3]{1,0,2:T(8,128)S(1)} %collective-permute-done.2) | data formatting | bytes 125568 | tf_op jit(solution)/shard_map/ppermute | solution.py:69
  70.1 2.4 %copy.32 = f32[6,872,3]{2,1,0:T(8,128)} copy(f32[6,872,3]{1,0,2:T(8,128)S(1)} %collective-permute-done.3) | data formatting | bytes 125568 | tf_op jit(solution)/shard_map/ppermute | solution.py:68
  72.5 5.5 %pad_maximum_fusion.state_ref = f32[6,872,256]{2,1,0:T(8,128)} fusion(f32[6,872,3]{2,1,0:T(8,128)} %copy.32, f32[6,872,3]{2,1,0:T(8,128)} %copy.31, f32[6,2,128]{2,1,0:T(2,128)S(1)} %broadcast_in_dim.14, f32[6,3,128]{2,1,0:T(4,128)S(1)} %collective-permute-done.1, f32[3,864,128]{2,1,0:T(8,128)S(1)} %bitcast.68, f32[3,864,128]{2,1,0:T(8,128)S(1)} %bitcast.71, ...), kind=kLoop, calls=%fused_computation | loop fusion | flops 9375744 | bytes 8162944 | tf_op jit(solution)/shard_map/concatenate | solution.py:71
  78.0 5.0 %shard_map.95 = f32[3,864,128]{2,1,0:T(8,128)} custom-call(f32[6,872,256]{2,1,0:T(8,128)} %pad_maximum_fusion.state_ref), custom_call_target="tpu_custom_call" | custom-call | tf_op jit(solution)/shard_map/pallas_call | solution.py:106
  83.0 2.8 %fusion.46 = (f32[1024,128]{1,0:T(8,128)}, f32[1024,128]{1,0:T(8,128)S(1)}, f32[1024,128]{1,0:T(8,128)S(1)}, f32[1024,128]{1,0:T(8,128)S(1)}, f32[1024]{0:T(1024)S(1)}) fusion(f32[1024,640]{1,0:T(8,128)} %bitcast.9), kind=kLoop, calls=%fused_computation.89 | loop fusion | flops 130048 | bytes 4722688 | tf_op jit(solution)/shard_map/slice | solution.py:185
  85.8 2.1 %copy.46 = f32[1024,128]{0,1:T(8,128)} copy(f32[1024,128]{1,0:T(8,128)} %get-tuple-element.6) | data formatting | bytes 1048576
  88.9 3.4 %fusion.16 = f32[1024,128]{0,1:T(8,128)} fusion(f32[1024,128]{0,1:T(8,128)} %copy.46, s32[1024]{0:T(1024)S(1)} %convert_element_type.32, f32[3,864,128]{2,1,0:T(8,128)} %shard_map.95), kind=kOutput, calls=%fused_computation.25 | convolution fusion | flops 1359970304 | bytes 1495040 | tf_op jit(solution)/shard_map/dot_general | solution.py:183
  92.3 3.4 %fusion.17 = f32[1024,128]{0,1:T(8,128)} fusion(f32[1024,128]{0,1:T(8,128)} %copy.47, s32[1024]{0:T(1024)S(1)} %convert_element_type.32, f32[3,864,128]{2,1,0:T(8,128)} %shard_map.95), kind=kOutput, calls=%fused_computation.26 | convolution fusion | flops 1359970304 | bytes 1495040 | tf_op jit(solution)/shard_map/dot_general | solution.py:183
  96.1 3.2 %multiply_multiply_fusion.3 = (f32[1024,128]{0,1:T(8,128)S(1)}, f32[1024,128]{0,1:T(8,128)S(1)}, f32[1024,128]{0,1:T(8,128)S(1)}) fusion(f32[1024,128]{0,1:T(8,128)S(1)} %copy.44, f32[1024,128]{0,1:T(8,128)} %fusion.17, f32[1024,128]{0,1:T(8,128)} %fusion.16, f32[1024,128]{0,1:T(8,128)S(1)} %copy.45, f32[3,864,128]{2,1,0:T(8,128)} %shard_map.95, ...), kind=kOutput, calls=%fused_computation.46 | convolution fusion | flops 1362198528 | bytes 4116480 | tf_op jit(solution)/shard_map/dot_general | solution.py:183
  102.2 9.0 %all-to-all-start.1 = ((f32[128,8,384]{2,1,0:T(8,128)}), f32[128,8,384]{2,1,0:T(8,128)S(1)}, u32[]{:S(2)}, u32[]{:S(2)}) async-start(f32[128,8,384]{2,1,0:T(8,128)} %bitcast.77), calls=%async_computation.1 | async-start | bytes 3145728 | tf_op jit(solution)/shard_map/all_to_all | solution.py:197
  111.2 2.8 %fusion.19 = f32[1,864,128]{2,1,0:T(8,128)S(1)} fusion(f32[1024,128]{0,1:T(8,128)} %copy-done.14, s32[1024]{0:T(1024)S(1)} %convert_element_type.32, f32[3,864,128]{2,1,0:T(8,128)S(1)} %bitcast.72), kind=kOutput, calls=%fused_computation.28 | convolution fusion | flops 1359949824 | bytes 1413120 | tf_op jit(solution)/shard_map/dot_general | solution.py:203
  114.1 2.9 %fusion.22 = f32[1,864,128]{2,1,0:T(8,128)S(1)} fusion(f32[1024,128]{0,1:T(8,128)} %copy-done.13, s32[1024]{0:T(1024)S(1)} %convert_element_type.32, f32[3,864,128]{2,1,0:T(8,128)S(1)} %bitcast.73), kind=kOutput, calls=%fused_computation.31 | convolution fusion | flops 1360060416 | bytes 1413120 | tf_op jit(solution)/shard_map/dot_general | solution.py:203
  118.8 3.3 %collective-permute-start.4 = (f32[3,3,128]{2,1,0:T(4,128)S(1)}, f32[3,3,128]{2,1,0:T(4,128)S(1)}, u32[]{:S(2)}, u32[]{:S(2)}) collective-permute-start(f32[3,3,128]{2,1,0:T(4,128)S(1)} %get-tuple-element.16), channel_id=1, source_target_pairs={{0,8},{8,16},{16,24},{24,32},{32,40},{40,48},{48,56},{56,64},{64,7... | collective-permute-start | bytes 13832 | tf_op jit(solution)/shard_map/ppermute | solution.py:60
  123.4 3.3 %collective-permute-done.4 = f32[3,3,128]{2,1,0:T(4,128)S(1)} collective-permute-done((f32[3,3,128]{2,1,0:T(4,128)S(1)}, f32[3,3,128]{2,1,0:T(4,128)S(1)}, u32[]{:S(2)}, u32[]{:S(2)}) %collective-permute-start.4) | collective-permute-done | bytes 4640 | tf_op jit(solution)/shard_map/ppermute | solution.py:60
  126.7 3.0 %collective-permute-done.5 = f32[3,3,128]{2,1,0:T(4,128)S(1)} collective-permute-done((f32[3,3,128]{2,1,0:T(4,128)S(1)}, f32[3,3,128]{2,1,0:T(4,128)S(1)}, u32[]{:S(2)}, u32[]{:S(2)}) %collective-permute-start.5) | collective-permute-done | bytes 4640 | tf_op jit(solution)/shard_map/ppermute | solution.py:61
  129.8 1.9 %fusion.47 = (f32[3,872,3]{2,1,0:T(8,128)}, f32[3,872,3]{2,1,0:T(8,128)}) fusion(f32[3,872,128]{2,1,0:T(8,128)S(1)} %pad_maximum_fusion.5), kind=kLoop, calls=%fused_computation.90 | loop fusion | bytes 125568 | tf_op jit(solution)/shard_map/slice | solution.py:69
  133.5 2.8 %collective-permute-start.6 = (f32[3,872,3]{1,2,0:T(4,128)S(1)}, f32[3,872,3]{1,2,0:T(4,128)S(1)}, u32[]{:S(2)}, u32[]{:S(2)}) collective-permute-start(f32[3,872,3]{1,2,0:T(4,128)S(1)} %copy.35), channel_id=1, source_target_pairs={{1,0},{2,1},{3,2},{4,3},{5,4},{6,5},{7,6},{9,8},{10,9},{11,10},{12... | collective-permute-start | bytes 94184 | tf_op jit(solution)/shard_map/ppermute | solution.py:69
  138.0 3.4 %collective-permute-start.7 = (f32[3,872,3]{1,2,0:T(4,128)S(1)}, f32[3,872,3]{1,2,0:T(4,128)S(1)}, u32[]{:S(2)}, u32[]{:S(2)}) collective-permute-start(f32[3,872,3]{1,2,0:T(4,128)S(1)} %copy.36), channel_id=1, source_target_pairs={{0,1},{1,2},{2,3},{3,4},{4,5},{5,6},{6,7},{8,9},{9,10},{10,11},{11... | collective-permute-start | bytes 94184 | tf_op jit(solution)/shard_map/ppermute | solution.py:68
  141.4 3.5 %slice.114.diff_ref = f32[3,872,256]{2,1,0:T(8,128)} slice(f32[6,872,256]{2,1,0:T(8,128)} %pad_maximum_fusion.state_ref), slice={[3:6], [0:872], [0:256]} | slice | bytes 5357568 | tf_op jit(solution)/shard_map/slice | solution.py:175
  148.0 3.8 %pad_maximum_fusion.2.state_ref = f32[3,872,256]{2,1,0:T(8,128)} fusion(f32[3,872,3]{2,1,0:T(8,128)} %copy.38, f32[3,872,3]{2,1,0:T(8,128)} %copy.37, f32[3,2,128]{2,1,0:T(2,128)S(1)} %broadcast_in_dim.16, f32[3,3,128]{2,1,0:T(4,128)S(1)} %collective-permute-done.5, f32[1,864,128]{2,1,0:T(8,128)S(1)} %copy-done.10, f32[1,864,128]{2,1,0:T(8,128)S(1)} %copy-done.8, ...), kind=kLoop, calls=%fused_computation.9 | loop fusion | flops 5357568 | bytes 4081984 | tf_op jit(solution)/shard_map/concatenate | solution.py:71
  151.8 8.1 %shard_map.96 = f32[3,864,128]{2,1,0:T(8,128)} custom-call(f32[3,872,256]{2,1,0:T(8,128)} %pad_maximum_fusion.2.state_ref, f32[3,872,256]{2,1,0:T(8,128)} %slice.114.diff_ref), custom_call_target="tpu_custom_call" | custom-call | tf_op jit(solution)/shard_map/pallas_call | solution.py:116
  161.5 5.6 %fusion.26 = f32[256,3,128]{2,0,1:T(8,128)} fusion(f32[3,128,1024]{2,1,0:T(8,128)} %bitcast.78, f32[1024,256]{1,0:T(8,128)S(1)} %copy-done.4), kind=kOutput, calls=%fused_computation.35 | convolution fusion | flops 1207959552 | bytes 3014656 | tf_op jit(solution)/shard_map/dot_general | solution.py:50
  (85 shorter events, 25.5 us)
Async XLA Ops:
  0.6 4.1 %copy-start = (f32[512,128]{1,0:T(8,128)S(1)}, f32[512,128]{1,0:T(8,128)}, u32[]{:S(2)}) copy-start(f32[512,128]{1,0:T(8,128)} %param.12) | copy-start | bytes 786436
  0.6 5.4 %copy-start.15 = (f32[256,3,128]{2,0,1:T(8,128)S(1)}, f32[256,3,128]{2,0,1:T(8,128)}, u32[]{:S(2)}) copy-start(f32[256,3,128]{2,0,1:T(8,128)} %param.10) | copy-start | bytes 1179652
  0.7 5.5 %copy-start.17 = (s32[512]{0:T(512)S(1)}, s32[512]{0:T(512)}, u32[]{:S(2)}) copy-start(s32[512]{0:T(512)} %param.15) | copy-start | bytes 6148
  4.7 4.0 %copy-start.3 = (f32[1024,256]{1,0:T(8,128)}, f32[1024,256]{1,0:T(8,128)S(1)}, u32[]{:S(2)}) copy-start(f32[1024,256]{1,0:T(8,128)S(1)} %fusion.8) | copy-start | bytes 3145732
  7.1 1.6 copy-start.16
  11.3 11.9 %copy-start.1 = (f32[864,3,128]{2,0,1:T(8,128)S(1)}, f32[864,3,128]{2,0,1:T(8,128)}, u32[]{:S(2)}) copy-start(f32[864,3,128]{2,0,1:T(8,128)} %param.9) | copy-start | bytes 3981316
  11.3 11.9 %copy-start.2 = (f32[864,3,128]{2,0,1:T(8,128)S(1)}, f32[864,3,128]{2,0,1:T(8,128)}, u32[]{:S(2)}) copy-start(f32[864,3,128]{2,0,1:T(8,128)} %param.8) | copy-start | bytes 3981316
  11.3 71.7 %all-to-all-start = ((f32[128,8,640]{2,1,0:T(8,128)}), f32[128,8,640]{2,1,0:T(8,128)}, u32[]{:S(2)}, u32[]{:S(2)}) async-start(f32[128,8,640]{2,1,0:T(8,128)} %bitcast.75), calls=%async_computation | async-start | bytes 5242880 | tf_op jit(solution)/shard_map/all_to_all | solution.py:170
  23.2 26.6 %collective-permute-start = (f32[6,3,128]{2,1,0:T(4,128)S(1)}, f32[6,3,128]{2,1,0:T(4,128)S(1)}, u32[]{:S(2)}, u32[]{:S(2)}) collective-permute-start(f32[6,3,128]{2,1,0:T(4,128)S(1)} %get-tuple-element.4), channel_id=1, source_target_pairs={{0,8},{8,16},{16,24},{24,32},{32,40},{40,48},{48,56},{56,64},{64,7... | collective-permute-start | bytes 27656 | tf_op jit(solution)/shard_map/ppermute | solution.py:60
  26.5 26.2 %collective-permute-start.1 = (f32[6,3,128]{2,1,0:T(4,128)S(1)}, f32[6,3,128]{2,1,0:T(4,128)S(1)}, u32[]{:S(2)}, u32[]{:S(2)}) collective-permute-start(f32[6,3,128]{2,1,0:T(4,128)S(1)} %get-tuple-element.5), channel_id=1, source_target_pairs={{8,0},{16,8},{24,16},{32,24},{40,32},{48,40},{56,48},{64,56},{72,6... | collective-permute-start | bytes 27656 | tf_op jit(solution)/shard_map/ppermute | solution.py:61
  58.9 8.9 %collective-permute-start.2 = (f32[6,872,3]{1,0,2:T(8,128)S(1)}, f32[6,872,3]{1,0,2:T(8,128)S(1)}, u32[]{:S(2)}, u32[]{:S(2)}) collective-permute-start(f32[6,872,3]{1,0,2:T(8,128)S(1)} %copy.29), channel_id=1, source_target_pairs={{1,0},{2,1},{3,2},{4,3},{5,4},{6,5},{7,6},{9,8},{10,9},{11,10},{12... | collective-permute-start | bytes 188360 | tf_op jit(solution)/shard_map/ppermute | solution.py:69
  64.4 5.7 %collective-permute-start.3 = (f32[6,872,3]{1,0,2:T(8,128)S(1)}, f32[6,872,3]{1,0,2:T(8,128)S(1)}, u32[]{:S(2)}, u32[]{:S(2)}) collective-permute-start(f32[6,872,3]{1,0,2:T(8,128)S(1)} %copy.30), channel_id=1, source_target_pairs={{0,1},{1,2},{2,3},{3,4},{4,5},{5,6},{6,7},{8,9},{9,10},{10,11},{11... | collective-permute-start | bytes 188360 | tf_op jit(solution)/shard_map/ppermute | solution.py:68
  99.3 0.8 copy-start.11
  99.3 1.0 copy-start.13
  99.3 1.1 copy-start.14
  102.2 57.7 %all-to-all-start.1 = ((f32[128,8,384]{2,1,0:T(8,128)}), f32[128,8,384]{2,1,0:T(8,128)S(1)}, u32[]{:S(2)}, u32[]{:S(2)}) async-start(f32[128,8,384]{2,1,0:T(8,128)} %bitcast.77), calls=%async_computation.1 | async-start | bytes 3145728 | tf_op jit(solution)/shard_map/all_to_all | solution.py:197
  111.2 5.8 %copy-start.12 = (f32[1024,128]{0,1:T(8,128)S(1)}, f32[1024,128]{0,1:T(8,128)}, u32[]{:S(2)}) copy-start(f32[1024,128]{0,1:T(8,128)} %copy-done.11) | copy-start | bytes 1572868
  114.1 15.6 %copy-start.5 = (f32[1,864,128]{2,1,0:T(8,128)}, f32[1,864,128]{2,1,0:T(8,128)S(1)}, u32[]{:S(2)}) copy-start(f32[1,864,128]{2,1,0:T(8,128)S(1)} %fusion.19) | copy-start | bytes 1327108
  117.0 12.7 %copy-start.7 = (f32[1,864,128]{2,1,0:T(8,128)}, f32[1,864,128]{2,1,0:T(8,128)S(1)}, u32[]{:S(2)}) copy-start(f32[1,864,128]{2,1,0:T(8,128)S(1)} %fusion.22) | copy-start | bytes 1327108
  118.8 10.9 %copy-start.9 = (f32[1,864,128]{2,1,0:T(8,128)}, f32[1,864,128]{2,1,0:T(8,128)S(1)}, u32[]{:S(2)}) copy-start(f32[1,864,128]{2,1,0:T(8,128)S(1)} %fusion.25) | copy-start | bytes 1327108
  118.8 7.9 %collective-permute-start.4 = (f32[3,3,128]{2,1,0:T(4,128)S(1)}, f32[3,3,128]{2,1,0:T(4,128)S(1)}, u32[]{:S(2)}, u32[]{:S(2)}) collective-permute-start(f32[3,3,128]{2,1,0:T(4,128)S(1)} %get-tuple-element.16), channel_id=1, source_target_pairs={{0,8},{8,16},{16,24},{24,32},{32,40},{40,48},{48,56},{56,64},{64,7... | collective-permute-start | bytes 13832 | tf_op jit(solution)/shard_map/ppermute | solution.py:60
  122.1 7.6 %collective-permute-start.5 = (f32[3,3,128]{2,1,0:T(4,128)S(1)}, f32[3,3,128]{2,1,0:T(4,128)S(1)}, u32[]{:S(2)}, u32[]{:S(2)}) collective-permute-start(f32[3,3,128]{2,1,0:T(4,128)S(1)} %get-tuple-element.17), channel_id=1, source_target_pairs={{8,0},{16,8},{24,16},{32,24},{40,32},{48,40},{56,48},{64,56},{72,6... | collective-permute-start | bytes 13832 | tf_op jit(solution)/shard_map/ppermute | solution.py:61
  133.5 11.5 %collective-permute-start.6 = (f32[3,872,3]{1,2,0:T(4,128)S(1)}, f32[3,872,3]{1,2,0:T(4,128)S(1)}, u32[]{:S(2)}, u32[]{:S(2)}) collective-permute-start(f32[3,872,3]{1,2,0:T(4,128)S(1)} %copy.35), channel_id=1, source_target_pairs={{1,0},{2,1},{3,2},{4,3},{5,4},{6,5},{7,6},{9,8},{10,9},{11,10},{12... | collective-permute-start | bytes 94184 | tf_op jit(solution)/shard_map/ppermute | solution.py:69
  138.0 8.4 %collective-permute-start.7 = (f32[3,872,3]{1,2,0:T(4,128)S(1)}, f32[3,872,3]{1,2,0:T(4,128)S(1)}, u32[]{:S(2)}, u32[]{:S(2)}) collective-permute-start(f32[3,872,3]{1,2,0:T(4,128)S(1)} %copy.36), channel_id=1, source_target_pairs={{0,1},{1,2},{2,3},{3,4},{4,5},{5,6},{6,7},{8,9},{9,10},{10,11},{11... | collective-permute-start | bytes 94184 | tf_op jit(solution)/shard_map/ppermute | solution.py:68
  144.9 3.1 %copy-start.6 = (f32[1,864,128]{2,1,0:T(8,128)S(1)}, f32[1,864,128]{2,1,0:T(8,128)}, u32[]{:S(2)}) copy-start(f32[1,864,128]{2,1,0:T(8,128)} %copy-done.5) | copy-start | bytes 1327108
  144.9 3.1 %copy-start.8 = (f32[1,864,128]{2,1,0:T(8,128)S(1)}, f32[1,864,128]{2,1,0:T(8,128)}, u32[]{:S(2)}) copy-start(f32[1,864,128]{2,1,0:T(8,128)} %copy-done.7) | copy-start | bytes 1327108
  144.9 3.1 %copy-start.10 = (f32[1,864,128]{2,1,0:T(8,128)S(1)}, f32[1,864,128]{2,1,0:T(8,128)}, u32[]{:S(2)}) copy-start(f32[1,864,128]{2,1,0:T(8,128)} %copy-done.9) | copy-start | bytes 1327108
  159.9 1.6 copy-start.4

commit v3 on v2

--- a/solution.py
+++ b/solution.py
@@ -10,6 +10,7 @@
 ITERS = 3
 HIGHEST = lax.Precision.HIGHEST
 HALO = ITERS
+EDGE = 8
 
 
 def with_halo(block, sides, width):
@@ -51,74 +52,67 @@
     return total.reshape((chosen.shape[0],) + values.shape[1:])
 
 
-def planes_with_halo(block, rows_padded, lanes):
+def halo_parts(block):
     chans, rows, width = block.shape
     atm_n = lax.axis_size("atm")
     ocn_n = lax.axis_size("ocn")
     fwd = [(i, i + 1) for i in range(atm_n - 1)]
     bwd = [(t, s) for s, t in fwd]
-    up = lax.ppermute(block[:, rows - HALO :, :], "atm", fwd)
-    down = lax.ppermute(block[:, :HALO, :], "atm", bwd)
-    extra = rows_padded - rows - 2 * HALO
-    tall = jnp.concatenate(
-        [up, block, down, jnp.zeros((chans, extra, width), block.dtype)], axis=1
-    )
+    up = lax.ppermute(block[:, rows - EDGE :, :], "atm", fwd)
+    down = lax.ppermute(block[:, :EDGE, :], "atm", bwd)
+    tall = jnp.concatenate([up, block, down], axis=1)
     fwd = [(i, i + 1) for i in range(ocn_n - 1)]
     bwd = [(t, s) for s, t in fwd]
     left = lax.ppermute(tall[:, :, width - HALO :], "ocn", fwd)
     right = lax.ppermute(tall[:, :, :HALO], "ocn", bwd)
-    gap = lanes - width - 2 * HALO
-    return jnp.concatenate(
-        [tall, right, jnp.zeros((chans, rows_padded, gap), block.dtype), left], axis=2
-    )
-
-
-def diffuse_kernel(rows, width, state_ref, diff_ref, out_ref):
-    rows_padded, lanes = state_ref.shape[1], state_ref.shape[2]
-    for chan in range(state_ref.shape[0]):
-        state = state_ref[chan]
-        diff = diff_ref[chan]
+    side = jnp.concatenate(
+        [right, jnp.zeros((chans, rows + 2 * EDGE, width - 2 * HALO), block.dtype), left], axis=2
+    )
+    return up, down, side
+
+
+def assemble(block, up, down, side):
+    tall = jnp.concatenate([up, block, down], axis=0)
+    return jnp.concatenate([tall, side], axis=1)
+
+
+def stencil_sum(state):
+    rows_padded, lanes = state.shape
+    return (
+        pltpu.roll(state, rows_padded - 1, 0)
+        + pltpu.roll(state, 1, 0)
+        + pltpu.roll(state, lanes - 1, 1)
+        + pltpu.roll(state, 1, 1)
+    )
+
+
+def smooth_kernel(block_ref, up_ref, down_ref, side_ref, out_ref):
+    rows, width = out_ref.shape[1], out_ref.shape[2]
+    for chan in range(out_ref.shape[0]):
+        state = assemble(block_ref[chan], up_ref[chan], down_ref[chan], side_ref[chan])
+        out_ref[chan] = (0.5 * state + 0.125 * stencil_sum(state))[EDGE : EDGE + rows, :width]
+
+
+def diffuse_kernel(block_ref, up_ref, down_ref, side_ref, dblock_ref, dup_ref, ddown_ref,
+                   dside_ref, out_ref):
+    rows, width = out_ref.shape[1], out_ref.shape[2]
+    first = dblock_ref.shape[0] - out_ref.shape[0]
+    for chan in range(out_ref.shape[0]):
+        state = assemble(block_ref[chan], up_ref[chan], down_ref[chan], side_ref[chan])
+        dc = first + chan
+        diff = assemble(dblock_ref[dc], dup_ref[dc], ddown_ref[dc], dside_ref[dc])
         for iteration in range(ITERS):
-            around = (
-                pltpu.roll(state, rows_padded - 1, 0)
-                + pltpu.roll(state, 1, 0)
-                + pltpu.roll(state, lanes - 1, 1)
-                + pltpu.roll(state, 1, 1)
-            )
-            state = state + diff * (around - 4.0 * state)
-        out_ref[chan] = state[HALO : HALO + rows, :width]
-
-
-def smooth_kernel(rows, width, state_ref, out_ref):
-    rows_padded, lanes = state_ref.shape[1], state_ref.shape[2]
-    for chan in range(out_ref.shape[0]):
-        state = state_ref[chan]
-        around = (
-            pltpu.roll(state, rows_padded - 1, 0)
-            + pltpu.roll(state, 1, 0)
-            + pltpu.roll(state, lanes - 1, 1)
-            + pltpu.roll(state, 1, 1)
-        )
-        out_ref[chan] = (0.5 * state + 0.125 * around)[HALO : HALO + rows, :width]
-
-
-def smooth(state_ext, chans, rows, width):
+            state = state + diff * (stencil_sum(state) - 4.0 * state)
+        out_ref[chan] = state[EDGE : EDGE + rows, :width]
+
+
+def vmem_call(kernel, out_shape, args):
     return pl.pallas_call(
-        functools.partial(smooth_kernel, rows, width),
-        out_shape=jax.ShapeDtypeStruct((chans, rows, width), jnp.float32),
-        in_specs=[pl.BlockSpec(memory_space=pltpu.VMEM)],
+        kernel,
+        out_shape=out_shape,
+        in_specs=[pl.BlockSpec(memory_space=pltpu.VMEM)] * len(args),
         out_specs=pl.BlockSpec(memory_space=pltpu.VMEM),
-    )(state_ext)
-
-
-def diffuse(state_ext, diff_ext, rows, width):
-    chans = state_ext.shape[0]
-    return pl.pallas_call(
-        functools.partial(diffuse_kernel, rows, width),
-        out_shape=jax.ShapeDtypeStruct((chans, rows, width), jnp.float32),
-        in_specs=[pl.BlockSpec(memory_space=pltpu.VMEM)] * 2,
-        out_specs=pl.BlockSpec(memory_space=pltpu.VMEM),
-    )(state_ext, diff_ext)
+    )(*args)
 
 
 def per_device(
@@ -171,9 +165,9 @@
 
     atm_planes = jnp.transpose(atm_state, (1, 0, 2))
     both = jnp.concatenate([atm_planes, jnp.transpose(diffusivity, (1, 0, 2))], axis=0)
-    both_ext = planes_with_halo(both, rows_padded, lanes)
-    diff_ext = both_ext[chan_count:]
-    smoothed = smooth(both_ext, chan_count, row_count, seg_width)
+    both_parts = halo_parts(both)
+    plane_shape = jax.ShapeDtypeStruct((chan_count, row_count, seg_width), jnp.float32)
+    smoothed = vmem_call(smooth_kernel, plane_shape, (both,) + both_parts)
 
     in_labels = jnp.max(incoming[:, plane + seg_width :], axis=1).astype(jnp.int32)
     row_pick = (
@@ -204,8 +198,9 @@
                                              preferred_element_type=jnp.float32)
          for c in range(chan_count)]
     )
-    state_ext = planes_with_halo(forced, rows_padded, lanes)
-    current = diffuse(state_ext, diff_ext, row_count, seg_width)
+    forced_parts = halo_parts(forced)
+    ocean_flux, forced, forced_parts = lax.optimization_barrier((ocean_flux, forced, forced_parts))
+    current = vmem_call(diffuse_kernel, plane_shape, (forced,) + forced_parts + (both,) + both_parts)
     return (jnp.transpose(current, (1, 0, 2)), ocean_flux)
 
 

time: 168 us -> 166 us (0.988)
  local copies, waits for them, and re-layouts: 36.7 us -> 33.9 us
  matrix products: 28 us -> 26.1 us
    slice x7, local copies, waits for them, and re-layouts: 17.7 us -> 14.3 us  [the longest x4 9.71 us: halo_parts(): right = lax.ppermute(tall[:, :, :HALO], 'ocn', bwd)]
    concatenate x4 -> x6, other arithmetic: 9.63 us -> 10.2 us  [the longest x2 8.16 us: halo_parts(): jnp.concatenate([right, jnp.zeros((chans, rows + 2 * EDGE, width - 2 * HA...]
    unnamed x42 -> x48, local copies, waits for them, and re-layouts: 4.8 us -> 5.22 us
  transfers between devices with their start and end apart: 10 -> 10, of which waited for: 4 -> 4; matrix products, arithmetic and copies ran while one was open for 25% -> 24% of each run, Pallas kernels for 8% -> 3%
where the time goes in v3:
time: 166 us; the launch traced here: 165 us
  starting transfers between devices  42.1 us (25%)
  local copies, waits for them, and re-layouts  33.9 us (20%)
  waiting for transfers between devices  32.7 us (20%)
  matrix products  26.1 us (16%)
  other arithmetic  14.6 us (9%)
  Pallas kernels  14.1 us (8%)
    ppermute x2, waiting for transfers between devices, halo_parts(): up = lax.ppermute(block[:, rows - EDGE:, :], 'atm', fwd)  26.8 us
    pallas_call x2, Pallas kernels, vmem_call(): pl.pallas_call(kernel, out_shape=out_shape, in_specs=[pl.BlockSpec(memory...  14.1 us
    all_to_all x1, starting transfers between devices, per_device(): lax.all_to_all(outgoing, ('atm', 'ocn'), split_axis=0, concat_axis=0, til...  11.9 us
    dot_general x3, matrix products, per_device(): jnp.dot(pick_rows, smoothed[c], precision=HIGHEST, preferred_element_type...  9.94 us
    slice x4, local copies, waits for them, and re-layouts, halo_parts(): right = lax.ppermute(tall[:, :, :HALO], 'ocn', bwd)  9.71 us
    all_to_all x1, starting transfers between devices, per_device(): lax.all_to_all(jnp.concatenate(weighted, axis=1), ('atm', 'ocn'), split_a...  8.87 us
    dot_general x4, matrix products, select_rows(): jnp.dot(chosen, flat, precision=precision, preferred_element_type=jnp.flo...  8.64 us
    concatenate x2, other arithmetic, halo_parts(): jnp.concatenate([right, jnp.zeros((chans, rows + 2 * EDGE, width - 2 * HA...  8.16 us
  transfers between devices with their start and end apart: 10, of which 4 were waited for; matrix products, arithmetic and copies ran while one was open for 24% of the time, Pallas kernels for 3%

profile of v3, /device:TPU:1, one launch (start us, length us, event | category | flops | bytes accessed | tf_op | source)
XLA Modules:
  0.0 164.6 jit_solution(15496415639026066106)
XLA Ops:
  7.9 2.1 %copy.26 = f32[1024,640]{1,0:T(8,128)} copy(f32[1024,640]{0,1:T(8,128)S(1)} %pad_maximum_fusion.3) | data formatting | bytes 5242880 | tf_op jit(solution)/shard_map/concatenate | solution.py:163
  10.1 11.9 %all-to-all-start = ((f32[128,8,640]{2,1,0:T(8,128)}), f32[128,8,640]{2,1,0:T(8,128)}, u32[]{:S(2)}, u32[]{:S(2)}) async-start(f32[128,8,640]{2,1,0:T(8,128)} %bitcast.75), calls=%async_computation | async-start | bytes 5242880 | tf_op jit(solution)/shard_map/all_to_all | solution.py:164
  22.0 3.3 %collective-permute-start = (f32[6,8,128]{2,1,0:T(8,128)S(1)}, f32[6,8,128]{2,1,0:T(8,128)S(1)}, u32[]{:S(2)}, u32[]{:S(2)}) collective-permute-start(f32[6,8,128]{2,1,0:T(8,128)S(1)} %get-tuple-element.15), channel_id=1, source_target_pairs={{0,8},{8,16},{16,24},{24,32},{32,40},{40,48},{48,56},{56,64},{64,7... | collective-permute-start | bytes 73736 | tf_op jit(solution)/shard_map/ppermute | solution.py:61
  26.6 22.3 %collective-permute-done.up_ref.dup_ref = f32[6,8,128]{2,1,0:T(8,128)S(1)} collective-permute-done((f32[6,8,128]{2,1,0:T(8,128)S(1)}, f32[6,8,128]{2,1,0:T(8,128)S(1)}, u32[]{:S(2)}, u32[]{:S(2)}) %collective-permute-start) | collective-permute-done | bytes 24608 | tf_op jit(solution)/shard_map/ppermute | solution.py:61
  48.9 2.9 %collective-permute-done.1.down_ref.ddown_ref = f32[6,8,128]{2,1,0:T(8,128)S(1)} collective-permute-done((f32[6,8,128]{2,1,0:T(8,128)S(1)}, f32[6,8,128]{2,1,0:T(8,128)S(1)}, u32[]{:S(2)}, u32[]{:S(2)}) %collective-permute-start.1) | collective-permute-done | bytes 24608 | tf_op jit(solution)/shard_map/ppermute | solution.py:62
  52.4 3.2 %fusion.47 = (f32[6,880,3]{2,1,0:T(8,128)}, f32[6,880,3]{2,1,0:T(8,128)}) fusion(f32[6,880,128]{2,1,0:T(8,128)S(1)} %pad_maximum_fusion.1), kind=kLoop, calls=%fused_computation.91 | loop fusion | bytes 253440 | tf_op jit(solution)/shard_map/slice | solution.py:67
  55.5 2.8 %copy.29 = f32[6,880,3]{1,0,2:T(8,128)S(1)} copy(f32[6,880,3]{2,1,0:T(8,128)} %get-tuple-element.12) | data formatting | bytes 126720 | tf_op jit(solution)/shard_map/slice | solution.py:67
  58.4 2.7 %collective-permute-start.2 = (f32[6,880,3]{1,0,2:T(8,128)S(1)}, f32[6,880,3]{1,0,2:T(8,128)S(1)}, u32[]{:S(2)}, u32[]{:S(2)}) collective-permute-start(f32[6,880,3]{1,0,2:T(8,128)S(1)} %copy.29), channel_id=1, source_target_pairs={{1,0},{2,1},{3,2},{4,3},{5,4},{6,5},{7,6},{9,8},{10,9},{11,10},{12... | collective-permute-start | bytes 190088 | tf_op jit(solution)/shard_map/ppermute | solution.py:67
  61.0 2.8 %copy.30 = f32[6,880,3]{1,0,2:T(8,128)S(1)} copy(f32[6,880,3]{2,1,0:T(8,128)} %get-tuple-element.13) | data formatting | bytes 126720 | tf_op jit(solution)/shard_map/slice | solution.py:66
  63.9 3.3 %collective-permute-start.3 = (f32[6,880,3]{1,0,2:T(8,128)S(1)}, f32[6,880,3]{1,0,2:T(8,128)S(1)}, u32[]{:S(2)}, u32[]{:S(2)}) collective-permute-start(f32[6,880,3]{1,0,2:T(8,128)S(1)} %copy.30), channel_id=1, source_target_pairs={{0,1},{1,2},{2,3},{3,4},{4,5},{5,6},{6,7},{8,9},{9,10},{10,11},{11... | collective-permute-start | bytes 190088 | tf_op jit(solution)/shard_map/ppermute | solution.py:66
  69.0 2.3 %copy.31 = f32[6,880,3]{2,1,0:T(8,128)} copy(f32[6,880,3]{1,0,2:T(8,128)S(1)} %collective-permute-done.2) | data formatting | bytes 126720 | tf_op jit(solution)/shard_map/ppermute | solution.py:67
  71.3 2.4 %copy.32 = f32[6,880,3]{2,1,0:T(8,128)} copy(f32[6,880,3]{1,0,2:T(8,128)S(1)} %collective-permute-done.3) | data formatting | bytes 126720 | tf_op jit(solution)/shard_map/ppermute | solution.py:66
  73.7 4.9 %pad_maximum_fusion.2.side_ref.dside_ref = f32[6,880,128]{2,1,0:T(8,128)} fusion(f32[6,880,3]{2,1,0:T(8,128)} %copy.32, f32[6,880,3]{2,1,0:T(8,128)} %copy.31, f32[128]{0:T(128)S(1)} %pad.15.clone), kind=kLoop, calls=%fused_computation.13 | loop fusion | flops 1351680 | bytes 2830592 | tf_op jit(solution)/shard_map/concatenate | solution.py:68
  78.6 5.1 %shard_map.95 = f32[3,864,128]{2,1,0:T(8,128)} custom-call(f32[6,864,128]{2,1,0:T(8,128)} %pad_maximum_fusion.block_ref.dblock_ref, f32[6,8,128]{2,1,0:T(8,128)} %copy-done.13, f32[6,8,128]{2,1,0:T(8,128)} %copy-done.14, f32[6,880,128]{2,1,0:T(8,128)} %pad_maximum_fusion.2.side_ref.dside_ref), custom_call_target="tpu_custom_call" | custom-call | tf_op jit(solution)/shard_map/pallas_call | solution.py:110
  83.7 2.8 %fusion.48 = (f32[1024,128]{1,0:T(8,128)}, f32[1024,128]{1,0:T(8,128)S(1)}, f32[1024,128]{1,0:T(8,128)S(1)}, f32[1024]{0:T(1024)S(1)}, f32[1024,128]{1,0:T(8,128)S(1)}) fusion(f32[1024,640]{1,0:T(8,128)} %bitcast.8), kind=kLoop, calls=%fused_computation.92 | loop fusion | flops 130048 | bytes 4722688 | tf_op jit(solution)/shard_map/slice | solution.py:179
  86.5 2.1 %copy.46 = f32[1024,128]{0,1:T(8,128)} copy(f32[1024,128]{1,0:T(8,128)} %get-tuple-element.16) | data formatting | bytes 1048576
  89.5 3.5 %fusion.16 = f32[1024,128]{0,1:T(8,128)} fusion(f32[1024,128]{0,1:T(8,128)} %copy.46, s32[1024]{0:T(1024)S(1)} %convert_element_type.32, f32[3,864,128]{2,1,0:T(8,128)} %shard_map.95), kind=kOutput, calls=%fused_computation.31 | convolution fusion | flops 1359970304 | bytes 1495040 | tf_op jit(solution)/shard_map/dot_general | solution.py:177
  93.0 3.3 %fusion.17 = f32[1024,128]{0,1:T(8,128)} fusion(f32[1024,128]{0,1:T(8,128)S(1)} %copy-done.6, s32[1024]{0:T(1024)S(1)} %convert_element_type.32, f32[3,864,128]{2,1,0:T(8,128)} %shard_map.95), kind=kOutput, calls=%fused_computation.32 | convolution fusion | flops 1359970304 | bytes 1495040 | tf_op jit(solution)/shard_map/dot_general | solution.py:177
  96.7 3.2 %multiply_multiply_fusion.3 = (f32[1024,128]{0,1:T(8,128)S(1)}, f32[1024,128]{0,1:T(8,128)S(1)}, f32[1024,128]{0,1:T(8,128)S(1)}) fusion(f32[1024,128]{0,1:T(8,128)S(1)} %copy.44, f32[1024,128]{0,1:T(8,128)} %fusion.17, f32[1024,128]{0,1:T(8,128)} %fusion.16, f32[1024,128]{0,1:T(8,128)S(1)} %copy.45, f32[3,864,128]{2,1,0:T(8,128)} %shard_map.95, ...), kind=kOutput, calls=%fused_computation.52 | convolution fusion | flops 1362198528 | bytes 4116480 | tf_op jit(solution)/shard_map/dot_general | solution.py:177
  102.8 8.9 %all-to-all-start.1 = ((f32[128,8,384]{2,1,0:T(8,128)}), f32[128,8,384]{2,1,0:T(8,128)S(1)}, u32[]{:S(2)}, u32[]{:S(2)}) async-start(f32[128,8,384]{2,1,0:T(8,128)} %bitcast.77), calls=%async_computation.1 | async-start | bytes 3145728 | tf_op jit(solution)/shard_map/all_to_all | solution.py:191
  111.7 2.9 %fusion.19 = f32[1,864,128]{2,1,0:T(8,128)S(1)} fusion(f32[1024,128]{0,1:T(8,128)} %copy-done.11, s32[1024]{0:T(1024)S(1)} %convert_element_type.32, f32[3,864,128]{2,1,0:T(8,128)S(1)} %bitcast.72), kind=kOutput, calls=%fused_computation.34 | convolution fusion | flops 1359949824 | bytes 1413120 | tf_op jit(solution)/shard_map/dot_general | solution.py:197
  118.1 3.3 %collective-permute-start.4 = (f32[3,8,128]{2,1,0:T(8,128)S(1)}, f32[3,8,128]{2,1,0:T(8,128)S(1)}, u32[]{:S(2)}, u32[]{:S(2)}) collective-permute-start(f32[3,8,128]{2,1,0:T(8,128)S(1)} %get-tuple-element.27), channel_id=1, source_target_pairs={{0,8},{8,16},{16,24},{24,32},{32,40},{40,48},{48,56},{56,64},{64,7... | collective-permute-start | bytes 36872 | tf_op jit(solution)/shard_map/ppermute | solution.py:61
  122.7 4.5 %collective-permute-done.4.up_ref = f32[3,8,128]{2,1,0:T(8,128)S(1)} collective-permute-done((f32[3,8,128]{2,1,0:T(8,128)S(1)}, f32[3,8,128]{2,1,0:T(8,128)S(1)}, u32[]{:S(2)}, u32[]{:S(2)}) %collective-permute-start.4) | collective-permute-done | bytes 12320 | tf_op jit(solution)/shard_map/ppermute | solution.py:61
  127.2 3.0 %collective-permute-done.5.down_ref = f32[3,8,128]{2,1,0:T(8,128)S(1)} collective-permute-done((f32[3,8,128]{2,1,0:T(8,128)S(1)}, f32[3,8,128]{2,1,0:T(8,128)S(1)}, u32[]{:S(2)}, u32[]{:S(2)}) %collective-permute-start.5) | collective-permute-done | bytes 12320 | tf_op jit(solution)/shard_map/ppermute | solution.py:62
  130.3 2.0 %fusion.49 = (f32[3,880,3]{2,1,0:T(8,128)}, f32[3,880,3]{2,1,0:T(8,128)}) fusion(f32[3,880,128]{2,1,0:T(8,128)S(1)} %pad_maximum_fusion.5), kind=kLoop, calls=%fused_computation.93 | loop fusion | bytes 126720 | tf_op jit(solution)/shard_map/slice | solution.py:67
  132.3 1.7 %copy.38 = f32[3,880,3]{1,2,0:T(4,128)S(1)} copy(f32[3,880,3]{2,1,0:T(8,128)} %get-tuple-element.24) | data formatting | bytes 63360 | tf_op jit(solution)/shard_map/slice | solution.py:67
  134.0 2.8 %collective-permute-start.6 = (f32[3,880,3]{1,2,0:T(4,128)S(1)}, f32[3,880,3]{1,2,0:T(4,128)S(1)}, u32[]{:S(2)}, u32[]{:S(2)}) collective-permute-start(f32[3,880,3]{1,2,0:T(4,128)S(1)} %copy.38), channel_id=1, source_target_pairs={{1,0},{2,1},{3,2},{4,3},{5,4},{6,5},{7,6},{9,8},{10,9},{11,10},{12... | collective-permute-start | bytes 95048 | tf_op jit(solution)/shard_map/ppermute | solution.py:67
  136.9 1.7 %copy.39 = f32[3,880,3]{1,2,0:T(4,128)S(1)} copy(f32[3,880,3]{2,1,0:T(8,128)} %get-tuple-element.25) | data formatting | bytes 63360 | tf_op jit(solution)/shard_map/slice | solution.py:66
  138.6 3.4 %collective-permute-start.7 = (f32[3,880,3]{1,2,0:T(4,128)S(1)}, f32[3,880,3]{1,2,0:T(4,128)S(1)}, u32[]{:S(2)}, u32[]{:S(2)}) collective-permute-start(f32[3,880,3]{1,2,0:T(4,128)S(1)} %copy.39), channel_id=1, source_target_pairs={{0,1},{1,2},{2,3},{3,4},{4,5},{5,6},{6,7},{8,9},{9,10},{10,11},{11... | collective-permute-start | bytes 95048 | tf_op jit(solution)/shard_map/ppermute | solution.py:66
  145.1 3.3 %pad_maximum_fusion.6.side_ref = f32[3,880,128]{2,1,0:T(8,128)} fusion(f32[3,880,3]{2,1,0:T(8,128)} %copy.41, f32[3,880,3]{2,1,0:T(8,128)} %copy.40, f32[128]{0:T(128)S(1)} %pad.15.clone), kind=kLoop, calls=%fused_computation.27 | loop fusion | flops 675840 | bytes 1415552 | tf_op jit(solution)/shard_map/concatenate | solution.py:68
  150.1 5.6 %fusion.26 = f32[256,3,128]{2,0,1:T(8,128)} fusion(f32[3,128,1024]{2,1,0:T(8,128)} %bitcast.78, f32[1024,256]{1,0:T(8,128)S(1)} %copy-done.4), kind=kOutput, calls=%fused_computation.41 | convolution fusion | flops 1207959552 | bytes 3014656 | tf_op jit(solution)/shard_map/dot_general | solution.py:51
  155.6 8.9 %shard_map.96 = f32[3,864,128]{2,1,0:T(8,128)} custom-call(f32[3,864,128]{2,1,0:T(8,128)} %copy-done.5, f32[3,8,128]{2,1,0:T(8,128)} %copy-done.16, f32[3,8,128]{2,1,0:T(8,128)} %copy-done.17, f32[3,880,128]{2,1,0:T(8,128)} %pad_maximum_fusion.6.side_ref, f32[6,864,128]{2,1,0:T(8,128)} %pad_maximum_fusion.block_ref.dblock_ref, f32[6,8,128]{2,1,0:T(8,128)} %copy-done.13, ...), custom_call_target="tpu_custom_call" | custom-call | tf_op jit(solution)/shard_map/pallas_call | solution.py:110
  (90 shorter events, 24.7 us)
Async XLA Ops:
  0.6 2.8 %copy-start = (f32[512,128]{1,0:T(8,128)S(1)}, f32[512,128]{1,0:T(8,128)}, u32[]{:S(2)}) copy-start(f32[512,128]{1,0:T(8,128)} %param.12) | copy-start | bytes 786436
  0.6 2.2 %copy-start.18 = (s32[512,1]{0,1:T(1,128)S(1)}, s32[512,1]{0,1:T(1,128)}, u32[]{:S(2)}) copy-start(s32[512,1]{0,1:T(1,128)} %param.14) | copy-start | bytes 6148
  0.7 2.2 %copy-start.20 = (s32[512]{0:T(512)S(1)}, s32[512]{0:T(512)}, u32[]{:S(2)}) copy-start(s32[512]{0:T(512)} %param.13) | copy-start | bytes 6148
  1.8 2.9 %copy-start.12 = (f32[256,3,128]{2,0,1:T(8,128)S(1)}, f32[256,3,128]{2,0,1:T(8,128)}, u32[]{:S(2)}) copy-start(f32[256,3,128]{2,0,1:T(8,128)} %param.10) | copy-start | bytes 1179652
  2.8 2.1 %copy-start.19 = (s32[512]{0:T(512)S(1)}, s32[512]{0:T(512)}, u32[]{:S(2)}) copy-start(s32[512]{0:T(512)} %param.15) | copy-start | bytes 6148
  3.4 4.0 %copy-start.3 = (f32[1024,256]{1,0:T(8,128)}, f32[1024,256]{1,0:T(8,128)S(1)}, u32[]{:S(2)}) copy-start(f32[1024,256]{1,0:T(8,128)S(1)} %fusion.8) | copy-start | bytes 3145732
  5.9 1.5 copy-start.15
  10.0 11.9 %copy-start.1 = (f32[864,3,128]{2,0,1:T(8,128)S(1)}, f32[864,3,128]{2,0,1:T(8,128)}, u32[]{:S(2)}) copy-start(f32[864,3,128]{2,0,1:T(8,128)} %param.9) | copy-start | bytes 3981316
  10.0 11.9 %copy-start.2 = (f32[864,3,128]{2,0,1:T(8,128)S(1)}, f32[864,3,128]{2,0,1:T(8,128)}, u32[]{:S(2)}) copy-start(f32[864,3,128]{2,0,1:T(8,128)} %param.8) | copy-start | bytes 3981316
  10.1 73.6 %all-to-all-start = ((f32[128,8,640]{2,1,0:T(8,128)}), f32[128,8,640]{2,1,0:T(8,128)}, u32[]{:S(2)}, u32[]{:S(2)}) async-start(f32[128,8,640]{2,1,0:T(8,128)} %bitcast.75), calls=%async_computation | async-start | bytes 5242880 | tf_op jit(solution)/shard_map/all_to_all | solution.py:164
  22.0 26.9 %collective-permute-start = (f32[6,8,128]{2,1,0:T(8,128)S(1)}, f32[6,8,128]{2,1,0:T(8,128)S(1)}, u32[]{:S(2)}, u32[]{:S(2)}) collective-permute-start(f32[6,8,128]{2,1,0:T(8,128)S(1)} %get-tuple-element.15), channel_id=1, source_target_pairs={{0,8},{8,16},{16,24},{24,32},{32,40},{40,48},{48,56},{56,64},{64,7... | collective-permute-start | bytes 73736 | tf_op jit(solution)/shard_map/ppermute | solution.py:61
  25.3 26.5 %collective-permute-start.1 = (f32[6,8,128]{2,1,0:T(8,128)S(1)}, f32[6,8,128]{2,1,0:T(8,128)S(1)}, u32[]{:S(2)}, u32[]{:S(2)}) collective-permute-start(f32[6,8,128]{2,1,0:T(8,128)S(1)} %get-tuple-element.14), channel_id=1, source_target_pairs={{8,0},{16,8},{24,16},{32,24},{40,32},{48,40},{56,48},{64,56},{72,6... | collective-permute-start | bytes 73736 | tf_op jit(solution)/shard_map/ppermute | solution.py:62
  48.9 3.1 %copy-start.13 = (f32[6,8,128]{2,1,0:T(8,128)}, f32[6,8,128]{2,1,0:T(8,128)S(1)}, u32[]{:S(2)}) copy-start(f32[6,8,128]{2,1,0:T(8,128)S(1)} %collective-permute-done.up_ref.dup_ref) | copy-start | bytes 73732
  51.8 0.6 copy-start.14
  58.4 10.7 %collective-permute-start.2 = (f32[6,880,3]{1,0,2:T(8,128)S(1)}, f32[6,880,3]{1,0,2:T(8,128)S(1)}, u32[]{:S(2)}, u32[]{:S(2)}) collective-permute-start(f32[6,880,3]{1,0,2:T(8,128)S(1)} %copy.29), channel_id=1, source_target_pairs={{1,0},{2,1},{3,2},{4,3},{5,4},{6,5},{7,6},{9,8},{10,9},{11,10},{12... | collective-permute-start | bytes 190088 | tf_op jit(solution)/shard_map/ppermute | solution.py:67
  63.9 7.5 %collective-permute-start.3 = (f32[6,880,3]{1,0,2:T(8,128)S(1)}, f32[6,880,3]{1,0,2:T(8,128)S(1)}, u32[]{:S(2)}, u32[]{:S(2)}) collective-permute-start(f32[6,880,3]{1,0,2:T(8,128)S(1)} %copy.30), channel_id=1, source_target_pairs={{0,1},{1,2},{2,3},{3,4},{4,5},{5,6},{6,7},{8,9},{9,10},{10,11},{11... | collective-permute-start | bytes 190088 | tf_op jit(solution)/shard_map/ppermute | solution.py:66
  89.5 3.5 %copy-start.6 = (f32[1024,128]{0,1:T(8,128)S(1)}, f32[1024,128]{0,1:T(8,128)}, u32[]{:S(2)}) copy-start(f32[1024,128]{0,1:T(8,128)} %copy.47) | copy-start | bytes 1572868
  99.9 0.8 copy-start.7
  99.9 1.0 copy-start.9
  99.9 1.1 copy-start.11
  102.8 45.7 %all-to-all-start.1 = ((f32[128,8,384]{2,1,0:T(8,128)}), f32[128,8,384]{2,1,0:T(8,128)S(1)}, u32[]{:S(2)}, u32[]{:S(2)}) async-start(f32[128,8,384]{2,1,0:T(8,128)} %bitcast.77), calls=%async_computation.1 | async-start | bytes 3145728 | tf_op jit(solution)/shard_map/all_to_all | solution.py:191
  111.6 2.9 %copy-start.10 = (f32[1024,128]{0,1:T(8,128)S(1)}, f32[1024,128]{0,1:T(8,128)}, u32[]{:S(2)}) copy-start(f32[1024,128]{0,1:T(8,128)} %copy-done.9) | copy-start | bytes 1572868
  111.6 4.6 %copy-start.8 = (f32[1024,128]{0,1:T(8,128)S(1)}, f32[1024,128]{0,1:T(8,128)}, u32[]{:S(2)}) copy-start(f32[1024,128]{0,1:T(8,128)} %copy-done.7) | copy-start | bytes 1572868
  118.1 9.1 %copy-start.5 = (f32[3,864,128]{2,1,0:T(8,128)}, f32[3,864,128]{2,1,0:T(8,128)S(1)}, u32[]{:S(2)}) copy-start(f32[3,864,128]{2,1,0:T(8,128)S(1)} %pad_maximum_fusion.7.block_ref) | copy-start | bytes 3981316
  118.1 9.1 %collective-permute-start.4 = (f32[3,8,128]{2,1,0:T(8,128)S(1)}, f32[3,8,128]{2,1,0:T(8,128)S(1)}, u32[]{:S(2)}, u32[]{:S(2)}) collective-permute-start(f32[3,8,128]{2,1,0:T(8,128)S(1)} %get-tuple-element.27), channel_id=1, source_target_pairs={{0,8},{8,16},{16,24},{24,32},{32,40},{40,48},{48,56},{56,64},{64,7... | collective-permute-start | bytes 36872 | tf_op jit(solution)/shard_map/ppermute | solution.py:61
  121.4 8.8 %collective-permute-start.5 = (f32[3,8,128]{2,1,0:T(8,128)S(1)}, f32[3,8,128]{2,1,0:T(8,128)S(1)}, u32[]{:S(2)}, u32[]{:S(2)}) collective-permute-start(f32[3,8,128]{2,1,0:T(8,128)S(1)} %get-tuple-element.26), channel_id=1, source_target_pairs={{8,0},{16,8},{24,16},{32,24},{40,32},{48,40},{56,48},{64,56},{72,6... | collective-permute-start | bytes 36872 | tf_op jit(solution)/shard_map/ppermute | solution.py:62
  127.2 5.1 %copy-start.16 = (f32[3,8,128]{2,1,0:T(8,128)}, f32[3,8,128]{2,1,0:T(8,128)S(1)}, u32[]{:S(2)}) copy-start(f32[3,8,128]{2,1,0:T(8,128)S(1)} %collective-permute-done.4.up_ref) | copy-start | bytes 36868
  130.2 2.1 %copy-start.17 = (f32[3,8,128]{2,1,0:T(8,128)}, f32[3,8,128]{2,1,0:T(8,128)S(1)}, u32[]{:S(2)}) copy-start(f32[3,8,128]{2,1,0:T(8,128)S(1)} %collective-permute-done.5.down_ref) | copy-start | bytes 36868
  134.0 8.0 %collective-permute-start.6 = (f32[3,880,3]{1,2,0:T(4,128)S(1)}, f32[3,880,3]{1,2,0:T(4,128)S(1)}, u32[]{:S(2)}, u32[]{:S(2)}) collective-permute-start(f32[3,880,3]{1,2,0:T(4,128)S(1)} %copy.38), channel_id=1, source_target_pairs={{1,0},{2,1},{3,2},{4,3},{5,4},{6,5},{7,6},{9,8},{10,9},{11,10},{12... | collective-permute-start | bytes 95048 | tf_op jit(solution)/shard_map/ppermute | solution.py:67
  138.6 5.0 %collective-permute-start.7 = (f32[3,880,3]{1,2,0:T(4,128)S(1)}, f32[3,880,3]{1,2,0:T(4,128)S(1)}, u32[]{:S(2)}, u32[]{:S(2)}) collective-permute-start(f32[3,880,3]{1,2,0:T(4,128)S(1)} %copy.39), channel_id=1, source_target_pairs={{0,1},{1,2},{2,3},{3,4},{4,5},{5,6},{6,7},{8,9},{9,10},{10,11},{11... | collective-permute-start | bytes 95048 | tf_op jit(solution)/shard_map/ppermute | solution.py:66
  148.4 1.6 copy-start.4

commit v4 on v3

--- a/solution.py
+++ b/solution.py
@@ -52,28 +52,77 @@
     return total.reshape((chosen.shape[0],) + values.shape[1:])
 
 
-def halo_parts(block):
-    chans, rows, width = block.shape
-    atm_n = lax.axis_size("atm")
-    ocn_n = lax.axis_size("ocn")
-    fwd = [(i, i + 1) for i in range(atm_n - 1)]
-    bwd = [(t, s) for s, t in fwd]
-    up = lax.ppermute(block[:, rows - EDGE :, :], "atm", fwd)
-    down = lax.ppermute(block[:, :EDGE, :], "atm", bwd)
-    tall = jnp.concatenate([up, block, down], axis=1)
-    fwd = [(i, i + 1) for i in range(ocn_n - 1)]
-    bwd = [(t, s) for s, t in fwd]
-    left = lax.ppermute(tall[:, :, width - HALO :], "ocn", fwd)
-    right = lax.ppermute(tall[:, :, :HALO], "ocn", bwd)
-    side = jnp.concatenate(
-        [right, jnp.zeros((chans, rows + 2 * EDGE, width - 2 * HALO), block.dtype), left], axis=2
-    )
-    return up, down, side
-
-
-def assemble(block, up, down, side):
-    tall = jnp.concatenate([up, block, down], axis=0)
-    return jnp.concatenate([tall, side], axis=1)
+MESH = pl.DeviceIdType.MESH
+
+
+def exchange(sizes, x_ref, rows_buf, cols_buf, colsend, tall_s, side_s, send_sem, recv_sem):
+    atm_n, ocn_n = sizes
+    chans, rows, width = x_ref.shape
+    rows_padded = tall_s.shape[1]
+    me_a = lax.axis_index("atm")
+    me_o = lax.axis_index("ocn")
+    up = lax.rem(me_a + atm_n - 1, atm_n)
+    down = lax.rem(me_a + 1, atm_n)
+    left = lax.rem(me_o + ocn_n - 1, ocn_n)
+    right = lax.rem(me_o + 1, ocn_n)
+    barrier = pltpu.get_barrier_semaphore()
+    for peer in ((up, me_o), (down, me_o), (me_a, left), (me_a, right)):
+        pl.semaphore_signal(barrier, 1, device_id=peer, device_id_type=MESH)
+    pl.semaphore_wait(barrier, 4)
+
+    to_down = pltpu.make_async_remote_copy(
+        x_ref.at[:, rows - EDGE :, :], rows_buf.at[0], send_sem.at[0], recv_sem.at[0],
+        device_id=(down, me_o), device_id_type=MESH)
+    to_up = pltpu.make_async_remote_copy(
+        x_ref.at[:, :EDGE, :], rows_buf.at[1], send_sem.at[1], recv_sem.at[1],
+        device_id=(up, me_o), device_id_type=MESH)
+    to_down.start()
+    to_up.start()
+    to_down.wait()
+    to_up.wait()
+
+    has_up = me_a > 0
+    has_down = me_a < atm_n - 1
+    has_left = me_o > 0
+    has_right = me_o < ocn_n - 1
+    spare = jnp.zeros((rows_padded - rows - 2 * EDGE, width), jnp.float32)
+    for c in range(chans):
+        top = jnp.where(has_up, rows_buf[0, c], 0.0)
+        bottom = jnp.where(has_down, rows_buf[1, c], 0.0)
+        tall = jnp.concatenate([top, x_ref[c], bottom, spare], axis=0)
+        tall_s[c] = tall
+        flipped = tall.T
+        colsend[0, c] = flipped[:EDGE]
+        colsend[1, c] = flipped[width - EDGE :]
+
+    to_left = pltpu.make_async_remote_copy(
+        colsend.at[0], cols_buf.at[1], send_sem.at[2], recv_sem.at[2],
+        device_id=(me_a, left), device_id_type=MESH)
+    to_right = pltpu.make_async_remote_copy(
+        colsend.at[1], cols_buf.at[0], send_sem.at[3], recv_sem.at[3],
+        device_id=(me_a, right), device_id_type=MESH)
+    to_left.start()
+    to_right.start()
+    to_left.wait()
+    to_right.wait()
+
+    middle = jnp.zeros((width - 2 * EDGE, rows_padded), jnp.float32)
+    for c in range(chans):
+        from_left = jnp.where(has_left, cols_buf[0, c], 0.0)
+        from_right = jnp.where(has_right, cols_buf[1, c], 0.0)
+        side_s[c] = jnp.concatenate([from_right, middle, from_left], axis=0).T
+
+
+def exchange_scratch(chans, rows_padded, width):
+    return [
+        pltpu.VMEM((2, chans, EDGE, width), jnp.float32),
+        pltpu.VMEM((2, chans, EDGE, rows_padded), jnp.float32),
+        pltpu.VMEM((2, chans, EDGE, rows_padded), jnp.float32),
+        pltpu.VMEM((chans, rows_padded, width), jnp.float32),
+        pltpu.VMEM((chans, rows_padded, width), jnp.float32),
+        pltpu.SemaphoreType.DMA((4,)),
+        pltpu.SemaphoreType.DMA((4,)),
+    ]
 
 
 def stencil_sum(state):
@@ -86,33 +135,59 @@
     )
 
 
-def smooth_kernel(block_ref, up_ref, down_ref, side_ref, out_ref):
+def smooth_kernel(sizes, x_ref, out_ref, tall_out, side_out, *scratch):
+    rows_buf, cols_buf, colsend, tall_s, side_s, send_sem, recv_sem = scratch
+    exchange(sizes, x_ref, rows_buf, cols_buf, colsend, tall_s, side_s, send_sem, recv_sem)
     rows, width = out_ref.shape[1], out_ref.shape[2]
+    tall_out[...] = tall_s[...]
+    side_out[...] = side_s[...]
     for chan in range(out_ref.shape[0]):
-        state = assemble(block_ref[chan], up_ref[chan], down_ref[chan], side_ref[chan])
+        state = jnp.concatenate([tall_s[chan], side_s[chan]], axis=1)
         out_ref[chan] = (0.5 * state + 0.125 * stencil_sum(state))[EDGE : EDGE + rows, :width]
 
 
-def diffuse_kernel(block_ref, up_ref, down_ref, side_ref, dblock_ref, dup_ref, ddown_ref,
-                   dside_ref, out_ref):
+def diffuse_kernel(sizes, x_ref, dtall_ref, dside_ref, out_ref, *scratch):
+    rows_buf, cols_buf, colsend, tall_s, side_s, send_sem, recv_sem = scratch
+    exchange(sizes, x_ref, rows_buf, cols_buf, colsend, tall_s, side_s, send_sem, recv_sem)
     rows, width = out_ref.shape[1], out_ref.shape[2]
-    first = dblock_ref.shape[0] - out_ref.shape[0]
+    first = dtall_ref.shape[0] - out_ref.shape[0]
     for chan in range(out_ref.shape[0]):
-        state = assemble(block_ref[chan], up_ref[chan], down_ref[chan], side_ref[chan])
-        dc = first + chan
-        diff = assemble(dblock_ref[dc], dup_ref[dc], ddown_ref[dc], dside_ref[dc])
+        state = jnp.concatenate([tall_s[chan], side_s[chan]], axis=1)
+        diff = jnp.concatenate([dtall_ref[first + chan], dside_ref[first + chan]], axis=1)
         for iteration in range(ITERS):
             state = state + diff * (stencil_sum(state) - 4.0 * state)
         out_ref[chan] = state[EDGE : EDGE + rows, :width]
 
 
-def vmem_call(kernel, out_shape, args):
+def smooth_call(sizes, both, chans, rows_padded):
+    total, rows, width = both.shape
+    vmem = pl.BlockSpec(memory_space=pltpu.VMEM)
     return pl.pallas_call(
-        kernel,
-        out_shape=out_shape,
-        in_specs=[pl.BlockSpec(memory_space=pltpu.VMEM)] * len(args),
-        out_specs=pl.BlockSpec(memory_space=pltpu.VMEM),
-    )(*args)
+        functools.partial(smooth_kernel, sizes),
+        out_shape=(
+            jax.ShapeDtypeStruct((chans, rows, width), jnp.float32),
+            jax.ShapeDtypeStruct((total, rows_padded, width), jnp.float32),
+            jax.ShapeDtypeStruct((total, rows_padded, width), jnp.float32),
+        ),
+        in_specs=[vmem],
+        out_specs=(vmem, vmem, vmem),
+        scratch_shapes=exchange_scratch(total, rows_padded, width),
+        compiler_params=pltpu.CompilerParams(collective_id=0, has_side_effects=True),
+    )(both)
+
+
+def diffuse_call(sizes, forced, dtall, dside):
+    chans, rows, width = forced.shape
+    rows_padded = dtall.shape[1]
+    vmem = pl.BlockSpec(memory_space=pltpu.VMEM)
+    return pl.pallas_call(
+        functools.partial(diffuse_kernel, sizes),
+        out_shape=jax.ShapeDtypeStruct((chans, rows, width), jnp.float32),
+        in_specs=[vmem] * 3,
+        out_specs=vmem,
+        scratch_shapes=exchange_scratch(chans, rows_padded, width),
+        compiler_params=pltpu.CompilerParams(collective_id=1, has_side_effects=True),
+    )(forced, dtall, dside)
 
 
 def per_device(
@@ -133,8 +208,6 @@
     ov_rows = intersection_seg.shape[0]
     capacity = max(2, 2 * ov_rows // devices)
     slots = devices * capacity
-    rows_padded = -(-(row_count + 2 * HALO) // 8) * 8
-    lanes = 2 * seg_width
 
     target = intersection_dest[:, 0]
     matches = (target[:, None] == jnp.arange(devices, dtype=jnp.int32)[None, :]).astype(jnp.int32)
@@ -165,9 +238,9 @@
 
     atm_planes = jnp.transpose(atm_state, (1, 0, 2))
     both = jnp.concatenate([atm_planes, jnp.transpose(diffusivity, (1, 0, 2))], axis=0)
-    both_parts = halo_parts(both)
-    plane_shape = jax.ShapeDtypeStruct((chan_count, row_count, seg_width), jnp.float32)
-    smoothed = vmem_call(smooth_kernel, plane_shape, (both,) + both_parts)
+    sizes = (atm_count, ocn_count)
+    rows_padded = -(-(row_count + 2 * EDGE) // 128) * 128
+    smoothed, dtall, dside = smooth_call(sizes, both, chan_count, rows_padded)
 
     in_labels = jnp.max(incoming[:, plane + seg_width :], axis=1).astype(jnp.int32)
     row_pick = (
@@ -198,9 +271,8 @@
                                              preferred_element_type=jnp.float32)
          for c in range(chan_count)]
     )
-    forced_parts = halo_parts(forced)
-    ocean_flux, forced, forced_parts = lax.optimization_barrier((ocean_flux, forced, forced_parts))
-    current = vmem_call(diffuse_kernel, plane_shape, (forced,) + forced_parts + (both,) + both_parts)
+    ocean_flux, forced = lax.optimization_barrier((ocean_flux, forced))
+    current = diffuse_call(sizes, forced, dtall, dside)
     return (jnp.transpose(current, (1, 0, 2)), ocean_flux)
 
 

time: 166 us -> 139 us (0.84)
  Pallas kernels: 14.1 us -> 59.9 us
  starting transfers between devices: 42.1 us -> 16.7 us
  local copies, waits for them, and re-layouts: 33.9 us -> 13.3 us
  waiting for transfers between devices: 32.7 us -> 16.9 us
  other arithmetic: 14.6 us -> 8.19 us
  matrix products: 26.1 us -> 22.1 us
    pallas_call x2, Pallas kernels: 14.1 us -> 59.9 us  [the longest x1 40 us: smooth_call(): pl.pallas_call(functools.partial(smooth_kernel, sizes), out_shape=(jax.Sh...]
    ppermute x8 -> x0, waiting for transfers between devices: 32.7 us -> none  [the longest x2 26.8 us: halo_parts(): up = lax.ppermute(block[:, rows - EDGE:, :], 'atm', fwd)]
    ppermute x8 -> x0, starting transfers between devices: 21.3 us -> none  [the longest x2 6.71 us: halo_parts(): left = lax.ppermute(tall[:, :, width - HALO:], 'ocn', fwd)]
    all_to_all x1, waiting for transfers between devices: 0.01 us -> 16.9 us  [per_device(): lax.all_to_all(jnp.concatenate(weighted, axis=1), ('atm', 'ocn'), split_a...]
    slice x7 -> x0, local copies, waits for them, and re-layouts: 14.3 us -> none  [the longest x4 9.71 us: halo_parts(): right = lax.ppermute(tall[:, :, :HALO], 'ocn', bwd)]
    concatenate x4 -> x0, other arithmetic: 8.42 us -> none  [the longest x2 8.16 us: halo_parts(): jnp.concatenate([right, jnp.zeros((chans, rows + 2 * EDGE, width - 2 * HA...]
    ppermute x4 -> x0, local copies, waits for them, and re-layouts: 7.82 us -> none  [the longest x2 3.95 us: halo_parts(): left = lax.ppermute(tall[:, :, width - HALO:], 'ocn', fwd)]
    dot_general x3, matrix products: 9.94 us -> 5.94 us  [per_device(): jnp.dot(pick_rows, smoothed[c], precision=HIGHEST, preferred_element_type...]
  transfers between devices with their start and end apart: 10 -> 2, of which waited for: 4 -> 1; matrix products, arithmetic and copies ran while one was open for 24% -> 8% of each run, Pallas kernels for 3% -> 29%
where the time goes in v4:
time: 139 us; the launch traced here: 138 us
  Pallas kernels  59.9 us (43%)
  matrix products  22.1 us (16%)
  waiting for transfers between devices  16.9 us (12%)
  starting transfers between devices  16.7 us (12%)
  local copies, waits for them, and re-layouts  13.3 us (10%)
  other arithmetic  8.19 us (6%)
    pallas_call x1, Pallas kernels, smooth_call(): pl.pallas_call(functools.partial(smooth_kernel, sizes), out_shape=(jax.Sh...  40 us
    pallas_call x1, Pallas kernels, diffuse_call(): pl.pallas_call(functools.partial(diffuse_kernel, sizes), out_shape=jax.Sh...  19.8 us
    all_to_all x1, waiting for transfers between devices, per_device(): lax.all_to_all(jnp.concatenate(weighted, axis=1), ('atm', 'ocn'), split_a...  16.9 us
    all_to_all x1, starting transfers between devices, per_device(): lax.all_to_all(outgoing, ('atm', 'ocn'), split_axis=0, concat_axis=0, til...  11.5 us
    dot_general x4, matrix products, select_rows(): jnp.dot(chosen, flat, precision=precision, preferred_element_type=jnp.flo...  8.65 us
    unnamed x37, local copies, waits for them, and re-layouts  6.74 us
    dot_general x3, matrix products, per_device(): jnp.dot(row_pick, weighted[c], precision=HIGHEST, preferred_element_type=...  6.31 us
    dot_general x3, matrix products, per_device(): jnp.dot(pick_rows, smoothed[c], precision=HIGHEST, preferred_element_type...  5.94 us
  transfers between devices with their start and end apart: 2, of which 1 were waited for; matrix products, arithmetic and copies ran while one was open for 8% of the time, Pallas kernels for 29%

profile of v4, /device:TPU:1, one launch (start us, length us, event | category | flops | bytes accessed | tf_op | source)
XLA Modules:
  0.0 138.1 jit_solution(18085826988862592409)
XLA Ops:
  0.7 0.8 fusion.47
  1.4 0.8 copy.12
  2.2 0.2 fusion.43
  2.5 0.9 fusion.41
  3.7 1.3 fusion.7
  5.2 0.6 fusion.6
  5.9 0.6 fusion.8
  6.6 1.5 %fusion.52 = f32[1024,384]{0,1:T(8,128)S(1)} fusion(f32[1024,256]{1,0:T(8,128)S(1)} %fusion.8, f32[256,384]{0,1:T(8,128)S(1)} %bitcast.71), kind=kOutput, calls=%fused_computation.85 | convolution fusion | flops 1207959552 | bytes 3014656 | tf_op jit(solution)/shard_map/dot_general | solution.py:51
  8.0 0.3 convolution_multiply_fusion
  8.6 2.2 %copy.15 = f32[1024,640]{1,0:T(8,128)} copy(f32[1024,640]{0,1:T(8,128)S(1)} %pad_maximum_fusion.1) | data formatting | bytes 5242880 | tf_op jit(solution)/shard_map/concatenate | solution.py:236
  10.7 11.5 %all-to-all-start = ((f32[128,8,640]{2,1,0:T(8,128)}), f32[128,8,640]{2,1,0:T(8,128)S(1)}, u32[]{:S(2)}, u32[]{:S(2)}) async-start(f32[128,8,640]{2,1,0:T(8,128)} %bitcast.67), calls=%async_computation | async-start | bytes 5242880 | tf_op jit(solution)/shard_map/all_to_all | solution.py:237
  22.2 3.4 %pad_maximum_fusion.x_ref = f32[6,864,128]{2,1,0:T(8,128)} fusion(f32[3,864,128]{2,1,0:T(8,128)} %bitcast.72, f32[3,864,128]{2,1,0:T(8,128)} %bitcast.73), kind=kLoop, calls=%fused_computation.7 | loop fusion | flops 663552 | bytes 5308416 | tf_op jit(solution)/shard_map/concatenate | solution.py:240
  25.6 40.0 %shard_map.95 = (f32[3,864,128]{2,1,0:T(8,128)}, f32[6,896,128]{2,1,0:T(8,128)}, f32[6,896,128]{2,1,0:T(8,128)}) custom-call(f32[6,864,128]{2,1,0:T(8,128)} %pad_maximum_fusion.x_ref), custom_call_target="tpu_custom_call" | custom-call | tf_op jit(solution)/shard_map/pallas_call | solution.py:165
  65.7 1.3 fusion.51
  67.0 1.3 copy.27
  68.3 1.2 copy.26
  69.8 0.2 copy.28
  70.0 2.6 %fusion.17 = f32[1024,128]{0,1:T(8,128)S(1)} fusion(f32[1024,128]{0,1:T(8,128)S(1)} %copy.28, s32[1024]{0:T(1024)S(1)} %convert_element_type.32, f32[3,864,128]{2,1,0:T(8,128)} %get-tuple-element.7), kind=kOutput, calls=%fused_computation.24 | convolution fusion | flops 1359970304 | bytes 1495040 | tf_op jit(solution)/shard_map/dot_general | solution.py:250
  72.6 1.5 %fusion.16 = f32[1024,128]{0,1:T(8,128)S(1)} fusion(f32[1024,128]{0,1:T(8,128)S(1)} %copy.27, s32[1024]{0:T(1024)S(1)} %convert_element_type.32, f32[3,864,128]{2,1,0:T(8,128)S(1)} %copy-done.13), kind=kOutput, calls=%fused_computation.23 | convolution fusion | flops 1359970304 | bytes 1495040 | tf_op jit(solution)/shard_map/dot_general | solution.py:250
  74.1 1.9 %multiply_multiply_fusion.3 = (f32[1024,128]{0,1:T(8,128)S(1)}, f32[1024,128]{0,1:T(8,128)S(1)}, f32[1024,128]{0,1:T(8,128)S(1)}) fusion(f32[1024,128]{0,1:T(8,128)S(1)} %copy.25, f32[1024,128]{0,1:T(8,128)S(1)} %fusion.17, f32[1024,128]{0,1:T(8,128)S(1)} %fusion.16, f32[1024,128]{0,1:T(8,128)S(1)} %copy.26, f32[3,864,128]{2,1,0:T(8,128)S(1)} %copy-done.13, ...), kind=kOutput, calls=%fused_computation.44 | convolution fusion | flops 1362198528 | bytes 4116480 | tf_op jit(solution)/shard_map/dot_general | solution.py:250
  76.0 0.8 copy-done.5
  77.3 1.7 %copy.20 = f32[1024,384]{1,0:T(8,128)} copy(f32[1024,384]{0,1:T(8,128)S(1)} %pad_maximum_fusion.2) | data formatting | bytes 3145728 | tf_op jit(solution)/shard_map/concatenate | solution.py:265
  78.9 5.2 %all-to-all-start.1 = ((f32[128,8,384]{2,1,0:T(8,128)}), f32[128,8,384]{2,1,0:T(8,128)S(1)}, u32[]{:S(2)}, u32[]{:S(2)}) async-start(f32[128,8,384]{2,1,0:T(8,128)} %bitcast.14), calls=%async_computation.1 | async-start | bytes 3145728 | tf_op jit(solution)/shard_map/all_to_all | solution.py:264
  84.1 2.9 %fusion.19 = f32[1,864,128]{2,1,0:T(8,128)S(1)} fusion(f32[1024,128]{0,1:T(8,128)} %copy-done.9, s32[1024]{0:T(1024)S(1)} %convert_element_type.32, f32[3,864,128]{2,1,0:T(8,128)S(1)} %bitcast.74), kind=kOutput, calls=%fused_computation.26 | convolution fusion | flops 1359949824 | bytes 1413120 | tf_op jit(solution)/shard_map/dot_general | solution.py:270
  87.0 1.7 %fusion.25 = f32[1,864,128]{2,1,0:T(8,128)S(1)} fusion(f32[1024,128]{0,1:T(8,128)S(1)} %copy-done.8, s32[1024]{0:T(1024)S(1)} %convert_element_type.32, f32[3,864,128]{2,1,0:T(8,128)S(1)} %bitcast.75), kind=kOutput, calls=%fused_computation.32 | convolution fusion | flops 1360060416 | bytes 1413120 | tf_op jit(solution)/shard_map/dot_general | solution.py:270
  88.7 1.7 %fusion.22 = f32[1,864,128]{2,1,0:T(8,128)S(1)} fusion(f32[1024,128]{0,1:T(8,128)S(1)} %copy-done.6, s32[1024]{0:T(1024)S(1)} %convert_element_type.32, f32[3,864,128]{2,1,0:T(8,128)S(1)} %bitcast.76), kind=kOutput, calls=%fused_computation.29 | convolution fusion | flops 1360060416 | bytes 1413120 | tf_op jit(solution)/shard_map/dot_general | solution.py:270
  90.5 1.1 pad_maximum_fusion.3.x_ref
  91.6 16.9 %all-to-all-done.1 = f32[128,8,384]{2,1,0:T(8,128)S(1)} async-done(((f32[128,8,384]{2,1,0:T(8,128)}), f32[128,8,384]{2,1,0:T(8,128)S(1)}, u32[]{:S(2)}, u32[]{:S(2)}) %all-to-all-start.1) | async-done | bytes 1572896 | tf_op jit(solution)/shard_map/all_to_all | solution.py:264
  108.6 1.6 %copy.21 = f32[384,1024]{1,0:T(8,128)} copy(f32[384,1024]{0,1:T(8,128)S(1)} %bitcast.68) | data formatting | bytes 3145728 | tf_op jit(solution)/shard_map/dot_general | solution.py:51
  110.2 5.6 %fusion.26 = f32[256,3,128]{2,0,1:T(8,128)} fusion(f32[3,128,1024]{2,1,0:T(8,128)} %bitcast.69, f32[1024,256]{1,0:T(8,128)S(1)} %copy-done.2), kind=kOutput, calls=%fused_computation.33 | convolution fusion | flops 1207959552 | bytes 3014656 | tf_op jit(solution)/shard_map/dot_general | solution.py:51
  115.8 19.8 %shard_map.96 = f32[3,864,128]{2,1,0:T(8,128)} custom-call(f32[3,864,128]{2,1,0:T(8,128)} %pad_maximum_fusion.3.x_ref, f32[6,896,128]{2,1,0:T(8,128)} %get-tuple-element.9.dtall_ref, f32[6,896,128]{2,1,0:T(8,128)} %get-tuple-element.10.dside_ref), custom_call_target="tpu_custom_call" | custom-call | tf_op jit(solution)/shard_map/pallas_call | solution.py:183
  135.7 2.5 %copy.30 = f32[864,3,128]{2,0,1:T(8,128)} copy(f32[864,3,128]{2,0,1:T(8,128)} %bitcast.70) | data formatting | bytes 2654208
  (45 shorter events, 1.5 us)
Async XLA Ops:
  0.6 3.0 %copy-start = (f32[512,128]{1,0:T(8,128)S(1)}, f32[512,128]{1,0:T(8,128)}, u32[]{:S(2)}) copy-start(f32[512,128]{1,0:T(8,128)} %param.12) | copy-start | bytes 786436
  0.6 2.8 %copy-start.12 = (s32[512,1]{0,1:T(1,128)S(1)}, s32[512,1]{0,1:T(1,128)}, u32[]{:S(2)}) copy-start(s32[512,1]{0,1:T(1,128)} %param.14) | copy-start | bytes 6148
  0.7 2.8 %copy-start.10 = (f32[256,3,128]{2,0,1:T(8,128)S(1)}, f32[256,3,128]{2,0,1:T(8,128)}, u32[]{:S(2)}) copy-start(f32[256,3,128]{2,0,1:T(8,128)} %param.10) | copy-start | bytes 1179652
  5.2 0.7 copy-start.14
  6.5 1.5 %copy-start.1 = (f32[1024,256]{1,0:T(8,128)}, f32[1024,256]{1,0:T(8,128)S(1)}, u32[]{:S(2)}) copy-start(f32[1024,256]{1,0:T(8,128)S(1)} %fusion.8) | copy-start | bytes 3145732
  6.5 1.5 %copy-start.11 = (s32[256,128]{1,0:T(8,128)S(1)}, s32[256,128]{1,0:T(8,128)}, u32[]{:S(2)}) copy-start(s32[256,128]{1,0:T(8,128)} %param.11) | copy-start | bytes 393220
  10.7 54.9 %all-to-all-start = ((f32[128,8,640]{2,1,0:T(8,128)}), f32[128,8,640]{2,1,0:T(8,128)S(1)}, u32[]{:S(2)}, u32[]{:S(2)}) async-start(f32[128,8,640]{2,1,0:T(8,128)} %bitcast.67), calls=%async_computation | async-start | bytes 5242880 | tf_op jit(solution)/shard_map/all_to_all | solution.py:237
  67.0 2.6 %copy-start.3 = (f32[1024,128]{1,0:T(8,128)S(1)}, f32[1024,128]{1,0:T(8,128)}, u32[]{:S(2)}) copy-start(f32[1024,128]{1,0:T(8,128)} %get-tuple-element.14) | copy-start | bytes 1572868
  70.0 2.6 %copy-start.13 = (f32[3,864,128]{2,1,0:T(8,128)S(1)}, f32[3,864,128]{2,1,0:T(8,128)}, u32[]{:S(2)}) copy-start(f32[3,864,128]{2,1,0:T(8,128)} %get-tuple-element.7) | copy-start | bytes 3981316
  75.9 0.8 copy-start.5
  76.0 1.0 copy-start.7
  76.0 1.1 copy-start.9
  78.9 5.2 %copy-start.4 = (f32[864,3,128]{2,0,1:T(8,128)S(1)}, f32[864,3,128]{2,0,1:T(8,128)}, u32[]{:S(2)}) copy-start(f32[864,3,128]{2,0,1:T(8,128)} %param.8) | copy-start | bytes 3981316
  78.9 29.7 %all-to-all-start.1 = ((f32[128,8,384]{2,1,0:T(8,128)}), f32[128,8,384]{2,1,0:T(8,128)S(1)}, u32[]{:S(2)}, u32[]{:S(2)}) async-start(f32[128,8,384]{2,1,0:T(8,128)} %bitcast.14), calls=%async_computation.1 | async-start | bytes 3145728 | tf_op jit(solution)/shard_map/all_to_all | solution.py:264
  84.1 2.9 %copy-start.8 = (f32[1024,128]{0,1:T(8,128)S(1)}, f32[1024,128]{0,1:T(8,128)}, u32[]{:S(2)}) copy-start(f32[1024,128]{0,1:T(8,128)} %copy-done.7) | copy-start | bytes 1572868
  84.1 4.6 %copy-start.6 = (f32[1024,128]{0,1:T(8,128)S(1)}, f32[1024,128]{0,1:T(8,128)}, u32[]{:S(2)}) copy-start(f32[1024,128]{0,1:T(8,128)} %copy-done.5) | copy-start | bytes 1572868
  108.6 1.7 %copy-start.2 = (f32[1024,256]{1,0:T(8,128)S(1)}, f32[1024,256]{1,0:T(8,128)}, u32[]{:S(2)}) copy-start(f32[1024,256]{1,0:T(8,128)} %copy-done.1) | copy-start | bytes 3145732

commit v5 on v4

--- a/solution.py
+++ b/solution.py
@@ -271,7 +271,6 @@
                                              preferred_element_type=jnp.float32)
          for c in range(chan_count)]
     )
-    ocean_flux, forced = lax.optimization_barrier((ocean_flux, forced))
     current = diffuse_call(sizes, forced, dtall, dside)
     return (jnp.transpose(current, (1, 0, 2)), ocean_flux)
 

time: 139 us -> 126 us (0.906)
  waiting for transfers between devices: 16.9 us -> 0.01 us
  Pallas kernels: 59.9 us -> 65.4 us
  local copies, waits for them, and re-layouts: 13.3 us -> 11.9 us
    all_to_all x1, waiting for transfers between devices: 16.9 us -> 0.01 us  [per_device(): lax.all_to_all(jnp.concatenate(weighted, axis=1), ('atm', 'ocn'), split_a...]
    pallas_call x1, Pallas kernels: 19.8 us -> 25.4 us  [diffuse_call(): pl.pallas_call(functools.partial(diffuse_kernel, sizes), out_shape=jax.Sh...]
    unnamed x37 -> x39, local copies, waits for them, and re-layouts: 6.74 us -> 5.36 us
  transfers between devices with their start and end apart: 2 -> 2, of which waited for: 1 -> 0; matrix products, arithmetic and copies ran while one was open for 8% -> 9% of each run, Pallas kernels for 29% -> 52%
where the time goes in v5:
time: 126 us
  Pallas kernels  65.4 us (52%)
  matrix products  22.2 us (18%)
  starting transfers between devices  16.7 us (13%)
  local copies, waits for them, and re-layouts  11.9 us (9%)
  other arithmetic  8.22 us (7%)
    pallas_call x1, Pallas kernels, smooth_call(): pl.pallas_call(functools.partial(smooth_kernel, sizes), out_shape=(jax.Sh...  40 us
    pallas_call x1, Pallas kernels, diffuse_call(): pl.pallas_call(functools.partial(diffuse_kernel, sizes), out_shape=jax.Sh...  25.4 us
    all_to_all x1, starting transfers between devices, per_device(): lax.all_to_all(outgoing, ('atm', 'ocn'), split_axis=0, concat_axis=0, til...  11.5 us
    dot_general x4, matrix products, select_rows(): jnp.dot(chosen, flat, precision=precision, preferred_element_type=jnp.flo...  8.76 us
    dot_general x3, matrix products, per_device(): jnp.dot(row_pick, weighted[c], precision=HIGHEST, preferred_element_type=...  6.31 us
    dot_general x3, matrix products, per_device(): jnp.dot(pick_rows, smoothed[c], precision=HIGHEST, preferred_element_type...  5.93 us
    unnamed x39, local copies, waits for them, and re-layouts  5.36 us
    all_to_all x1, starting transfers between devices, per_device(): lax.all_to_all(jnp.concatenate(weighted, axis=1), ('atm', 'ocn'), split_a...  5.18 us
  transfers between devices with their start and end apart: 2, of which 0 were waited for; matrix products, arithmetic and copies ran while one was open for 9% of the time, Pallas kernels for 52%

profile of v5, /device:TPU:1, one launch (start us, length us, event | category | flops | bytes accessed | tf_op | source)
XLA Modules:
  0.0 125.5 jit_solution(9598452034393275672)
XLA Ops:
  0.7 0.8 fusion.47
  1.4 0.8 copy.12
  2.2 0.2 fusion.43
  2.5 0.9 fusion.41
  3.7 1.3 %fusion.7 = f32[1024,128]{0,1:T(8,128)S(1)} fusion(f32[512,128]{1,0:T(8,128)S(1)} %copy-done, s32[512]{0:T(512)S(1)} %multiply_add_fusion.1), kind=kOutput, calls=%fused_computation.11 | convolution fusion | flops 805830656 | bytes 788480 | tf_op jit(solution)/shard_map/dot_general | solution.py:51
  5.2 0.6 fusion.6
  5.9 0.6 fusion.8
  6.6 1.5 %fusion.52 = f32[1024,384]{0,1:T(8,128)S(1)} fusion(f32[1024,256]{1,0:T(8,128)S(1)} %fusion.8, f32[256,384]{0,1:T(8,128)S(1)} %bitcast.71), kind=kOutput, calls=%fused_computation.85 | convolution fusion | flops 1207959552 | bytes 3014656 | tf_op jit(solution)/shard_map/dot_general | solution.py:51
  8.0 0.3 convolution_multiply_fusion
  8.6 2.2 %copy.15 = f32[1024,640]{1,0:T(8,128)} copy(f32[1024,640]{0,1:T(8,128)S(1)} %pad_maximum_fusion.1) | data formatting | bytes 5242880 | tf_op jit(solution)/shard_map/concatenate | solution.py:236
  10.7 11.5 %all-to-all-start = ((f32[128,8,640]{2,1,0:T(8,128)}), f32[128,8,640]{2,1,0:T(8,128)S(1)}, u32[]{:S(2)}, u32[]{:S(2)}) async-start(f32[128,8,640]{2,1,0:T(8,128)} %bitcast.67), calls=%async_computation | async-start | bytes 5242880 | tf_op jit(solution)/shard_map/all_to_all | solution.py:237
  22.3 3.4 %pad_maximum_fusion.x_ref = f32[6,864,128]{2,1,0:T(8,128)} fusion(f32[3,864,128]{2,1,0:T(8,128)} %bitcast.72, f32[3,864,128]{2,1,0:T(8,128)} %bitcast.73), kind=kLoop, calls=%fused_computation.7 | loop fusion | flops 663552 | bytes 5308416 | tf_op jit(solution)/shard_map/concatenate | solution.py:240
  25.7 40.0 %shard_map.95 = (f32[3,864,128]{2,1,0:T(8,128)}, f32[6,896,128]{2,1,0:T(8,128)}, f32[6,896,128]{2,1,0:T(8,128)}) custom-call(f32[6,864,128]{2,1,0:T(8,128)} %pad_maximum_fusion.x_ref), custom_call_target="tpu_custom_call" | custom-call | tf_op jit(solution)/shard_map/pallas_call | solution.py:165
  65.7 1.3 %fusion.51 = (f32[1024,128]{1,0:T(8,128)}, f32[1024,128]{1,0:T(8,128)}, f32[1024,128]{1,0:T(8,128)}, f32[1024,128]{1,0:T(8,128)S(1)}, f32[1024]{0:T(1024)S(1)}) fusion(f32[1024,640]{1,0:T(8,128)S(1)} %bitcast.66), kind=kLoop, calls=%fused_computation.84 | loop fusion | flops 130048 | bytes 4722688 | tf_op jit(solution)/shard_map/slice | solution.py:252
  67.0 1.3 %copy.27 = f32[1024,128]{0,1:T(8,128)S(1)} copy(f32[1024,128]{1,0:T(8,128)} %get-tuple-element.8) | data formatting | bytes 1048576
  68.3 1.2 copy.26
  69.6 0.2 copy.25
  69.8 0.2 copy.28
  70.0 2.6 %fusion.17 = f32[1024,128]{0,1:T(8,128)S(1)} fusion(f32[1024,128]{0,1:T(8,128)S(1)} %copy.28, s32[1024]{0:T(1024)S(1)} %convert_element_type.32, f32[3,864,128]{2,1,0:T(8,128)} %get-tuple-element.5), kind=kOutput, calls=%fused_computation.24 | convolution fusion | flops 1359970304 | bytes 1495040 | tf_op jit(solution)/shard_map/dot_general | solution.py:250
  72.6 1.5 %fusion.16 = f32[1024,128]{0,1:T(8,128)S(1)} fusion(f32[1024,128]{0,1:T(8,128)S(1)} %copy.27, s32[1024]{0:T(1024)S(1)} %convert_element_type.32, f32[3,864,128]{2,1,0:T(8,128)S(1)} %copy-done.14), kind=kOutput, calls=%fused_computation.23 | convolution fusion | flops 1359970304 | bytes 1495040 | tf_op jit(solution)/shard_map/dot_general | solution.py:250
  74.1 1.9 %multiply_multiply_fusion.3 = (f32[1024,128]{0,1:T(8,128)S(1)}, f32[1024,128]{0,1:T(8,128)S(1)}, f32[1024,128]{0,1:T(8,128)S(1)}) fusion(f32[1024,128]{0,1:T(8,128)S(1)} %copy.25, f32[1024,128]{0,1:T(8,128)S(1)} %fusion.17, f32[1024,128]{0,1:T(8,128)S(1)} %fusion.16, f32[1024,128]{0,1:T(8,128)S(1)} %copy.26, f32[3,864,128]{2,1,0:T(8,128)S(1)} %copy-done.14, ...), kind=kOutput, calls=%fused_computation.44 | convolution fusion | flops 1362198528 | bytes 4116480 | tf_op jit(solution)/shard_map/dot_general | solution.py:250
  76.0 0.8 copy-done.6
  77.3 1.7 %copy.20 = f32[1024,384]{1,0:T(8,128)} copy(f32[1024,384]{0,1:T(8,128)S(1)} %pad_maximum_fusion.2) | data formatting | bytes 3145728 | tf_op jit(solution)/shard_map/concatenate | solution.py:265
  79.0 5.2 %all-to-all-start.1 = ((f32[128,8,384]{2,1,0:T(8,128)}), f32[128,8,384]{2,1,0:T(8,128)S(1)}, u32[]{:S(2)}, u32[]{:S(2)}) async-start(f32[128,8,384]{2,1,0:T(8,128)} %bitcast.21), calls=%async_computation.1 | async-start | bytes 3145728 | tf_op jit(solution)/shard_map/all_to_all | solution.py:264
  84.2 2.9 %fusion.19 = f32[1,864,128]{2,1,0:T(8,128)S(1)} fusion(f32[1024,128]{0,1:T(8,128)} %copy-done.10, s32[1024]{0:T(1024)S(1)} %convert_element_type.32, f32[3,864,128]{2,1,0:T(8,128)S(1)} %bitcast.74), kind=kOutput, calls=%fused_computation.26 | convolution fusion | flops 1359949824 | bytes 1413120 | tf_op jit(solution)/shard_map/dot_general | solution.py:270
  87.1 1.7 %fusion.25 = f32[1,864,128]{2,1,0:T(8,128)S(1)} fusion(f32[1024,128]{0,1:T(8,128)S(1)} %copy-done.9, s32[1024]{0:T(1024)S(1)} %convert_element_type.32, f32[3,864,128]{2,1,0:T(8,128)S(1)} %bitcast.75), kind=kOutput, calls=%fused_computation.32 | convolution fusion | flops 1360060416 | bytes 1413120 | tf_op jit(solution)/shard_map/dot_general | solution.py:270
  88.8 1.7 %fusion.22 = f32[1,864,128]{2,1,0:T(8,128)S(1)} fusion(f32[1024,128]{0,1:T(8,128)S(1)} %copy-done.7, s32[1024]{0:T(1024)S(1)} %convert_element_type.32, f32[3,864,128]{2,1,0:T(8,128)S(1)} %bitcast.76), kind=kOutput, calls=%fused_computation.29 | convolution fusion | flops 1360060416 | bytes 1413120 | tf_op jit(solution)/shard_map/dot_general | solution.py:270
  90.5 1.1 pad_maximum_fusion.3.x_ref
  91.7 25.4 %shard_map.96 = f32[3,864,128]{2,1,0:T(8,128)} custom-call(f32[3,864,128]{2,1,0:T(8,128)} %pad_maximum_fusion.3.x_ref, f32[6,896,128]{2,1,0:T(8,128)} %get-tuple-element.6.dtall_ref, f32[6,896,128]{2,1,0:T(8,128)} %get-tuple-element.7.dside_ref), custom_call_target="tpu_custom_call" | custom-call | tf_op jit(solution)/shard_map/pallas_call | solution.py:183
  117.1 1.6 %copy.21 = f32[384,1024]{1,0:T(8,128)} copy(f32[384,1024]{0,1:T(8,128)S(1)} %bitcast.68) | data formatting | bytes 3145728 | tf_op jit(solution)/shard_map/dot_general | solution.py:51
  118.8 5.7 %fusion.26 = f32[256,3,128]{2,0,1:T(8,128)} fusion(f32[3,128,1024]{2,1,0:T(8,128)} %bitcast.69, f32[1024,256]{1,0:T(8,128)S(1)} %copy-done.2), kind=kOutput, calls=%fused_computation.33 | convolution fusion | flops 1207959552 | bytes 3014656 | tf_op jit(solution)/shard_map/dot_general | solution.py:51
  124.5 1.1 copy.30
  (47 shorter events, 1.4 us)
Async XLA Ops:
  0.6 3.0 %copy-start = (f32[512,128]{1,0:T(8,128)S(1)}, f32[512,128]{1,0:T(8,128)}, u32[]{:S(2)}) copy-start(f32[512,128]{1,0:T(8,128)} %param.12) | copy-start | bytes 786436
  0.6 2.8 %copy-start.13 = (s32[512,1]{0,1:T(1,128)S(1)}, s32[512,1]{0,1:T(1,128)}, u32[]{:S(2)}) copy-start(s32[512,1]{0,1:T(1,128)} %param.14) | copy-start | bytes 6148
  0.7 2.8 %copy-start.11 = (f32[256,3,128]{2,0,1:T(8,128)S(1)}, f32[256,3,128]{2,0,1:T(8,128)}, u32[]{:S(2)}) copy-start(f32[256,3,128]{2,0,1:T(8,128)} %param.10) | copy-start | bytes 1179652
  5.2 0.7 copy-start.15
  6.5 1.5 %copy-start.1 = (f32[1024,256]{1,0:T(8,128)}, f32[1024,256]{1,0:T(8,128)S(1)}, u32[]{:S(2)}) copy-start(f32[1024,256]{1,0:T(8,128)S(1)} %fusion.8) | copy-start | bytes 3145732
  6.5 1.5 %copy-start.12 = (s32[256,128]{1,0:T(8,128)S(1)}, s32[256,128]{1,0:T(8,128)}, u32[]{:S(2)}) copy-start(s32[256,128]{1,0:T(8,128)} %param.11) | copy-start | bytes 393220
  10.7 54.9 %all-to-all-start = ((f32[128,8,640]{2,1,0:T(8,128)}), f32[128,8,640]{2,1,0:T(8,128)S(1)}, u32[]{:S(2)}, u32[]{:S(2)}) async-start(f32[128,8,640]{2,1,0:T(8,128)} %bitcast.67), calls=%async_computation | async-start | bytes 5242880 | tf_op jit(solution)/shard_map/all_to_all | solution.py:237
  67.0 2.6 %copy-start.4 = (f32[1024,128]{1,0:T(8,128)S(1)}, f32[1024,128]{1,0:T(8,128)}, u32[]{:S(2)}) copy-start(f32[1024,128]{1,0:T(8,128)} %get-tuple-element.10) | copy-start | bytes 1572868
  70.0 2.6 %copy-start.14 = (f32[3,864,128]{2,1,0:T(8,128)S(1)}, f32[3,864,128]{2,1,0:T(8,128)}, u32[]{:S(2)}) copy-start(f32[3,864,128]{2,1,0:T(8,128)} %get-tuple-element.5) | copy-start | bytes 3981316
  76.0 0.8 copy-start.6
  76.0 1.0 copy-start.8
  76.0 1.1 copy-start.10
  79.0 5.2 %copy-start.5 = (f32[864,3,128]{2,0,1:T(8,128)S(1)}, f32[864,3,128]{2,0,1:T(8,128)}, u32[]{:S(2)}) copy-start(f32[864,3,128]{2,0,1:T(8,128)} %param.8) | copy-start | bytes 3981316
  79.0 38.1 %all-to-all-start.1 = ((f32[128,8,384]{2,1,0:T(8,128)}), f32[128,8,384]{2,1,0:T(8,128)S(1)}, u32[]{:S(2)}, u32[]{:S(2)}) async-start(f32[128,8,384]{2,1,0:T(8,128)} %bitcast.21), calls=%async_computation.1 | async-start | bytes 3145728 | tf_op jit(solution)/shard_map/all_to_all | solution.py:264
  84.2 2.9 %copy-start.9 = (f32[1024,128]{0,1:T(8,128)S(1)}, f32[1024,128]{0,1:T(8,128)}, u32[]{:S(2)}) copy-start(f32[1024,128]{0,1:T(8,128)} %copy-done.8) | copy-start | bytes 1572868
  84.2 4.6 %copy-start.7 = (f32[1024,128]{0,1:T(8,128)S(1)}, f32[1024,128]{0,1:T(8,128)}, u32[]{:S(2)}) copy-start(f32[1024,128]{0,1:T(8,128)} %copy-done.6) | copy-start | bytes 1572868
  117.1 1.7 %copy-start.2 = (f32[1024,256]{1,0:T(8,128)S(1)}, f32[1024,256]{1,0:T(8,128)}, u32[]{:S(2)}) copy-start(f32[1024,256]{1,0:T(8,128)} %copy-done.1) | copy-start | bytes 3145732
  118.8 5.7 %copy-start.3 = (f32[3,864,128]{2,1,0:T(8,128)S(1)}, f32[3,864,128]{2,1,0:T(8,128)}, u32[]{:S(2)}) copy-start(f32[3,864,128]{2,1,0:T(8,128)} %shard_map.96) | copy-start | bytes 3981316

commit v6 on v5

--- a/solution.py
+++ b/solution.py
@@ -234,13 +234,14 @@
     out_area = select_rows(slot_pick.astype(jnp.float32), intersection_area)
     out_weight = out_area * out_mask
     outgoing = jnp.concatenate([out_ocean, out_weight, out_label], axis=1)
-    incoming = lax.all_to_all(outgoing, ("atm", "ocn"), split_axis=0, concat_axis=0, tiled=True)
 
     atm_planes = jnp.transpose(atm_state, (1, 0, 2))
     both = jnp.concatenate([atm_planes, jnp.transpose(diffusivity, (1, 0, 2))], axis=0)
     sizes = (atm_count, ocn_count)
     rows_padded = -(-(row_count + 2 * EDGE) // 128) * 128
     smoothed, dtall, dside = smooth_call(sizes, both, chan_count, rows_padded)
+    outgoing, smoothed = lax.optimization_barrier((outgoing, smoothed))
+    incoming = lax.all_to_all(outgoing, ("atm", "ocn"), split_axis=0, concat_axis=0, tiled=True)
 
     in_labels = jnp.max(incoming[:, plane + seg_width :], axis=1).astype(jnp.int32)
     row_pick = (

time: 126 us -> 138 us (1.095)
  blocking collectives: 0 us -> 44 us
  Pallas kernels: 65.4 us -> 45.9 us
  starting transfers between devices: 16.7 us -> 5.13 us
  other arithmetic: 8.22 us -> 6.49 us
  matrix products: 22.2 us -> 23.8 us
    all_to_all x0 -> x1, blocking collectives: none -> 44 us  [per_device(): lax.all_to_all(outgoing, ('atm', 'ocn'), split_axis=0, concat_axis=0, til...]
    pallas_call x1, Pallas kernels: 40 us -> 20.4 us  [smooth_call(): pl.pallas_call(functools.partial(smooth_kernel, sizes), out_shape=(jax.Sh...]
    all_to_all x1 -> x0, starting transfers between devices: 11.5 us -> none  [per_device(): lax.all_to_all(outgoing, ('atm', 'ocn'), split_axis=0, concat_axis=0, til...]
    concatenate x1 -> x0, local copies, waits for them, and re-layouts: 2.19 us -> none  [per_device(): outgoing = jnp.concatenate([out_ocean, out_weight, out_label], axis=1)]
    optimization_barrier x0 -> x1, local copies, waits for them, and re-layouts: none -> 2.1 us  [per_device(): outgoing, smoothed = lax.optimization_barrier((outgoing, smoothed))]
    concatenate x1, other arithmetic: 3.41 us -> 1.67 us  [per_device(): jnp.concatenate([atm_planes, jnp.transpose(diffusivity, (1, 0, 2))], axis=0)]
    unnamed x39 -> x41, local copies, waits for them, and re-layouts: 5.36 us -> 4.26 us
  transfers between devices with their start and end apart: 2 -> 1, of which waited for: 0 -> 0; matrix products, arithmetic and copies ran while one was open for 9% -> 5% of each run, Pallas kernels for 52% -> 19%
where the time goes in v6:
time: 138 us; the launch traced here: 137 us
  Pallas kernels  45.9 us (33%)
  blocking collectives  44 us (32%)
  matrix products  23.8 us (17%)
  local copies, waits for them, and re-layouts  10.7 us (8%)
  other arithmetic  6.49 us (5%)
  starting transfers between devices  5.13 us (4%)
    all_to_all x1, blocking collectives, per_device(): lax.all_to_all(outgoing, ('atm', 'ocn'), split_axis=0, concat_axis=0, til...  44 us
    pallas_call x1, Pallas kernels, diffuse_call(): pl.pallas_call(functools.partial(diffuse_kernel, sizes), out_shape=jax.Sh...  25.6 us
    pallas_call x1, Pallas kernels, smooth_call(): pl.pallas_call(functools.partial(smooth_kernel, sizes), out_shape=(jax.Sh...  20.4 us
    dot_general x4, matrix products, select_rows(): jnp.dot(chosen, flat, precision=precision, preferred_element_type=jnp.flo...  9.54 us
    dot_general x3, matrix products, per_device(): jnp.dot(pick_rows, smoothed[c], precision=HIGHEST, preferred_element_type...  6.7 us
    dot_general x3, matrix products, per_device(): jnp.dot(row_pick, weighted[c], precision=HIGHEST, preferred_element_type=...  6.31 us
    all_to_all x1, starting transfers between devices, per_device(): lax.all_to_all(jnp.concatenate(weighted, axis=1), ('atm', 'ocn'), split_a...  5.13 us
    unnamed x41, local copies, waits for them, and re-layouts  4.26 us
  transfers between devices with their start and end apart: 1, of which 0 were waited for; matrix products, arithmetic and copies ran while one was open for 5% of the time, Pallas kernels for 19%

profile of v6, /device:TPU:1, one launch (start us, length us, event | category | flops | bytes accessed | tf_op | source)
XLA Modules:
  0.0 137.0 jit_solution(5157553219695514034)
XLA Ops:
  0.7 0.8 fusion.47
  1.4 0.8 copy.12
  2.2 0.2 fusion.43
  2.5 0.9 fusion.41
  3.7 2.1 %fusion.7 = f32[1024,128]{0,1:T(8,128)} fusion(f32[512,128]{1,0:T(8,128)S(1)} %copy-done, s32[512]{0:T(512)S(1)} %multiply_add_fusion.1), kind=kOutput, calls=%fused_computation.11 | convolution fusion | flops 805830656 | bytes 788480 | tf_op jit(solution)/shard_map/dot_general | solution.py:51
  6.0 0.6 fusion.6
  6.7 0.6 fusion.8
  7.4 0.6 copy-done.4
  8.0 0.6 copy-done.5
  8.6 1.7 %pad_maximum_fusion.x_ref = f32[6,864,128]{2,1,0:T(8,128)} fusion(f32[3,864,128]{2,1,0:T(8,128)S(1)} %bitcast.72, f32[3,864,128]{2,1,0:T(8,128)S(1)} %bitcast.73), kind=kLoop, calls=%fused_computation.7 | loop fusion | flops 663552 | bytes 5308416 | tf_op jit(solution)/shard_map/concatenate | solution.py:239
  10.2 20.4 %shard_map.95 = (f32[3,864,128]{2,1,0:T(8,128)}, f32[6,896,128]{2,1,0:T(8,128)}, f32[6,896,128]{2,1,0:T(8,128)}) custom-call(f32[6,864,128]{2,1,0:T(8,128)} %pad_maximum_fusion.x_ref), custom_call_target="tpu_custom_call" | custom-call | tf_op jit(solution)/shard_map/pallas_call | solution.py:165
  30.6 1.5 %fusion.52 = f32[1024,384]{0,1:T(8,128)S(1)} fusion(f32[1024,256]{1,0:T(8,128)S(1)} %fusion.8, f32[256,384]{0,1:T(8,128)S(1)} %bitcast.71), kind=kOutput, calls=%fused_computation.85 | convolution fusion | flops 1207959552 | bytes 3014656 | tf_op jit(solution)/shard_map/dot_general | solution.py:51
  32.1 0.3 convolution_multiply_fusion
  32.4 0.2 pad_maximum_fusion.1
  32.7 2.1 %copy.15 = f32[1024,640]{1,0:T(8,128)} copy(f32[1024,640]{0,1:T(8,128)S(1)} %pad_maximum_fusion.1) | data formatting | bytes 5242880 | tf_op jit(solution)/shard_map/optimization_barrier | solution.py:243
  34.8 44.0 %all_to_all.24 = f32[128,8,640]{2,1,0:T(8,128)S(1)} all-to-all(f32[128,8,640]{2,1,0:T(8,128)} %bitcast.67), channel_id=1, replica_groups=mesh['atm'=16,'ocn'=8] {'atm','ocn'}, dimensions={0} | all-to-all | bytes 5242880 | tf_op jit(solution)/shard_map/all_to_all | solution.py:244
  78.7 0.3 fusion.51
  79.8 2.6 %fusion.16 = f32[1024,128]{0,1:T(8,128)S(1)} fusion(f32[1024,128]{0,1:T(8,128)S(1)} %copy.27, s32[1024]{0:T(1024)S(1)} %convert_element_type.32, f32[3,864,128]{2,1,0:T(8,128)} %get-tuple-element.9), kind=kOutput, calls=%fused_computation.23 | convolution fusion | flops 1359970304 | bytes 1495040 | tf_op jit(solution)/shard_map/dot_general | solution.py:251
  82.5 1.5 %fusion.17 = f32[1024,128]{0,1:T(8,128)S(1)} fusion(f32[1024,128]{0,1:T(8,128)S(1)} %copy.28, s32[1024]{0:T(1024)S(1)} %convert_element_type.32, f32[3,864,128]{2,1,0:T(8,128)S(1)} %copy-done.15), kind=kOutput, calls=%fused_computation.24 | convolution fusion | flops 1359970304 | bytes 1495040 | tf_op jit(solution)/shard_map/dot_general | solution.py:251
  83.9 2.7 %multiply_multiply_fusion.3 = (f32[1024,128]{0,1:T(8,128)}, f32[1024,128]{0,1:T(8,128)S(1)}, f32[1024,128]{0,1:T(8,128)S(1)}) fusion(f32[1024,128]{0,1:T(8,128)S(1)} %copy.25, f32[1024,128]{0,1:T(8,128)S(1)} %fusion.17, f32[1024,128]{0,1:T(8,128)S(1)} %fusion.16, f32[1024,128]{0,1:T(8,128)S(1)} %copy.26, f32[3,864,128]{2,1,0:T(8,128)S(1)} %copy-done.15, ...), kind=kOutput, calls=%fused_computation.44 | convolution fusion | flops 1362198528 | bytes 4116480 | tf_op jit(solution)/shard_map/dot_general | solution.py:251
  86.6 0.8 copy-done.8
  87.5 1.2 pad_maximum_fusion.2
  88.7 1.7 %copy.20 = f32[1024,384]{1,0:T(8,128)} copy(f32[1024,384]{0,1:T(8,128)S(1)} %pad_maximum_fusion.2) | data formatting | bytes 3145728 | tf_op jit(solution)/shard_map/concatenate | solution.py:266
  90.4 5.1 %all-to-all-start.1 = ((f32[128,8,384]{2,1,0:T(8,128)}), f32[128,8,384]{2,1,0:T(8,128)S(1)}, u32[]{:S(2)}, u32[]{:S(2)}) async-start(f32[128,8,384]{2,1,0:T(8,128)} %bitcast.21), calls=%async_computation.1 | async-start | bytes 3145728 | tf_op jit(solution)/shard_map/all_to_all | solution.py:265
  95.6 2.9 %fusion.19 = f32[1,864,128]{2,1,0:T(8,128)S(1)} fusion(f32[1024,128]{0,1:T(8,128)} %get-tuple-element.17, s32[1024]{0:T(1024)S(1)} %convert_element_type.32, f32[3,864,128]{2,1,0:T(8,128)S(1)} %bitcast.74), kind=kOutput, calls=%fused_computation.26 | convolution fusion | flops 1359949824 | bytes 1413120 | tf_op jit(solution)/shard_map/dot_general | solution.py:271
  98.4 1.7 %fusion.25 = f32[1,864,128]{2,1,0:T(8,128)S(1)} fusion(f32[1024,128]{0,1:T(8,128)S(1)} %copy-done.11, s32[1024]{0:T(1024)S(1)} %convert_element_type.32, f32[3,864,128]{2,1,0:T(8,128)S(1)} %bitcast.75), kind=kOutput, calls=%fused_computation.32 | convolution fusion | flops 1360060416 | bytes 1413120 | tf_op jit(solution)/shard_map/dot_general | solution.py:271
  100.2 1.7 %fusion.22 = f32[1,864,128]{2,1,0:T(8,128)S(1)} fusion(f32[1024,128]{0,1:T(8,128)S(1)} %copy-done.9, s32[1024]{0:T(1024)S(1)} %convert_element_type.32, f32[3,864,128]{2,1,0:T(8,128)S(1)} %bitcast.76), kind=kOutput, calls=%fused_computation.29 | convolution fusion | flops 1360060416 | bytes 1413120 | tf_op jit(solution)/shard_map/dot_general | solution.py:271
  101.9 1.1 pad_maximum_fusion.3.x_ref
  103.0 25.6 %shard_map.96 = f32[3,864,128]{2,1,0:T(8,128)} custom-call(f32[3,864,128]{2,1,0:T(8,128)} %pad_maximum_fusion.3.x_ref, f32[6,896,128]{2,1,0:T(8,128)} %get-tuple-element.10.dtall_ref, f32[6,896,128]{2,1,0:T(8,128)} %get-tuple-element.11.dside_ref), custom_call_target="tpu_custom_call" | custom-call | tf_op jit(solution)/shard_map/pallas_call | solution.py:183
  128.6 1.6 %copy.21 = f32[384,1024]{1,0:T(8,128)} copy(f32[384,1024]{0,1:T(8,128)S(1)} %bitcast.68) | data formatting | bytes 3145728 | tf_op jit(solution)/shard_map/dot_general | solution.py:51
  130.3 5.7 %fusion.26 = f32[256,3,128]{2,0,1:T(8,128)} fusion(f32[3,128,1024]{2,1,0:T(8,128)} %bitcast.69, f32[1024,256]{1,0:T(8,128)S(1)} %copy-done.2), kind=kOutput, calls=%fused_computation.33 | convolution fusion | flops 1207959552 | bytes 3014656 | tf_op jit(solution)/shard_map/dot_general | solution.py:51
  136.0 1.1 copy.30
  (48 shorter events, 1.6 us)
Async XLA Ops:
  0.6 3.0 %copy-start = (f32[512,128]{1,0:T(8,128)S(1)}, f32[512,128]{1,0:T(8,128)}, u32[]{:S(2)}) copy-start(f32[512,128]{1,0:T(8,128)} %param.12) | copy-start | bytes 786436
  0.6 2.8 %copy-start.14 = (s32[512,1]{0,1:T(1,128)S(1)}, s32[512,1]{0,1:T(1,128)}, u32[]{:S(2)}) copy-start(s32[512,1]{0,1:T(1,128)} %param.14) | copy-start | bytes 6148
  0.7 2.8 %copy-start.12 = (f32[256,3,128]{2,0,1:T(8,128)S(1)}, f32[256,3,128]{2,0,1:T(8,128)}, u32[]{:S(2)}) copy-start(f32[256,3,128]{2,0,1:T(8,128)} %param.10) | copy-start | bytes 1179652
  6.0 0.7 copy-start.16
  6.6 1.3 copy-start.4
  6.7 1.9 %copy-start.5 = (f32[864,3,128]{2,0,1:T(8,128)S(1)}, f32[864,3,128]{2,0,1:T(8,128)}, u32[]{:S(2)}) copy-start(f32[864,3,128]{2,0,1:T(8,128)} %param.8) | copy-start | bytes 3981316
  7.3 24.8 %copy-start.1 = (f32[1024,256]{1,0:T(8,128)}, f32[1024,256]{1,0:T(8,128)S(1)}, u32[]{:S(2)}) copy-start(f32[1024,256]{1,0:T(8,128)S(1)} %fusion.8) | copy-start | bytes 3145732
  30.6 1.5 %copy-start.7 = (f32[1024,128]{0,1:T(8,128)S(1)}, f32[1024,128]{0,1:T(8,128)}, u32[]{:S(2)}) copy-start(f32[1024,128]{0,1:T(8,128)} %fusion.7) | copy-start | bytes 1572868
  30.6 1.5 %copy-start.13 = (s32[256,128]{1,0:T(8,128)S(1)}, s32[256,128]{1,0:T(8,128)}, u32[]{:S(2)}) copy-start(s32[256,128]{1,0:T(8,128)} %param.11) | copy-start | bytes 393220
  79.8 2.6 %copy-start.15 = (f32[3,864,128]{2,1,0:T(8,128)S(1)}, f32[3,864,128]{2,1,0:T(8,128)}, u32[]{:S(2)}) copy-start(f32[3,864,128]{2,1,0:T(8,128)} %get-tuple-element.9) | copy-start | bytes 3981316
  86.6 0.8 copy-start.8
  86.6 1.0 copy-start.10
  90.4 5.1 %copy-start.6 = (f32[864,3,128]{2,0,1:T(8,128)S(1)}, f32[864,3,128]{2,0,1:T(8,128)}, u32[]{:S(2)}) copy-start(f32[864,3,128]{2,0,1:T(8,128)} %param.8) | copy-start | bytes 3981316
  90.4 38.2 %all-to-all-start.1 = ((f32[128,8,384]{2,1,0:T(8,128)}), f32[128,8,384]{2,1,0:T(8,128)S(1)}, u32[]{:S(2)}, u32[]{:S(2)}) async-start(f32[128,8,384]{2,1,0:T(8,128)} %bitcast.21), calls=%async_computation.1 | async-start | bytes 3145728 | tf_op jit(solution)/shard_map/all_to_all | solution.py:265
  95.5 2.9 %copy-start.11 = (f32[1024,128]{0,1:T(8,128)S(1)}, f32[1024,128]{0,1:T(8,128)}, u32[]{:S(2)}) copy-start(f32[1024,128]{0,1:T(8,128)} %copy-done.10) | copy-start | bytes 1572868
  95.5 4.6 %copy-start.9 = (f32[1024,128]{0,1:T(8,128)S(1)}, f32[1024,128]{0,1:T(8,128)}, u32[]{:S(2)}) copy-start(f32[1024,128]{0,1:T(8,128)} %copy-done.8) | copy-start | bytes 1572868
  128.6 1.6 %copy-start.2 = (f32[1024,256]{1,0:T(8,128)S(1)}, f32[1024,256]{1,0:T(8,128)}, u32[]{:S(2)}) copy-start(f32[1024,256]{1,0:T(8,128)} %copy-done.1) | copy-start | bytes 3145732
  130.3 5.7 %copy-start.3 = (f32[3,864,128]{2,1,0:T(8,128)S(1)}, f32[3,864,128]{2,1,0:T(8,128)}, u32[]{:S(2)}) copy-start(f32[3,864,128]{2,1,0:T(8,128)} %shard_map.96) | copy-start | bytes 3981316

commit v7 on v5

--- a/solution.py
+++ b/solution.py
@@ -65,63 +65,74 @@
     down = lax.rem(me_a + 1, atm_n)
     left = lax.rem(me_o + ocn_n - 1, ocn_n)
     right = lax.rem(me_o + 1, ocn_n)
+    peers = ((up, me_o), (down, me_o), (me_a, left), (me_a, right),
+             (up, left), (up, right), (down, left), (down, right))
     barrier = pltpu.get_barrier_semaphore()
-    for peer in ((up, me_o), (down, me_o), (me_a, left), (me_a, right)):
+    for peer in peers:
         pl.semaphore_signal(barrier, 1, device_id=peer, device_id_type=MESH)
-    pl.semaphore_wait(barrier, 4)
-
-    to_down = pltpu.make_async_remote_copy(
-        x_ref.at[:, rows - EDGE :, :], rows_buf.at[0], send_sem.at[0], recv_sem.at[0],
-        device_id=(down, me_o), device_id_type=MESH)
-    to_up = pltpu.make_async_remote_copy(
-        x_ref.at[:, :EDGE, :], rows_buf.at[1], send_sem.at[1], recv_sem.at[1],
-        device_id=(up, me_o), device_id_type=MESH)
-    to_down.start()
-    to_up.start()
-    to_down.wait()
-    to_up.wait()
+    pl.semaphore_wait(barrier, len(peers))
+
+    spare = jnp.zeros((rows_padded - rows, width), jnp.float32)
+    for c in range(chans):
+        flipped = jnp.concatenate([x_ref[c], spare], axis=0).T
+        colsend[0, c] = flipped[:EDGE]
+        colsend[1, c] = flipped[width - EDGE :]
+
+    last = x_ref.at[:, rows - EDGE :, :]
+    first = x_ref.at[:, :EDGE, :]
+    plan = (
+        (last, rows_buf.at[0], (down, me_o)),
+        (first, rows_buf.at[1], (up, me_o)),
+        (last, rows_buf.at[2], (down, right)),
+        (last, rows_buf.at[3], (down, left)),
+        (first, rows_buf.at[4], (up, right)),
+        (first, rows_buf.at[5], (up, left)),
+        (colsend.at[0], cols_buf.at[1], (me_a, left)),
+        (colsend.at[1], cols_buf.at[0], (me_a, right)),
+    )
+    copies = []
+    for k, (src, dst, peer) in enumerate(plan):
+        copy = pltpu.make_async_remote_copy(
+            src, dst, send_sem.at[k], recv_sem.at[k], device_id=peer, device_id_type=MESH)
+        copy.start()
+        copies.append(copy)
+    for copy in copies:
+        copy.wait()
 
     has_up = me_a > 0
     has_down = me_a < atm_n - 1
     has_left = me_o > 0
     has_right = me_o < ocn_n - 1
-    spare = jnp.zeros((rows_padded - rows - 2 * EDGE, width), jnp.float32)
+    lane = lax.broadcasted_iota(jnp.int32, (EDGE, width), 1)
+    low_lanes = lane < EDGE
+    high_lanes = lane >= width - EDGE
+    tail = jnp.zeros((rows_padded - rows - 2 * EDGE, width), jnp.float32)
+    middle = jnp.zeros((width - 2 * EDGE, rows_padded), jnp.float32)
     for c in range(chans):
         top = jnp.where(has_up, rows_buf[0, c], 0.0)
         bottom = jnp.where(has_down, rows_buf[1, c], 0.0)
-        tall = jnp.concatenate([top, x_ref[c], bottom, spare], axis=0)
-        tall_s[c] = tall
-        flipped = tall.T
-        colsend[0, c] = flipped[:EDGE]
-        colsend[1, c] = flipped[width - EDGE :]
-
-    to_left = pltpu.make_async_remote_copy(
-        colsend.at[0], cols_buf.at[1], send_sem.at[2], recv_sem.at[2],
-        device_id=(me_a, left), device_id_type=MESH)
-    to_right = pltpu.make_async_remote_copy(
-        colsend.at[1], cols_buf.at[0], send_sem.at[3], recv_sem.at[3],
-        device_id=(me_a, right), device_id_type=MESH)
-    to_left.start()
-    to_right.start()
-    to_left.wait()
-    to_right.wait()
-
-    middle = jnp.zeros((width - 2 * EDGE, rows_padded), jnp.float32)
-    for c in range(chans):
+        tall_s[c] = jnp.concatenate([top, x_ref[c], bottom, tail], axis=0)
         from_left = jnp.where(has_left, cols_buf[0, c], 0.0)
         from_right = jnp.where(has_right, cols_buf[1, c], 0.0)
-        side_s[c] = jnp.concatenate([from_right, middle, from_left], axis=0).T
+        own = jnp.concatenate([from_right, middle, from_left], axis=0).T
+        corner_top = jnp.where(
+            low_lanes & (has_up & has_right), rows_buf[3, c],
+            jnp.where(high_lanes & (has_up & has_left), rows_buf[2, c], 0.0))
+        corner_bottom = jnp.where(
+            low_lanes & (has_down & has_right), rows_buf[5, c],
+            jnp.where(high_lanes & (has_down & has_left), rows_buf[4, c], 0.0))
+        side_s[c] = jnp.concatenate([corner_top, own[:rows], corner_bottom, tail], axis=0)
 
 
 def exchange_scratch(chans, rows_padded, width):
     return [
-        pltpu.VMEM((2, chans, EDGE, width), jnp.float32),
+        pltpu.VMEM((6, chans, EDGE, width), jnp.float32),
         pltpu.VMEM((2, chans, EDGE, rows_padded), jnp.float32),
         pltpu.VMEM((2, chans, EDGE, rows_padded), jnp.float32),
         pltpu.VMEM((chans, rows_padded, width), jnp.float32),
         pltpu.VMEM((chans, rows_padded, width), jnp.float32),
-        pltpu.SemaphoreType.DMA((4,)),
-        pltpu.SemaphoreType.DMA((4,)),
+        pltpu.SemaphoreType.DMA((8,)),
+        pltpu.SemaphoreType.DMA((8,)),
     ]
 
 
@@ -139,8 +150,9 @@
     rows_buf, cols_buf, colsend, tall_s, side_s, send_sem, recv_sem = scratch
     exchange(sizes, x_ref, rows_buf, cols_buf, colsend, tall_s, side_s, send_sem, recv_sem)
     rows, width = out_ref.shape[1], out_ref.shape[2]
-    tall_out[...] = tall_s[...]
-    side_out[...] = side_s[...]
+    kept = tall_out.shape[0]
+    tall_out[...] = tall_s[kept:]
+    side_out[...] = side_s[kept:]
     for chan in range(out_ref.shape[0]):
         state = jnp.concatenate([tall_s[chan], side_s[chan]], axis=1)
         out_ref[chan] = (0.5 * state + 0.125 * stencil_sum(state))[EDGE : EDGE + rows, :width]
@@ -166,8 +178,8 @@
         functools.partial(smooth_kernel, sizes),
         out_shape=(
             jax.ShapeDtypeStruct((chans, rows, width), jnp.float32),
-            jax.ShapeDtypeStruct((total, rows_padded, width), jnp.float32),
-            jax.ShapeDtypeStruct((total, rows_padded, width), jnp.float32),
+            jax.ShapeDtypeStruct((total - chans, rows_padded, width), jnp.float32),
+            jax.ShapeDtypeStruct((total - chans, rows_padded, width), jnp.float32),
         ),
         in_specs=[vmem],
         out_specs=(vmem, vmem, vmem),

time: 126 us -> 120 us (0.952)
  Pallas kernels: 65.4 us -> 59.5 us
    pallas_call x1, Pallas kernels: 25.4 us -> 22.3 us  [diffuse_call(): pl.pallas_call(functools.partial(diffuse_kernel, sizes), out_shape=jax.Sh...]
    pallas_call x1, Pallas kernels: 40 us -> 37.2 us  [smooth_call(): pl.pallas_call(functools.partial(smooth_kernel, sizes), out_shape=(jax.Sh...]
  transfers between devices with their start and end apart: 2 -> 2, of which waited for: 0 -> 0; matrix products, arithmetic and copies ran while one was open for 9% -> 9% of each run, Pallas kernels for 52% -> 50%
where the time goes in v7:
time: 120 us
  Pallas kernels  59.5 us (50%)
  matrix products  22.2 us (18%)
  starting transfers between devices  16.8 us (14%)
  local copies, waits for them, and re-layouts  11.9 us (10%)
  other arithmetic  8.2 us (7%)
    pallas_call x1, Pallas kernels, smooth_call(): pl.pallas_call(functools.partial(smooth_kernel, sizes), out_shape=(jax.Sh...  37.2 us
    pallas_call x1, Pallas kernels, diffuse_call(): pl.pallas_call(functools.partial(diffuse_kernel, sizes), out_shape=jax.Sh...  22.3 us
    all_to_all x1, starting transfers between devices, per_device(): lax.all_to_all(outgoing, ('atm', 'ocn'), split_axis=0, concat_axis=0, til...  11.5 us
    dot_general x4, matrix products, select_rows(): jnp.dot(chosen, flat, precision=precision, preferred_element_type=jnp.flo...  8.76 us
    dot_general x3, matrix products, per_device(): jnp.dot(row_pick, weighted[c], precision=HIGHEST, preferred_element_type=...  6.31 us
    dot_general x3, matrix products, per_device(): jnp.dot(pick_rows, smoothed[c], precision=HIGHEST, preferred_element_type...  5.94 us
    unnamed x39, local copies, waits for them, and re-layouts  5.4 us
    all_to_all x1, starting transfers between devices, per_device(): lax.all_to_all(jnp.concatenate(weighted, axis=1), ('atm', 'ocn'), split_a...  5.33 us
  transfers between devices with their start and end apart: 2, of which 0 were waited for; matrix products, arithmetic and copies ran while one was open for 9% of the time, Pallas kernels for 50%

profile of v7, /device:TPU:1, one launch (start us, length us, event | category | flops | bytes accessed | tf_op | source)
XLA Modules:
  0.0 119.7 jit_solution(15191653906816793400)
XLA Ops:
  0.7 0.8 fusion.47
  1.4 0.8 copy.12
  2.2 0.2 fusion.43
  2.5 0.9 fusion.41
  3.7 1.3 %fusion.7 = f32[1024,128]{0,1:T(8,128)S(1)} fusion(f32[512,128]{1,0:T(8,128)S(1)} %copy-done, s32[512]{0:T(512)S(1)} %multiply_add_fusion.1), kind=kOutput, calls=%fused_computation.11 | convolution fusion | flops 805830656 | bytes 788480 | tf_op jit(solution)/shard_map/dot_general | solution.py:51
  5.2 0.6 fusion.6
  5.9 0.6 fusion.8
  6.6 1.5 %fusion.52 = f32[1024,384]{0,1:T(8,128)S(1)} fusion(f32[1024,256]{1,0:T(8,128)S(1)} %fusion.8, f32[256,384]{0,1:T(8,128)S(1)} %bitcast.71), kind=kOutput, calls=%fused_computation.85 | convolution fusion | flops 1207959552 | bytes 3014656 | tf_op jit(solution)/shard_map/dot_general | solution.py:51
  8.0 0.3 convolution_multiply_fusion
  8.6 2.1 %copy.15 = f32[1024,640]{1,0:T(8,128)} copy(f32[1024,640]{0,1:T(8,128)S(1)} %pad_maximum_fusion.1) | data formatting | bytes 5242880 | tf_op jit(solution)/shard_map/concatenate | solution.py:248
  10.7 11.5 %all-to-all-start = ((f32[128,8,640]{2,1,0:T(8,128)}), f32[128,8,640]{2,1,0:T(8,128)S(1)}, u32[]{:S(2)}, u32[]{:S(2)}) async-start(f32[128,8,640]{2,1,0:T(8,128)} %bitcast.67), calls=%async_computation | async-start | bytes 5242880 | tf_op jit(solution)/shard_map/all_to_all | solution.py:249
  22.2 3.4 %pad_maximum_fusion.x_ref = f32[6,864,128]{2,1,0:T(8,128)} fusion(f32[3,864,128]{2,1,0:T(8,128)} %bitcast.72, f32[3,864,128]{2,1,0:T(8,128)} %bitcast.73), kind=kLoop, calls=%fused_computation.7 | loop fusion | flops 663552 | bytes 5308416 | tf_op jit(solution)/shard_map/concatenate | solution.py:252
  25.6 37.2 %shard_map.95 = (f32[3,864,128]{2,1,0:T(8,128)}, f32[3,896,128]{2,1,0:T(8,128)}, f32[3,896,128]{2,1,0:T(8,128)}) custom-call(f32[6,864,128]{2,1,0:T(8,128)} %pad_maximum_fusion.x_ref), custom_call_target="tpu_custom_call" | custom-call | tf_op jit(solution)/shard_map/pallas_call | solution.py:177
  62.8 1.3 %fusion.51 = (f32[1024,128]{1,0:T(8,128)}, f32[1024,128]{1,0:T(8,128)}, f32[1024,128]{1,0:T(8,128)}, f32[1024,128]{1,0:T(8,128)S(1)}, f32[1024]{0:T(1024)S(1)}) fusion(f32[1024,640]{1,0:T(8,128)S(1)} %bitcast.66), kind=kLoop, calls=%fused_computation.84 | loop fusion | flops 130048 | bytes 4722688 | tf_op jit(solution)/shard_map/slice | solution.py:264
  64.1 1.3 %copy.27 = f32[1024,128]{0,1:T(8,128)S(1)} copy(f32[1024,128]{1,0:T(8,128)} %get-tuple-element.8) | data formatting | bytes 1048576
  65.4 1.2 %copy.26 = f32[1024,128]{0,1:T(8,128)S(1)} copy(f32[1024,128]{1,0:T(8,128)} %get-tuple-element.9) | data formatting | bytes 1048576
  66.9 0.2 copy.28
  67.1 2.6 %fusion.17 = f32[1024,128]{0,1:T(8,128)S(1)} fusion(f32[1024,128]{0,1:T(8,128)S(1)} %copy.28, s32[1024]{0:T(1024)S(1)} %convert_element_type.32, f32[3,864,128]{2,1,0:T(8,128)} %get-tuple-element.5), kind=kOutput, calls=%fused_computation.24 | convolution fusion | flops 1359970304 | bytes 1495040 | tf_op jit(solution)/shard_map/dot_general | solution.py:262
  69.7 1.5 %fusion.16 = f32[1024,128]{0,1:T(8,128)S(1)} fusion(f32[1024,128]{0,1:T(8,128)S(1)} %copy.27, s32[1024]{0:T(1024)S(1)} %convert_element_type.32, f32[3,864,128]{2,1,0:T(8,128)S(1)} %copy-done.14), kind=kOutput, calls=%fused_computation.23 | convolution fusion | flops 1359970304 | bytes 1495040 | tf_op jit(solution)/shard_map/dot_general | solution.py:262
  71.2 1.9 %multiply_multiply_fusion.3 = (f32[1024,128]{0,1:T(8,128)S(1)}, f32[1024,128]{0,1:T(8,128)S(1)}, f32[1024,128]{0,1:T(8,128)S(1)}) fusion(f32[1024,128]{0,1:T(8,128)S(1)} %copy.25, f32[1024,128]{0,1:T(8,128)S(1)} %fusion.17, f32[1024,128]{0,1:T(8,128)S(1)} %fusion.16, f32[1024,128]{0,1:T(8,128)S(1)} %copy.26, f32[3,864,128]{2,1,0:T(8,128)S(1)} %copy-done.14, ...), kind=kOutput, calls=%fused_computation.44 | convolution fusion | flops 1362198528 | bytes 4116480 | tf_op jit(solution)/shard_map/dot_general | solution.py:262
  73.1 0.8 copy-done.6
  74.0 0.2 copy-done.10
  74.4 1.6 %copy.20 = f32[1024,384]{1,0:T(8,128)} copy(f32[1024,384]{0,1:T(8,128)S(1)} %pad_maximum_fusion.2) | data formatting | bytes 3145728 | tf_op jit(solution)/shard_map/concatenate | solution.py:277
  76.1 5.3 %all-to-all-start.1 = ((f32[128,8,384]{2,1,0:T(8,128)}), f32[128,8,384]{2,1,0:T(8,128)S(1)}, u32[]{:S(2)}, u32[]{:S(2)}) async-start(f32[128,8,384]{2,1,0:T(8,128)} %bitcast.21), calls=%async_computation.1 | async-start | bytes 3145728 | tf_op jit(solution)/shard_map/all_to_all | solution.py:276
  81.4 2.9 %fusion.19 = f32[1,864,128]{2,1,0:T(8,128)S(1)} fusion(f32[1024,128]{0,1:T(8,128)} %copy-done.10, s32[1024]{0:T(1024)S(1)} %convert_element_type.32, f32[3,864,128]{2,1,0:T(8,128)S(1)} %bitcast.74), kind=kOutput, calls=%fused_computation.26 | convolution fusion | flops 1359949824 | bytes 1413120 | tf_op jit(solution)/shard_map/dot_general | solution.py:282
  84.3 1.7 %fusion.25 = f32[1,864,128]{2,1,0:T(8,128)S(1)} fusion(f32[1024,128]{0,1:T(8,128)S(1)} %copy-done.9, s32[1024]{0:T(1024)S(1)} %convert_element_type.32, f32[3,864,128]{2,1,0:T(8,128)S(1)} %bitcast.75), kind=kOutput, calls=%fused_computation.32 | convolution fusion | flops 1360060416 | bytes 1413120 | tf_op jit(solution)/shard_map/dot_general | solution.py:282
  86.1 1.7 %fusion.22 = f32[1,864,128]{2,1,0:T(8,128)S(1)} fusion(f32[1024,128]{0,1:T(8,128)S(1)} %copy-done.7, s32[1024]{0:T(1024)S(1)} %convert_element_type.32, f32[3,864,128]{2,1,0:T(8,128)S(1)} %bitcast.76), kind=kOutput, calls=%fused_computation.29 | convolution fusion | flops 1360060416 | bytes 1413120 | tf_op jit(solution)/shard_map/dot_general | solution.py:282
  87.8 1.1 pad_maximum_fusion.3.x_ref
  88.9 22.3 %shard_map.96 = f32[3,864,128]{2,1,0:T(8,128)} custom-call(f32[3,864,128]{2,1,0:T(8,128)} %pad_maximum_fusion.3.x_ref, f32[3,896,128]{2,1,0:T(8,128)} %get-tuple-element.6.dtall_ref, f32[3,896,128]{2,1,0:T(8,128)} %get-tuple-element.7.dside_ref), custom_call_target="tpu_custom_call" | custom-call | tf_op jit(solution)/shard_map/pallas_call | solution.py:195
  111.3 1.6 %copy.21 = f32[384,1024]{1,0:T(8,128)} copy(f32[384,1024]{0,1:T(8,128)S(1)} %bitcast.68) | data formatting | bytes 3145728 | tf_op jit(solution)/shard_map/dot_general | solution.py:51
  112.9 5.7 %fusion.26 = f32[256,3,128]{2,0,1:T(8,128)} fusion(f32[3,128,1024]{2,1,0:T(8,128)} %bitcast.69, f32[1024,256]{1,0:T(8,128)S(1)} %copy-done.2), kind=kOutput, calls=%fused_computation.33 | convolution fusion | flops 1207959552 | bytes 3014656 | tf_op jit(solution)/shard_map/dot_general | solution.py:51
  118.6 1.1 copy.30
  (47 shorter events, 1.3 us)
Async XLA Ops:
  0.6 3.0 %copy-start = (f32[512,128]{1,0:T(8,128)S(1)}, f32[512,128]{1,0:T(8,128)}, u32[]{:S(2)}) copy-start(f32[512,128]{1,0:T(8,128)} %param.12) | copy-start | bytes 786436
  0.6 2.8 %copy-start.13 = (s32[512,1]{0,1:T(1,128)S(1)}, s32[512,1]{0,1:T(1,128)}, u32[]{:S(2)}) copy-start(s32[512,1]{0,1:T(1,128)} %param.14) | copy-start | bytes 6148
  0.7 2.8 %copy-start.11 = (f32[256,3,128]{2,0,1:T(8,128)S(1)}, f32[256,3,128]{2,0,1:T(8,128)}, u32[]{:S(2)}) copy-start(f32[256,3,128]{2,0,1:T(8,128)} %param.10) | copy-start | bytes 1179652
  5.2 0.7 copy-start.15
  6.5 1.5 %copy-start.1 = (f32[1024,256]{1,0:T(8,128)}, f32[1024,256]{1,0:T(8,128)S(1)}, u32[]{:S(2)}) copy-start(f32[1024,256]{1,0:T(8,128)S(1)} %fusion.8) | copy-start | bytes 3145732
  6.5 1.5 %copy-start.12 = (s32[256,128]{1,0:T(8,128)S(1)}, s32[256,128]{1,0:T(8,128)}, u32[]{:S(2)}) copy-start(s32[256,128]{1,0:T(8,128)} %param.11) | copy-start | bytes 393220
  10.7 52.1 %all-to-all-start = ((f32[128,8,640]{2,1,0:T(8,128)}), f32[128,8,640]{2,1,0:T(8,128)S(1)}, u32[]{:S(2)}, u32[]{:S(2)}) async-start(f32[128,8,640]{2,1,0:T(8,128)} %bitcast.67), calls=%async_computation | async-start | bytes 5242880 | tf_op jit(solution)/shard_map/all_to_all | solution.py:249
  64.1 2.6 %copy-start.4 = (f32[1024,128]{1,0:T(8,128)S(1)}, f32[1024,128]{1,0:T(8,128)}, u32[]{:S(2)}) copy-start(f32[1024,128]{1,0:T(8,128)} %get-tuple-element.10) | copy-start | bytes 1572868
  67.1 2.6 %copy-start.14 = (f32[3,864,128]{2,1,0:T(8,128)S(1)}, f32[3,864,128]{2,1,0:T(8,128)}, u32[]{:S(2)}) copy-start(f32[3,864,128]{2,1,0:T(8,128)} %get-tuple-element.5) | copy-start | bytes 3981316
  73.1 0.8 copy-start.6
  73.1 1.0 copy-start.8
  73.1 1.2 copy-start.10
  76.1 5.3 %copy-start.5 = (f32[864,3,128]{2,0,1:T(8,128)S(1)}, f32[864,3,128]{2,0,1:T(8,128)}, u32[]{:S(2)}) copy-start(f32[864,3,128]{2,0,1:T(8,128)} %param.8) | copy-start | bytes 3981316
  76.1 35.2 %all-to-all-start.1 = ((f32[128,8,384]{2,1,0:T(8,128)}), f32[128,8,384]{2,1,0:T(8,128)S(1)}, u32[]{:S(2)}, u32[]{:S(2)}) async-start(f32[128,8,384]{2,1,0:T(8,128)} %bitcast.21), calls=%async_computation.1 | async-start | bytes 3145728 | tf_op jit(solution)/shard_map/all_to_all | solution.py:276
  81.4 2.9 %copy-start.9 = (f32[1024,128]{0,1:T(8,128)S(1)}, f32[1024,128]{0,1:T(8,128)}, u32[]{:S(2)}) copy-start(f32[1024,128]{0,1:T(8,128)} %copy-done.8) | copy-start | bytes 1572868
  81.4 4.6 %copy-start.7 = (f32[1024,128]{0,1:T(8,128)S(1)}, f32[1024,128]{0,1:T(8,128)}, u32[]{:S(2)}) copy-start(f32[1024,128]{0,1:T(8,128)} %copy-done.6) | copy-start | bytes 1572868
  111.3 1.7 %copy-start.2 = (f32[1024,256]{1,0:T(8,128)S(1)}, f32[1024,256]{1,0:T(8,128)}, u32[]{:S(2)}) copy-start(f32[1024,256]{1,0:T(8,128)} %copy-done.1) | copy-start | bytes 3145732
  112.9 5.7 %copy-start.3 = (f32[3,864,128]{2,1,0:T(8,128)S(1)}, f32[3,864,128]{2,1,0:T(8,128)}, u32[]{:S(2)}) copy-start(f32[3,864,128]{2,1,0:T(8,128)} %shard_map.96) | copy-start | bytes 3981316

commit v8 on v7

--- a/solution.py
+++ b/solution.py
@@ -44,6 +44,20 @@
         ],
         axis=1,
     )
+
+
+def pick_dot(pick, values):
+    parts = []
+    rest = values
+    for part in range(3):
+        high = lax.reduce_precision(rest, exponent_bits=8, mantissa_bits=7)
+        parts.append(high.astype(jnp.bfloat16))
+        rest = rest - high
+    total = None
+    for part in parts:
+        term = jnp.dot(pick, part, preferred_element_type=jnp.float32)
+        total = term if total is None else total + term
+    return total
 
 
 def select_rows(chosen, values, precision=HIGHEST):
@@ -233,7 +247,8 @@
     ).astype(jnp.bfloat16)
     slot_seg = jnp.dot(slot_pick, seg_pick, preferred_element_type=jnp.float32)
     plane = chan_count * seg_width
-    out_ocean = select_rows(slot_seg, ocean_state.reshape(seg_count, plane))
+    slot_seg16 = slot_seg.astype(jnp.bfloat16)
+    out_ocean = pick_dot(slot_seg16, ocean_state.reshape(seg_count, plane))
     out_mask = select_rows(slot_seg, land_mask.astype(jnp.float32), None)
     row_high = (intersection_row // 32).astype(jnp.bfloat16)
     row_low = (intersection_row % 32).astype(jnp.bfloat16)
@@ -243,7 +258,7 @@
     )
     out_rows = jnp.dot(slot_pick, row_parts, preferred_element_type=jnp.float32)
     out_label = 32.0 * out_rows[:, :seg_width] + out_rows[:, seg_width:]
-    out_area = select_rows(slot_pick.astype(jnp.float32), intersection_area)
+    out_area = pick_dot(slot_pick, intersection_area)
     out_weight = out_area * out_mask
     outgoing = jnp.concatenate([out_ocean, out_weight, out_label], axis=1)
     incoming = lax.all_to_all(outgoing, ("atm", "ocn"), split_axis=0, concat_axis=0, tiled=True)
@@ -257,10 +272,9 @@
     in_labels = jnp.max(incoming[:, plane + seg_width :], axis=1).astype(jnp.int32)
     row_pick = (
         jnp.arange(row_count, dtype=jnp.int32)[:, None] == in_labels[None, :]
-    ).astype(jnp.float32)
+    ).astype(jnp.bfloat16)
     pick_rows = row_pick.T
-    air = [jnp.dot(pick_rows, smoothed[c], precision=HIGHEST, preferred_element_type=jnp.float32)
-           for c in range(chan_count)]
+    air = [pick_dot(pick_rows, smoothed[c]) for c in range(chan_count)]
     ocean = [incoming[:, c * seg_width : (c + 1) * seg_width] for c in range(chan_count)]
     in_weight = incoming[:, plane : plane + seg_width]
     wind_east = air[1] - ocean[1]
@@ -276,11 +290,10 @@
     returned = lax.all_to_all(
         jnp.concatenate(weighted, axis=1), ("atm", "ocn"), split_axis=0, concat_axis=0, tiled=True
     )
-    ocean_flux = select_rows(slot_seg.T, returned).reshape(seg_count, chan_count, seg_width)
+    ocean_flux = pick_dot(slot_seg16.T, returned).reshape(seg_count, chan_count, seg_width)
     signs = (1.0, -1.0, -1.0)
     forced = jnp.stack(
-        [atm_planes[c] + signs[c] * jnp.dot(row_pick, weighted[c], precision=HIGHEST,
-                                             preferred_element_type=jnp.float32)
+        [atm_planes[c] + signs[c] * pick_dot(row_pick, weighted[c])
          for c in range(chan_count)]
     )
     current = diffuse_call(sizes, forced, dtall, dside)

time: 120 us -> 123 us (1.025)
  matrix products: 22.2 us -> 26.4 us
  local copies, waits for them, and re-layouts: 11.9 us -> 10.4 us
    dot_general x6 -> x27, matrix products: 12.3 us -> 24.8 us  [pick_dot(): term = jnp.dot(pick, part, preferred_element_type=jnp.float32)]
    dot_general x4 -> x1, matrix products: 8.76 us -> 0.31 us  [select_rows(): jnp.dot(chosen, flat, precision=precision, preferred_element_type=jnp.flo...]
    dot_general x1 -> x0, local copies, waits for them, and re-layouts: 1.64 us -> none  [select_rows(): jnp.dot(chosen, flat, precision=precision, preferred_element_type=jnp.flo...]
    unnamed x39 -> x44, local copies, waits for them, and re-layouts: 5.4 us -> 5.37 us
  transfers between devices with their start and end apart: 2 -> 2, of which waited for: 0 -> 0; matrix products, arithmetic and copies ran while one was open for 9% -> 9% of each run, Pallas kernels for 50% -> 48%
where the time goes in v8:
time: 123 us; the launch traced here: 122 us
  Pallas kernels  58.8 us (48%)
  matrix products  26.4 us (21%)
  starting transfers between devices  17 us (14%)
  local copies, waits for them, and re-layouts  10.4 us (8%)
  other arithmetic  8.46 us (7%)
    pallas_call x1, Pallas kernels, smooth_call(): pl.pallas_call(functools.partial(smooth_kernel, sizes), out_shape=(jax.Sh...  37 us
    dot_general x27, matrix products, pick_dot(): term = jnp.dot(pick, part, preferred_element_type=jnp.float32)  24.8 us
    pallas_call x1, Pallas kernels, diffuse_call(): pl.pallas_call(functools.partial(diffuse_kernel, sizes), out_shape=jax.Sh...  21.8 us
    all_to_all x1, starting transfers between devices, per_device(): lax.all_to_all(outgoing, ('atm', 'ocn'), split_axis=0, concat_axis=0, til...  11.7 us
    unnamed x44, local copies, waits for them, and re-layouts  5.37 us
    all_to_all x1, starting transfers between devices, per_device(): lax.all_to_all(jnp.concatenate(weighted, axis=1), ('atm', 'ocn'), split_a...  5.33 us
    concatenate x1, other arithmetic, per_device(): jnp.concatenate([atm_planes, jnp.transpose(diffusivity, (1, 0, 2))], axis=0)  3.4 us
  transfers between devices with their start and end apart: 2, of which 0 were waited for; matrix products, arithmetic and copies ran while one was open for 9% of the time, Pallas kernels for 48%

profile of v8, /device:TPU:1, one launch (start us, length us, event | category | flops | bytes accessed | tf_op | source)
XLA Modules:
  0.0 122.2 jit_solution(2171448197149468170)
XLA Ops:
  0.7 0.7 fusion.108
  1.4 0.8 copy.12
  2.5 0.9 fusion.98
  9.4 2.1 %copy.15 = f32[1024,640]{1,0:T(8,128)} copy(f32[1024,640]{0,1:T(8,128)S(1)} %pad_maximum_fusion.1) | data formatting | bytes 5242880 | tf_op jit(solution)/shard_map/concatenate | solution.py:263
  11.5 11.7 %all-to-all-start = ((f32[128,8,640]{2,1,0:T(8,128)}), f32[128,8,640]{2,1,0:T(8,128)S(1)}, u32[]{:S(2)}, u32[]{:S(2)}) async-start(f32[128,8,640]{2,1,0:T(8,128)} %bitcast.100), calls=%async_computation | async-start | bytes 5242880 | tf_op jit(solution)/shard_map/all_to_all | solution.py:264
  23.2 3.4 %pad_maximum_fusion.x_ref = f32[6,864,128]{2,1,0:T(8,128)} fusion(f32[3,864,128]{2,1,0:T(8,128)} %bitcast.104, f32[3,864,128]{2,1,0:T(8,128)} %bitcast.105), kind=kLoop, calls=%fused_computation.19 | loop fusion | flops 663552 | bytes 5308416 | tf_op jit(solution)/shard_map/concatenate | solution.py:267
  26.6 37.0 %shard_map.95 = (f32[3,864,128]{2,1,0:T(8,128)}, f32[3,896,128]{2,1,0:T(8,128)}, f32[3,896,128]{2,1,0:T(8,128)}) custom-call(f32[6,864,128]{2,1,0:T(8,128)} %pad_maximum_fusion.x_ref), custom_call_target="tpu_custom_call" | custom-call | tf_op jit(solution)/shard_map/pallas_call | solution.py:191
  63.7 1.5 %fusion.112 = (f32[1024,128]{1,0:T(8,128)}, f32[1024,128]{1,0:T(8,128)}, f32[1024,128]{1,0:T(8,128)}, f32[1024,128]{1,0:T(8,128)}, f32[1024]{0:T(1024)S(1)}) fusion(f32[1024,640]{1,0:T(8,128)S(1)} %bitcast.99), kind=kLoop, calls=%fused_computation.176 | loop fusion | flops 130048 | bytes 4722688 | tf_op jit(solution)/shard_map/slice | solution.py:278
  65.5 1.6 %fusion.16 = f32[1024,128]{0,1:T(8,128)} fusion(s32[1024]{0:T(1024)S(1)} %convert_element_type.122, f32[3,864,128]{2,1,0:T(8,128)S(1)} %copy-done.14), kind=kOutput, calls=%fused_computation.17 | convolution fusion | flops 227819520 | bytes 970752 | tf_op jit(solution)/shard_map/dot_general | solution.py:58
  67.1 1.6 %fusion.13 = f32[1024,128]{0,1:T(8,128)} fusion(s32[1024]{0:T(1024)S(1)} %convert_element_type.122, f32[3,864,128]{2,1,0:T(8,128)S(1)} %copy-done.14), kind=kOutput, calls=%fused_computation.14 | convolution fusion | flops 227819520 | bytes 970752 | tf_op jit(solution)/shard_map/dot_general | solution.py:58
  68.7 1.6 %fusion.10 = f32[1024,128]{0,1:T(8,128)} fusion(s32[1024]{0:T(1024)S(1)} %convert_element_type.122, f32[3,864,128]{2,1,0:T(8,128)S(1)} %copy-done.14), kind=kOutput, calls=%fused_computation.11 | convolution fusion | flops 227819520 | bytes 970752 | tf_op jit(solution)/shard_map/dot_general | solution.py:58
  71.5 2.1 %fusion.45 = f32[1024,128]{0,1:T(8,128)S(1)} fusion(f32[1024,128]{0,1:T(8,128)} %fusion.16, s32[1024]{0:T(1024)S(1)} %convert_element_type.122, f32[3,864,128]{2,1,0:T(8,128)} %get-tuple-element.5), kind=kOutput, calls=%fused_computation.57 | convolution fusion | flops 227729408 | bytes 1495040 | tf_op jit(solution)/shard_map/dot_general | solution.py:58
  73.6 1.8 %fusion.47 = f32[1024,128]{0,1:T(8,128)S(1)} fusion(f32[1024,128]{0,1:T(8,128)} %fusion.13, s32[1024]{0:T(1024)S(1)} %convert_element_type.122, f32[3,864,128]{2,1,0:T(8,128)S(1)} %copy-done.15), kind=kOutput, calls=%fused_computation.59 | convolution fusion | flops 227729408 | bytes 1495040 | tf_op jit(solution)/shard_map/dot_general | solution.py:58
  75.4 0.8 fusion.49
  76.2 0.8 fusion.52
  77.0 0.8 fusion.51
  77.8 1.2 multiply_multiply_fusion.3
  79.0 0.7 fusion.7
  79.7 1.5 %fusion.54 = f32[864,128]{1,0:T(8,128)} fusion(f32[864,128]{1,0:T(8,128)S(1)} %fusion.7, s32[1024]{0:T(1024)S(1)} %convert_element_type.122, f32[1024,128]{0,1:T(8,128)S(1)} %get-tuple-element.17), kind=kOutput, calls=%fused_computation.66 | convolution fusion | flops 227749888 | bytes 1413120 | tf_op jit(solution)/shard_map/dot_general | solution.py:58
  81.4 1.6 %copy.20 = f32[1024,384]{1,0:T(8,128)} copy(f32[1024,384]{0,1:T(8,128)S(1)} %pad_maximum_fusion.2) | data formatting | bytes 3145728 | tf_op jit(solution)/shard_map/concatenate | solution.py:291
  83.0 5.3 %all-to-all-start.1 = ((f32[128,8,384]{2,1,0:T(8,128)}), f32[128,8,384]{2,1,0:T(8,128)S(1)}, u32[]{:S(2)}, u32[]{:S(2)}) async-start(f32[128,8,384]{2,1,0:T(8,128)} %bitcast.101), calls=%async_computation.1 | async-start | bytes 3145728 | tf_op jit(solution)/shard_map/all_to_all | solution.py:290
  88.4 0.7 fusion.1
  89.8 1.8 %fusion.67 = f32[1,864,128]{2,1,0:T(8,128)S(1)} fusion(f32[864,128]{1,0:T(8,128)} %fusion.54, s32[1024]{0:T(1024)S(1)} %convert_element_type.122, f32[3,864,128]{2,1,0:T(8,128)S(1)} %bitcast.106, f32[1024,128]{0,1:T(8,128)S(1)} %copy-done.10), kind=kOutput, calls=%fused_computation.79 | convolution fusion | flops 228384768 | bytes 1855488 | tf_op jit(solution)/shard_map/dot_general | solution.py:58
  91.6 0.7 fusion.58
  92.3 0.8 fusion.62
  93.1 0.7 fusion.4
  93.8 0.7 fusion.56
  94.5 0.8 fusion.65
  95.3 1.1 pad_maximum_fusion.3.x_ref
  96.4 21.8 %shard_map.96 = f32[3,864,128]{2,1,0:T(8,128)} custom-call(f32[3,864,128]{2,1,0:T(8,128)} %pad_maximum_fusion.3.x_ref, f32[3,896,128]{2,1,0:T(8,128)} %get-tuple-element.6.dtall_ref, f32[3,896,128]{2,1,0:T(8,128)} %get-tuple-element.7.dside_ref), custom_call_target="tpu_custom_call" | custom-call | tf_op jit(solution)/shard_map/pallas_call | solution.py:209
  119.9 0.9 copy.22
  121.1 1.1 copy.28
  (71 shorter events, 10.5 us)
Async XLA Ops:
  0.6 2.8 %copy-start.13 = (s32[512,1]{0,1:T(1,128)S(1)}, s32[512,1]{0,1:T(1,128)}, u32[]{:S(2)}) copy-start(s32[512,1]{0,1:T(1,128)} %param.14) | copy-start | bytes 6148
  0.6 2.8 %copy-start.11 = (f32[256,3,128]{2,0,1:T(8,128)S(1)}, f32[256,3,128]{2,0,1:T(8,128)}, u32[]{:S(2)}) copy-start(f32[256,3,128]{2,0,1:T(8,128)} %param.10) | copy-start | bytes 1179652
  2.4 1.3 %copy-start.16 = (s32[512]{0:T(512)S(1)}, s32[512]{0:T(512)}, u32[]{:S(2)}) copy-start(s32[512]{0:T(512)} %param.13) | copy-start | bytes 6148
  3.5 1.0 copy-start.6
  7.6 0.9 copy-start.12
  11.5 52.1 %all-to-all-start = ((f32[128,8,640]{2,1,0:T(8,128)}), f32[128,8,640]{2,1,0:T(8,128)S(1)}, u32[]{:S(2)}, u32[]{:S(2)}) async-start(f32[128,8,640]{2,1,0:T(8,128)} %bitcast.100), calls=%async_computation | async-start | bytes 5242880 | tf_op jit(solution)/shard_map/all_to_all | solution.py:264
  63.7 1.9 %copy-start.14 = (f32[3,864,128]{2,1,0:T(8,128)S(1)}, f32[3,864,128]{2,1,0:T(8,128)}, u32[]{:S(2)}) copy-start(f32[3,864,128]{2,1,0:T(8,128)} %get-tuple-element.5) | copy-start | bytes 3981316
  67.1 3.2 %copy-start.4 = (f32[1024,128]{1,0:T(8,128)S(1)}, f32[1024,128]{1,0:T(8,128)}, u32[]{:S(2)}) copy-start(f32[1024,128]{1,0:T(8,128)} %get-tuple-element.12) | copy-start | bytes 1572868
  68.7 1.8 %copy-start.3 = (f32[1024,128]{1,0:T(8,128)S(1)}, f32[1024,128]{1,0:T(8,128)}, u32[]{:S(2)}) copy-start(f32[1024,128]{1,0:T(8,128)} %get-tuple-element.13) | copy-start | bytes 1572868
  68.7 2.0 %copy-start.2 = (f32[1024,128]{1,0:T(8,128)S(1)}, f32[1024,128]{1,0:T(8,128)}, u32[]{:S(2)}) copy-start(f32[1024,128]{1,0:T(8,128)} %get-tuple-element.14) | copy-start | bytes 1572868
  70.3 1.0 copy-start.1
  71.5 2.1 %copy-start.15 = (f32[3,864,128]{2,1,0:T(8,128)S(1)}, f32[3,864,128]{2,1,0:T(8,128)}, u32[]{:S(2)}) copy-start(f32[3,864,128]{2,1,0:T(8,128)} %get-tuple-element.5) | copy-start | bytes 3981316
  71.5 3.9 %copy-start.17 = (f32[1024,128]{0,1:T(8,128)S(1)}, f32[1024,128]{0,1:T(8,128)}, u32[]{:S(2)}) copy-start(f32[1024,128]{0,1:T(8,128)} %fusion.10) | copy-start | bytes 1572868
  79.0 2.2 %copy-start.7 = (f32[1024,128]{0,1:T(8,128)}, f32[1024,128]{0,1:T(8,128)S(1)}, u32[]{:S(2)}) copy-start(f32[1024,128]{0,1:T(8,128)S(1)} %get-tuple-element.18) | copy-start | bytes 1572868
  79.0 2.2 %copy-start.9 = (f32[1024,128]{0,1:T(8,128)}, f32[1024,128]{0,1:T(8,128)S(1)}, u32[]{:S(2)}) copy-start(f32[1024,128]{0,1:T(8,128)S(1)} %get-tuple-element.17) | copy-start | bytes 1572868
  83.0 5.3 %copy-start.8 = (f32[1024,128]{0,1:T(8,128)S(1)}, f32[1024,128]{0,1:T(8,128)}, u32[]{:S(2)}) copy-start(f32[1024,128]{0,1:T(8,128)} %copy-done.7) | copy-start | bytes 1572868
  83.0 35.2 %all-to-all-start.1 = ((f32[128,8,384]{2,1,0:T(8,128)}), f32[128,8,384]{2,1,0:T(8,128)S(1)}, u32[]{:S(2)}, u32[]{:S(2)}) async-start(f32[128,8,384]{2,1,0:T(8,128)} %bitcast.101), calls=%async_computation.1 | async-start | bytes 3145728 | tf_op jit(solution)/shard_map/all_to_all | solution.py:290
  88.4 1.3 %copy-start.5 = (f32[864,3,128]{2,0,1:T(8,128)S(1)}, f32[864,3,128]{2,0,1:T(8,128)}, u32[]{:S(2)}) copy-start(f32[864,3,128]{2,0,1:T(8,128)} %param.8) | copy-start | bytes 3981316
  88.4 1.4 %copy-start.10 = (f32[1024,128]{0,1:T(8,128)S(1)}, f32[1024,128]{0,1:T(8,128)}, u32[]{:S(2)}) copy-start(f32[1024,128]{0,1:T(8,128)} %copy-done.9) | copy-start | bytes 1572868
  119.7 1.4 %copy-start = (f32[3,864,128]{2,1,0:T(8,128)S(1)}, f32[3,864,128]{2,1,0:T(8,128)}, u32[]{:S(2)}) copy-start(f32[3,864,128]{2,1,0:T(8,128)} %shard_map.96) | copy-start | bytes 3981316

commit v9 on v7

--- a/solution.py
+++ b/solution.py
@@ -44,6 +44,20 @@
         ],
         axis=1,
     )
+
+
+def pick_dot(pick, values):
+    parts = []
+    rest = values
+    for part in range(3):
+        high = lax.reduce_precision(rest, exponent_bits=8, mantissa_bits=7)
+        parts.append(high.astype(jnp.bfloat16))
+        rest = rest - high
+    total = None
+    for part in parts:
+        term = jnp.dot(pick, part, preferred_element_type=jnp.float32)
+        total = term if total is None else total + term
+    return total
 
 
 def select_rows(chosen, values, precision=HIGHEST):
@@ -276,7 +290,6 @@
     returned = lax.all_to_all(
         jnp.concatenate(weighted, axis=1), ("atm", "ocn"), split_axis=0, concat_axis=0, tiled=True
     )
-    ocean_flux = select_rows(slot_seg.T, returned).reshape(seg_count, chan_count, seg_width)
     signs = (1.0, -1.0, -1.0)
     forced = jnp.stack(
         [atm_planes[c] + signs[c] * jnp.dot(row_pick, weighted[c], precision=HIGHEST,
@@ -284,6 +297,9 @@
          for c in range(chan_count)]
     )
     current = diffuse_call(sizes, forced, dtall, dside)
+    current, returned = lax.optimization_barrier((current, returned))
+    seg_of_slot = slot_seg.T.astype(jnp.bfloat16)
+    ocean_flux = pick_dot(seg_of_slot, returned).reshape(seg_count, chan_count, seg_width)
     return (jnp.transpose(current, (1, 0, 2)), ocean_flux)
 
 

time: 120 us -> 119 us (level)
  matrix products: 22.2 us -> 18.3 us
  other arithmetic: 8.2 us -> 10.1 us
    dot_general x4 -> x3, matrix products: 8.76 us -> 3.05 us  [select_rows(): jnp.dot(chosen, flat, precision=precision, preferred_element_type=jnp.flo...]
    concatenate x1, other arithmetic: 0.18 us -> 1.85 us  [per_device(): outgoing = jnp.concatenate([out_ocean, out_weight, out_label], axis=1)]
    dot_general x1 -> x0, local copies, waits for them, and re-layouts: 1.64 us -> none  [select_rows(): jnp.dot(chosen, flat, precision=precision, preferred_element_type=jnp.flo...]
    dot_general x0 -> x3, matrix products: none -> 1.44 us  [pick_dot(): term = jnp.dot(pick, part, preferred_element_type=jnp.float32)]
    unnamed x39 -> x38, local copies, waits for them, and re-layouts: 5.4 us -> 6.02 us
where the time goes in v9:
time: 119 us; the launch traced here: 118 us
  Pallas kernels  59.6 us (50%)
  matrix products  18.3 us (15%)
  starting transfers between devices  17 us (14%)
  local copies, waits for them, and re-layouts  12.1 us (10%)
  other arithmetic  10.1 us (8%)
    pallas_call x1, Pallas kernels, smooth_call(): pl.pallas_call(functools.partial(smooth_kernel, sizes), out_shape=(jax.Sh...  37.3 us
    pallas_call x1, Pallas kernels, diffuse_call(): pl.pallas_call(functools.partial(diffuse_kernel, sizes), out_shape=jax.Sh...  22.3 us
    all_to_all x1, starting transfers between devices, per_device(): lax.all_to_all(outgoing, ('atm', 'ocn'), split_axis=0, concat_axis=0, til...  11.9 us
    dot_general x3, matrix products, per_device(): jnp.dot(row_pick, weighted[c], precision=HIGHEST, preferred_element_type=...  6.49 us
    dot_general x3, matrix products, per_device(): jnp.dot(pick_rows, smoothed[c], precision=HIGHEST, preferred_element_type...  6.09 us
    unnamed x38, local copies, waits for them, and re-layouts  6.02 us
    all_to_all x1, starting transfers between devices, per_device(): lax.all_to_all(jnp.concatenate(weighted, axis=1), ('atm', 'ocn'), split_a...  5.04 us
    concatenate x1, local copies, waits for them, and re-layouts, per_device(): outgoing = jnp.concatenate([out_ocean, out_weight, out_label], axis=1)  3.24 us
  transfers between devices with their start and end apart: 2, of which 0 were waited for; matrix products, arithmetic and copies ran while one was open for 9% of the time, Pallas kernels for 50%

profile of v9, /device:TPU:1, one launch (start us, length us, event | category | flops | bytes accessed | tf_op | source)
XLA Modules:
  0.0 118.2 jit_solution(9156005820712515946)
XLA Ops:
  0.7 0.8 fusion.49
  1.4 0.8 copy.12
  2.5 0.9 fusion.43
  3.7 1.3 %fusion.7 = f32[1024,128]{0,1:T(8,128)S(1)} fusion(f32[512,128]{1,0:T(8,128)S(1)} %copy-done, s32[512]{0:T(512)S(1)} %multiply_add_fusion.1), kind=kOutput, calls=%fused_computation.15 | convolution fusion | flops 805830656 | bytes 788480 | tf_op jit(solution)/shard_map/dot_general | solution.py:65
  5.2 0.6 fusion.6
  5.9 0.6 fusion.8
  6.5 1.5 %fusion.57 = f32[1024,384]{0,1:T(8,128)S(1)} fusion(f32[1024,256]{1,0:T(8,128)S(1)} %fusion.8, f32[256,384]{0,1:T(8,128)S(1)} %bitcast.67), kind=kOutput, calls=%fused_computation.95 | convolution fusion | flops 1207959552 | bytes 3014656 | tf_op jit(solution)/shard_map/dot_general | solution.py:65
  8.3 1.8 %pad_maximum_fusion.1 = f32[1024,640]{0,1:T(8,128)} fusion(f32[1024,128]{0,1:T(8,128)S(1)} %slice_add_fusion, f32[1024,128]{0,1:T(8,128)S(1)} %convolution_multiply_fusion, f32[1024,384]{0,1:T(8,128)S(1)} %fusion.57), kind=kLoop, calls=%fused_computation.8 | loop fusion | flops 1310720 | bytes 5242880 | tf_op jit(solution)/shard_map/concatenate | solution.py:262
  10.2 3.2 %copy.15 = f32[1024,640]{1,0:T(8,128)} copy(f32[1024,640]{0,1:T(8,128)} %pad_maximum_fusion.1) | data formatting | bytes 5242880 | tf_op jit(solution)/shard_map/concatenate | solution.py:262
  13.4 11.9 %all-to-all-start = ((f32[128,8,640]{2,1,0:T(8,128)}), f32[128,8,640]{2,1,0:T(8,128)}, u32[]{:S(2)}, u32[]{:S(2)}) async-start(f32[128,8,640]{2,1,0:T(8,128)} %bitcast.63), calls=%async_computation | async-start | bytes 5242880 | tf_op jit(solution)/shard_map/all_to_all | solution.py:263
  25.4 3.0 %pad_maximum_fusion.x_ref = f32[6,864,128]{2,1,0:T(8,128)} fusion(f32[3,864,128]{2,1,0:T(8,128)S(1)} %bitcast.68, f32[3,864,128]{2,1,0:T(8,128)} %bitcast.69), kind=kLoop, calls=%fused_computation.7 | loop fusion | flops 663552 | bytes 5308416 | tf_op jit(solution)/shard_map/concatenate | solution.py:266
  28.4 37.3 %shard_map.95 = (f32[3,864,128]{2,1,0:T(8,128)}, f32[3,896,128]{2,1,0:T(8,128)}, f32[3,896,128]{2,1,0:T(8,128)}) custom-call(f32[6,864,128]{2,1,0:T(8,128)} %pad_maximum_fusion.x_ref), custom_call_target="tpu_custom_call" | custom-call | tf_op jit(solution)/shard_map/pallas_call | solution.py:191
  65.7 2.0 %fusion.56 = (f32[1024,128]{1,0:T(8,128)S(1)}, f32[1024,128]{1,0:T(8,128)S(1)}, f32[1024,128]{1,0:T(8,128)S(1)}, f32[1024,128]{1,0:T(8,128)S(1)}, f32[1024]{0:T(1024)S(1)}) fusion(f32[1024,640]{1,0:T(8,128)} %bitcast.9), kind=kLoop, calls=%fused_computation.94 | loop fusion | flops 130048 | bytes 4722688 | tf_op jit(solution)/shard_map/slice | solution.py:278
  67.6 1.0 copy.25
  69.0 1.0 copy.26
  70.0 2.8 %fusion.19 = f32[1024,128]{0,1:T(8,128)S(1)} fusion(f32[1024,128]{0,1:T(8,128)} %copy.26, s32[1024]{0:T(1024)S(1)} %convert_element_type.45, f32[3,864,128]{2,1,0:T(8,128)} %get-tuple-element.7), kind=kOutput, calls=%fused_computation.30 | convolution fusion | flops 1359970304 | bytes 1495040 | tf_op jit(solution)/shard_map/dot_general | solution.py:276
  72.8 1.5 %fusion.18 = f32[1024,128]{0,1:T(8,128)S(1)} fusion(f32[1024,128]{0,1:T(8,128)S(1)} %copy-done.4, s32[1024]{0:T(1024)S(1)} %convert_element_type.45, f32[3,864,128]{2,1,0:T(8,128)S(1)} %copy-done.13), kind=kOutput, calls=%fused_computation.29 | convolution fusion | flops 1359970304 | bytes 1495040 | tf_op jit(solution)/shard_map/dot_general | solution.py:276
  74.3 1.9 %multiply_multiply_fusion.3 = (f32[1024,128]{0,1:T(8,128)S(1)}, f32[1024,128]{0,1:T(8,128)S(1)}, f32[1024,128]{0,1:T(8,128)S(1)}) fusion(f32[1024,128]{0,1:T(8,128)S(1)} %copy.23, f32[1024,128]{0,1:T(8,128)S(1)} %fusion.19, f32[1024,128]{0,1:T(8,128)S(1)} %fusion.18, f32[1024,128]{0,1:T(8,128)S(1)} %copy.24, f32[3,864,128]{2,1,0:T(8,128)S(1)} %copy-done.13, ...), kind=kOutput, calls=%fused_computation.51 | convolution fusion | flops 1362198528 | bytes 4116480 | tf_op jit(solution)/shard_map/dot_general | solution.py:276
  76.2 0.8 copy-done.5
  77.5 1.6 %copy.20 = f32[1024,384]{1,0:T(8,128)} copy(f32[1024,384]{0,1:T(8,128)S(1)} %pad_maximum_fusion.2) | data formatting | bytes 3145728 | tf_op jit(solution)/shard_map/concatenate | solution.py:291
  79.1 5.0 %all-to-all-start.1 = ((f32[128,8,384]{2,1,0:T(8,128)}), f32[128,8,384]{2,1,0:T(8,128)S(1)}, u32[]{:S(2)}, u32[]{:S(2)}) async-start(f32[128,8,384]{2,1,0:T(8,128)} %bitcast.64), calls=%async_computation.1 | async-start | bytes 3145728 | tf_op jit(solution)/shard_map/all_to_all | solution.py:290
  84.2 3.0 %fusion.21 = f32[1,864,128]{2,1,0:T(8,128)S(1)} fusion(f32[1024,128]{0,1:T(8,128)} %copy-done.9, s32[1024]{0:T(1024)S(1)} %convert_element_type.45, f32[3,864,128]{2,1,0:T(8,128)} %bitcast.70), kind=kOutput, calls=%fused_computation.32 | convolution fusion | flops 1359949824 | bytes 1413120 | tf_op jit(solution)/shard_map/dot_general | solution.py:295
  87.2 1.7 %fusion.27 = f32[1,864,128]{2,1,0:T(8,128)S(1)} fusion(f32[1024,128]{0,1:T(8,128)S(1)} %copy-done.8, s32[1024]{0:T(1024)S(1)} %convert_element_type.45, f32[3,864,128]{2,1,0:T(8,128)S(1)} %bitcast.71), kind=kOutput, calls=%fused_computation.38 | convolution fusion | flops 1360060416 | bytes 1413120 | tf_op jit(solution)/shard_map/dot_general | solution.py:295
  89.0 1.7 %fusion.24 = f32[1,864,128]{2,1,0:T(8,128)S(1)} fusion(f32[1024,128]{0,1:T(8,128)S(1)} %copy-done.6, s32[1024]{0:T(1024)S(1)} %convert_element_type.45, f32[3,864,128]{2,1,0:T(8,128)S(1)} %bitcast.72), kind=kOutput, calls=%fused_computation.35 | convolution fusion | flops 1360060416 | bytes 1413120 | tf_op jit(solution)/shard_map/dot_general | solution.py:295
  90.7 1.1 pad_maximum_fusion.3.x_ref
  91.9 22.3 %shard_map.96 = f32[3,864,128]{2,1,0:T(8,128)} custom-call(f32[3,864,128]{2,1,0:T(8,128)} %pad_maximum_fusion.3.x_ref, f32[3,896,128]{2,1,0:T(8,128)} %get-tuple-element.8.dtall_ref, f32[3,896,128]{2,1,0:T(8,128)} %get-tuple-element.9.dside_ref), custom_call_target="tpu_custom_call" | custom-call | tf_op jit(solution)/shard_map/pallas_call | solution.py:209
  114.2 0.5 fusion.32
  114.7 0.5 convolution_add_fusion.1
  115.2 0.5 convolution_add_fusion
  115.9 0.9 copy.22
  116.8 0.3 copy-done.1
  117.1 1.1 copy.28
  (48 shorter events, 2.2 us)
Async XLA Ops:
  0.6 3.0 %copy-start = (f32[512,128]{1,0:T(8,128)S(1)}, f32[512,128]{1,0:T(8,128)}, u32[]{:S(2)}) copy-start(f32[512,128]{1,0:T(8,128)} %param.12) | copy-start | bytes 786436
  0.6 2.8 %copy-start.12 = (s32[512,1]{0,1:T(1,128)S(1)}, s32[512,1]{0,1:T(1,128)}, u32[]{:S(2)}) copy-start(s32[512,1]{0,1:T(1,128)} %param.14) | copy-start | bytes 6148
  0.7 2.8 %copy-start.10 = (f32[256,3,128]{2,0,1:T(8,128)S(1)}, f32[256,3,128]{2,0,1:T(8,128)}, u32[]{:S(2)}) copy-start(f32[256,3,128]{2,0,1:T(8,128)} %param.10) | copy-start | bytes 1179652
  5.2 0.7 copy-start.14
  6.5 1.5 %copy-start.11 = (s32[256,128]{1,0:T(8,128)S(1)}, s32[256,128]{1,0:T(8,128)}, u32[]{:S(2)}) copy-start(s32[256,128]{1,0:T(8,128)} %param.11) | copy-start | bytes 393220
  13.4 11.9 %copy-start.2 = (f32[864,3,128]{2,0,1:T(8,128)S(1)}, f32[864,3,128]{2,0,1:T(8,128)}, u32[]{:S(2)}) copy-start(f32[864,3,128]{2,0,1:T(8,128)} %param.9) | copy-start | bytes 3981316
  13.4 52.2 %all-to-all-start = ((f32[128,8,640]{2,1,0:T(8,128)}), f32[128,8,640]{2,1,0:T(8,128)}, u32[]{:S(2)}, u32[]{:S(2)}) async-start(f32[128,8,640]{2,1,0:T(8,128)} %bitcast.63), calls=%async_computation | async-start | bytes 5242880 | tf_op jit(solution)/shard_map/all_to_all | solution.py:263
  69.0 3.8 %copy-start.4 = (f32[1024,128]{0,1:T(8,128)S(1)}, f32[1024,128]{0,1:T(8,128)}, u32[]{:S(2)}) copy-start(f32[1024,128]{0,1:T(8,128)} %copy.25) | copy-start | bytes 1572868
  70.0 2.8 %copy-start.13 = (f32[3,864,128]{2,1,0:T(8,128)S(1)}, f32[3,864,128]{2,1,0:T(8,128)}, u32[]{:S(2)}) copy-start(f32[3,864,128]{2,1,0:T(8,128)} %get-tuple-element.7) | copy-start | bytes 3981316
  76.2 0.8 copy-start.5
  76.2 1.0 copy-start.7
  76.2 1.1 copy-start.9
  79.1 8.1 %copy-start.8 = (f32[1024,128]{0,1:T(8,128)S(1)}, f32[1024,128]{0,1:T(8,128)}, u32[]{:S(2)}) copy-start(f32[1024,128]{0,1:T(8,128)} %copy-done.7) | copy-start | bytes 1572868
  79.1 35.1 %all-to-all-start.1 = ((f32[128,8,384]{2,1,0:T(8,128)}), f32[128,8,384]{2,1,0:T(8,128)S(1)}, u32[]{:S(2)}, u32[]{:S(2)}) async-start(f32[128,8,384]{2,1,0:T(8,128)} %bitcast.64), calls=%async_computation.1 | async-start | bytes 3145728 | tf_op jit(solution)/shard_map/all_to_all | solution.py:290
  84.2 3.1 %copy-start.3 = (f32[864,3,128]{2,0,1:T(8,128)S(1)}, f32[864,3,128]{2,0,1:T(8,128)}, u32[]{:S(2)}) copy-start(f32[864,3,128]{2,0,1:T(8,128)} %param.8) | copy-start | bytes 3981316
  84.2 4.8 %copy-start.6 = (f32[1024,128]{0,1:T(8,128)S(1)}, f32[1024,128]{0,1:T(8,128)}, u32[]{:S(2)}) copy-start(f32[1024,128]{0,1:T(8,128)} %copy-done.5) | copy-start | bytes 1572868
  115.7 1.4 %copy-start.1 = (f32[3,864,128]{2,1,0:T(8,128)S(1)}, f32[3,864,128]{2,1,0:T(8,128)}, u32[]{:S(2)}) copy-start(f32[3,864,128]{2,1,0:T(8,128)} %shard_map.96) | copy-start | bytes 3981316

commit v10 on v9

--- a/solution.py
+++ b/solution.py
@@ -160,6 +160,13 @@
     )
 
 
+CHUNK = 96
+
+
+def chunk_rows(rows):
+    return CHUNK if rows % CHUNK == 0 else rows
+
+
 def smooth_kernel(sizes, x_ref, out_ref, tall_out, side_out, *scratch):
     rows_buf, cols_buf, colsend, tall_s, side_s, send_sem, recv_sem = scratch
     exchange(sizes, x_ref, rows_buf, cols_buf, colsend, tall_s, side_s, send_sem, recv_sem)
@@ -167,9 +174,17 @@
     kept = tall_out.shape[0]
     tall_out[...] = tall_s[kept:]
     side_out[...] = side_s[kept:]
+    step = chunk_rows(rows)
+    span = step + 2 * EDGE
     for chan in range(out_ref.shape[0]):
-        state = jnp.concatenate([tall_s[chan], side_s[chan]], axis=1)
-        out_ref[chan] = (0.5 * state + 0.125 * stencil_sum(state))[EDGE : EDGE + rows, :width]
+        def body(k, carry):
+            start = pl.multiple_of(k * step, 8)
+            state = jnp.concatenate(
+                [tall_s[chan, pl.ds(start, span), :], side_s[chan, pl.ds(start, span), :]], axis=1)
+            done = 0.5 * state + 0.125 * stencil_sum(state)
+            out_ref[chan, pl.ds(start, step), :] = done[EDGE : EDGE + step, :width]
+            return carry
+        lax.fori_loop(0, rows // step, body, 0)
 
 
 def diffuse_kernel(sizes, x_ref, dtall_ref, dside_ref, out_ref, *scratch):
@@ -177,12 +192,21 @@
     exchange(sizes, x_ref, rows_buf, cols_buf, colsend, tall_s, side_s, send_sem, recv_sem)
     rows, width = out_ref.shape[1], out_ref.shape[2]
     first = dtall_ref.shape[0] - out_ref.shape[0]
+    step = chunk_rows(rows)
+    span = step + 2 * EDGE
     for chan in range(out_ref.shape[0]):
-        state = jnp.concatenate([tall_s[chan], side_s[chan]], axis=1)
-        diff = jnp.concatenate([dtall_ref[first + chan], dside_ref[first + chan]], axis=1)
-        for iteration in range(ITERS):
-            state = state + diff * (stencil_sum(state) - 4.0 * state)
-        out_ref[chan] = state[EDGE : EDGE + rows, :width]
+        def body(k, carry):
+            start = pl.multiple_of(k * step, 8)
+            window = pl.ds(start, span)
+            state = jnp.concatenate(
+                [tall_s[chan, window, :], side_s[chan, window, :]], axis=1)
+            diff = jnp.concatenate(
+                [dtall_ref[first + chan, window, :], dside_ref[first + chan, window, :]], axis=1)
+            for iteration in range(ITERS):
+                state = state + diff * (stencil_sum(state) - 4.0 * state)
+            out_ref[chan, pl.ds(start, step), :] = state[EDGE : EDGE + step, :width]
+            return carry
+        lax.fori_loop(0, rows // step, body, 0)
 
 
 def smooth_call(sizes, both, chans, rows_padded):

time: 119 us -> 126 us (1.059)
  Pallas kernels: 59.6 us -> 67.2 us
    pallas_call x1, Pallas kernels: 22.3 us -> 28 us  [diffuse_call(): pl.pallas_call(functools.partial(diffuse_kernel, sizes), out_shape=jax.Sh...]
    pallas_call x1, Pallas kernels: 37.3 us -> 39.3 us  [smooth_call(): pl.pallas_call(functools.partial(smooth_kernel, sizes), out_shape=(jax.Sh...]
  transfers between devices with their start and end apart: 2 -> 2, of which waited for: 0 -> 0; matrix products, arithmetic and copies ran while one was open for 9% -> 8% of each run, Pallas kernels for 50% -> 53%
where the time goes in v10:
time: 126 us
  Pallas kernels  67.2 us (53%)
  matrix products  18.3 us (15%)
  starting transfers between devices  17 us (13%)
  local copies, waits for them, and re-layouts  12.1 us (10%)
  other arithmetic  10.1 us (8%)
    pallas_call x1, Pallas kernels, smooth_call(): pl.pallas_call(functools.partial(smooth_kernel, sizes), out_shape=(jax.Sh...  39.3 us
    pallas_call x1, Pallas kernels, diffuse_call(): pl.pallas_call(functools.partial(diffuse_kernel, sizes), out_shape=jax.Sh...  28 us
    all_to_all x1, starting transfers between devices, per_device(): lax.all_to_all(outgoing, ('atm', 'ocn'), split_axis=0, concat_axis=0, til...  11.9 us
    dot_general x3, matrix products, per_device(): jnp.dot(row_pick, weighted[c], precision=HIGHEST, preferred_element_type=...  6.49 us
    dot_general x3, matrix products, per_device(): jnp.dot(pick_rows, smoothed[c], precision=HIGHEST, preferred_element_type...  6.09 us
    unnamed x38, local copies, waits for them, and re-layouts  6.02 us
    all_to_all x1, starting transfers between devices, per_device(): lax.all_to_all(jnp.concatenate(weighted, axis=1), ('atm', 'ocn'), split_a...  5.03 us
    concatenate x1, local copies, waits for them, and re-layouts, per_device(): outgoing = jnp.concatenate([out_ocean, out_weight, out_label], axis=1)  3.24 us
  transfers between devices with their start and end apart: 2, of which 0 were waited for; matrix products, arithmetic and copies ran while one was open for 8% of the time, Pallas kernels for 53%

profile of v10, /device:TPU:1, one launch (start us, length us, event | category | flops | bytes accessed | tf_op | source)
XLA Modules:
  0.0 125.8 jit_solution(17959161658403549597)
XLA Ops:
  0.7 0.8 fusion.49
  1.4 0.8 copy.12
  2.5 0.9 fusion.43
  3.7 1.3 %fusion.7 = f32[1024,128]{0,1:T(8,128)S(1)} fusion(f32[512,128]{1,0:T(8,128)S(1)} %copy-done, s32[512]{0:T(512)S(1)} %multiply_add_fusion.1), kind=kOutput, calls=%fused_computation.15 | convolution fusion | flops 805830656 | bytes 788480 | tf_op jit(solution)/shard_map/dot_general | solution.py:65
  5.2 0.6 fusion.6
  5.9 0.6 fusion.8
  6.5 1.5 %fusion.57 = f32[1024,384]{0,1:T(8,128)S(1)} fusion(f32[1024,256]{1,0:T(8,128)S(1)} %fusion.8, f32[256,384]{0,1:T(8,128)S(1)} %bitcast.67), kind=kOutput, calls=%fused_computation.95 | convolution fusion | flops 1207959552 | bytes 3014656 | tf_op jit(solution)/shard_map/dot_general | solution.py:65
  8.3 1.8 %pad_maximum_fusion.1 = f32[1024,640]{0,1:T(8,128)} fusion(f32[1024,128]{0,1:T(8,128)S(1)} %slice_add_fusion, f32[1024,128]{0,1:T(8,128)S(1)} %convolution_multiply_fusion, f32[1024,384]{0,1:T(8,128)S(1)} %fusion.57), kind=kLoop, calls=%fused_computation.8 | loop fusion | flops 1310720 | bytes 5242880 | tf_op jit(solution)/shard_map/concatenate | solution.py:286
  10.2 3.2 %copy.15 = f32[1024,640]{1,0:T(8,128)} copy(f32[1024,640]{0,1:T(8,128)} %pad_maximum_fusion.1) | data formatting | bytes 5242880 | tf_op jit(solution)/shard_map/concatenate | solution.py:286
  13.4 11.9 %all-to-all-start = ((f32[128,8,640]{2,1,0:T(8,128)}), f32[128,8,640]{2,1,0:T(8,128)}, u32[]{:S(2)}, u32[]{:S(2)}) async-start(f32[128,8,640]{2,1,0:T(8,128)} %bitcast.63), calls=%async_computation | async-start | bytes 5242880 | tf_op jit(solution)/shard_map/all_to_all | solution.py:287
  25.4 3.0 %pad_maximum_fusion.x_ref = f32[6,864,128]{2,1,0:T(8,128)} fusion(f32[3,864,128]{2,1,0:T(8,128)S(1)} %bitcast.68, f32[3,864,128]{2,1,0:T(8,128)} %bitcast.69), kind=kLoop, calls=%fused_computation.7 | loop fusion | flops 663552 | bytes 5308416 | tf_op jit(solution)/shard_map/concatenate | solution.py:290
  28.4 39.3 %shard_map.95 = (f32[3,864,128]{2,1,0:T(8,128)}, f32[3,896,128]{2,1,0:T(8,128)}, f32[3,896,128]{2,1,0:T(8,128)}) custom-call(f32[6,864,128]{2,1,0:T(8,128)} %pad_maximum_fusion.x_ref), custom_call_target="tpu_custom_call" | custom-call | tf_op jit(solution)/shard_map/pallas_call | solution.py:215
  67.6 2.0 %fusion.56 = (f32[1024,128]{1,0:T(8,128)S(1)}, f32[1024,128]{1,0:T(8,128)S(1)}, f32[1024,128]{1,0:T(8,128)S(1)}, f32[1024,128]{1,0:T(8,128)S(1)}, f32[1024]{0:T(1024)S(1)}) fusion(f32[1024,640]{1,0:T(8,128)} %bitcast.9), kind=kLoop, calls=%fused_computation.94 | loop fusion | flops 130048 | bytes 4722688 | tf_op jit(solution)/shard_map/slice | solution.py:302
  69.6 1.0 copy.25
  71.0 1.0 copy.26
  72.0 2.8 %fusion.19 = f32[1024,128]{0,1:T(8,128)S(1)} fusion(f32[1024,128]{0,1:T(8,128)} %copy.26, s32[1024]{0:T(1024)S(1)} %convert_element_type.45, f32[3,864,128]{2,1,0:T(8,128)} %get-tuple-element.7), kind=kOutput, calls=%fused_computation.30 | convolution fusion | flops 1359970304 | bytes 1495040 | tf_op jit(solution)/shard_map/dot_general | solution.py:300
  74.8 1.5 %fusion.18 = f32[1024,128]{0,1:T(8,128)S(1)} fusion(f32[1024,128]{0,1:T(8,128)S(1)} %copy-done.4, s32[1024]{0:T(1024)S(1)} %convert_element_type.45, f32[3,864,128]{2,1,0:T(8,128)S(1)} %copy-done.13), kind=kOutput, calls=%fused_computation.29 | convolution fusion | flops 1359970304 | bytes 1495040 | tf_op jit(solution)/shard_map/dot_general | solution.py:300
  76.3 1.9 %multiply_multiply_fusion.3 = (f32[1024,128]{0,1:T(8,128)S(1)}, f32[1024,128]{0,1:T(8,128)S(1)}, f32[1024,128]{0,1:T(8,128)S(1)}) fusion(f32[1024,128]{0,1:T(8,128)S(1)} %copy.23, f32[1024,128]{0,1:T(8,128)S(1)} %fusion.19, f32[1024,128]{0,1:T(8,128)S(1)} %fusion.18, f32[1024,128]{0,1:T(8,128)S(1)} %copy.24, f32[3,864,128]{2,1,0:T(8,128)S(1)} %copy-done.13, ...), kind=kOutput, calls=%fused_computation.51 | convolution fusion | flops 1362198528 | bytes 4116480 | tf_op jit(solution)/shard_map/dot_general | solution.py:300
  78.2 0.8 copy-done.5
  79.5 1.6 %copy.20 = f32[1024,384]{1,0:T(8,128)} copy(f32[1024,384]{0,1:T(8,128)S(1)} %pad_maximum_fusion.2) | data formatting | bytes 3145728 | tf_op jit(solution)/shard_map/concatenate | solution.py:315
  81.1 5.0 %all-to-all-start.1 = ((f32[128,8,384]{2,1,0:T(8,128)}), f32[128,8,384]{2,1,0:T(8,128)S(1)}, u32[]{:S(2)}, u32[]{:S(2)}) async-start(f32[128,8,384]{2,1,0:T(8,128)} %bitcast.64), calls=%async_computation.1 | async-start | bytes 3145728 | tf_op jit(solution)/shard_map/all_to_all | solution.py:314
  86.2 3.0 %fusion.21 = f32[1,864,128]{2,1,0:T(8,128)S(1)} fusion(f32[1024,128]{0,1:T(8,128)} %copy-done.9, s32[1024]{0:T(1024)S(1)} %convert_element_type.45, f32[3,864,128]{2,1,0:T(8,128)} %bitcast.70), kind=kOutput, calls=%fused_computation.32 | convolution fusion | flops 1359949824 | bytes 1413120 | tf_op jit(solution)/shard_map/dot_general | solution.py:319
  89.2 1.7 %fusion.27 = f32[1,864,128]{2,1,0:T(8,128)S(1)} fusion(f32[1024,128]{0,1:T(8,128)S(1)} %copy-done.8, s32[1024]{0:T(1024)S(1)} %convert_element_type.45, f32[3,864,128]{2,1,0:T(8,128)S(1)} %bitcast.71), kind=kOutput, calls=%fused_computation.38 | convolution fusion | flops 1360060416 | bytes 1413120 | tf_op jit(solution)/shard_map/dot_general | solution.py:319
  91.0 1.7 %fusion.24 = f32[1,864,128]{2,1,0:T(8,128)S(1)} fusion(f32[1024,128]{0,1:T(8,128)S(1)} %copy-done.6, s32[1024]{0:T(1024)S(1)} %convert_element_type.45, f32[3,864,128]{2,1,0:T(8,128)S(1)} %bitcast.72), kind=kOutput, calls=%fused_computation.35 | convolution fusion | flops 1360060416 | bytes 1413120 | tf_op jit(solution)/shard_map/dot_general | solution.py:319
  92.7 1.1 pad_maximum_fusion.3.x_ref
  93.8 28.0 %shard_map.96 = f32[3,864,128]{2,1,0:T(8,128)} custom-call(f32[3,864,128]{2,1,0:T(8,128)} %pad_maximum_fusion.3.x_ref, f32[3,896,128]{2,1,0:T(8,128)} %get-tuple-element.8.dtall_ref, f32[3,896,128]{2,1,0:T(8,128)} %get-tuple-element.9.dside_ref), custom_call_target="tpu_custom_call" | custom-call | tf_op jit(solution)/shard_map/pallas_call | solution.py:233
  121.8 0.5 fusion.32
  122.3 0.5 convolution_add_fusion.1
  122.8 0.5 convolution_add_fusion
  123.5 0.9 copy.22
  124.4 0.3 copy-done.1
  124.7 1.1 copy.28
  (48 shorter events, 2.2 us)
Async XLA Ops:
  0.6 3.0 %copy-start = (f32[512,128]{1,0:T(8,128)S(1)}, f32[512,128]{1,0:T(8,128)}, u32[]{:S(2)}) copy-start(f32[512,128]{1,0:T(8,128)} %param.12) | copy-start | bytes 786436
  0.6 2.8 %copy-start.12 = (s32[512,1]{0,1:T(1,128)S(1)}, s32[512,1]{0,1:T(1,128)}, u32[]{:S(2)}) copy-start(s32[512,1]{0,1:T(1,128)} %param.14) | copy-start | bytes 6148
  0.7 2.8 %copy-start.10 = (f32[256,3,128]{2,0,1:T(8,128)S(1)}, f32[256,3,128]{2,0,1:T(8,128)}, u32[]{:S(2)}) copy-start(f32[256,3,128]{2,0,1:T(8,128)} %param.10) | copy-start | bytes 1179652
  5.2 0.7 copy-start.14
  6.5 1.5 %copy-start.11 = (s32[256,128]{1,0:T(8,128)S(1)}, s32[256,128]{1,0:T(8,128)}, u32[]{:S(2)}) copy-start(s32[256,128]{1,0:T(8,128)} %param.11) | copy-start | bytes 393220
  13.4 11.9 %copy-start.2 = (f32[864,3,128]{2,0,1:T(8,128)S(1)}, f32[864,3,128]{2,0,1:T(8,128)}, u32[]{:S(2)}) copy-start(f32[864,3,128]{2,0,1:T(8,128)} %param.9) | copy-start | bytes 3981316
  13.4 54.2 %all-to-all-start = ((f32[128,8,640]{2,1,0:T(8,128)}), f32[128,8,640]{2,1,0:T(8,128)}, u32[]{:S(2)}, u32[]{:S(2)}) async-start(f32[128,8,640]{2,1,0:T(8,128)} %bitcast.63), calls=%async_computation | async-start | bytes 5242880 | tf_op jit(solution)/shard_map/all_to_all | solution.py:287
  71.0 3.8 %copy-start.4 = (f32[1024,128]{0,1:T(8,128)S(1)}, f32[1024,128]{0,1:T(8,128)}, u32[]{:S(2)}) copy-start(f32[1024,128]{0,1:T(8,128)} %copy.25) | copy-start | bytes 1572868
  72.0 2.8 %copy-start.13 = (f32[3,864,128]{2,1,0:T(8,128)S(1)}, f32[3,864,128]{2,1,0:T(8,128)}, u32[]{:S(2)}) copy-start(f32[3,864,128]{2,1,0:T(8,128)} %get-tuple-element.7) | copy-start | bytes 3981316
  78.2 0.8 copy-start.5
  78.2 1.0 copy-start.7
  78.2 1.1 copy-start.9
  81.1 8.1 %copy-start.8 = (f32[1024,128]{0,1:T(8,128)S(1)}, f32[1024,128]{0,1:T(8,128)}, u32[]{:S(2)}) copy-start(f32[1024,128]{0,1:T(8,128)} %copy-done.7) | copy-start | bytes 1572868
  81.1 40.7 %all-to-all-start.1 = ((f32[128,8,384]{2,1,0:T(8,128)}), f32[128,8,384]{2,1,0:T(8,128)S(1)}, u32[]{:S(2)}, u32[]{:S(2)}) async-start(f32[128,8,384]{2,1,0:T(8,128)} %bitcast.64), calls=%async_computation.1 | async-start | bytes 3145728 | tf_op jit(solution)/shard_map/all_to_all | solution.py:314
  86.1 3.1 %copy-start.3 = (f32[864,3,128]{2,0,1:T(8,128)S(1)}, f32[864,3,128]{2,0,1:T(8,128)}, u32[]{:S(2)}) copy-start(f32[864,3,128]{2,0,1:T(8,128)} %param.8) | copy-start | bytes 3981316
  86.2 4.8 %copy-start.6 = (f32[1024,128]{0,1:T(8,128)S(1)}, f32[1024,128]{0,1:T(8,128)}, u32[]{:S(2)}) copy-start(f32[1024,128]{0,1:T(8,128)} %copy-done.5) | copy-start | bytes 1572868
  123.3 1.4 %copy-start.1 = (f32[3,864,128]{2,1,0:T(8,128)S(1)}, f32[3,864,128]{2,1,0:T(8,128)}, u32[]{:S(2)}) copy-start(f32[3,864,128]{2,1,0:T(8,128)} %shard_map.96) | copy-start | bytes 3981316

commit v11 on v9

--- a/solution.py
+++ b/solution.py
@@ -172,14 +172,18 @@
         out_ref[chan] = (0.5 * state + 0.125 * stencil_sum(state))[EDGE : EDGE + rows, :width]
 
 
-def diffuse_kernel(sizes, x_ref, dtall_ref, dside_ref, out_ref, *scratch):
+def exchange_kernel(sizes, x_ref, tall_out, side_out, *scratch):
     rows_buf, cols_buf, colsend, tall_s, side_s, send_sem, recv_sem = scratch
     exchange(sizes, x_ref, rows_buf, cols_buf, colsend, tall_s, side_s, send_sem, recv_sem)
+    tall_out[...] = tall_s[...]
+    side_out[...] = side_s[...]
+
+
+def diffuse_kernel(tall_ref, side_ref, dtall_ref, dside_ref, out_ref):
     rows, width = out_ref.shape[1], out_ref.shape[2]
-    first = dtall_ref.shape[0] - out_ref.shape[0]
     for chan in range(out_ref.shape[0]):
-        state = jnp.concatenate([tall_s[chan], side_s[chan]], axis=1)
-        diff = jnp.concatenate([dtall_ref[first + chan], dside_ref[first + chan]], axis=1)
+        state = jnp.concatenate([tall_ref[chan], side_ref[chan]], axis=1)
+        diff = jnp.concatenate([dtall_ref[chan], dside_ref[chan]], axis=1)
         for iteration in range(ITERS):
             state = state + diff * (stencil_sum(state) - 4.0 * state)
         out_ref[chan] = state[EDGE : EDGE + rows, :width]
@@ -202,18 +206,29 @@
     )(both)
 
 
-def diffuse_call(sizes, forced, dtall, dside):
+def exchange_call(sizes, forced, rows_padded):
     chans, rows, width = forced.shape
-    rows_padded = dtall.shape[1]
+    vmem = pl.BlockSpec(memory_space=pltpu.VMEM)
+    plane = jax.ShapeDtypeStruct((chans, rows_padded, width), jnp.float32)
+    return pl.pallas_call(
+        functools.partial(exchange_kernel, sizes),
+        out_shape=(plane, plane),
+        in_specs=[vmem],
+        out_specs=(vmem, vmem),
+        scratch_shapes=exchange_scratch(chans, rows_padded, width),
+        compiler_params=pltpu.CompilerParams(collective_id=1, has_side_effects=True),
+    )(forced)
+
+
+def diffuse_call(tall, side, dtall, dside, rows):
+    chans, rows_padded, width = tall.shape
     vmem = pl.BlockSpec(memory_space=pltpu.VMEM)
     return pl.pallas_call(
-        functools.partial(diffuse_kernel, sizes),
+        diffuse_kernel,
         out_shape=jax.ShapeDtypeStruct((chans, rows, width), jnp.float32),
-        in_specs=[vmem] * 3,
+        in_specs=[vmem] * 4,
         out_specs=vmem,
-        scratch_shapes=exchange_scratch(chans, rows_padded, width),
-        compiler_params=pltpu.CompilerParams(collective_id=1, has_side_effects=True),
-    )(forced, dtall, dside)
+    )(tall, side, dtall, dside)
 
 
 def per_device(
@@ -287,16 +302,16 @@
         in_weight * (0.6 * factor * wind_speed * wind_east),
         in_weight * (0.6 * factor * wind_speed * wind_north),
     ]
-    returned = lax.all_to_all(
-        jnp.concatenate(weighted, axis=1), ("atm", "ocn"), split_axis=0, concat_axis=0, tiled=True
-    )
     signs = (1.0, -1.0, -1.0)
     forced = jnp.stack(
         [atm_planes[c] + signs[c] * jnp.dot(row_pick, weighted[c], precision=HIGHEST,
                                              preferred_element_type=jnp.float32)
          for c in range(chan_count)]
     )
-    current = diffuse_call(sizes, forced, dtall, dside)
+    tall, side = exchange_call(sizes, forced, rows_padded)
+    sent, tall, side = lax.optimization_barrier((jnp.concatenate(weighted, axis=1), tall, side))
+    returned = lax.all_to_all(sent, ("atm", "ocn"), split_axis=0, concat_axis=0, tiled=True)
+    current = diffuse_call(tall, side, dtall, dside, row_count)
     current, returned = lax.optimization_barrier((current, returned))
     seg_of_slot = slot_seg.T.astype(jnp.bfloat16)
     ocean_flux = pick_dot(seg_of_slot, returned).reshape(seg_count, chan_count, seg_width)

time: 119 us -> 130 us (1.092)
  waiting for transfers between devices: 0.01 us -> 16.7 us
  Pallas kernels: 59.6 us -> 57.1 us
  local copies, waits for them, and re-layouts: 12.1 us -> 9.6 us
    all_to_all x1, waiting for transfers between devices: 0.01 us -> 16.7 us  [per_device(): lax.all_to_all(sent, ('atm', 'ocn'), split_axis=0, concat_axis=0, tiled=T...]
    unnamed x38 -> x25, local copies, waits for them, and re-layouts: 6.02 us -> 3.52 us
    pallas_call x1 -> x2, Pallas kernels: 22.3 us -> 20.1 us  [the longest x1 11.9 us: exchange_call(): pl.pallas_call(functools.partial(exchange_kernel, sizes), out_shape=(plan...]
    concatenate x1 -> x0, local copies, waits for them, and re-layouts: 1.63 us -> none  [per_device(): jnp.concatenate(weighted, axis=1)]
    optimization_barrier x0 -> x1, local copies, waits for them, and re-layouts: none -> 1.63 us  [per_device(): lax.optimization_barrier((jnp.concatenate(weighted, axis=1), tall, side))]
  transfers between devices with their start and end apart: 2 -> 2, of which waited for: 0 -> 1; matrix products, arithmetic and copies ran while one was open for 9% -> 2% of each run, Pallas kernels for 50% -> 35%
where the time goes in v11:
time: 130 us; the launch traced here: 129 us
  Pallas kernels  57.1 us (44%)
  starting transfers between devices  17.5 us (13%)
  matrix products  17.3 us (13%)
  waiting for transfers between devices  16.7 us (13%)
  other arithmetic  10.1 us (8%)
  local copies, waits for them, and re-layouts  9.6 us (7%)
    pallas_call x1, Pallas kernels, smooth_call(): pl.pallas_call(functools.partial(smooth_kernel, sizes), out_shape=(jax.Sh...  37.1 us
    all_to_all x1, waiting for transfers between devices, per_device(): lax.all_to_all(sent, ('atm', 'ocn'), split_axis=0, concat_axis=0, tiled=T...  16.7 us
    all_to_all x1, starting transfers between devices, per_device(): lax.all_to_all(outgoing, ('atm', 'ocn'), split_axis=0, concat_axis=0, til...  12.1 us
    pallas_call x1, Pallas kernels, exchange_call(): pl.pallas_call(functools.partial(exchange_kernel, sizes), out_shape=(plan...  11.9 us
    pallas_call x1, Pallas kernels, diffuse_call(): pl.pallas_call(diffuse_kernel, out_shape=jax.ShapeDtypeStruct((chans, row...  8.13 us
    dot_general x3, matrix products, per_device(): jnp.dot(pick_rows, smoothed[c], precision=HIGHEST, preferred_element_type...  6.09 us
    dot_general x3, matrix products, per_device(): jnp.dot(row_pick, weighted[c], precision=HIGHEST, preferred_element_type=...  5.47 us
    all_to_all x1, starting transfers between devices, per_device(): lax.all_to_all(sent, ('atm', 'ocn'), split_axis=0, concat_axis=0, tiled=T...  5.38 us
  transfers between devices with their start and end apart: 2, of which 1 were waited for; matrix products, arithmetic and copies ran while one was open for 2% of the time, Pallas kernels for 35%

profile of v11, /device:TPU:1, one launch (start us, length us, event | category | flops | bytes accessed | tf_op | source)
XLA Modules:
  0.0 129.3 jit_solution(8077615239513441663)
XLA Ops:
  0.7 0.8 fusion.49
  1.4 0.8 copy.12
  2.5 0.9 fusion.43
  3.7 1.3 fusion.7
  5.2 0.6 fusion.6
  5.9 0.6 fusion.8
  6.5 1.5 %fusion.57 = f32[1024,384]{0,1:T(8,128)S(1)} fusion(f32[1024,256]{1,0:T(8,128)S(1)} %fusion.8, f32[256,384]{0,1:T(8,128)S(1)} %bitcast.66), kind=kOutput, calls=%fused_computation.95 | convolution fusion | flops 1207959552 | bytes 3014656 | tf_op jit(solution)/shard_map/dot_general | solution.py:65
  8.0 0.3 convolution_multiply_fusion
  8.3 1.9 %pad_maximum_fusion.1 = f32[1024,640]{0,1:T(8,128)} fusion(f32[1024,128]{0,1:T(8,128)S(1)} %slice_add_fusion, f32[1024,128]{0,1:T(8,128)S(1)} %convolution_multiply_fusion, f32[1024,384]{0,1:T(8,128)S(1)} %fusion.57), kind=kLoop, calls=%fused_computation.8 | loop fusion | flops 1310720 | bytes 5242880 | tf_op jit(solution)/shard_map/concatenate | solution.py:277
  10.2 3.2 %copy.15 = f32[1024,640]{1,0:T(8,128)} copy(f32[1024,640]{0,1:T(8,128)} %pad_maximum_fusion.1) | data formatting | bytes 5242880 | tf_op jit(solution)/shard_map/concatenate | solution.py:277
  13.4 12.1 %all-to-all-start = ((f32[128,8,640]{2,1,0:T(8,128)}), f32[128,8,640]{2,1,0:T(8,128)}, u32[]{:S(2)}, u32[]{:S(2)}) async-start(f32[128,8,640]{2,1,0:T(8,128)} %bitcast.63), calls=%async_computation | async-start | bytes 5242880 | tf_op jit(solution)/shard_map/all_to_all | solution.py:278
  25.5 3.0 %pad_maximum_fusion.x_ref = f32[6,864,128]{2,1,0:T(8,128)} fusion(f32[3,864,128]{2,1,0:T(8,128)S(1)} %bitcast.67, f32[3,864,128]{2,1,0:T(8,128)} %bitcast.68), kind=kLoop, calls=%fused_computation.7 | loop fusion | flops 663552 | bytes 5308416 | tf_op jit(solution)/shard_map/concatenate | solution.py:281
  28.5 37.1 %shard_map.95 = (f32[3,864,128]{2,1,0:T(8,128)}, f32[3,896,128]{2,1,0:T(8,128)}, f32[3,896,128]{2,1,0:T(8,128)}) custom-call(f32[6,864,128]{2,1,0:T(8,128)} %pad_maximum_fusion.x_ref), custom_call_target="tpu_custom_call" | custom-call | tf_op jit(solution)/shard_map/pallas_call | solution.py:195
  65.7 2.0 %fusion.56 = (f32[1024,128]{1,0:T(8,128)S(1)}, f32[1024,128]{1,0:T(8,128)S(1)}, f32[1024,128]{1,0:T(8,128)S(1)}, f32[1024]{0:T(1024)S(1)}, f32[1024,128]{1,0:T(8,128)S(1)}) fusion(f32[1024,640]{1,0:T(8,128)} %bitcast.7), kind=kLoop, calls=%fused_computation.94 | loop fusion | flops 130048 | bytes 4722688 | tf_op jit(solution)/shard_map/slice | solution.py:293
  67.6 1.0 copy.25
  69.1 1.0 copy.26
  70.0 2.8 %fusion.19 = f32[1024,128]{0,1:T(8,128)S(1)} fusion(f32[1024,128]{0,1:T(8,128)} %copy.26, s32[1024]{0:T(1024)S(1)} %convert_element_type.45, f32[3,864,128]{2,1,0:T(8,128)} %get-tuple-element.12), kind=kOutput, calls=%fused_computation.30 | convolution fusion | flops 1359970304 | bytes 1495040 | tf_op jit(solution)/shard_map/dot_general | solution.py:291
  72.8 1.5 %fusion.18 = f32[1024,128]{0,1:T(8,128)S(1)} fusion(f32[1024,128]{0,1:T(8,128)S(1)} %copy-done.3, s32[1024]{0:T(1024)S(1)} %convert_element_type.45, f32[3,864,128]{2,1,0:T(8,128)S(1)} %copy-done.7), kind=kOutput, calls=%fused_computation.29 | convolution fusion | flops 1359970304 | bytes 1495040 | tf_op jit(solution)/shard_map/dot_general | solution.py:291
  74.3 1.9 %multiply_multiply_fusion.3 = (f32[1024,128]{0,1:T(8,128)S(1)}, f32[1024,128]{0,1:T(8,128)S(1)}, f32[1024,128]{0,1:T(8,128)S(1)}) fusion(f32[1024,128]{0,1:T(8,128)S(1)} %copy.23, f32[1024,128]{0,1:T(8,128)S(1)} %fusion.19, f32[1024,128]{0,1:T(8,128)S(1)} %fusion.18, f32[1024,128]{0,1:T(8,128)S(1)} %copy.24, f32[3,864,128]{2,1,0:T(8,128)S(1)} %copy-done.7, ...), kind=kOutput, calls=%fused_computation.51 | convolution fusion | flops 1362198528 | bytes 4116480 | tf_op jit(solution)/shard_map/dot_general | solution.py:291
  76.2 1.8 %fusion.21 = f32[1,864,128]{2,1,0:T(8,128)S(1)} fusion(f32[1024,128]{0,1:T(8,128)S(1)} %get-tuple-element.31, s32[1024]{0:T(1024)S(1)} %convert_element_type.45, f32[3,864,128]{2,1,0:T(8,128)S(1)} %bitcast.69), kind=kOutput, calls=%fused_computation.32 | convolution fusion | flops 1359949824 | bytes 1413120 | tf_op jit(solution)/shard_map/dot_general | solution.py:307
  78.0 1.7 %fusion.27 = f32[1,864,128]{2,1,0:T(8,128)S(1)} fusion(f32[1024,128]{0,1:T(8,128)S(1)} %get-tuple-element.32, s32[1024]{0:T(1024)S(1)} %convert_element_type.45, f32[3,864,128]{2,1,0:T(8,128)S(1)} %bitcast.70), kind=kOutput, calls=%fused_computation.38 | convolution fusion | flops 1360060416 | bytes 1413120 | tf_op jit(solution)/shard_map/dot_general | solution.py:307
  79.7 2.0 %fusion.24 = f32[1,864,128]{2,1,0:T(8,128)S(1)} fusion(f32[1024,128]{0,1:T(8,128)S(1)} %get-tuple-element.33, s32[1024]{0:T(1024)S(1)} %convert_element_type.45, f32[3,864,128]{2,1,0:T(8,128)S(1)} %bitcast.71), kind=kOutput, calls=%fused_computation.35 | convolution fusion | flops 1360060416 | bytes 1413120 | tf_op jit(solution)/shard_map/dot_general | solution.py:307
  81.8 1.1 pad_maximum_fusion.3.x_ref
  83.0 11.9 %shard_map.96 = (f32[3,896,128]{2,1,0:T(8,128)}, f32[3,896,128]{2,1,0:T(8,128)}) custom-call(f32[3,864,128]{2,1,0:T(8,128)} %pad_maximum_fusion.3.x_ref), custom_call_target="tpu_custom_call" | custom-call | tf_op jit(solution)/shard_map/pallas_call | solution.py:213
  94.9 1.6 %copy.20 = f32[1024,384]{1,0:T(8,128)} copy(f32[1024,384]{0,1:T(8,128)S(1)} %pad_maximum_fusion.2) | data formatting | bytes 3145728 | tf_op jit(solution)/shard_map/optimization_barrier | solution.py:312
  96.5 5.4 %all-to-all-start.1 = ((f32[128,8,384]{2,1,0:T(8,128)}), f32[128,8,384]{2,1,0:T(8,128)S(1)}, u32[]{:S(2)}, u32[]{:S(2)}) async-start(f32[128,8,384]{2,1,0:T(8,128)} %bitcast.64), calls=%async_computation.1 | async-start | bytes 3145728 | tf_op jit(solution)/shard_map/all_to_all | solution.py:313
  101.9 8.1 %shard_map.97 = f32[3,864,128]{2,1,0:T(8,128)} custom-call(f32[3,896,128]{2,1,0:T(8,128)} %get-tuple-element.15.tall_ref, f32[3,896,128]{2,1,0:T(8,128)} %get-tuple-element.16.side_ref, f32[3,896,128]{2,1,0:T(8,128)} %get-tuple-element.17.dtall_ref, f32[3,896,128]{2,1,0:T(8,128)} %get-tuple-element.18.dside_ref), custom_call_target="tpu_custom_call" | custom-call | tf_op jit(solution)/shard_map/pallas_call | solution.py:226
  110.0 16.7 %all-to-all-done.1 = f32[128,8,384]{2,1,0:T(8,128)S(1)} async-done(((f32[128,8,384]{2,1,0:T(8,128)}), f32[128,8,384]{2,1,0:T(8,128)S(1)}, u32[]{:S(2)}, u32[]{:S(2)}) %all-to-all-start.1) | async-done | bytes 1572896 | tf_op jit(solution)/shard_map/all_to_all | solution.py:313
  126.7 0.5 fusion.32
  127.2 0.5 convolution_add_fusion.1
  127.7 0.5 convolution_add_fusion
  128.4 0.9 copy.22
  (36 shorter events, 1.5 us)
Async XLA Ops:
  0.6 3.0 %copy-start = (f32[512,128]{1,0:T(8,128)S(1)}, f32[512,128]{1,0:T(8,128)}, u32[]{:S(2)}) copy-start(f32[512,128]{1,0:T(8,128)} %param.12) | copy-start | bytes 786436
  0.6 2.8 %copy-start.6 = (s32[512,1]{0,1:T(1,128)S(1)}, s32[512,1]{0,1:T(1,128)}, u32[]{:S(2)}) copy-start(s32[512,1]{0,1:T(1,128)} %param.14) | copy-start | bytes 6148
  0.7 2.8 %copy-start.4 = (f32[256,3,128]{2,0,1:T(8,128)S(1)}, f32[256,3,128]{2,0,1:T(8,128)}, u32[]{:S(2)}) copy-start(f32[256,3,128]{2,0,1:T(8,128)} %param.10) | copy-start | bytes 1179652
  5.2 0.7 copy-start.8
  6.5 1.5 %copy-start.5 = (s32[256,128]{1,0:T(8,128)S(1)}, s32[256,128]{1,0:T(8,128)}, u32[]{:S(2)}) copy-start(s32[256,128]{1,0:T(8,128)} %param.11) | copy-start | bytes 393220
  13.4 12.1 %copy-start.1 = (f32[864,3,128]{2,0,1:T(8,128)S(1)}, f32[864,3,128]{2,0,1:T(8,128)}, u32[]{:S(2)}) copy-start(f32[864,3,128]{2,0,1:T(8,128)} %param.9) | copy-start | bytes 3981316
  13.4 52.2 %all-to-all-start = ((f32[128,8,640]{2,1,0:T(8,128)}), f32[128,8,640]{2,1,0:T(8,128)}, u32[]{:S(2)}, u32[]{:S(2)}) async-start(f32[128,8,640]{2,1,0:T(8,128)} %bitcast.63), calls=%async_computation | async-start | bytes 5242880 | tf_op jit(solution)/shard_map/all_to_all | solution.py:278
  69.0 3.8 %copy-start.3 = (f32[1024,128]{0,1:T(8,128)S(1)}, f32[1024,128]{0,1:T(8,128)}, u32[]{:S(2)}) copy-start(f32[1024,128]{0,1:T(8,128)} %copy.25) | copy-start | bytes 1572868
  70.0 2.8 %copy-start.7 = (f32[3,864,128]{2,1,0:T(8,128)S(1)}, f32[3,864,128]{2,1,0:T(8,128)}, u32[]{:S(2)}) copy-start(f32[3,864,128]{2,1,0:T(8,128)} %get-tuple-element.12) | copy-start | bytes 3981316
  74.3 1.9 %copy-start.2 = (f32[864,3,128]{2,0,1:T(8,128)S(1)}, f32[864,3,128]{2,0,1:T(8,128)}, u32[]{:S(2)}) copy-start(f32[864,3,128]{2,0,1:T(8,128)} %param.8) | copy-start | bytes 3981316
  96.5 30.2 %all-to-all-start.1 = ((f32[128,8,384]{2,1,0:T(8,128)}), f32[128,8,384]{2,1,0:T(8,128)S(1)}, u32[]{:S(2)}, u32[]{:S(2)}) async-start(f32[128,8,384]{2,1,0:T(8,128)} %bitcast.64), calls=%async_computation.1 | async-start | bytes 3145728 | tf_op jit(solution)/shard_map/all_to_all | solution.py:313

commit v12 on v9

--- a/solution.py
+++ b/solution.py
@@ -259,7 +259,10 @@
     out_label = 32.0 * out_rows[:, :seg_width] + out_rows[:, seg_width:]
     out_area = select_rows(slot_pick.astype(jnp.float32), intersection_area)
     out_weight = out_area * out_mask
-    outgoing = jnp.concatenate([out_ocean, out_weight, out_label], axis=1)
+    slot_label = out_label[:, 0].astype(jnp.int32).reshape(devices, capacity)
+    in_labels = lax.all_to_all(
+        slot_label, ("atm", "ocn"), split_axis=0, concat_axis=0, tiled=True).reshape(slots)
+    outgoing = jnp.concatenate([out_ocean, out_weight], axis=1)
     incoming = lax.all_to_all(outgoing, ("atm", "ocn"), split_axis=0, concat_axis=0, tiled=True)
 
     atm_planes = jnp.transpose(atm_state, (1, 0, 2))
@@ -268,7 +271,6 @@
     rows_padded = -(-(row_count + 2 * EDGE) // 128) * 128
     smoothed, dtall, dside = smooth_call(sizes, both, chan_count, rows_padded)
 
-    in_labels = jnp.max(incoming[:, plane + seg_width :], axis=1).astype(jnp.int32)
     row_pick = (
         jnp.arange(row_count, dtype=jnp.int32)[:, None] == in_labels[None, :]
     ).astype(jnp.float32)

time: 119 us -> 124 us (1.042)
  starting transfers between devices: 17 us -> 22.9 us
  Pallas kernels: 59.6 us -> 53.9 us
  local copies, waits for them, and re-layouts: 12.1 us -> 15.8 us
  waiting for transfers between devices: 0.01 us -> 3.46 us
  other arithmetic: 10.1 us -> 7.6 us
    all_to_all x0 -> x1, starting transfers between devices: none -> 11.5 us  [per_device(): lax.all_to_all(slot_label, ('atm', 'ocn'), split_axis=0, concat_axis=0, t...]
    pallas_call x1, Pallas kernels: 37.3 us -> 31.6 us  [smooth_call(): pl.pallas_call(functools.partial(smooth_kernel, sizes), out_shape=(jax.Sh...]
    all_to_all x1, starting transfers between devices: 11.9 us -> 6.31 us  [per_device(): lax.all_to_all(outgoing, ('atm', 'ocn'), split_axis=0, concat_axis=0, til...]
    all_to_all x0 -> x1, waiting for transfers between devices: none -> 3.46 us  [per_device(): lax.all_to_all(slot_label, ('atm', 'ocn'), split_axis=0, concat_axis=0, t...]
    unnamed x38 -> x40, local copies, waits for them, and re-layouts: 6.02 us -> 8.23 us
    slice x1 -> x0, other arithmetic: 1.97 us -> none  [per_device(): incoming[:, c * seg_width:(c + 1) * seg_width]]
    concatenate x1, other arithmetic: 1.85 us -> 0.14 us  [per_device(): outgoing = jnp.concatenate([out_ocean, out_weight], axis=1)]
    slice x0 -> x2, local copies, waits for them, and re-layouts: none -> 1.5 us  [the longest x1 1.4 us: per_device(): incoming[:, c * seg_width:(c + 1) * seg_width]]
  transfers between devices with their start and end apart: 2 -> 3, of which waited for: 0 -> 1; matrix products, arithmetic and copies ran while one was open for 9% -> 15% of each run, Pallas kernels for 50% -> 44%
where the time goes in v12:
time: 124 us; the launch traced here: 123 us
  Pallas kernels  53.9 us (43%)
  starting transfers between devices  22.9 us (18%)
  matrix products  18.3 us (15%)
  local copies, waits for them, and re-layouts  15.8 us (13%)
  other arithmetic  7.6 us (6%)
  waiting for transfers between devices  3.46 us (3%)
    pallas_call x1, Pallas kernels, smooth_call(): pl.pallas_call(functools.partial(smooth_kernel, sizes), out_shape=(jax.Sh...  31.6 us
    pallas_call x1, Pallas kernels, diffuse_call(): pl.pallas_call(functools.partial(diffuse_kernel, sizes), out_shape=jax.Sh...  22.3 us
    all_to_all x1, starting transfers between devices, per_device(): lax.all_to_all(slot_label, ('atm', 'ocn'), split_axis=0, concat_axis=0, t...  11.5 us
    unnamed x40, local copies, waits for them, and re-layouts  8.23 us
    dot_general x3, matrix products, per_device(): jnp.dot(row_pick, weighted[c], precision=HIGHEST, preferred_element_type=...  6.49 us
    all_to_all x1, starting transfers between devices, per_device(): lax.all_to_all(outgoing, ('atm', 'ocn'), split_axis=0, concat_axis=0, til...  6.31 us
    dot_general x3, matrix products, per_device(): jnp.dot(pick_rows, smoothed[c], precision=HIGHEST, preferred_element_type...  6.08 us
    all_to_all x1, starting transfers between devices, per_device(): lax.all_to_all(jnp.concatenate(weighted, axis=1), ('atm', 'ocn'), split_a...  5.14 us
  transfers between devices with their start and end apart: 3, of which 1 were waited for; matrix products, arithmetic and copies ran while one was open for 15% of the time, Pallas kernels for 44%

profile of v12, /device:TPU:1, one launch (start us, length us, event | category | flops | bytes accessed | tf_op | source)
XLA Modules:
  0.0 123.1 jit_solution(16763556043204023010)
XLA Ops:
  0.7 0.7 fusion.51
  1.4 0.8 copy.23
  2.5 0.9 fusion.43
  3.7 0.6 fusion.8
  4.5 0.7 convert_element_type.52
  5.2 11.5 %all-to-all-start = ((s32[128,1,8]{2,1,0:T(1,128)}), s32[128,1,8]{2,1,0:T(1,128)S(1)}, u32[]{:S(2)}, u32[]{:S(2)}) async-start(s32[128,1,8]{2,1,0:T(1,128)} %bitcast.7), calls=%async_computation | async-start | bytes 131072 | tf_op jit(solution)/shard_map/all_to_all | solution.py:263
  16.9 1.3 %fusion.6 = f32[1024,128]{0,1:T(8,128)S(1)} fusion(f32[512,128]{1,0:T(8,128)S(1)} %copy-done, s32[512]{0:T(512)S(1)} %multiply_add_fusion.1), kind=kOutput, calls=%fused_computation.14 | convolution fusion | flops 805830656 | bytes 788480 | tf_op jit(solution)/shard_map/dot_general | solution.py:65
  18.2 0.6 fusion.7
  18.8 1.5 %fusion.60 = f32[1024,384]{0,1:T(8,128)S(1)} fusion(f32[1024,256]{1,0:T(8,128)S(1)} %fusion.7, f32[256,384]{0,1:T(8,128)S(1)} %bitcast.69), kind=kOutput, calls=%fused_computation.97 | convolution fusion | flops 1207959552 | bytes 3014656 | tf_op jit(solution)/shard_map/dot_general | solution.py:65
  20.8 1.8 %copy.27 = f32[1024,512]{1,0:T(8,128)} copy(f32[1024,512]{0,1:T(8,128)S(1)} %pad_maximum_fusion.1) | data formatting | bytes 4194304 | tf_op jit(solution)/shard_map/concatenate | solution.py:265
  22.6 3.5 %all-to-all-done = s32[128,1,8]{2,1,0:T(1,128)S(1)} async-done(((s32[128,1,8]{2,1,0:T(1,128)}), s32[128,1,8]{2,1,0:T(1,128)S(1)}, u32[]{:S(2)}, u32[]{:S(2)}) %all-to-all-start) | async-done | bytes 4128 | tf_op jit(solution)/shard_map/all_to_all | solution.py:263
  26.1 6.3 %all-to-all-start.1 = ((f32[128,8,512]{2,1,0:T(8,128)}), f32[128,8,512]{2,1,0:T(8,128)S(1)}, u32[]{:S(2)}, u32[]{:S(2)}) async-start(f32[128,8,512]{2,1,0:T(8,128)} %bitcast.65), calls=%async_computation.1 | async-start | bytes 4194304 | tf_op jit(solution)/shard_map/all_to_all | solution.py:266
  32.4 3.4 %pad_maximum_fusion.x_ref = f32[6,864,128]{2,1,0:T(8,128)} fusion(f32[3,864,128]{2,1,0:T(8,128)} %bitcast.70, f32[3,864,128]{2,1,0:T(8,128)} %bitcast.71), kind=kLoop, calls=%fused_computation.7 | loop fusion | flops 663552 | bytes 5308416 | tf_op jit(solution)/shard_map/concatenate | solution.py:269
  35.8 31.6 %shard_map.95 = (f32[3,864,128]{2,1,0:T(8,128)}, f32[3,896,128]{2,1,0:T(8,128)}, f32[3,896,128]{2,1,0:T(8,128)}) custom-call(f32[6,864,128]{2,1,0:T(8,128)} %pad_maximum_fusion.x_ref), custom_call_target="tpu_custom_call" | custom-call | tf_op jit(solution)/shard_map/pallas_call | solution.py:191
  67.9 0.8 reduce.7
  68.8 1.4 %fusion.58 = (f32[1024,128]{1,0:T(8,128)}, f32[1024,128]{1,0:T(8,128)}, f32[1024,128]{1,0:T(8,128)}, f32[1024,128]{1,0:T(8,128)}) fusion(f32[1024,512]{1,0:T(8,128)S(1)} %bitcast.64), kind=kLoop, calls=%fused_computation.95 | loop fusion | bytes 4194304 | tf_op jit(solution)/shard_map/slice | solution.py:280
  70.2 2.1 %copy.37 = f32[1024,128]{0,1:T(8,128)} copy(f32[1024,128]{1,0:T(8,128)} %get-tuple-element.21) | data formatting | bytes 1048576
  72.3 1.2 %copy.36 = f32[1024,128]{0,1:T(8,128)S(1)} copy(f32[1024,128]{1,0:T(8,128)} %get-tuple-element.22) | data formatting | bytes 1048576
  73.8 1.0 copy.38
  74.8 2.8 %fusion.19 = f32[1024,128]{0,1:T(8,128)S(1)} fusion(f32[1024,128]{0,1:T(8,128)} %copy.38, s32[1024]{0:T(1024)S(1)} %eq.77, f32[3,864,128]{2,1,0:T(8,128)} %get-tuple-element.7), kind=kOutput, calls=%fused_computation.30 | convolution fusion | flops 1359970304 | bytes 1495040 | tf_op jit(solution)/shard_map/dot_general | solution.py:278
  77.6 1.5 %fusion.18 = f32[1024,128]{0,1:T(8,128)S(1)} fusion(f32[1024,128]{0,1:T(8,128)S(1)} %copy-done.5, s32[1024]{0:T(1024)S(1)} %eq.77, f32[3,864,128]{2,1,0:T(8,128)S(1)} %copy-done.14), kind=kOutput, calls=%fused_computation.29 | convolution fusion | flops 1359970304 | bytes 1495040 | tf_op jit(solution)/shard_map/dot_general | solution.py:278
  79.1 1.9 %multiply_multiply_fusion.3 = (f32[1024,128]{0,1:T(8,128)S(1)}, f32[1024,128]{0,1:T(8,128)S(1)}, f32[1024,128]{0,1:T(8,128)S(1)}) fusion(f32[1024,128]{0,1:T(8,128)S(1)} %copy.35, f32[1024,128]{0,1:T(8,128)S(1)} %fusion.19, f32[1024,128]{0,1:T(8,128)S(1)} %fusion.18, f32[1024,128]{0,1:T(8,128)S(1)} %copy.36, f32[3,864,128]{2,1,0:T(8,128)S(1)} %copy-done.14, ...), kind=kOutput, calls=%fused_computation.48 | convolution fusion | flops 1362198528 | bytes 4116480 | tf_op jit(solution)/shard_map/dot_general | solution.py:278
  81.0 0.8 copy-done.6
  82.3 1.6 %copy.32 = f32[1024,384]{1,0:T(8,128)} copy(f32[1024,384]{0,1:T(8,128)S(1)} %pad_maximum_fusion.2) | data formatting | bytes 3145728 | tf_op jit(solution)/shard_map/concatenate | solution.py:293
  83.9 5.1 %all-to-all-start.2 = ((f32[128,8,384]{2,1,0:T(8,128)}), f32[128,8,384]{2,1,0:T(8,128)S(1)}, u32[]{:S(2)}, u32[]{:S(2)}) async-start(f32[128,8,384]{2,1,0:T(8,128)} %bitcast.66), calls=%async_computation.2 | async-start | bytes 3145728 | tf_op jit(solution)/shard_map/all_to_all | solution.py:292
  89.1 3.0 %fusion.21 = f32[1,864,128]{2,1,0:T(8,128)S(1)} fusion(f32[1024,128]{0,1:T(8,128)} %copy-done.10, s32[1024]{0:T(1024)S(1)} %eq.77, f32[3,864,128]{2,1,0:T(8,128)} %bitcast.72), kind=kOutput, calls=%fused_computation.32 | convolution fusion | flops 1359949824 | bytes 1413120 | tf_op jit(solution)/shard_map/dot_general | solution.py:297
  92.1 1.7 %fusion.27 = f32[1,864,128]{2,1,0:T(8,128)S(1)} fusion(f32[1024,128]{0,1:T(8,128)S(1)} %copy-done.9, s32[1024]{0:T(1024)S(1)} %eq.77, f32[3,864,128]{2,1,0:T(8,128)S(1)} %bitcast.73), kind=kOutput, calls=%fused_computation.38 | convolution fusion | flops 1360060416 | bytes 1413120 | tf_op jit(solution)/shard_map/dot_general | solution.py:297
  93.9 1.7 %fusion.24 = f32[1,864,128]{2,1,0:T(8,128)S(1)} fusion(f32[1024,128]{0,1:T(8,128)S(1)} %copy-done.7, s32[1024]{0:T(1024)S(1)} %eq.77, f32[3,864,128]{2,1,0:T(8,128)S(1)} %bitcast.74), kind=kOutput, calls=%fused_computation.35 | convolution fusion | flops 1360060416 | bytes 1413120 | tf_op jit(solution)/shard_map/dot_general | solution.py:297
  95.6 1.1 pad_maximum_fusion.3.x_ref
  96.8 22.3 %shard_map.96 = f32[3,864,128]{2,1,0:T(8,128)} custom-call(f32[3,864,128]{2,1,0:T(8,128)} %pad_maximum_fusion.3.x_ref, f32[3,896,128]{2,1,0:T(8,128)} %get-tuple-element.8.dtall_ref, f32[3,896,128]{2,1,0:T(8,128)} %get-tuple-element.9.dside_ref), custom_call_target="tpu_custom_call" | custom-call | tf_op jit(solution)/shard_map/pallas_call | solution.py:209
  120.8 0.9 copy.34
  122.0 1.1 copy.40
  (56 shorter events, 4.6 us)
Async XLA Ops:
  0.6 16.3 %copy-start = (f32[512,128]{1,0:T(8,128)S(1)}, f32[512,128]{1,0:T(8,128)}, u32[]{:S(2)}) copy-start(f32[512,128]{1,0:T(8,128)} %param.12) | copy-start | bytes 786436
  0.6 2.8 %copy-start.13 = (s32[512,1]{0,1:T(1,128)S(1)}, s32[512,1]{0,1:T(1,128)}, u32[]{:S(2)}) copy-start(s32[512,1]{0,1:T(1,128)} %param.14) | copy-start | bytes 6148
  3.7 13.0 %copy-start.11 = (f32[256,3,128]{2,0,1:T(8,128)S(1)}, f32[256,3,128]{2,0,1:T(8,128)}, u32[]{:S(2)}) copy-start(f32[256,3,128]{2,0,1:T(8,128)} %param.10) | copy-start | bytes 1179652
  4.4 13.8 %copy-start.15 = (s32[512]{0:T(512)S(1)}, s32[512]{0:T(512)}, u32[]{:S(2)}) copy-start(s32[512]{0:T(512)} %param.13) | copy-start | bytes 6148
  5.2 20.8 %all-to-all-start = ((s32[128,1,8]{2,1,0:T(1,128)}), s32[128,1,8]{2,1,0:T(1,128)S(1)}, u32[]{:S(2)}, u32[]{:S(2)}) async-start(s32[128,1,8]{2,1,0:T(1,128)} %bitcast.7), calls=%async_computation | async-start | bytes 131072 | tf_op jit(solution)/shard_map/all_to_all | solution.py:263
  18.8 1.5 %copy-start.12 = (s32[256,128]{1,0:T(8,128)S(1)}, s32[256,128]{1,0:T(8,128)}, u32[]{:S(2)}) copy-start(s32[256,128]{1,0:T(8,128)} %param.11) | copy-start | bytes 393220
  26.1 42.7 %all-to-all-start.1 = ((f32[128,8,512]{2,1,0:T(8,128)}), f32[128,8,512]{2,1,0:T(8,128)S(1)}, u32[]{:S(2)}, u32[]{:S(2)}) async-start(f32[128,8,512]{2,1,0:T(8,128)} %bitcast.65), calls=%async_computation.1 | async-start | bytes 4194304 | tf_op jit(solution)/shard_map/all_to_all | solution.py:266
  70.2 3.4 %copy-start.3 = (f32[1024,128]{1,0:T(8,128)S(1)}, f32[1024,128]{1,0:T(8,128)}, u32[]{:S(2)}) copy-start(f32[1024,128]{1,0:T(8,128)} %get-tuple-element.23) | copy-start | bytes 1572868
  70.2 3.6 %copy-start.2 = (f32[1024,128]{1,0:T(8,128)S(1)}, f32[1024,128]{1,0:T(8,128)}, u32[]{:S(2)}) copy-start(f32[1024,128]{1,0:T(8,128)} %get-tuple-element.24) | copy-start | bytes 1572868
  73.8 3.8 %copy-start.5 = (f32[1024,128]{0,1:T(8,128)S(1)}, f32[1024,128]{0,1:T(8,128)}, u32[]{:S(2)}) copy-start(f32[1024,128]{0,1:T(8,128)} %copy.37) | copy-start | bytes 1572868
  74.8 2.8 %copy-start.14 = (f32[3,864,128]{2,1,0:T(8,128)S(1)}, f32[3,864,128]{2,1,0:T(8,128)}, u32[]{:S(2)}) copy-start(f32[3,864,128]{2,1,0:T(8,128)} %get-tuple-element.7) | copy-start | bytes 3981316
  80.9 0.8 copy-start.6
  80.9 1.0 copy-start.8
  81.0 1.1 copy-start.10
  83.9 8.2 %copy-start.9 = (f32[1024,128]{0,1:T(8,128)S(1)}, f32[1024,128]{0,1:T(8,128)}, u32[]{:S(2)}) copy-start(f32[1024,128]{0,1:T(8,128)} %copy-done.8) | copy-start | bytes 1572868
  83.9 35.2 %all-to-all-start.2 = ((f32[128,8,384]{2,1,0:T(8,128)}), f32[128,8,384]{2,1,0:T(8,128)S(1)}, u32[]{:S(2)}, u32[]{:S(2)}) async-start(f32[128,8,384]{2,1,0:T(8,128)} %bitcast.66), calls=%async_computation.2 | async-start | bytes 3145728 | tf_op jit(solution)/shard_map/all_to_all | solution.py:292
  89.1 3.1 %copy-start.4 = (f32[864,3,128]{2,0,1:T(8,128)S(1)}, f32[864,3,128]{2,0,1:T(8,128)}, u32[]{:S(2)}) copy-start(f32[864,3,128]{2,0,1:T(8,128)} %param.8) | copy-start | bytes 3981316
  89.1 4.8 %copy-start.7 = (f32[1024,128]{0,1:T(8,128)S(1)}, f32[1024,128]{0,1:T(8,128)}, u32[]{:S(2)}) copy-start(f32[1024,128]{0,1:T(8,128)} %copy-done.6) | copy-start | bytes 1572868
  120.6 1.4 %copy-start.1 = (f32[3,864,128]{2,1,0:T(8,128)S(1)}, f32[3,864,128]{2,1,0:T(8,128)}, u32[]{:S(2)}) copy-start(f32[3,864,128]{2,1,0:T(8,128)} %shard_map.96) | copy-start | bytes 3981316

commit v13 on v9

--- a/solution.py
+++ b/solution.py
@@ -163,13 +163,14 @@
 def smooth_kernel(sizes, x_ref, out_ref, tall_out, side_out, *scratch):
     rows_buf, cols_buf, colsend, tall_s, side_s, send_sem, recv_sem = scratch
     exchange(sizes, x_ref, rows_buf, cols_buf, colsend, tall_s, side_s, send_sem, recv_sem)
-    rows, width = out_ref.shape[1], out_ref.shape[2]
     kept = tall_out.shape[0]
+    rows, width = out_ref.shape[0], out_ref.shape[1] // kept
     tall_out[...] = tall_s[kept:]
     side_out[...] = side_s[kept:]
-    for chan in range(out_ref.shape[0]):
+    for chan in range(kept):
         state = jnp.concatenate([tall_s[chan], side_s[chan]], axis=1)
-        out_ref[chan] = (0.5 * state + 0.125 * stencil_sum(state))[EDGE : EDGE + rows, :width]
+        done = 0.5 * state + 0.125 * stencil_sum(state)
+        out_ref[:, chan * width : (chan + 1) * width] = done[EDGE : EDGE + rows, :width]
 
 
 def diffuse_kernel(sizes, x_ref, dtall_ref, dside_ref, out_ref, *scratch):
@@ -191,7 +192,7 @@
     return pl.pallas_call(
         functools.partial(smooth_kernel, sizes),
         out_shape=(
-            jax.ShapeDtypeStruct((chans, rows, width), jnp.float32),
+            jax.ShapeDtypeStruct((rows, chans * width), jnp.float32),
             jax.ShapeDtypeStruct((total - chans, rows_padded, width), jnp.float32),
             jax.ShapeDtypeStruct((total - chans, rows_padded, width), jnp.float32),
         ),
@@ -273,8 +274,8 @@
         jnp.arange(row_count, dtype=jnp.int32)[:, None] == in_labels[None, :]
     ).astype(jnp.float32)
     pick_rows = row_pick.T
-    air = [jnp.dot(pick_rows, smoothed[c], precision=HIGHEST, preferred_element_type=jnp.float32)
-           for c in range(chan_count)]
+    air_all = jnp.dot(pick_rows, smoothed, precision=HIGHEST, preferred_element_type=jnp.float32)
+    air = [air_all[:, c * seg_width : (c + 1) * seg_width] for c in range(chan_count)]
     ocean = [incoming[:, c * seg_width : (c + 1) * seg_width] for c in range(chan_count)]
     in_weight = incoming[:, plane : plane + seg_width]
     wind_east = air[1] - ocean[1]
@@ -291,9 +292,10 @@
         jnp.concatenate(weighted, axis=1), ("atm", "ocn"), split_axis=0, concat_axis=0, tiled=True
     )
     signs = (1.0, -1.0, -1.0)
+    sent = jnp.concatenate(weighted, axis=1)
+    air_sum = jnp.dot(row_pick, sent, precision=HIGHEST, preferred_element_type=jnp.float32)
     forced = jnp.stack(
-        [atm_planes[c] + signs[c] * jnp.dot(row_pick, weighted[c], precision=HIGHEST,
-                                             preferred_element_type=jnp.float32)
+        [atm_planes[c] + signs[c] * air_sum[:, c * seg_width : (c + 1) * seg_width]
          for c in range(chan_count)]
     )
     current = diffuse_call(sizes, forced, dtall, dside)

time: 119 us -> 118 us (level)
  matrix products: 18.3 us -> 14.1 us
  Pallas kernels: 59.6 us -> 61.7 us
  other arithmetic: 10.1 us -> 12 us
    dot_general x6 -> x2, matrix products: 12.6 us -> 8.37 us  [the longest x1 4.27 us: per_device(): jnp.dot(row_pick, sent, precision=HIGHEST, preferred_element_type=jnp.flo...]
    pallas_call x1, Pallas kernels: 22.3 us -> 24.4 us  [diffuse_call(): pl.pallas_call(functools.partial(diffuse_kernel, sizes), out_shape=jax.Sh...]
    unnamed x38 -> x32, local copies, waits for them, and re-layouts: 6.02 us -> 5.29 us
  transfers between devices with their start and end apart: 2 -> 2, of which waited for: 0 -> 0; matrix products, arithmetic and copies ran while one was open for 9% -> 7% of each run, Pallas kernels for 50% -> 53%
where the time goes in v13:
time: 118 us; the launch traced here: 117 us
  Pallas kernels  61.7 us (52%)
  starting transfers between devices  16.9 us (14%)
  matrix products  14.1 us (12%)
  other arithmetic  12 us (10%)
  local copies, waits for them, and re-layouts  11.4 us (10%)
    pallas_call x1, Pallas kernels, smooth_call(): pl.pallas_call(functools.partial(smooth_kernel, sizes), out_shape=(jax.Sh...  37.3 us
    pallas_call x1, Pallas kernels, diffuse_call(): pl.pallas_call(functools.partial(diffuse_kernel, sizes), out_shape=jax.Sh...  24.4 us
    all_to_all x1, starting transfers between devices, per_device(): lax.all_to_all(outgoing, ('atm', 'ocn'), split_axis=0, concat_axis=0, til...  11.9 us
    unnamed x32, local copies, waits for them, and re-layouts  5.29 us
    all_to_all x1, starting transfers between devices, per_device(): lax.all_to_all(jnp.concatenate(weighted, axis=1), ('atm', 'ocn'), split_a...  5.03 us
    dot_general x1, matrix products, per_device(): jnp.dot(row_pick, sent, precision=HIGHEST, preferred_element_type=jnp.flo...  4.27 us
    dot_general x1, matrix products, per_device(): jnp.dot(pick_rows, smoothed, precision=HIGHEST, preferred_element_type=jn...  4.1 us
    concatenate x1, local copies, waits for them, and re-layouts, per_device(): outgoing = jnp.concatenate([out_ocean, out_weight, out_label], axis=1)  3.24 us
  transfers between devices with their start and end apart: 2, of which 0 were waited for; matrix products, arithmetic and copies ran while one was open for 7% of the time, Pallas kernels for 53%

profile of v13, /device:TPU:1, one launch (start us, length us, event | category | flops | bytes accessed | tf_op | source)
XLA Modules:
  0.0 117.1 jit_solution(3319156004110489287)
XLA Ops:
  0.7 0.8 fusion.29
  1.4 0.8 copy.12
  2.2 0.2 fusion.25
  2.5 0.9 fusion.23
  3.7 1.3 %fusion.3 = f32[1024,128]{0,1:T(8,128)S(1)} fusion(f32[512,128]{1,0:T(8,128)S(1)} %copy-done, s32[512]{0:T(512)S(1)} %multiply_add_fusion.1), kind=kOutput, calls=%fused_computation.11 | convolution fusion | flops 805830656 | bytes 788480 | tf_op jit(solution)/shard_map/dot_general | solution.py:65
  5.2 0.6 fusion.2
  5.9 0.6 fusion.4
  6.5 1.5 %fusion.37 = f32[1024,384]{0,1:T(8,128)S(1)} fusion(f32[1024,256]{1,0:T(8,128)S(1)} %fusion.4, f32[256,384]{0,1:T(8,128)S(1)} %bitcast.56), kind=kOutput, calls=%fused_computation.81 | convolution fusion | flops 1207959552 | bytes 3014656 | tf_op jit(solution)/shard_map/dot_general | solution.py:65
  8.0 0.3 convolution_multiply_fusion
  8.3 1.9 %pad_maximum_fusion.1 = f32[1024,640]{0,1:T(8,128)} fusion(f32[1024,128]{0,1:T(8,128)S(1)} %slice_add_fusion, f32[1024,128]{0,1:T(8,128)S(1)} %convolution_multiply_fusion, f32[1024,384]{0,1:T(8,128)S(1)} %fusion.37), kind=kLoop, calls=%fused_computation.4 | loop fusion | flops 1310720 | bytes 5242880 | tf_op jit(solution)/shard_map/concatenate | solution.py:263
  10.2 3.2 %copy.15 = f32[1024,640]{1,0:T(8,128)} copy(f32[1024,640]{0,1:T(8,128)} %pad_maximum_fusion.1) | data formatting | bytes 5242880 | tf_op jit(solution)/shard_map/concatenate | solution.py:263
  13.4 11.9 %all-to-all-start = ((f32[128,8,640]{2,1,0:T(8,128)}), f32[128,8,640]{2,1,0:T(8,128)}, u32[]{:S(2)}, u32[]{:S(2)}) async-start(f32[128,8,640]{2,1,0:T(8,128)} %bitcast.50), calls=%async_computation | async-start | bytes 5242880 | tf_op jit(solution)/shard_map/all_to_all | solution.py:264
  25.4 3.0 %pad_maximum_fusion.x_ref = f32[6,864,128]{2,1,0:T(8,128)} fusion(f32[3,864,128]{2,1,0:T(8,128)} %bitcast.57, f32[3,864,128]{2,1,0:T(8,128)S(1)} %bitcast.52), kind=kLoop, calls=%fused_computation.3 | loop fusion | flops 663552 | bytes 5308416 | tf_op jit(solution)/shard_map/concatenate | solution.py:267
  28.4 37.3 %shard_map.95 = (f32[864,384]{1,0:T(8,128)}, f32[3,896,128]{2,1,0:T(8,128)}, f32[3,896,128]{2,1,0:T(8,128)}) custom-call(f32[6,864,128]{2,1,0:T(8,128)} %pad_maximum_fusion.x_ref), custom_call_target="tpu_custom_call" | custom-call | tf_op jit(solution)/shard_map/pallas_call | solution.py:192
  65.7 2.8 %fusion.36 = (f32[1024,128]{1,0:T(8,128)S(1)}, f32[1024,128]{1,0:T(8,128)S(1)}, f32[1024,128]{1,0:T(8,128)S(1)}, f32[1024,128]{1,0:T(8,128)}, f32[1024]{0:T(1024)S(1)}) fusion(f32[1024,640]{1,0:T(8,128)} %bitcast.9), kind=kLoop, calls=%fused_computation.80 | loop fusion | flops 130048 | bytes 4722688 | tf_op jit(solution)/shard_map/slice | solution.py:279
  69.1 1.2 %copy.26 = f32[1024,128]{0,1:T(8,128)S(1)} copy(f32[1024,128]{1,0:T(8,128)} %get-tuple-element.26) | data formatting | bytes 1048576
  70.3 4.1 %fusion.1 = f32[1024,384]{0,1:T(8,128)S(1)} fusion(f32[864,384]{1,0:T(8,128)} %get-tuple-element.7, s32[1024]{0:T(1024)S(1)} %convert_element_type.45), kind=kOutput, calls=%fused_computation.2 | convolution fusion | flops 4077748224 | bytes 2904064 | tf_op jit(solution)/shard_map/dot_general | solution.py:277
  74.4 0.4 multiply_multiply_fusion.3
  74.9 0.5 multiply_multiply_fusion.1
  75.4 0.2 copy-done.4
  75.7 0.5 copy-done.6
  76.5 1.6 %copy.20 = f32[1024,384]{1,0:T(8,128)} copy(f32[1024,384]{0,1:T(8,128)S(1)} %pad_maximum_fusion.2) | data formatting | bytes 3145728 | tf_op jit(solution)/shard_map/concatenate | solution.py:295
  78.1 5.0 %all-to-all-start.1 = ((f32[128,8,384]{2,1,0:T(8,128)}), f32[128,8,384]{2,1,0:T(8,128)S(1)}, u32[]{:S(2)}, u32[]{:S(2)}) async-start(f32[128,8,384]{2,1,0:T(8,128)} %bitcast.51), calls=%async_computation.1 | async-start | bytes 3145728 | tf_op jit(solution)/shard_map/all_to_all | solution.py:291
  83.2 4.3 %fusion = f32[864,384]{1,0:T(8,128)S(1)} fusion(s32[1024]{0:T(1024)S(1)} %convert_element_type.45, f32[1024,128]{0,1:T(8,128)} %copy-done.7, f32[1024,128]{0,1:T(8,128)} %copy-done.6, f32[1024,128]{0,1:T(8,128)S(1)} %copy-done.5), kind=kOutput, calls=%fused_computation.1 | convolution fusion | flops 4078534656 | bytes 2904064 | tf_op jit(solution)/shard_map/dot_general | solution.py:296
  87.6 1.1 pad_maximum_fusion.3.x_ref
  88.7 24.4 %shard_map.96 = f32[3,864,128]{2,1,0:T(8,128)} custom-call(f32[3,864,128]{2,1,0:T(8,128)} %pad_maximum_fusion.3.x_ref, f32[3,896,128]{2,1,0:T(8,128)} %get-tuple-element.8.dtall_ref, f32[3,896,128]{2,1,0:T(8,128)} %get-tuple-element.9.dside_ref), custom_call_target="tpu_custom_call" | custom-call | tf_op jit(solution)/shard_map/pallas_call | solution.py:210
  113.2 0.5 fusion.13
  113.7 0.5 convolution_add_fusion.1
  114.2 0.5 convolution_add_fusion
  114.8 0.9 copy.22
  115.8 0.3 copy-done.3
  116.1 1.1 copy.28
  (41 shorter events, 1.8 us)
Async XLA Ops:
  0.6 3.0 %copy-start = (f32[512,128]{1,0:T(8,128)S(1)}, f32[512,128]{1,0:T(8,128)}, u32[]{:S(2)}) copy-start(f32[512,128]{1,0:T(8,128)} %param.12) | copy-start | bytes 786436
  0.6 2.8 %copy-start.10 = (s32[512,1]{0,1:T(1,128)S(1)}, s32[512,1]{0,1:T(1,128)}, u32[]{:S(2)}) copy-start(s32[512,1]{0,1:T(1,128)} %param.14) | copy-start | bytes 6148
  0.7 2.8 %copy-start.8 = (f32[256,3,128]{2,0,1:T(8,128)S(1)}, f32[256,3,128]{2,0,1:T(8,128)}, u32[]{:S(2)}) copy-start(f32[256,3,128]{2,0,1:T(8,128)} %param.10) | copy-start | bytes 1179652
  5.2 0.7 copy-start.11
  6.5 1.5 %copy-start.9 = (s32[256,128]{1,0:T(8,128)S(1)}, s32[256,128]{1,0:T(8,128)}, u32[]{:S(2)}) copy-start(s32[256,128]{1,0:T(8,128)} %param.11) | copy-start | bytes 393220
  13.4 11.9 %copy-start.1 = (f32[864,3,128]{2,0,1:T(8,128)S(1)}, f32[864,3,128]{2,0,1:T(8,128)}, u32[]{:S(2)}) copy-start(f32[864,3,128]{2,0,1:T(8,128)} %param.8) | copy-start | bytes 3981316
  13.4 52.2 %all-to-all-start = ((f32[128,8,640]{2,1,0:T(8,128)}), f32[128,8,640]{2,1,0:T(8,128)}, u32[]{:S(2)}, u32[]{:S(2)}) async-start(f32[128,8,640]{2,1,0:T(8,128)} %bitcast.50), calls=%async_computation | async-start | bytes 5242880 | tf_op jit(solution)/shard_map/all_to_all | solution.py:264
  74.9 0.8 copy-start.4
  75.4 0.8 copy-start.6
  75.4 1.0 copy-start.7
  78.1 5.0 %copy-start.5 = (f32[1024,128]{0,1:T(8,128)S(1)}, f32[1024,128]{0,1:T(8,128)}, u32[]{:S(2)}) copy-start(f32[1024,128]{0,1:T(8,128)} %copy-done.4) | copy-start | bytes 1572868
  78.1 35.1 %all-to-all-start.1 = ((f32[128,8,384]{2,1,0:T(8,128)}), f32[128,8,384]{2,1,0:T(8,128)S(1)}, u32[]{:S(2)}, u32[]{:S(2)}) async-start(f32[128,8,384]{2,1,0:T(8,128)} %bitcast.51), calls=%async_computation.1 | async-start | bytes 3145728 | tf_op jit(solution)/shard_map/all_to_all | solution.py:291
  83.2 4.3 %copy-start.2 = (f32[864,3,128]{2,0,1:T(8,128)S(1)}, f32[864,3,128]{2,0,1:T(8,128)}, u32[]{:S(2)}) copy-start(f32[864,3,128]{2,0,1:T(8,128)} %param.8) | copy-start | bytes 3981316
  114.7 1.4 %copy-start.3 = (f32[3,864,128]{2,1,0:T(8,128)S(1)}, f32[3,864,128]{2,1,0:T(8,128)}, u32[]{:S(2)}) copy-start(f32[3,864,128]{2,1,0:T(8,128)} %shard_map.96) | copy-start | bytes 3981316

commit v14 on v13

--- a/solution.py
+++ b/solution.py
@@ -181,8 +181,9 @@
     for chan in range(out_ref.shape[0]):
         state = jnp.concatenate([tall_s[chan], side_s[chan]], axis=1)
         diff = jnp.concatenate([dtall_ref[first + chan], dside_ref[first + chan]], axis=1)
+        keep = 1.0 - 4.0 * diff
         for iteration in range(ITERS):
-            state = state + diff * (stencil_sum(state) - 4.0 * state)
+            state = state * keep + diff * stencil_sum(state)
         out_ref[chan] = state[EDGE : EDGE + rows, :width]
 
 

time: 118 us -> 118 us (level)
  no operation moved by 1% of the time
where the time goes in v14:
time: 118 us; the launch traced here: 117 us
  Pallas kernels  61.9 us (52%)
  starting transfers between devices  16.9 us (14%)
  matrix products  14.1 us (12%)
  other arithmetic  12 us (10%)
  local copies, waits for them, and re-layouts  11.4 us (10%)
    pallas_call x1, Pallas kernels, smooth_call(): pl.pallas_call(functools.partial(smooth_kernel, sizes), out_shape=(jax.Sh...  37.3 us
    pallas_call x1, Pallas kernels, diffuse_call(): pl.pallas_call(functools.partial(diffuse_kernel, sizes), out_shape=jax.Sh...  24.7 us
    all_to_all x1, starting transfers between devices, per_device(): lax.all_to_all(outgoing, ('atm', 'ocn'), split_axis=0, concat_axis=0, til...  11.9 us
    unnamed x32, local copies, waits for them, and re-layouts  5.29 us
    all_to_all x1, starting transfers between devices, per_device(): lax.all_to_all(jnp.concatenate(weighted, axis=1), ('atm', 'ocn'), split_a...  5.03 us
    dot_general x1, matrix products, per_device(): jnp.dot(row_pick, sent, precision=HIGHEST, preferred_element_type=jnp.flo...  4.27 us
    dot_general x1, matrix products, per_device(): jnp.dot(pick_rows, smoothed, precision=HIGHEST, preferred_element_type=jn...  4.1 us
    concatenate x1, local copies, waits for them, and re-layouts, per_device(): outgoing = jnp.concatenate([out_ocean, out_weight, out_label], axis=1)  3.24 us
  transfers between devices with their start and end apart: 2, of which 0 were waited for; matrix products, arithmetic and copies ran while one was open for 7% of the time, Pallas kernels for 53%

profile of v14, /device:TPU:1, one launch (start us, length us, event | category | flops | bytes accessed | tf_op | source)
XLA Modules:
  0.0 117.4 jit_solution(15231851944308772749)
XLA Ops:
  0.7 0.8 fusion.29
  1.4 0.8 copy.12
  2.2 0.2 fusion.25
  2.5 0.9 fusion.23
  3.7 1.3 %fusion.3 = f32[1024,128]{0,1:T(8,128)S(1)} fusion(f32[512,128]{1,0:T(8,128)S(1)} %copy-done, s32[512]{0:T(512)S(1)} %multiply_add_fusion.1), kind=kOutput, calls=%fused_computation.11 | convolution fusion | flops 805830656 | bytes 788480 | tf_op jit(solution)/shard_map/dot_general | solution.py:65
  5.2 0.6 fusion.2
  5.9 0.6 fusion.4
  6.5 1.5 %fusion.37 = f32[1024,384]{0,1:T(8,128)S(1)} fusion(f32[1024,256]{1,0:T(8,128)S(1)} %fusion.4, f32[256,384]{0,1:T(8,128)S(1)} %bitcast.56), kind=kOutput, calls=%fused_computation.81 | convolution fusion | flops 1207959552 | bytes 3014656 | tf_op jit(solution)/shard_map/dot_general | solution.py:65
  8.0 0.3 convolution_multiply_fusion
  8.3 1.9 %pad_maximum_fusion.1 = f32[1024,640]{0,1:T(8,128)} fusion(f32[1024,128]{0,1:T(8,128)S(1)} %slice_add_fusion, f32[1024,128]{0,1:T(8,128)S(1)} %convolution_multiply_fusion, f32[1024,384]{0,1:T(8,128)S(1)} %fusion.37), kind=kLoop, calls=%fused_computation.4 | loop fusion | flops 1310720 | bytes 5242880 | tf_op jit(solution)/shard_map/concatenate | solution.py:264
  10.2 3.2 %copy.15 = f32[1024,640]{1,0:T(8,128)} copy(f32[1024,640]{0,1:T(8,128)} %pad_maximum_fusion.1) | data formatting | bytes 5242880 | tf_op jit(solution)/shard_map/concatenate | solution.py:264
  13.4 11.9 %all-to-all-start = ((f32[128,8,640]{2,1,0:T(8,128)}), f32[128,8,640]{2,1,0:T(8,128)}, u32[]{:S(2)}, u32[]{:S(2)}) async-start(f32[128,8,640]{2,1,0:T(8,128)} %bitcast.50), calls=%async_computation | async-start | bytes 5242880 | tf_op jit(solution)/shard_map/all_to_all | solution.py:265
  25.4 3.0 %pad_maximum_fusion.x_ref = f32[6,864,128]{2,1,0:T(8,128)} fusion(f32[3,864,128]{2,1,0:T(8,128)} %bitcast.57, f32[3,864,128]{2,1,0:T(8,128)S(1)} %bitcast.52), kind=kLoop, calls=%fused_computation.3 | loop fusion | flops 663552 | bytes 5308416 | tf_op jit(solution)/shard_map/concatenate | solution.py:268
  28.4 37.3 %shard_map.95 = (f32[864,384]{1,0:T(8,128)}, f32[3,896,128]{2,1,0:T(8,128)}, f32[3,896,128]{2,1,0:T(8,128)}) custom-call(f32[6,864,128]{2,1,0:T(8,128)} %pad_maximum_fusion.x_ref), custom_call_target="tpu_custom_call" | custom-call | tf_op jit(solution)/shard_map/pallas_call | solution.py:193
  65.7 2.8 %fusion.36 = (f32[1024,128]{1,0:T(8,128)S(1)}, f32[1024,128]{1,0:T(8,128)S(1)}, f32[1024,128]{1,0:T(8,128)S(1)}, f32[1024,128]{1,0:T(8,128)}, f32[1024]{0:T(1024)S(1)}) fusion(f32[1024,640]{1,0:T(8,128)} %bitcast.9), kind=kLoop, calls=%fused_computation.80 | loop fusion | flops 130048 | bytes 4722688 | tf_op jit(solution)/shard_map/slice | solution.py:280
  69.1 1.2 %copy.26 = f32[1024,128]{0,1:T(8,128)S(1)} copy(f32[1024,128]{1,0:T(8,128)} %get-tuple-element.26) | data formatting | bytes 1048576
  70.3 4.1 %fusion.1 = f32[1024,384]{0,1:T(8,128)S(1)} fusion(f32[864,384]{1,0:T(8,128)} %get-tuple-element.7, s32[1024]{0:T(1024)S(1)} %convert_element_type.45), kind=kOutput, calls=%fused_computation.2 | convolution fusion | flops 4077748224 | bytes 2904064 | tf_op jit(solution)/shard_map/dot_general | solution.py:278
  74.4 0.4 multiply_multiply_fusion.3
  74.9 0.5 multiply_multiply_fusion.1
  75.4 0.2 copy-done.4
  75.7 0.5 copy-done.6
  76.5 1.6 %copy.20 = f32[1024,384]{1,0:T(8,128)} copy(f32[1024,384]{0,1:T(8,128)S(1)} %pad_maximum_fusion.2) | data formatting | bytes 3145728 | tf_op jit(solution)/shard_map/concatenate | solution.py:296
  78.1 5.0 %all-to-all-start.1 = ((f32[128,8,384]{2,1,0:T(8,128)}), f32[128,8,384]{2,1,0:T(8,128)S(1)}, u32[]{:S(2)}, u32[]{:S(2)}) async-start(f32[128,8,384]{2,1,0:T(8,128)} %bitcast.51), calls=%async_computation.1 | async-start | bytes 3145728 | tf_op jit(solution)/shard_map/all_to_all | solution.py:292
  83.2 4.3 %fusion = f32[864,384]{1,0:T(8,128)S(1)} fusion(s32[1024]{0:T(1024)S(1)} %convert_element_type.45, f32[1024,128]{0,1:T(8,128)} %copy-done.7, f32[1024,128]{0,1:T(8,128)} %copy-done.6, f32[1024,128]{0,1:T(8,128)S(1)} %copy-done.5), kind=kOutput, calls=%fused_computation.1 | convolution fusion | flops 4078534656 | bytes 2904064 | tf_op jit(solution)/shard_map/dot_general | solution.py:297
  87.6 1.1 pad_maximum_fusion.3.x_ref
  88.7 24.7 %shard_map.96 = f32[3,864,128]{2,1,0:T(8,128)} custom-call(f32[3,864,128]{2,1,0:T(8,128)} %pad_maximum_fusion.3.x_ref, f32[3,896,128]{2,1,0:T(8,128)} %get-tuple-element.8.dtall_ref, f32[3,896,128]{2,1,0:T(8,128)} %get-tuple-element.9.dside_ref), custom_call_target="tpu_custom_call" | custom-call | tf_op jit(solution)/shard_map/pallas_call | solution.py:211
  113.4 0.5 fusion.13
  113.9 0.5 convolution_add_fusion.1
  114.4 0.5 convolution_add_fusion
  115.1 0.9 copy.22
  116.0 0.3 copy-done.3
  116.3 1.1 copy.28
  (41 shorter events, 1.8 us)
Async XLA Ops:
  0.6 3.0 %copy-start = (f32[512,128]{1,0:T(8,128)S(1)}, f32[512,128]{1,0:T(8,128)}, u32[]{:S(2)}) copy-start(f32[512,128]{1,0:T(8,128)} %param.12) | copy-start | bytes 786436
  0.6 2.8 %copy-start.10 = (s32[512,1]{0,1:T(1,128)S(1)}, s32[512,1]{0,1:T(1,128)}, u32[]{:S(2)}) copy-start(s32[512,1]{0,1:T(1,128)} %param.14) | copy-start | bytes 6148
  0.7 2.8 %copy-start.8 = (f32[256,3,128]{2,0,1:T(8,128)S(1)}, f32[256,3,128]{2,0,1:T(8,128)}, u32[]{:S(2)}) copy-start(f32[256,3,128]{2,0,1:T(8,128)} %param.10) | copy-start | bytes 1179652
  5.2 0.7 copy-start.11
  6.5 1.5 %copy-start.9 = (s32[256,128]{1,0:T(8,128)S(1)}, s32[256,128]{1,0:T(8,128)}, u32[]{:S(2)}) copy-start(s32[256,128]{1,0:T(8,128)} %param.11) | copy-start | bytes 393220
  13.4 11.9 %copy-start.1 = (f32[864,3,128]{2,0,1:T(8,128)S(1)}, f32[864,3,128]{2,0,1:T(8,128)}, u32[]{:S(2)}) copy-start(f32[864,3,128]{2,0,1:T(8,128)} %param.8) | copy-start | bytes 3981316
  13.4 52.2 %all-to-all-start = ((f32[128,8,640]{2,1,0:T(8,128)}), f32[128,8,640]{2,1,0:T(8,128)}, u32[]{:S(2)}, u32[]{:S(2)}) async-start(f32[128,8,640]{2,1,0:T(8,128)} %bitcast.50), calls=%async_computation | async-start | bytes 5242880 | tf_op jit(solution)/shard_map/all_to_all | solution.py:265
  74.9 0.8 copy-start.4
  75.4 0.8 copy-start.6
  75.4 1.0 copy-start.7
  78.1 5.0 %copy-start.5 = (f32[1024,128]{0,1:T(8,128)S(1)}, f32[1024,128]{0,1:T(8,128)}, u32[]{:S(2)}) copy-start(f32[1024,128]{0,1:T(8,128)} %copy-done.4) | copy-start | bytes 1572868
  78.1 35.3 %all-to-all-start.1 = ((f32[128,8,384]{2,1,0:T(8,128)}), f32[128,8,384]{2,1,0:T(8,128)S(1)}, u32[]{:S(2)}, u32[]{:S(2)}) async-start(f32[128,8,384]{2,1,0:T(8,128)} %bitcast.51), calls=%async_computation.1 | async-start | bytes 3145728 | tf_op jit(solution)/shard_map/all_to_all | solution.py:292
  83.2 4.3 %copy-start.2 = (f32[864,3,128]{2,0,1:T(8,128)S(1)}, f32[864,3,128]{2,0,1:T(8,128)}, u32[]{:S(2)}) copy-start(f32[864,3,128]{2,0,1:T(8,128)} %param.8) | copy-start | bytes 3981316
  114.9 1.4 %copy-start.3 = (f32[3,864,128]{2,1,0:T(8,128)S(1)}, f32[3,864,128]{2,1,0:T(8,128)}, u32[]{:S(2)}) copy-start(f32[3,864,128]{2,1,0:T(8,128)} %shard_map.96) | copy-start | bytes 3981316

commit v15 on v13

--- a/solution.py
+++ b/solution.py
@@ -173,14 +173,18 @@
         out_ref[:, chan * width : (chan + 1) * width] = done[EDGE : EDGE + rows, :width]
 
 
-def diffuse_kernel(sizes, x_ref, dtall_ref, dside_ref, out_ref, *scratch):
+SIGNS = (1.0, -1.0, -1.0)
+
+
+def diffuse_kernel(sizes, both_ref, sum_ref, dtall_ref, dside_ref, out_ref, forced_s, *scratch):
     rows_buf, cols_buf, colsend, tall_s, side_s, send_sem, recv_sem = scratch
-    exchange(sizes, x_ref, rows_buf, cols_buf, colsend, tall_s, side_s, send_sem, recv_sem)
     rows, width = out_ref.shape[1], out_ref.shape[2]
-    first = dtall_ref.shape[0] - out_ref.shape[0]
+    for chan in range(out_ref.shape[0]):
+        forced_s[chan] = both_ref[chan] + SIGNS[chan] * sum_ref[:, chan * width : (chan + 1) * width]
+    exchange(sizes, forced_s, rows_buf, cols_buf, colsend, tall_s, side_s, send_sem, recv_sem)
     for chan in range(out_ref.shape[0]):
         state = jnp.concatenate([tall_s[chan], side_s[chan]], axis=1)
-        diff = jnp.concatenate([dtall_ref[first + chan], dside_ref[first + chan]], axis=1)
+        diff = jnp.concatenate([dtall_ref[chan], dside_ref[chan]], axis=1)
         for iteration in range(ITERS):
             state = state + diff * (stencil_sum(state) - 4.0 * state)
         out_ref[chan] = state[EDGE : EDGE + rows, :width]
@@ -203,18 +207,19 @@
     )(both)
 
 
-def diffuse_call(sizes, forced, dtall, dside):
-    chans, rows, width = forced.shape
-    rows_padded = dtall.shape[1]
+def diffuse_call(sizes, both, air_sum, dtall, dside):
+    chans, rows_padded, width = dtall.shape
+    rows = both.shape[1]
     vmem = pl.BlockSpec(memory_space=pltpu.VMEM)
     return pl.pallas_call(
         functools.partial(diffuse_kernel, sizes),
         out_shape=jax.ShapeDtypeStruct((chans, rows, width), jnp.float32),
-        in_specs=[vmem] * 3,
+        in_specs=[vmem] * 4,
         out_specs=vmem,
-        scratch_shapes=exchange_scratch(chans, rows_padded, width),
+        scratch_shapes=[pltpu.VMEM((chans, rows, width), jnp.float32)]
+        + exchange_scratch(chans, rows_padded, width),
         compiler_params=pltpu.CompilerParams(collective_id=1, has_side_effects=True),
-    )(forced, dtall, dside)
+    )(both, air_sum, dtall, dside)
 
 
 def per_device(
@@ -291,14 +296,9 @@
     returned = lax.all_to_all(
         jnp.concatenate(weighted, axis=1), ("atm", "ocn"), split_axis=0, concat_axis=0, tiled=True
     )
-    signs = (1.0, -1.0, -1.0)
     sent = jnp.concatenate(weighted, axis=1)
     air_sum = jnp.dot(row_pick, sent, precision=HIGHEST, preferred_element_type=jnp.float32)
-    forced = jnp.stack(
-        [atm_planes[c] + signs[c] * air_sum[:, c * seg_width : (c + 1) * seg_width]
-         for c in range(chan_count)]
-    )
-    current = diffuse_call(sizes, forced, dtall, dside)
+    current = diffuse_call(sizes, both, air_sum, dtall, dside)
     current, returned = lax.optimization_barrier((current, returned))
     seg_of_slot = slot_seg.T.astype(jnp.bfloat16)
     ocean_flux = pick_dot(seg_of_slot, returned).reshape(seg_count, chan_count, seg_width)

time: 118 us -> 118 us (level)
  other arithmetic: 12 us -> 10.7 us
    another operation x5 -> x3, other arithmetic: 1.54 us -> 0.26 us  [the longest x2 1.28 us: per_device(): jnp.stack([atm_planes[c] + signs[c] * air_sum[:, c * seg_width:(c + 1) *...]
    unnamed x32 -> x30, local copies, waits for them, and re-layouts: 5.29 us -> 5.3 us
where the time goes in v15:
time: 118 us; the launch traced here: 117 us
  Pallas kernels  62.1 us (53%)
  starting transfers between devices  16.9 us (14%)
  matrix products  15 us (13%)
  local copies, waits for them, and re-layouts  11.4 us (10%)
  other arithmetic  10.7 us (9%)
    pallas_call x1, Pallas kernels, smooth_call(): pl.pallas_call(functools.partial(smooth_kernel, sizes), out_shape=(jax.Sh...  37.2 us
    pallas_call x1, Pallas kernels, diffuse_call(): pl.pallas_call(functools.partial(diffuse_kernel, sizes), out_shape=jax.Sh...  24.9 us
    all_to_all x1, starting transfers between devices, per_device(): lax.all_to_all(outgoing, ('atm', 'ocn'), split_axis=0, concat_axis=0, til...  11.9 us
    unnamed x30, local copies, waits for them, and re-layouts  5.3 us
    dot_general x1, matrix products, per_device(): jnp.dot(row_pick, sent, precision=HIGHEST, preferred_element_type=jnp.flo...  5.21 us
    all_to_all x1, starting transfers between devices, per_device(): lax.all_to_all(jnp.concatenate(weighted, axis=1), ('atm', 'ocn'), split_a...  5.03 us
    dot_general x1, matrix products, per_device(): jnp.dot(pick_rows, smoothed, precision=HIGHEST, preferred_element_type=jn...  4.1 us
    concatenate x1, local copies, waits for them, and re-layouts, per_device(): outgoing = jnp.concatenate([out_ocean, out_weight, out_label], axis=1)  3.23 us
  transfers between devices with their start and end apart: 2, of which 0 were waited for; matrix products, arithmetic and copies ran while one was open for 7% of the time, Pallas kernels for 53%

profile of v15, /device:TPU:1, one launch (start us, length us, event | category | flops | bytes accessed | tf_op | source)
XLA Modules:
  0.0 117.2 jit_solution(2958238653364340368)
XLA Ops:
  0.7 0.8 fusion.24
  1.4 0.8 copy.12
  2.2 0.2 fusion.20
  2.5 0.9 fusion.18
  3.7 1.3 %fusion.3 = f32[1024,128]{0,1:T(8,128)S(1)} fusion(f32[512,128]{1,0:T(8,128)S(1)} %copy-done, s32[512]{0:T(512)S(1)} %multiply_add_fusion.1), kind=kOutput, calls=%fused_computation.11 | convolution fusion | flops 805830656 | bytes 788480 | tf_op jit(solution)/shard_map/dot_general | solution.py:65
  5.2 0.6 fusion.2
  5.9 0.6 fusion.4
  6.5 1.5 %fusion.32 = f32[1024,384]{0,1:T(8,128)S(1)} fusion(f32[1024,256]{1,0:T(8,128)S(1)} %fusion.4, f32[256,384]{0,1:T(8,128)S(1)} %bitcast.36), kind=kOutput, calls=%fused_computation.69 | convolution fusion | flops 1207959552 | bytes 3014656 | tf_op jit(solution)/shard_map/dot_general | solution.py:65
  8.0 0.3 convolution_multiply_fusion
  8.3 1.8 %pad_maximum_fusion.1 = f32[1024,640]{0,1:T(8,128)} fusion(f32[1024,128]{0,1:T(8,128)S(1)} %slice_add_fusion, f32[1024,128]{0,1:T(8,128)S(1)} %convolution_multiply_fusion, f32[1024,384]{0,1:T(8,128)S(1)} %fusion.32), kind=kLoop, calls=%fused_computation.4 | loop fusion | flops 1310720 | bytes 5242880 | tf_op jit(solution)/shard_map/concatenate | solution.py:268
  10.2 3.2 %copy.15 = f32[1024,640]{1,0:T(8,128)} copy(f32[1024,640]{0,1:T(8,128)} %pad_maximum_fusion.1) | data formatting | bytes 5242880 | tf_op jit(solution)/shard_map/concatenate | solution.py:268
  13.4 11.9 %all-to-all-start = ((f32[128,8,640]{2,1,0:T(8,128)}), f32[128,8,640]{2,1,0:T(8,128)}, u32[]{:S(2)}, u32[]{:S(2)}) async-start(f32[128,8,640]{2,1,0:T(8,128)} %bitcast.32), calls=%async_computation | async-start | bytes 5242880 | tf_op jit(solution)/shard_map/all_to_all | solution.py:269
  25.4 3.0 %pad_maximum_fusion.x_ref.both_ref = f32[6,864,128]{2,1,0:T(8,128)} fusion(f32[3,864,128]{2,1,0:T(8,128)S(1)} %bitcast.37, f32[3,864,128]{2,1,0:T(8,128)} %bitcast.38), kind=kLoop, calls=%fused_computation.3 | loop fusion | flops 663552 | bytes 5308416 | tf_op jit(solution)/shard_map/concatenate | solution.py:272
  28.4 37.2 %shard_map.95 = (f32[864,384]{1,0:T(8,128)}, f32[3,896,128]{2,1,0:T(8,128)}, f32[3,896,128]{2,1,0:T(8,128)}) custom-call(f32[6,864,128]{2,1,0:T(8,128)} %pad_maximum_fusion.x_ref.both_ref), custom_call_target="tpu_custom_call" | custom-call | tf_op jit(solution)/shard_map/pallas_call | solution.py:196
  65.6 2.8 %fusion.31 = (f32[1024,128]{1,0:T(8,128)S(1)}, f32[1024,128]{1,0:T(8,128)S(1)}, f32[1024,128]{1,0:T(8,128)S(1)}, f32[1024,128]{1,0:T(8,128)}, f32[1024]{0:T(1024)S(1)}) fusion(f32[1024,640]{1,0:T(8,128)} %bitcast.9), kind=kLoop, calls=%fused_computation.68 | loop fusion | flops 130048 | bytes 4722688 | tf_op jit(solution)/shard_map/slice | solution.py:284
  68.6 0.2 copy.24
  69.0 1.2 %copy.26 = f32[1024,128]{0,1:T(8,128)S(1)} copy(f32[1024,128]{1,0:T(8,128)} %get-tuple-element.23) | data formatting | bytes 1048576
  70.3 4.1 %fusion.1 = f32[1024,384]{0,1:T(8,128)S(1)} fusion(f32[864,384]{1,0:T(8,128)} %get-tuple-element.7, s32[1024]{0:T(1024)S(1)} %convert_element_type.45), kind=kOutput, calls=%fused_computation.2 | convolution fusion | flops 4077748224 | bytes 2904064 | tf_op jit(solution)/shard_map/dot_general | solution.py:282
  74.4 0.4 multiply_multiply_fusion.3
  74.8 0.5 multiply_multiply_fusion.1
  75.4 0.2 copy-done.2
  75.6 0.6 copy-done.4
  76.5 1.6 %copy.20 = f32[1024,384]{1,0:T(8,128)} copy(f32[1024,384]{0,1:T(8,128)S(1)} %pad_maximum_fusion.2) | data formatting | bytes 3145728 | tf_op jit(solution)/shard_map/concatenate | solution.py:299
  78.1 5.0 %all-to-all-start.1 = ((f32[128,8,384]{2,1,0:T(8,128)}), f32[128,8,384]{2,1,0:T(8,128)S(1)}, u32[]{:S(2)}, u32[]{:S(2)}) async-start(f32[128,8,384]{2,1,0:T(8,128)} %bitcast.33), calls=%async_computation.1 | async-start | bytes 3145728 | tf_op jit(solution)/shard_map/all_to_all | solution.py:296
  83.2 5.2 %fusion.sum_ref = f32[864,384]{1,0:T(8,128)} fusion(s32[1024]{0:T(1024)S(1)} %convert_element_type.45, f32[1024,128]{0,1:T(8,128)} %copy-done.5, f32[1024,128]{0,1:T(8,128)} %copy-done.4, f32[1024,128]{0,1:T(8,128)S(1)} %copy-done.3), kind=kOutput, calls=%fused_computation.1 | convolution fusion | flops 4078534656 | bytes 2904064 | tf_op jit(solution)/shard_map/dot_general | solution.py:300
  88.4 24.9 %shard_map.96 = f32[3,864,128]{2,1,0:T(8,128)} custom-call(f32[6,864,128]{2,1,0:T(8,128)} %pad_maximum_fusion.x_ref.both_ref, f32[864,384]{1,0:T(8,128)} %fusion.sum_ref, f32[3,896,128]{2,1,0:T(8,128)} %get-tuple-element.8.dtall_ref, f32[3,896,128]{2,1,0:T(8,128)} %get-tuple-element.9.dside_ref), custom_call_target="tpu_custom_call" | custom-call | tf_op jit(solution)/shard_map/pallas_call | solution.py:214
  113.2 0.5 fusion.13
  113.7 0.5 convolution_add_fusion.1
  114.2 0.5 convolution_add_fusion
  114.9 0.9 copy.22
  115.8 0.3 copy-done.1
  116.1 1.1 copy.28
  (37 shorter events, 1.5 us)
Async XLA Ops:
  0.6 3.0 %copy-start = (f32[512,128]{1,0:T(8,128)S(1)}, f32[512,128]{1,0:T(8,128)}, u32[]{:S(2)}) copy-start(f32[512,128]{1,0:T(8,128)} %param.12) | copy-start | bytes 786436
  0.6 2.8 %copy-start.9 = (s32[512,1]{0,1:T(1,128)S(1)}, s32[512,1]{0,1:T(1,128)}, u32[]{:S(2)}) copy-start(s32[512,1]{0,1:T(1,128)} %param.14) | copy-start | bytes 6148
  0.7 2.8 %copy-start.7 = (f32[256,3,128]{2,0,1:T(8,128)S(1)}, f32[256,3,128]{2,0,1:T(8,128)}, u32[]{:S(2)}) copy-start(f32[256,3,128]{2,0,1:T(8,128)} %param.10) | copy-start | bytes 1179652
  5.2 0.7 copy-start.10
  6.5 1.5 %copy-start.8 = (s32[256,128]{1,0:T(8,128)S(1)}, s32[256,128]{1,0:T(8,128)}, u32[]{:S(2)}) copy-start(s32[256,128]{1,0:T(8,128)} %param.11) | copy-start | bytes 393220
  13.4 11.9 %copy-start.6 = (f32[864,3,128]{2,0,1:T(8,128)S(1)}, f32[864,3,128]{2,0,1:T(8,128)}, u32[]{:S(2)}) copy-start(f32[864,3,128]{2,0,1:T(8,128)} %param.9) | copy-start | bytes 3981316
  13.4 52.2 %all-to-all-start = ((f32[128,8,640]{2,1,0:T(8,128)}), f32[128,8,640]{2,1,0:T(8,128)}, u32[]{:S(2)}, u32[]{:S(2)}) async-start(f32[128,8,640]{2,1,0:T(8,128)} %bitcast.32), calls=%async_computation | async-start | bytes 5242880 | tf_op jit(solution)/shard_map/all_to_all | solution.py:269
  74.8 0.8 copy-start.2
  75.4 0.8 copy-start.4
  75.4 1.0 copy-start.5
  78.1 5.0 %copy-start.3 = (f32[1024,128]{0,1:T(8,128)S(1)}, f32[1024,128]{0,1:T(8,128)}, u32[]{:S(2)}) copy-start(f32[1024,128]{0,1:T(8,128)} %copy-done.2) | copy-start | bytes 1572868
  78.1 35.1 %all-to-all-start.1 = ((f32[128,8,384]{2,1,0:T(8,128)}), f32[128,8,384]{2,1,0:T(8,128)S(1)}, u32[]{:S(2)}, u32[]{:S(2)}) async-start(f32[128,8,384]{2,1,0:T(8,128)} %bitcast.33), calls=%async_computation.1 | async-start | bytes 3145728 | tf_op jit(solution)/shard_map/all_to_all | solution.py:296
  114.7 1.4 %copy-start.1 = (f32[3,864,128]{2,1,0:T(8,128)S(1)}, f32[3,864,128]{2,1,0:T(8,128)}, u32[]{:S(2)}) copy-start(f32[3,864,128]{2,1,0:T(8,128)} %shard_map.96) | copy-start | bytes 3981316

commit v16 on v15

--- a/solution.py
+++ b/solution.py
@@ -58,6 +58,18 @@
         term = jnp.dot(pick, part, preferred_element_type=jnp.float32)
         total = term if total is None else total + term
     return total
+
+
+def pick_wide(pick, values):
+    parts = []
+    rest = values
+    for part in range(3):
+        high = lax.reduce_precision(rest, exponent_bits=8, mantissa_bits=7)
+        parts.append(high.astype(jnp.bfloat16))
+        rest = rest - high
+    width = values.shape[1]
+    total = jnp.dot(pick, jnp.concatenate(parts, axis=1), preferred_element_type=jnp.float32)
+    return (total[:, :width] + total[:, width : 2 * width]) + total[:, 2 * width :]
 
 
 def select_rows(chosen, values, precision=HIGHEST):
@@ -279,7 +291,7 @@
         jnp.arange(row_count, dtype=jnp.int32)[:, None] == in_labels[None, :]
     ).astype(jnp.float32)
     pick_rows = row_pick.T
-    air_all = jnp.dot(pick_rows, smoothed, precision=HIGHEST, preferred_element_type=jnp.float32)
+    air_all = pick_wide(pick_rows.astype(jnp.bfloat16), smoothed)
     air = [air_all[:, c * seg_width : (c + 1) * seg_width] for c in range(chan_count)]
     ocean = [incoming[:, c * seg_width : (c + 1) * seg_width] for c in range(chan_count)]
     in_weight = incoming[:, plane : plane + seg_width]
@@ -297,7 +309,7 @@
         jnp.concatenate(weighted, axis=1), ("atm", "ocn"), split_axis=0, concat_axis=0, tiled=True
     )
     sent = jnp.concatenate(weighted, axis=1)
-    air_sum = jnp.dot(row_pick, sent, precision=HIGHEST, preferred_element_type=jnp.float32)
+    air_sum = pick_wide(row_pick.astype(jnp.bfloat16), sent)
     current = diffuse_call(sizes, both, air_sum, dtall, dside)
     current, returned = lax.optimization_barrier((current, returned))
     seg_of_slot = slot_seg.T.astype(jnp.bfloat16)

time: 118 us -> 118 us (level)
  other arithmetic: 10.7 us -> 17.5 us
  local copies, waits for them, and re-layouts: 11.4 us -> 6.97 us
  matrix products: 15 us -> 12.6 us
    unnamed x30 -> x18, local copies, waits for them, and re-layouts: 5.3 us -> 2.5 us
    slice x1 -> x0, other arithmetic: 2.76 us -> none  [per_device(): incoming[:, c * seg_width:(c + 1) * seg_width]]
    all_to_all x0 -> x1, other arithmetic: none -> 2.41 us  [per_device(): lax.all_to_all(jnp.concatenate(weighted, axis=1), ('atm', 'ocn'), split_a...]
    dot_general x2, matrix products: 9.32 us -> 6.93 us  [pick_wide(): jnp.dot(pick, jnp.concatenate(parts, axis=1), preferred_element_type=jnp....]
    convert_element_type x0 -> x1, other arithmetic: none -> 1.64 us  [pick_wide(): parts.append(high.astype(jnp.bfloat16))]
    concatenate x1 -> x0, local copies, waits for them, and re-layouts: 1.64 us -> none  [per_device(): sent = jnp.concatenate(weighted, axis=1)]
    mul x1, other arithmetic: 0.43 us -> 1.99 us  [per_device(): in_weight * (0.8 * factor * wind_speed * temp_gap)]
    add x0 -> x2, other arithmetic: none -> 1.44 us  [pick_wide(): return total[:, :width] + total[:, width:2 * width] + total[:, 2 * width:]]
  transfers between devices with their start and end apart: 2 -> 2, of which waited for: 0 -> 0; matrix products, arithmetic and copies ran while one was open for 7% -> 9% of each run, Pallas kernels for 53% -> 53%
where the time goes in v16:
time: 118 us; the launch traced here: 117 us
  Pallas kernels  62.1 us (53%)
  other arithmetic  17.5 us (15%)
  starting transfers between devices  16.9 us (14%)
  matrix products  12.6 us (11%)
  local copies, waits for them, and re-layouts  6.97 us (6%)
    pallas_call x1, Pallas kernels, smooth_call(): pl.pallas_call(functools.partial(smooth_kernel, sizes), out_shape=(jax.Sh...  37.3 us
    pallas_call x1, Pallas kernels, diffuse_call(): pl.pallas_call(functools.partial(diffuse_kernel, sizes), out_shape=jax.Sh...  24.8 us
    all_to_all x1, starting transfers between devices, per_device(): lax.all_to_all(outgoing, ('atm', 'ocn'), split_axis=0, concat_axis=0, til...  11.9 us
    dot_general x2, matrix products, pick_wide(): jnp.dot(pick, jnp.concatenate(parts, axis=1), preferred_element_type=jnp....  6.93 us
    all_to_all x1, starting transfers between devices, per_device(): lax.all_to_all(jnp.concatenate(weighted, axis=1), ('atm', 'ocn'), split_a...  5.03 us
    concatenate x1, local copies, waits for them, and re-layouts, per_device(): outgoing = jnp.concatenate([out_ocean, out_weight, out_label], axis=1)  3.23 us
    dot_general x3, matrix products, select_rows(): jnp.dot(chosen, flat, precision=precision, preferred_element_type=jnp.flo...  3.05 us
    concatenate x1, other arithmetic, per_device(): jnp.concatenate([atm_planes, jnp.transpose(diffusivity, (1, 0, 2))], axis=0)  3.02 us
  transfers between devices with their start and end apart: 2, of which 0 were waited for; matrix products, arithmetic and copies ran while one was open for 9% of the time, Pallas kernels for 53%

profile of v16, /device:TPU:1, one launch (start us, length us, event | category | flops | bytes accessed | tf_op | source)
XLA Modules:
  0.0 117.1 jit_solution(4058492680104427570)
XLA Ops:
  0.7 0.8 fusion.39
  1.4 0.8 copy.13
  2.2 0.2 fusion.34
  2.5 0.9 fusion.32
  3.5 0.2 copy.15
  3.7 1.3 %fusion.7 = f32[1024,128]{0,1:T(8,128)S(1)} fusion(f32[512,128]{1,0:T(8,128)S(1)} %copy-done, s32[512]{0:T(512)S(1)} %multiply_add_fusion.1), kind=kOutput, calls=%fused_computation.22 | convolution fusion | flops 805830656 | bytes 788480 | tf_op jit(solution)/shard_map/dot_general | solution.py:77
  5.2 0.6 fusion.6
  5.9 0.6 fusion.8
  6.5 1.5 %fusion.48 = f32[1024,384]{0,1:T(8,128)S(1)} fusion(f32[1024,256]{1,0:T(8,128)S(1)} %fusion.8, f32[256,384]{0,1:T(8,128)S(1)} %bitcast.35), kind=kOutput, calls=%fused_computation.100 | convolution fusion | flops 1207959552 | bytes 3014656 | tf_op jit(solution)/shard_map/dot_general | solution.py:77
  8.0 0.3 convolution_multiply_fusion
  8.3 1.8 %pad_maximum_fusion.1 = f32[1024,640]{0,1:T(8,128)} fusion(f32[1024,128]{0,1:T(8,128)S(1)} %slice_add_fusion.4, f32[1024,128]{0,1:T(8,128)S(1)} %convolution_multiply_fusion, f32[1024,384]{0,1:T(8,128)S(1)} %fusion.48), kind=kLoop, calls=%fused_computation.5 | loop fusion | flops 1310720 | bytes 5242880 | tf_op jit(solution)/shard_map/concatenate | solution.py:280
  10.2 3.2 %copy.16 = f32[1024,640]{1,0:T(8,128)} copy(f32[1024,640]{0,1:T(8,128)} %pad_maximum_fusion.1) | data formatting | bytes 5242880 | tf_op jit(solution)/shard_map/concatenate | solution.py:280
  13.4 11.9 %all-to-all-start = ((f32[128,8,640]{2,1,0:T(8,128)}), f32[128,8,640]{2,1,0:T(8,128)}, u32[]{:S(2)}, u32[]{:S(2)}) async-start(f32[128,8,640]{2,1,0:T(8,128)} %bitcast.32), calls=%async_computation | async-start | bytes 5242880 | tf_op jit(solution)/shard_map/all_to_all | solution.py:281
  25.3 3.0 %pad_maximum_fusion.x_ref.both_ref = f32[6,864,128]{2,1,0:T(8,128)} fusion(f32[3,864,128]{2,1,0:T(8,128)S(1)} %bitcast.36, f32[3,864,128]{2,1,0:T(8,128)} %bitcast.37), kind=kLoop, calls=%fused_computation.4 | loop fusion | flops 663552 | bytes 5308416 | tf_op jit(solution)/shard_map/concatenate | solution.py:284
  28.4 37.3 %shard_map.95 = (f32[864,384]{1,0:T(8,128)}, f32[3,896,128]{2,1,0:T(8,128)}, f32[3,896,128]{2,1,0:T(8,128)}) custom-call(f32[6,864,128]{2,1,0:T(8,128)} %pad_maximum_fusion.x_ref.both_ref), custom_call_target="tpu_custom_call" | custom-call | tf_op jit(solution)/shard_map/pallas_call | solution.py:208
  65.6 1.6 %reduce-precision_convert_fusion.5 = (bf16[864,384]{1,0:T(8,128)(2,1)S(1)}, bf16[864,384]{1,0:T(8,128)(2,1)S(1)}, bf16[864,384]{1,0:T(8,128)(2,1)S(1)}) fusion(f32[864,384]{1,0:T(8,128)} %get-tuple-element.7), kind=kLoop, calls=%fused_computation.33 | loop fusion | flops 2654208 | bytes 3317760 | tf_op jit(solution)/shard_map/convert_element_type | solution.py:68
  67.3 1.2 %slice_reduce_fusion = f32[1024]{0:T(1024)S(1)} fusion(f32[1024,640]{1,0:T(8,128)} %bitcast.9), kind=kLoop, calls=%fused_computation.57 | loop fusion | flops 130048 | bytes 528384 | tf_op jit(solution)/shard_map/reduce_max | solution.py:289
  68.6 2.9 %fusion.9 = f32[1024,1152]{1,0:T(8,128)S(1)} fusion(bf16[864,384]{1,0:T(8,128)(2,1)S(1)} %get-tuple-element.25, bf16[864,384]{1,0:T(8,128)(2,1)S(1)} %get-tuple-element.26, bf16[864,384]{1,0:T(8,128)(2,1)S(1)} %get-tuple-element.24, s32[1024]{0:T(1024)S(1)} %convert_element_type.74), kind=kOutput, calls=%fused_computation.24 | convolution fusion | flops 2047057920 | bytes 6713344 | tf_op jit(solution)/shard_map/dot_general | solution.py:71
  71.5 0.2 slice_add_fusion
  71.7 2.0 %multiply_multiply_fusion.3 = (f32[1024,128]{1,0:T(8,128)S(1)}, f32[1024,128]{1,0:T(8,128)S(1)}) fusion(f32[1024,640]{1,0:T(8,128)} %bitcast.9, f32[1024,384]{1,0:T(8,128)S(1)} %slice_add_fusion), kind=kLoop, calls=%fused_computation.63 | loop fusion | flops 1835008 | bytes 4718592 | tf_op jit(solution)/shard_map/mul | solution.py:304
  73.7 1.9 %multiply_multiply_fusion.1 = (f32[1024,128]{1,0:T(8,128)S(1)}, f32[1024,128]{1,0:T(8,128)S(1)}) fusion(f32[1024,640]{1,0:T(8,128)} %bitcast.9, f32[1024,384]{1,0:T(8,128)S(1)} %slice_add_fusion, f32[1024,128]{1,0:T(8,128)S(1)} %get-tuple-element.17), kind=kLoop, calls=%fused_computation.61 | loop fusion | flops 1572864 | bytes 5242880 | tf_op jit(solution)/shard_map/mul | solution.py:305
  75.6 2.4 %fusion.36 = (f32[128,8,384]{2,1,0:T(8,128)}, bf16[1024,384]{1,0:T(8,128)(2,1)}, bf16[1024,384]{1,0:T(8,128)(2,1)}, bf16[1024,384]{1,0:T(8,128)(2,1)}) fusion(f32[1024,128]{1,0:T(8,128)S(1)} %get-tuple-element.19, f32[1024,128]{1,0:T(8,128)S(1)} %get-tuple-element.18, f32[1024,128]{1,0:T(8,128)S(1)} %get-tuple-element.16), kind=kLoop, calls=%fused_computation.78 | loop fusion | flops 3932160 | bytes 5505024 | tf_op jit(solution)/shard_map/all_to_all | solution.py:308
  78.0 5.0 %all-to-all-start.1 = ((f32[128,8,384]{2,1,0:T(8,128)}), f32[128,8,384]{2,1,0:T(8,128)S(1)}, u32[]{:S(2)}, u32[]{:S(2)}) async-start(f32[128,8,384]{2,1,0:T(8,128)} %get-tuple-element.20), calls=%async_computation.1 | async-start | bytes 3145728 | tf_op jit(solution)/shard_map/all_to_all | solution.py:308
  83.0 4.1 %fusion = f32[864,1152]{1,0:T(8,128)S(1)} fusion(bf16[1024,384]{1,0:T(8,128)(2,1)} %get-tuple-element.22, bf16[1024,384]{1,0:T(8,128)(2,1)} %get-tuple-element.21, bf16[1024,384]{1,0:T(8,128)(2,1)} %get-tuple-element.23, s32[1024]{0:T(1024)S(1)} %convert_element_type.74), kind=kOutput, calls=%fused_computation.6 | convolution fusion | flops 2048163840 | bytes 6344704 | tf_op jit(solution)/shard_map/dot_general | solution.py:71
  87.1 1.2 %slice_add_fusion.2.sum_ref = f32[864,384]{1,0:T(8,128)} fusion(f32[864,1152]{1,0:T(8,128)S(1)} %fusion), kind=kLoop, calls=%fused_computation.45 | loop fusion | flops 663552 | bytes 5308416 | tf_op jit(solution)/shard_map/add | solution.py:72
  88.3 24.8 %shard_map.96 = f32[3,864,128]{2,1,0:T(8,128)} custom-call(f32[6,864,128]{2,1,0:T(8,128)} %pad_maximum_fusion.x_ref.both_ref, f32[864,384]{1,0:T(8,128)} %slice_add_fusion.2.sum_ref, f32[3,896,128]{2,1,0:T(8,128)} %get-tuple-element.8.dtall_ref, f32[3,896,128]{2,1,0:T(8,128)} %get-tuple-element.9.dside_ref), custom_call_target="tpu_custom_call" | custom-call | tf_op jit(solution)/shard_map/pallas_call | solution.py:226
  113.1 0.5 fusion.27
  113.6 0.5 convolution_add_fusion.1
  114.1 0.5 convolution_add_fusion
  114.8 0.9 copy.18
  115.7 0.3 copy-done.1
  116.0 1.1 copy.20
  (27 shorter events, 0.6 us)
Async XLA Ops:
  0.6 3.0 %copy-start = (f32[512,128]{1,0:T(8,128)S(1)}, f32[512,128]{1,0:T(8,128)}, u32[]{:S(2)}) copy-start(f32[512,128]{1,0:T(8,128)} %param.12) | copy-start | bytes 786436
  0.6 2.8 %copy-start.5 = (s32[512,1]{0,1:T(1,128)S(1)}, s32[512,1]{0,1:T(1,128)}, u32[]{:S(2)}) copy-start(s32[512,1]{0,1:T(1,128)} %param.14) | copy-start | bytes 6148
  0.7 2.8 %copy-start.3 = (f32[256,3,128]{2,0,1:T(8,128)S(1)}, f32[256,3,128]{2,0,1:T(8,128)}, u32[]{:S(2)}) copy-start(f32[256,3,128]{2,0,1:T(8,128)} %param.10) | copy-start | bytes 1179652
  5.2 0.7 copy-start.6
  6.5 1.5 %copy-start.4 = (s32[256,128]{1,0:T(8,128)S(1)}, s32[256,128]{1,0:T(8,128)}, u32[]{:S(2)}) copy-start(s32[256,128]{1,0:T(8,128)} %param.11) | copy-start | bytes 393220
  13.4 11.9 %copy-start.2 = (f32[864,3,128]{2,0,1:T(8,128)S(1)}, f32[864,3,128]{2,0,1:T(8,128)}, u32[]{:S(2)}) copy-start(f32[864,3,128]{2,0,1:T(8,128)} %param.9) | copy-start | bytes 3981316
  13.4 53.9 %all-to-all-start = ((f32[128,8,640]{2,1,0:T(8,128)}), f32[128,8,640]{2,1,0:T(8,128)}, u32[]{:S(2)}, u32[]{:S(2)}) async-start(f32[128,8,640]{2,1,0:T(8,128)} %bitcast.32), calls=%async_computation | async-start | bytes 5242880 | tf_op jit(solution)/shard_map/all_to_all | solution.py:281
  78.0 35.1 %all-to-all-start.1 = ((f32[128,8,384]{2,1,0:T(8,128)}), f32[128,8,384]{2,1,0:T(8,128)S(1)}, u32[]{:S(2)}, u32[]{:S(2)}) async-start(f32[128,8,384]{2,1,0:T(8,128)} %get-tuple-element.20), calls=%async_computation.1 | async-start | bytes 3145728 | tf_op jit(solution)/shard_map/all_to_all | solution.py:308
  114.6 1.4 %copy-start.1 = (f32[3,864,128]{2,1,0:T(8,128)S(1)}, f32[3,864,128]{2,1,0:T(8,128)}, u32[]{:S(2)}) copy-start(f32[3,864,128]{2,1,0:T(8,128)} %shard_map.96) | copy-start | bytes 3981316

commit v17 on v15

--- a/solution.py
+++ b/solution.py
@@ -160,14 +160,12 @@
     )
 
 
-def smooth_kernel(sizes, x_ref, out_ref, tall_out, side_out, *scratch):
+def smooth_kernel(sizes, x_ref, out_ref, *scratch):
     rows_buf, cols_buf, colsend, tall_s, side_s, send_sem, recv_sem = scratch
     exchange(sizes, x_ref, rows_buf, cols_buf, colsend, tall_s, side_s, send_sem, recv_sem)
-    kept = tall_out.shape[0]
-    rows, width = out_ref.shape[0], out_ref.shape[1] // kept
-    tall_out[...] = tall_s[kept:]
-    side_out[...] = side_s[kept:]
-    for chan in range(kept):
+    chans = x_ref.shape[0]
+    rows, width = out_ref.shape[0], out_ref.shape[1] // chans
+    for chan in range(chans):
         state = jnp.concatenate([tall_s[chan], side_s[chan]], axis=1)
         done = 0.5 * state + 0.125 * stencil_sum(state)
         out_ref[:, chan * width : (chan + 1) * width] = done[EDGE : EDGE + rows, :width]
@@ -176,50 +174,47 @@
 SIGNS = (1.0, -1.0, -1.0)
 
 
-def diffuse_kernel(sizes, both_ref, sum_ref, dtall_ref, dside_ref, out_ref, forced_s, *scratch):
+def diffuse_kernel(sizes, both_ref, sum_ref, out_ref, forced_s, *scratch):
     rows_buf, cols_buf, colsend, tall_s, side_s, send_sem, recv_sem = scratch
-    rows, width = out_ref.shape[1], out_ref.shape[2]
-    for chan in range(out_ref.shape[0]):
+    chans, rows, width = out_ref.shape
+    for chan in range(chans):
         forced_s[chan] = both_ref[chan] + SIGNS[chan] * sum_ref[:, chan * width : (chan + 1) * width]
+        forced_s[chans + chan] = both_ref[chans + chan]
     exchange(sizes, forced_s, rows_buf, cols_buf, colsend, tall_s, side_s, send_sem, recv_sem)
-    for chan in range(out_ref.shape[0]):
+    for chan in range(chans):
         state = jnp.concatenate([tall_s[chan], side_s[chan]], axis=1)
-        diff = jnp.concatenate([dtall_ref[chan], dside_ref[chan]], axis=1)
+        diff = jnp.concatenate([tall_s[chans + chan], side_s[chans + chan]], axis=1)
         for iteration in range(ITERS):
             state = state + diff * (stencil_sum(state) - 4.0 * state)
         out_ref[chan] = state[EDGE : EDGE + rows, :width]
 
 
-def smooth_call(sizes, both, chans, rows_padded):
-    total, rows, width = both.shape
+def smooth_call(sizes, planes, rows_padded):
+    chans, rows, width = planes.shape
     vmem = pl.BlockSpec(memory_space=pltpu.VMEM)
     return pl.pallas_call(
         functools.partial(smooth_kernel, sizes),
-        out_shape=(
-            jax.ShapeDtypeStruct((rows, chans * width), jnp.float32),
-            jax.ShapeDtypeStruct((total - chans, rows_padded, width), jnp.float32),
-            jax.ShapeDtypeStruct((total - chans, rows_padded, width), jnp.float32),
-        ),
+        out_shape=jax.ShapeDtypeStruct((rows, chans * width), jnp.float32),
         in_specs=[vmem],
-        out_specs=(vmem, vmem, vmem),
-        scratch_shapes=exchange_scratch(total, rows_padded, width),
+        out_specs=vmem,
+        scratch_shapes=exchange_scratch(chans, rows_padded, width),
         compiler_params=pltpu.CompilerParams(collective_id=0, has_side_effects=True),
-    )(both)
-
-
-def diffuse_call(sizes, both, air_sum, dtall, dside):
-    chans, rows_padded, width = dtall.shape
-    rows = both.shape[1]
+    )(planes)
+
+
+def diffuse_call(sizes, both, air_sum, rows_padded):
+    total, rows, width = both.shape
+    chans = total // 2
     vmem = pl.BlockSpec(memory_space=pltpu.VMEM)
     return pl.pallas_call(
         functools.partial(diffuse_kernel, sizes),
         out_shape=jax.ShapeDtypeStruct((chans, rows, width), jnp.float32),
-        in_specs=[vmem] * 4,
+        in_specs=[vmem] * 2,
         out_specs=vmem,
-        scratch_shapes=[pltpu.VMEM((chans, rows, width), jnp.float32)]
-        + exchange_scratch(chans, rows_padded, width),
+        scratch_shapes=[pltpu.VMEM((total, rows, width), jnp.float32)]
+        + exchange_scratch(total, rows_padded, width),
         compiler_params=pltpu.CompilerParams(collective_id=1, has_side_effects=True),
-    )(both, air_sum, dtall, dside)
+    )(both, air_sum)
 
 
 def per_device(
@@ -272,7 +267,7 @@
     both = jnp.concatenate([atm_planes, jnp.transpose(diffusivity, (1, 0, 2))], axis=0)
     sizes = (atm_count, ocn_count)
     rows_padded = -(-(row_count + 2 * EDGE) // 128) * 128
-    smoothed, dtall, dside = smooth_call(sizes, both, chan_count, rows_padded)
+    smoothed = smooth_call(sizes, atm_planes, rows_padded)
 
     in_labels = jnp.max(incoming[:, plane + seg_width :], axis=1).astype(jnp.int32)
     row_pick = (
@@ -298,7 +293,7 @@
     )
     sent = jnp.concatenate(weighted, axis=1)
     air_sum = jnp.dot(row_pick, sent, precision=HIGHEST, preferred_element_type=jnp.float32)
-    current = diffuse_call(sizes, both, air_sum, dtall, dside)
+    current = diffuse_call(sizes, both, air_sum, rows_padded)
     current, returned = lax.optimization_barrier((current, returned))
     seg_of_slot = slot_seg.T.astype(jnp.bfloat16)
     ocean_flux = pick_dot(seg_of_slot, returned).reshape(seg_count, chan_count, seg_width)

time: 118 us -> 117 us (level)
  matrix products: 15 us -> 13.8 us
    dot_general x1, matrix products: 5.21 us -> 4.01 us  [per_device(): jnp.dot(row_pick, sent, precision=HIGHEST, preferred_element_type=jnp.flo...]
    unnamed x30 -> x32, local copies, waits for them, and re-layouts: 5.3 us -> 5.29 us
  transfers between devices with their start and end apart: 2 -> 2, of which waited for: 0 -> 0; matrix products, arithmetic and copies ran while one was open for 7% -> 6% of each run, Pallas kernels for 53% -> 53%
where the time goes in v17:
time: 117 us; the launch traced here: 116 us
  Pallas kernels  62.2 us (53%)
  starting transfers between devices  16.8 us (14%)
  matrix products  13.8 us (12%)
  local copies, waits for them, and re-layouts  11.4 us (10%)
  other arithmetic  11.2 us (10%)
    pallas_call x1, Pallas kernels, smooth_call(): pl.pallas_call(functools.partial(smooth_kernel, sizes), out_shape=jax.Sha...  38.2 us
    pallas_call x1, Pallas kernels, diffuse_call(): pl.pallas_call(functools.partial(diffuse_kernel, sizes), out_shape=jax.Sh...  24 us
    all_to_all x1, starting transfers between devices, per_device(): lax.all_to_all(outgoing, ('atm', 'ocn'), split_axis=0, concat_axis=0, til...  11.9 us
    unnamed x32, local copies, waits for them, and re-layouts  5.29 us
    all_to_all x1, starting transfers between devices, per_device(): lax.all_to_all(jnp.concatenate(weighted, axis=1), ('atm', 'ocn'), split_a...  4.92 us
    dot_general x1, matrix products, per_device(): jnp.dot(pick_rows, smoothed, precision=HIGHEST, preferred_element_type=jn...  4.1 us
    dot_general x1, matrix products, per_device(): jnp.dot(row_pick, sent, precision=HIGHEST, preferred_element_type=jnp.flo...  4.01 us
    concatenate x1, other arithmetic, per_device(): jnp.concatenate([atm_planes, jnp.transpose(diffusivity, (1, 0, 2))], axis=0)  3.54 us
  transfers between devices with their start and end apart: 2, of which 0 were waited for; matrix products, arithmetic and copies ran while one was open for 6% of the time, Pallas kernels for 53%

profile of v17, /device:TPU:1, one launch (start us, length us, event | category | flops | bytes accessed | tf_op | source)
XLA Modules:
  0.0 116.5 jit_solution(11873049654644856762)
XLA Ops:
  0.7 0.8 fusion.24
  1.4 0.8 copy.12
  2.2 0.2 fusion.20
  2.5 0.9 fusion.18
  3.7 1.3 %fusion.3 = f32[1024,128]{0,1:T(8,128)S(1)} fusion(f32[512,128]{1,0:T(8,128)S(1)} %copy-done, s32[512]{0:T(512)S(1)} %multiply_add_fusion.1), kind=kOutput, calls=%fused_computation.11 | convolution fusion | flops 805830656 | bytes 788480 | tf_op jit(solution)/shard_map/dot_general | solution.py:65
  5.2 0.6 fusion.2
  5.9 0.6 fusion.4
  6.5 1.5 %fusion.32 = f32[1024,384]{0,1:T(8,128)S(1)} fusion(f32[1024,256]{1,0:T(8,128)S(1)} %fusion.4, f32[256,384]{0,1:T(8,128)S(1)} %bitcast.38), kind=kOutput, calls=%fused_computation.69 | convolution fusion | flops 1207959552 | bytes 3014656 | tf_op jit(solution)/shard_map/dot_general | solution.py:65
  8.0 0.3 convolution_multiply_fusion
  8.3 1.8 %pad_maximum_fusion.1 = f32[1024,640]{0,1:T(8,128)} fusion(f32[1024,128]{0,1:T(8,128)S(1)} %slice_add_fusion, f32[1024,128]{0,1:T(8,128)S(1)} %convolution_multiply_fusion, f32[1024,384]{0,1:T(8,128)S(1)} %fusion.32), kind=kLoop, calls=%fused_computation.4 | loop fusion | flops 1310720 | bytes 5242880 | tf_op jit(solution)/shard_map/concatenate | solution.py:263
  10.2 3.2 %copy.15 = f32[1024,640]{1,0:T(8,128)} copy(f32[1024,640]{0,1:T(8,128)} %pad_maximum_fusion.1) | data formatting | bytes 5242880 | tf_op jit(solution)/shard_map/concatenate | solution.py:263
  13.4 11.9 %all-to-all-start = ((f32[128,8,640]{2,1,0:T(8,128)}), f32[128,8,640]{2,1,0:T(8,128)}, u32[]{:S(2)}, u32[]{:S(2)}) async-start(f32[128,8,640]{2,1,0:T(8,128)} %bitcast.32), calls=%async_computation | async-start | bytes 5242880 | tf_op jit(solution)/shard_map/all_to_all | solution.py:264
  25.3 38.2 %shard_map.95 = f32[864,384]{1,0:T(8,128)} custom-call(f32[3,864,128]{2,1,0:T(8,128)} %bitcast.34), custom_call_target="tpu_custom_call" | custom-call | tf_op jit(solution)/shard_map/pallas_call | solution.py:195
  63.6 2.8 %fusion.31 = (f32[1024,128]{1,0:T(8,128)S(1)}, f32[1024,128]{1,0:T(8,128)S(1)}, f32[1024,128]{1,0:T(8,128)S(1)}, f32[1024,128]{1,0:T(8,128)}, f32[1024]{0:T(1024)S(1)}) fusion(f32[1024,640]{1,0:T(8,128)} %bitcast.9), kind=kLoop, calls=%fused_computation.68 | loop fusion | flops 130048 | bytes 4722688 | tf_op jit(solution)/shard_map/slice | solution.py:279
  66.5 0.2 copy.24
  67.0 1.2 %copy.26 = f32[1024,128]{0,1:T(8,128)S(1)} copy(f32[1024,128]{1,0:T(8,128)} %get-tuple-element.17) | data formatting | bytes 1048576
  68.2 4.1 %fusion.1 = f32[1024,384]{0,1:T(8,128)S(1)} fusion(f32[864,384]{1,0:T(8,128)} %shard_map.95, s32[1024]{0:T(1024)S(1)} %convert_element_type.45), kind=kOutput, calls=%fused_computation.2 | convolution fusion | flops 4077748224 | bytes 2904064 | tf_op jit(solution)/shard_map/dot_general | solution.py:277
  72.3 0.4 multiply_multiply_fusion.3
  72.8 0.5 multiply_multiply_fusion.1
  73.3 0.2 copy-done.2
  73.5 0.6 copy-done.4
  74.4 1.6 %copy.20 = f32[1024,384]{1,0:T(8,128)} copy(f32[1024,384]{0,1:T(8,128)S(1)} %pad_maximum_fusion.2) | data formatting | bytes 3145728 | tf_op jit(solution)/shard_map/concatenate | solution.py:294
  76.0 4.9 %all-to-all-start.1 = ((f32[128,8,384]{2,1,0:T(8,128)}), f32[128,8,384]{2,1,0:T(8,128)S(1)}, u32[]{:S(2)}, u32[]{:S(2)}) async-start(f32[128,8,384]{2,1,0:T(8,128)} %bitcast.33), calls=%async_computation.1 | async-start | bytes 3145728 | tf_op jit(solution)/shard_map/all_to_all | solution.py:291
  81.0 3.5 %pad_maximum_fusion.both_ref = f32[6,864,128]{2,1,0:T(8,128)} fusion(f32[3,864,128]{2,1,0:T(8,128)} %bitcast.39, f32[3,864,128]{2,1,0:T(8,128)} %bitcast.35), kind=kLoop, calls=%fused_computation.3 | loop fusion | flops 663552 | bytes 5308416 | tf_op jit(solution)/shard_map/concatenate | solution.py:267
  84.5 4.0 %fusion.sum_ref = f32[864,384]{1,0:T(8,128)} fusion(s32[1024]{0:T(1024)S(1)} %convert_element_type.45, f32[1024,128]{0,1:T(8,128)S(1)} %copy-done.7, f32[1024,128]{0,1:T(8,128)S(1)} %copy-done.5, f32[1024,128]{0,1:T(8,128)S(1)} %copy-done.3), kind=kOutput, calls=%fused_computation.1 | convolution fusion | flops 4078534656 | bytes 2904064 | tf_op jit(solution)/shard_map/dot_general | solution.py:295
  88.5 24.0 %shard_map.96 = f32[3,864,128]{2,1,0:T(8,128)} custom-call(f32[6,864,128]{2,1,0:T(8,128)} %pad_maximum_fusion.both_ref, f32[864,384]{1,0:T(8,128)} %fusion.sum_ref), custom_call_target="tpu_custom_call" | custom-call | tf_op jit(solution)/shard_map/pallas_call | solution.py:209
  112.5 0.5 fusion.13
  113.0 0.5 convolution_add_fusion.1
  113.5 0.5 convolution_add_fusion
  114.2 0.9 copy.22
  115.1 0.3 copy-done.1
  115.4 1.1 copy.28
  (39 shorter events, 1.5 us)
Async XLA Ops:
  0.6 3.0 %copy-start = (f32[512,128]{1,0:T(8,128)S(1)}, f32[512,128]{1,0:T(8,128)}, u32[]{:S(2)}) copy-start(f32[512,128]{1,0:T(8,128)} %param.12) | copy-start | bytes 786436
  0.6 2.8 %copy-start.10 = (s32[512,1]{0,1:T(1,128)S(1)}, s32[512,1]{0,1:T(1,128)}, u32[]{:S(2)}) copy-start(s32[512,1]{0,1:T(1,128)} %param.14) | copy-start | bytes 6148
  0.7 2.8 %copy-start.8 = (f32[256,3,128]{2,0,1:T(8,128)S(1)}, f32[256,3,128]{2,0,1:T(8,128)}, u32[]{:S(2)}) copy-start(f32[256,3,128]{2,0,1:T(8,128)} %param.10) | copy-start | bytes 1179652
  5.2 0.7 copy-start.11
  6.5 1.5 %copy-start.9 = (s32[256,128]{1,0:T(8,128)S(1)}, s32[256,128]{1,0:T(8,128)}, u32[]{:S(2)}) copy-start(s32[256,128]{1,0:T(8,128)} %param.11) | copy-start | bytes 393220
  13.4 50.2 %all-to-all-start = ((f32[128,8,640]{2,1,0:T(8,128)}), f32[128,8,640]{2,1,0:T(8,128)}, u32[]{:S(2)}, u32[]{:S(2)}) async-start(f32[128,8,640]{2,1,0:T(8,128)} %bitcast.32), calls=%async_computation | async-start | bytes 5242880 | tf_op jit(solution)/shard_map/all_to_all | solution.py:264
  72.8 0.8 copy-start.2
  73.3 0.8 copy-start.4
  73.3 1.0 copy-start.6
  76.0 36.5 %all-to-all-start.1 = ((f32[128,8,384]{2,1,0:T(8,128)}), f32[128,8,384]{2,1,0:T(8,128)S(1)}, u32[]{:S(2)}, u32[]{:S(2)}) async-start(f32[128,8,384]{2,1,0:T(8,128)} %bitcast.33), calls=%async_computation.1 | async-start | bytes 3145728 | tf_op jit(solution)/shard_map/all_to_all | solution.py:291
  80.9 3.6 %copy-start.3 = (f32[1024,128]{0,1:T(8,128)S(1)}, f32[1024,128]{0,1:T(8,128)}, u32[]{:S(2)}) copy-start(f32[1024,128]{0,1:T(8,128)} %copy-done.2) | copy-start | bytes 1572868
  80.9 3.6 %copy-start.5 = (f32[1024,128]{0,1:T(8,128)S(1)}, f32[1024,128]{0,1:T(8,128)}, u32[]{:S(2)}) copy-start(f32[1024,128]{0,1:T(8,128)} %copy-done.4) | copy-start | bytes 1572868
  81.0 3.6 %copy-start.7 = (f32[1024,128]{0,1:T(8,128)S(1)}, f32[1024,128]{0,1:T(8,128)}, u32[]{:S(2)}) copy-start(f32[1024,128]{0,1:T(8,128)} %copy-done.6) | copy-start | bytes 1572868
  114.0 1.4 %copy-start.1 = (f32[3,864,128]{2,1,0:T(8,128)S(1)}, f32[3,864,128]{2,1,0:T(8,128)}, u32[]{:S(2)}) copy-start(f32[3,864,128]{2,1,0:T(8,128)} %shard_map.96) | copy-start | bytes 3981316

commit v18 on v17

--- a/solution.py
+++ b/solution.py
@@ -267,6 +267,7 @@
     both = jnp.concatenate([atm_planes, jnp.transpose(diffusivity, (1, 0, 2))], axis=0)
     sizes = (atm_count, ocn_count)
     rows_padded = -(-(row_count + 2 * EDGE) // 128) * 128
+    atm_planes, both = lax.optimization_barrier((atm_planes, both))
     smoothed = smooth_call(sizes, atm_planes, rows_padded)
 
     in_labels = jnp.max(incoming[:, plane + seg_width :], axis=1).astype(jnp.int32)

time: 117 us -> 117 us (level)
  matrix products: 13.8 us -> 15 us
    pallas_call x1, Pallas kernels: 38.2 us -> 35.2 us  [smooth_call(): pl.pallas_call(functools.partial(smooth_kernel, sizes), out_shape=jax.Sha...]
    pallas_call x1, Pallas kernels: 24 us -> 26.5 us  [diffuse_call(): pl.pallas_call(functools.partial(diffuse_kernel, sizes), out_shape=jax.Sh...]
    dot_general x1, matrix products: 4.01 us -> 5.21 us  [per_device(): jnp.dot(row_pick, sent, precision=HIGHEST, preferred_element_type=jnp.flo...]
    unnamed x32 -> x30, local copies, waits for them, and re-layouts: 5.29 us -> 5.3 us
  transfers between devices with their start and end apart: 2 -> 2, of which waited for: 0 -> 0; matrix products, arithmetic and copies ran while one was open for 6% -> 7% of each run, Pallas kernels for 53% -> 53%
where the time goes in v18:
time: 117 us
  Pallas kernels  61.7 us (53%)
  starting transfers between devices  16.8 us (14%)
  matrix products  15 us (13%)
  local copies, waits for them, and re-layouts  11.4 us (10%)
  other arithmetic  10.7 us (9%)
    pallas_call x1, Pallas kernels, smooth_call(): pl.pallas_call(functools.partial(smooth_kernel, sizes), out_shape=jax.Sha...  35.2 us
    pallas_call x1, Pallas kernels, diffuse_call(): pl.pallas_call(functools.partial(diffuse_kernel, sizes), out_shape=jax.Sh...  26.5 us
    all_to_all x1, starting transfers between devices, per_device(): lax.all_to_all(outgoing, ('atm', 'ocn'), split_axis=0, concat_axis=0, til...  11.9 us
    unnamed x30, local copies, waits for them, and re-layouts  5.3 us
    dot_general x1, matrix products, per_device(): jnp.dot(row_pick, sent, precision=HIGHEST, preferred_element_type=jnp.flo...  5.21 us
    all_to_all x1, starting transfers between devices, per_device(): lax.all_to_all(jnp.concatenate(weighted, axis=1), ('atm', 'ocn'), split_a...  4.93 us
    dot_general x1, matrix products, per_device(): jnp.dot(pick_rows, smoothed, precision=HIGHEST, preferred_element_type=jn...  4.1 us
    concatenate x1, local copies, waits for them, and re-layouts, per_device(): outgoing = jnp.concatenate([out_ocean, out_weight, out_label], axis=1)  3.22 us
  transfers between devices with their start and end apart: 2, of which 0 were waited for; matrix products, arithmetic and copies ran while one was open for 7% of the time, Pallas kernels for 53%

profile of v18, /device:TPU:1, one launch (start us, length us, event | category | flops | bytes accessed | tf_op | source)
XLA Modules:
  0.0 116.6 jit_solution(17295234782315796762)
XLA Ops:
  0.7 0.8 fusion.24
  1.4 0.8 copy.12
  2.2 0.2 fusion.20
  2.5 0.9 fusion.18
  3.7 1.3 %fusion.3 = f32[1024,128]{0,1:T(8,128)S(1)} fusion(f32[512,128]{1,0:T(8,128)S(1)} %copy-done, s32[512]{0:T(512)S(1)} %multiply_add_fusion.1), kind=kOutput, calls=%fused_computation.11 | convolution fusion | flops 805830656 | bytes 788480 | tf_op jit(solution)/shard_map/dot_general | solution.py:65
  5.2 0.6 fusion.2
  5.9 0.6 fusion.4
  6.5 1.5 %fusion.32 = f32[1024,384]{0,1:T(8,128)S(1)} fusion(f32[1024,256]{1,0:T(8,128)S(1)} %fusion.4, f32[256,384]{0,1:T(8,128)S(1)} %bitcast.38), kind=kOutput, calls=%fused_computation.69 | convolution fusion | flops 1207959552 | bytes 3014656 | tf_op jit(solution)/shard_map/dot_general | solution.py:65
  8.0 0.3 convolution_multiply_fusion
  8.3 1.9 %pad_maximum_fusion.1 = f32[1024,640]{0,1:T(8,128)} fusion(f32[1024,128]{0,1:T(8,128)S(1)} %slice_add_fusion, f32[1024,128]{0,1:T(8,128)S(1)} %convolution_multiply_fusion, f32[1024,384]{0,1:T(8,128)S(1)} %fusion.32), kind=kLoop, calls=%fused_computation.4 | loop fusion | flops 1310720 | bytes 5242880 | tf_op jit(solution)/shard_map/concatenate | solution.py:263
  10.2 3.2 %copy.15 = f32[1024,640]{1,0:T(8,128)} copy(f32[1024,640]{0,1:T(8,128)} %pad_maximum_fusion.1) | data formatting | bytes 5242880 | tf_op jit(solution)/shard_map/concatenate | solution.py:263
  13.4 11.9 %all-to-all-start = ((f32[128,8,640]{2,1,0:T(8,128)}), f32[128,8,640]{2,1,0:T(8,128)}, u32[]{:S(2)}, u32[]{:S(2)}) async-start(f32[128,8,640]{2,1,0:T(8,128)} %bitcast.32), calls=%async_computation | async-start | bytes 5242880 | tf_op jit(solution)/shard_map/all_to_all | solution.py:264
  25.3 3.0 %pad_maximum_fusion.both_ref = f32[6,864,128]{2,1,0:T(8,128)} fusion(f32[3,864,128]{2,1,0:T(8,128)} %bitcast.39, f32[3,864,128]{2,1,0:T(8,128)S(1)} %bitcast.35), kind=kLoop, calls=%fused_computation.3 | loop fusion | flops 663552 | bytes 5308416 | tf_op jit(solution)/shard_map/concatenate | solution.py:267
  28.4 35.2 %shard_map.95 = f32[864,384]{1,0:T(8,128)} custom-call(f32[3,864,128]{2,1,0:T(8,128)} %bitcast.34), custom_call_target="tpu_custom_call" | custom-call | tf_op jit(solution)/shard_map/pallas_call | solution.py:195
  63.6 2.8 %fusion.31 = (f32[1024,128]{1,0:T(8,128)S(1)}, f32[1024,128]{1,0:T(8,128)S(1)}, f32[1024,128]{1,0:T(8,128)S(1)}, f32[1024,128]{1,0:T(8,128)}, f32[1024]{0:T(1024)S(1)}) fusion(f32[1024,640]{1,0:T(8,128)} %bitcast.9), kind=kLoop, calls=%fused_computation.68 | loop fusion | flops 130048 | bytes 4722688 | tf_op jit(solution)/shard_map/slice | solution.py:280
  66.6 0.2 copy.24
  67.0 1.2 %copy.26 = f32[1024,128]{0,1:T(8,128)S(1)} copy(f32[1024,128]{1,0:T(8,128)} %get-tuple-element.21) | data formatting | bytes 1048576
  68.2 4.1 %fusion.1 = f32[1024,384]{0,1:T(8,128)S(1)} fusion(f32[864,384]{1,0:T(8,128)} %shard_map.95, s32[1024]{0:T(1024)S(1)} %convert_element_type.45), kind=kOutput, calls=%fused_computation.2 | convolution fusion | flops 4077748224 | bytes 2904064 | tf_op jit(solution)/shard_map/dot_general | solution.py:278
  72.3 0.4 multiply_multiply_fusion.3
  72.8 0.5 multiply_multiply_fusion.1
  73.3 0.2 copy-done.3
  73.6 0.6 copy-done.5
  74.4 1.6 %copy.20 = f32[1024,384]{1,0:T(8,128)} copy(f32[1024,384]{0,1:T(8,128)S(1)} %pad_maximum_fusion.2) | data formatting | bytes 3145728 | tf_op jit(solution)/shard_map/concatenate | solution.py:295
  76.0 4.9 %all-to-all-start.1 = ((f32[128,8,384]{2,1,0:T(8,128)}), f32[128,8,384]{2,1,0:T(8,128)S(1)}, u32[]{:S(2)}, u32[]{:S(2)}) async-start(f32[128,8,384]{2,1,0:T(8,128)} %bitcast.33), calls=%async_computation.1 | async-start | bytes 3145728 | tf_op jit(solution)/shard_map/all_to_all | solution.py:292
  81.0 5.2 %fusion.sum_ref = f32[864,384]{1,0:T(8,128)} fusion(s32[1024]{0:T(1024)S(1)} %convert_element_type.45, f32[1024,128]{0,1:T(8,128)} %copy-done.6, f32[1024,128]{0,1:T(8,128)} %copy-done.5, f32[1024,128]{0,1:T(8,128)S(1)} %copy-done.4), kind=kOutput, calls=%fused_computation.1 | convolution fusion | flops 4078534656 | bytes 2904064 | tf_op jit(solution)/shard_map/dot_general | solution.py:296
  86.2 26.5 %shard_map.96 = f32[3,864,128]{2,1,0:T(8,128)} custom-call(f32[6,864,128]{2,1,0:T(8,128)} %pad_maximum_fusion.both_ref, f32[864,384]{1,0:T(8,128)} %fusion.sum_ref), custom_call_target="tpu_custom_call" | custom-call | tf_op jit(solution)/shard_map/pallas_call | solution.py:209
  112.7 0.5 fusion.13
  113.1 0.5 convolution_add_fusion.1
  113.6 0.5 convolution_add_fusion
  114.3 0.9 copy.22
  115.2 0.3 copy-done.2
  115.5 1.1 copy.28
  (37 shorter events, 1.5 us)
Async XLA Ops:
  0.6 3.0 %copy-start = (f32[512,128]{1,0:T(8,128)S(1)}, f32[512,128]{1,0:T(8,128)}, u32[]{:S(2)}) copy-start(f32[512,128]{1,0:T(8,128)} %param.12) | copy-start | bytes 786436
  0.6 2.8 %copy-start.9 = (s32[512,1]{0,1:T(1,128)S(1)}, s32[512,1]{0,1:T(1,128)}, u32[]{:S(2)}) copy-start(s32[512,1]{0,1:T(1,128)} %param.14) | copy-start | bytes 6148
  0.7 2.8 %copy-start.7 = (f32[256,3,128]{2,0,1:T(8,128)S(1)}, f32[256,3,128]{2,0,1:T(8,128)}, u32[]{:S(2)}) copy-start(f32[256,3,128]{2,0,1:T(8,128)} %param.10) | copy-start | bytes 1179652
  5.2 0.7 copy-start.10
  6.5 1.5 %copy-start.8 = (s32[256,128]{1,0:T(8,128)S(1)}, s32[256,128]{1,0:T(8,128)}, u32[]{:S(2)}) copy-start(s32[256,128]{1,0:T(8,128)} %param.11) | copy-start | bytes 393220
  13.4 11.9 %copy-start.1 = (f32[864,3,128]{2,0,1:T(8,128)S(1)}, f32[864,3,128]{2,0,1:T(8,128)}, u32[]{:S(2)}) copy-start(f32[864,3,128]{2,0,1:T(8,128)} %param.8) | copy-start | bytes 3981316
  13.4 50.2 %all-to-all-start = ((f32[128,8,640]{2,1,0:T(8,128)}), f32[128,8,640]{2,1,0:T(8,128)}, u32[]{:S(2)}, u32[]{:S(2)}) async-start(f32[128,8,640]{2,1,0:T(8,128)} %bitcast.32), calls=%async_computation | async-start | bytes 5242880 | tf_op jit(solution)/shard_map/all_to_all | solution.py:264
  72.8 0.8 copy-start.3
  73.3 0.8 copy-start.5
  73.3 1.0 copy-start.6
  76.0 4.9 %copy-start.4 = (f32[1024,128]{0,1:T(8,128)S(1)}, f32[1024,128]{0,1:T(8,128)}, u32[]{:S(2)}) copy-start(f32[1024,128]{0,1:T(8,128)} %copy-done.3) | copy-start | bytes 1572868
  76.0 36.6 %all-to-all-start.1 = ((f32[128,8,384]{2,1,0:T(8,128)}), f32[128,8,384]{2,1,0:T(8,128)S(1)}, u32[]{:S(2)}, u32[]{:S(2)}) async-start(f32[128,8,384]{2,1,0:T(8,128)} %bitcast.33), calls=%async_computation.1 | async-start | bytes 3145728 | tf_op jit(solution)/shard_map/all_to_all | solution.py:292
  114.1 1.4 %copy-start.2 = (f32[3,864,128]{2,1,0:T(8,128)S(1)}, f32[3,864,128]{2,1,0:T(8,128)}, u32[]{:S(2)}) copy-start(f32[3,864,128]{2,1,0:T(8,128)} %shard_map.96) | copy-start | bytes 3981316

commit v19 on v17

--- a/solution.py
+++ b/solution.py
@@ -283,15 +283,12 @@
     wind_speed = jnp.sqrt(wind_east * wind_east + wind_north * wind_north + 0.5)
     temp_gap = ocean[0] - air[0]
     factor = 1.0 + 0.5 * jnp.tanh(temp_gap / wind_speed)
-    weighted = [
-        in_weight * (0.8 * factor * wind_speed * temp_gap),
-        in_weight * (0.6 * factor * wind_speed * wind_east),
-        in_weight * (0.6 * factor * wind_speed * wind_north),
-    ]
-    returned = lax.all_to_all(
-        jnp.concatenate(weighted, axis=1), ("atm", "ocn"), split_axis=0, concat_axis=0, tiled=True
-    )
-    sent = jnp.concatenate(weighted, axis=1)
+    shared = in_weight * factor * wind_speed
+    gap = air_all - incoming[:, :plane]
+    block = lax.broadcasted_iota(jnp.int32, (1, plane), 1) // seg_width
+    scale = jnp.where(block == 0, -0.8, 0.6).astype(jnp.float32)
+    sent = jnp.concatenate([shared] * chan_count, axis=1) * (scale * gap)
+    returned = lax.all_to_all(sent, ("atm", "ocn"), split_axis=0, concat_axis=0, tiled=True)
     air_sum = jnp.dot(row_pick, sent, precision=HIGHEST, preferred_element_type=jnp.float32)
     current = diffuse_call(sizes, both, air_sum, rows_padded)
     current, returned = lax.optimization_barrier((current, returned))

time: 117 us -> 116 us (level)
  local copies, waits for them, and re-layouts: 11.4 us -> 6.98 us
  other arithmetic: 11.2 us -> 14.1 us
  matrix products: 13.8 us -> 16 us
  Pallas kernels: 62.2 us -> 60.7 us
    all_to_all x0 -> x1, other arithmetic: none -> 2.94 us  [per_device(): lax.all_to_all(sent, ('atm', 'ocn'), split_axis=0, concat_axis=0, tiled=T...]
    unnamed x32 -> x20, local copies, waits for them, and re-layouts: 5.29 us -> 2.51 us
    slice x1 -> x0, other arithmetic: 2.76 us -> none  [per_device(): incoming[:, c * seg_width:(c + 1) * seg_width]]
    concatenate x1 -> x0, local copies, waits for them, and re-layouts: 1.64 us -> none  [per_device(): sent = jnp.concatenate(weighted, axis=1)]
    mul x2 -> x1, other arithmetic: 0.97 us -> 2.53 us  [per_device(): shared = in_weight * factor * wind_speed]
    dot_general x1, matrix products: 4.01 us -> 5.53 us  [per_device(): jnp.dot(row_pick, sent, precision=HIGHEST, preferred_element_type=jnp.flo...]
    pallas_call x1, Pallas kernels: 24 us -> 22.5 us  [diffuse_call(): pl.pallas_call(functools.partial(diffuse_kernel, sizes), out_shape=jax.Sh...]
    reduce_max x0 -> x1, other arithmetic: none -> 1.25 us  [per_device(): jnp.max(incoming[:, plane + seg_width:], axis=1).astype(jnp.int32)]
  transfers between devices with their start and end apart: 2 -> 2, of which waited for: 0 -> 0; matrix products, arithmetic and copies ran while one was open for 6% -> 8% of each run, Pallas kernels for 53% -> 53%
where the time goes in v19:
time: 116 us
  Pallas kernels  60.7 us (52%)
  starting transfers between devices  16.8 us (14%)
  matrix products  16 us (14%)
  other arithmetic  14.1 us (12%)
  local copies, waits for them, and re-layouts  6.98 us (6%)
    pallas_call x1, Pallas kernels, smooth_call(): pl.pallas_call(functools.partial(smooth_kernel, sizes), out_shape=jax.Sha...  38.2 us
    pallas_call x1, Pallas kernels, diffuse_call(): pl.pallas_call(functools.partial(diffuse_kernel, sizes), out_shape=jax.Sh...  22.5 us
    all_to_all x1, starting transfers between devices, per_device(): lax.all_to_all(outgoing, ('atm', 'ocn'), split_axis=0, concat_axis=0, til...  11.9 us
    dot_general x1, matrix products, per_device(): jnp.dot(row_pick, sent, precision=HIGHEST, preferred_element_type=jnp.flo...  5.53 us
    all_to_all x1, starting transfers between devices, per_device(): lax.all_to_all(sent, ('atm', 'ocn'), split_axis=0, concat_axis=0, tiled=T...  4.92 us
    dot_general x1, matrix products, per_device(): jnp.dot(pick_rows, smoothed, precision=HIGHEST, preferred_element_type=jn...  4.76 us
    concatenate x1, other arithmetic, per_device(): jnp.concatenate([atm_planes, jnp.transpose(diffusivity, (1, 0, 2))], axis=0)  3.52 us
    concatenate x1, local copies, waits for them, and re-layouts, per_device(): outgoing = jnp.concatenate([out_ocean, out_weight, out_label], axis=1)  3.23 us
  transfers between devices with their start and end apart: 2, of which 0 were waited for; matrix products, arithmetic and copies ran while one was open for 8% of the time, Pallas kernels for 53%

profile of v19, /device:TPU:1, one launch (start us, length us, event | category | flops | bytes accessed | tf_op | source)
XLA Modules:
  0.0 115.5 jit_solution(6671400171747355631)
XLA Ops:
  0.7 0.8 fusion.37
  1.4 0.8 copy.13
  2.2 0.2 fusion.33
  2.5 0.9 fusion.31
  3.5 0.2 copy.15
  3.7 1.3 %fusion.3 = f32[1024,128]{0,1:T(8,128)S(1)} fusion(f32[512,128]{1,0:T(8,128)S(1)} %copy-done, s32[512]{0:T(512)S(1)} %multiply_add_fusion), kind=kOutput, calls=%fused_computation.11 | convolution fusion | flops 805830656 | bytes 788480 | tf_op jit(solution)/shard_map/dot_general | solution.py:65
  4.9 0.1 broadcast_in_dim.10
  5.1 0.1 broadcast_in_dim.11
  5.2 0.6 fusion.2
  5.9 0.1 slice_add_fusion
  5.9 0.6 fusion.4
  6.5 1.5 %fusion.51 = f32[1024,384]{0,1:T(8,128)S(1)} fusion(f32[1024,256]{1,0:T(8,128)S(1)} %fusion.4, f32[256,384]{0,1:T(8,128)S(1)} %bitcast.38), kind=kOutput, calls=%fused_computation.85 | convolution fusion | flops 1207959552 | bytes 3014656 | tf_op jit(solution)/shard_map/dot_general | solution.py:65
  8.0 0.3 convolution_multiply_fusion
  8.3 1.9 %pad_maximum_fusion.1 = f32[1024,640]{0,1:T(8,128)} fusion(f32[1024,128]{0,1:T(8,128)S(1)} %slice_add_fusion, f32[1024,128]{0,1:T(8,128)S(1)} %convolution_multiply_fusion, f32[1024,384]{0,1:T(8,128)S(1)} %fusion.51), kind=kLoop, calls=%fused_computation.4 | loop fusion | flops 1310720 | bytes 5242880 | tf_op jit(solution)/shard_map/concatenate | solution.py:263
  10.2 3.2 %copy.16 = f32[1024,640]{1,0:T(8,128)} copy(f32[1024,640]{0,1:T(8,128)} %pad_maximum_fusion.1) | data formatting | bytes 5242880 | tf_op jit(solution)/shard_map/concatenate | solution.py:263
  13.4 11.9 %all-to-all-start = ((f32[128,8,640]{2,1,0:T(8,128)}), f32[128,8,640]{2,1,0:T(8,128)}, u32[]{:S(2)}, u32[]{:S(2)}) async-start(f32[128,8,640]{2,1,0:T(8,128)} %bitcast.33), calls=%async_computation | async-start | bytes 5242880 | tf_op jit(solution)/shard_map/all_to_all | solution.py:264
  25.3 38.2 %shard_map.95 = f32[864,384]{1,0:T(8,128)} custom-call(f32[3,864,128]{2,1,0:T(8,128)} %bitcast.34), custom_call_target="tpu_custom_call" | custom-call | tf_op jit(solution)/shard_map/pallas_call | solution.py:195
  63.6 1.2 %slice_reduce_fusion = f32[1024]{0:T(1024)S(1)} fusion(f32[1024,640]{1,0:T(8,128)} %bitcast.9), kind=kLoop, calls=%fused_computation.41 | loop fusion | flops 130048 | bytes 528384 | tf_op jit(solution)/shard_map/reduce_max | solution.py:272
  64.9 4.8 %fusion.1 = f32[1024,384]{1,0:T(8,128)S(1)} fusion(f32[864,384]{1,0:T(8,128)} %shard_map.95, s32[1024]{0:T(1024)S(1)} %convert_element_type.45), kind=kOutput, calls=%fused_computation.2 | convolution fusion | flops 4077748224 | bytes 2904064 | tf_op jit(solution)/shard_map/dot_general | solution.py:277
  69.6 2.5 %fusion.26 = f32[1024,128]{1,0:T(8,128)S(1)} fusion(f32[1024,384]{1,0:T(8,128)S(1)} %fusion.1, f32[1024,640]{1,0:T(8,128)} %bitcast.9), kind=kLoop, calls=%fused_computation.40 | loop fusion | flops 1572864 | bytes 4194304 | tf_op jit(solution)/shard_map/mul | solution.py:286
  72.2 2.9 %fusion.49 = f32[128,8,384]{2,1,0:T(8,128)} fusion(f32[1024,384]{1,0:T(8,128)S(1)} %fusion.1, f32[1024,640]{1,0:T(8,128)} %bitcast.9, f32[384]{0:T(512)S(1)} %fusion.42, f32[1024,128]{1,0:T(8,128)S(1)} %fusion.26), kind=kLoop, calls=%fused_computation.84 | loop fusion | flops 1966080 | bytes 5244416 | tf_op jit(solution)/shard_map/all_to_all | solution.py:291
  75.1 4.9 %all-to-all-start.1 = ((f32[128,8,384]{2,1,0:T(8,128)}), f32[128,8,384]{2,1,0:T(8,128)S(1)}, u32[]{:S(2)}, u32[]{:S(2)}) async-start(f32[128,8,384]{2,1,0:T(8,128)} %fusion.49), calls=%async_computation.1 | async-start | bytes 3145728 | tf_op jit(solution)/shard_map/all_to_all | solution.py:291
  80.1 3.5 %pad_maximum_fusion.both_ref = f32[6,864,128]{2,1,0:T(8,128)} fusion(f32[3,864,128]{2,1,0:T(8,128)} %bitcast.39, f32[3,864,128]{2,1,0:T(8,128)} %bitcast.35), kind=kLoop, calls=%fused_computation.3 | loop fusion | flops 663552 | bytes 5308416 | tf_op jit(solution)/shard_map/concatenate | solution.py:267
  83.6 5.5 %fusion.sum_ref = f32[864,384]{1,0:T(8,128)} fusion(s32[1024]{0:T(1024)S(1)} %convert_element_type.45, f32[1024,384]{1,0:T(8,128)S(1)} %copy-done.2, f32[1024,640]{1,0:T(8,128)} %bitcast.9, f32[1024,128]{1,0:T(8,128)S(1)} %fusion.26, f32[384]{0:T(512)S(1)} %fusion.42), kind=kOutput, calls=%fused_computation.1 | convolution fusion | flops 4079714304 | bytes 5002752 | tf_op jit(solution)/shard_map/dot_general | solution.py:292
  89.1 22.5 %shard_map.96 = f32[3,864,128]{2,1,0:T(8,128)} custom-call(f32[6,864,128]{2,1,0:T(8,128)} %pad_maximum_fusion.both_ref, f32[864,384]{1,0:T(8,128)} %fusion.sum_ref), custom_call_target="tpu_custom_call" | custom-call | tf_op jit(solution)/shard_map/pallas_call | solution.py:209
  111.6 0.5 fusion.15
  112.1 0.5 convolution_add_fusion.1
  112.6 0.5 convolution_add_fusion
  113.1 0.2 copy.17
  113.2 0.9 copy.18
  114.2 0.3 copy-done.3
  114.5 1.1 copy.20
  (26 shorter events, 0.2 us)
Async XLA Ops:
  0.6 3.0 %copy-start = (f32[512,128]{1,0:T(8,128)S(1)}, f32[512,128]{1,0:T(8,128)}, u32[]{:S(2)}) copy-start(f32[512,128]{1,0:T(8,128)} %param.12) | copy-start | bytes 786436
  0.6 2.8 %copy-start.6 = (s32[512,1]{0,1:T(1,128)S(1)}, s32[512,1]{0,1:T(1,128)}, u32[]{:S(2)}) copy-start(s32[512,1]{0,1:T(1,128)} %param.14) | copy-start | bytes 6148
  0.7 2.8 %copy-start.4 = (f32[256,3,128]{2,0,1:T(8,128)S(1)}, f32[256,3,128]{2,0,1:T(8,128)}, u32[]{:S(2)}) copy-start(f32[256,3,128]{2,0,1:T(8,128)} %param.10) | copy-start | bytes 1179652
  5.2 0.7 copy-start.7
  6.5 1.5 %copy-start.5 = (s32[256,128]{1,0:T(8,128)S(1)}, s32[256,128]{1,0:T(8,128)}, u32[]{:S(2)}) copy-start(s32[256,128]{1,0:T(8,128)} %param.11) | copy-start | bytes 393220
  13.4 50.2 %all-to-all-start = ((f32[128,8,640]{2,1,0:T(8,128)}), f32[128,8,640]{2,1,0:T(8,128)}, u32[]{:S(2)}, u32[]{:S(2)}) async-start(f32[128,8,640]{2,1,0:T(8,128)} %bitcast.33), calls=%async_computation | async-start | bytes 5242880 | tf_op jit(solution)/shard_map/all_to_all | solution.py:264
  69.6 2.5 %copy-start.1 = (f32[1024,384]{1,0:T(8,128)}, f32[1024,384]{1,0:T(8,128)S(1)}, u32[]{:S(2)}) copy-start(f32[1024,384]{1,0:T(8,128)S(1)} %fusion.1) | copy-start | bytes 4718596
  75.1 36.5 %all-to-all-start.1 = ((f32[128,8,384]{2,1,0:T(8,128)}), f32[128,8,384]{2,1,0:T(8,128)S(1)}, u32[]{:S(2)}, u32[]{:S(2)}) async-start(f32[128,8,384]{2,1,0:T(8,128)} %fusion.49), calls=%async_computation.1 | async-start | bytes 3145728 | tf_op jit(solution)/shard_map/all_to_all | solution.py:291
  80.0 3.5 %copy-start.2 = (f32[1024,384]{1,0:T(8,128)S(1)}, f32[1024,384]{1,0:T(8,128)}, u32[]{:S(2)}) copy-start(f32[1024,384]{1,0:T(8,128)} %copy-done.1) | copy-start | bytes 4718596
  113.1 1.4 %copy-start.3 = (f32[3,864,128]{2,1,0:T(8,128)S(1)}, f32[3,864,128]{2,1,0:T(8,128)}, u32[]{:S(2)}) copy-start(f32[3,864,128]{2,1,0:T(8,128)} %shard_map.96) | copy-start | bytes 3981316

commit v20 on v19

--- a/solution.py
+++ b/solution.py
@@ -273,7 +273,9 @@
     row_pick = (
         jnp.arange(row_count, dtype=jnp.int32)[:, None] == in_labels[None, :]
     ).astype(jnp.float32)
-    pick_rows = row_pick.T
+    pick_rows = (
+        in_labels[:, None] == jnp.arange(row_count, dtype=jnp.int32)[None, :]
+    ).astype(jnp.float32)
     air_all = jnp.dot(pick_rows, smoothed, precision=HIGHEST, preferred_element_type=jnp.float32)
     air = [air_all[:, c * seg_width : (c + 1) * seg_width] for c in range(chan_count)]
     ocean = [incoming[:, c * seg_width : (c + 1) * seg_width] for c in range(chan_count)]

time: 116 us -> 116 us (level)
  no operation moved by 1% of the time
where the time goes in v20:
time: 116 us
  Pallas kernels  60.7 us (52%)
  starting transfers between devices  16.8 us (14%)
  matrix products  16 us (14%)
  other arithmetic  14.1 us (12%)
  local copies, waits for them, and re-layouts  6.98 us (6%)
    pallas_call x1, Pallas kernels, smooth_call(): pl.pallas_call(functools.partial(smooth_kernel, sizes), out_shape=jax.Sha...  38.2 us
    pallas_call x1, Pallas kernels, diffuse_call(): pl.pallas_call(functools.partial(diffuse_kernel, sizes), out_shape=jax.Sh...  22.5 us
    all_to_all x1, starting transfers between devices, per_device(): lax.all_to_all(outgoing, ('atm', 'ocn'), split_axis=0, concat_axis=0, til...  11.9 us
    dot_general x1, matrix products, per_device(): jnp.dot(row_pick, sent, precision=HIGHEST, preferred_element_type=jnp.flo...  5.53 us
    all_to_all x1, starting transfers between devices, per_device(): lax.all_to_all(sent, ('atm', 'ocn'), split_axis=0, concat_axis=0, tiled=T...  4.92 us
    dot_general x1, matrix products, per_device(): jnp.dot(pick_rows, smoothed, precision=HIGHEST, preferred_element_type=jn...  4.76 us
    concatenate x1, other arithmetic, per_device(): jnp.concatenate([atm_planes, jnp.transpose(diffusivity, (1, 0, 2))], axis=0)  3.52 us
    concatenate x1, local copies, waits for them, and re-layouts, per_device(): outgoing = jnp.concatenate([out_ocean, out_weight, out_label], axis=1)  3.23 us
  transfers between devices with their start and end apart: 2, of which 0 were waited for; matrix products, arithmetic and copies ran while one was open for 8% of the time, Pallas kernels for 53%

profile of v20, /device:TPU:1, one launch (start us, length us, event | category | flops | bytes accessed | tf_op | source)
XLA Modules:
  0.0 115.5 jit_solution(8008136200503758673)
XLA Ops:
  0.7 0.8 fusion.37
  1.4 0.8 copy.13
  2.2 0.2 fusion.33
  2.5 0.9 fusion.31
  3.5 0.2 copy.15
  3.7 1.3 %fusion.3 = f32[1024,128]{0,1:T(8,128)S(1)} fusion(f32[512,128]{1,0:T(8,128)S(1)} %copy-done, s32[512]{0:T(512)S(1)} %multiply_add_fusion), kind=kOutput, calls=%fused_computation.12 | convolution fusion | flops 805830656 | bytes 788480 | tf_op jit(solution)/shard_map/dot_general | solution.py:65
  4.9 0.1 broadcast_in_dim.10
  5.1 0.1 broadcast_in_dim.11
  5.2 0.6 fusion.2
  5.9 0.1 slice_add_fusion
  5.9 0.6 fusion.4
  6.5 1.5 %fusion.51 = f32[1024,384]{0,1:T(8,128)S(1)} fusion(f32[1024,256]{1,0:T(8,128)S(1)} %fusion.4, f32[256,384]{0,1:T(8,128)S(1)} %bitcast.38), kind=kOutput, calls=%fused_computation.86 | convolution fusion | flops 1207959552 | bytes 3014656 | tf_op jit(solution)/shard_map/dot_general | solution.py:65
  8.0 0.3 convolution_multiply_fusion
  8.3 1.9 %pad_maximum_fusion.1 = f32[1024,640]{0,1:T(8,128)} fusion(f32[1024,128]{0,1:T(8,128)S(1)} %slice_add_fusion, f32[1024,128]{0,1:T(8,128)S(1)} %convolution_multiply_fusion, f32[1024,384]{0,1:T(8,128)S(1)} %fusion.51), kind=kLoop, calls=%fused_computation.5 | loop fusion | flops 1310720 | bytes 5242880 | tf_op jit(solution)/shard_map/concatenate | solution.py:263
  10.2 3.2 %copy.16 = f32[1024,640]{1,0:T(8,128)} copy(f32[1024,640]{0,1:T(8,128)} %pad_maximum_fusion.1) | data formatting | bytes 5242880 | tf_op jit(solution)/shard_map/concatenate | solution.py:263
  13.4 11.9 %all-to-all-start = ((f32[128,8,640]{2,1,0:T(8,128)}), f32[128,8,640]{2,1,0:T(8,128)}, u32[]{:S(2)}, u32[]{:S(2)}) async-start(f32[128,8,640]{2,1,0:T(8,128)} %bitcast.33), calls=%async_computation | async-start | bytes 5242880 | tf_op jit(solution)/shard_map/all_to_all | solution.py:264
  25.3 38.2 %shard_map.95 = f32[864,384]{1,0:T(8,128)} custom-call(f32[3,864,128]{2,1,0:T(8,128)} %bitcast.34), custom_call_target="tpu_custom_call" | custom-call | tf_op jit(solution)/shard_map/pallas_call | solution.py:195
  63.6 1.2 %slice_reduce_fusion = f32[1024]{0:T(1024)S(1)} fusion(f32[1024,640]{1,0:T(8,128)} %bitcast.9), kind=kLoop, calls=%fused_computation.42 | loop fusion | flops 130048 | bytes 528384 | tf_op jit(solution)/shard_map/reduce_max | solution.py:272
  64.9 4.8 %fusion = f32[1024,384]{1,0:T(8,128)S(1)} fusion(f32[864,384]{1,0:T(8,128)} %shard_map.95, s32[1024]{0:T(1024)S(1)} %convert_element_type.50), kind=kOutput, calls=%fused_computation.1 | convolution fusion | flops 4077748224 | bytes 2904064 | tf_op jit(solution)/shard_map/dot_general | solution.py:279
  69.6 2.5 %fusion.26 = f32[1024,128]{1,0:T(8,128)S(1)} fusion(f32[1024,384]{1,0:T(8,128)S(1)} %fusion, f32[1024,640]{1,0:T(8,128)} %bitcast.9), kind=kLoop, calls=%fused_computation.41 | loop fusion | flops 1572864 | bytes 4194304 | tf_op jit(solution)/shard_map/mul | solution.py:288
  72.2 2.9 %fusion.49 = f32[128,8,384]{2,1,0:T(8,128)} fusion(f32[1024,384]{1,0:T(8,128)S(1)} %fusion, f32[1024,640]{1,0:T(8,128)} %bitcast.9, f32[384]{0:T(512)S(1)} %fusion.42, f32[1024,128]{1,0:T(8,128)S(1)} %fusion.26), kind=kLoop, calls=%fused_computation.85 | loop fusion | flops 1966080 | bytes 5244416 | tf_op jit(solution)/shard_map/all_to_all | solution.py:293
  75.1 4.9 %all-to-all-start.1 = ((f32[128,8,384]{2,1,0:T(8,128)}), f32[128,8,384]{2,1,0:T(8,128)S(1)}, u32[]{:S(2)}, u32[]{:S(2)}) async-start(f32[128,8,384]{2,1,0:T(8,128)} %fusion.49), calls=%async_computation.1 | async-start | bytes 3145728 | tf_op jit(solution)/shard_map/all_to_all | solution.py:293
  80.0 3.5 %pad_maximum_fusion.both_ref = f32[6,864,128]{2,1,0:T(8,128)} fusion(f32[3,864,128]{2,1,0:T(8,128)} %bitcast.39, f32[3,864,128]{2,1,0:T(8,128)} %bitcast.35), kind=kLoop, calls=%fused_computation.4 | loop fusion | flops 663552 | bytes 5308416 | tf_op jit(solution)/shard_map/concatenate | solution.py:267
  83.6 5.5 %fusion.1.sum_ref = f32[864,384]{1,0:T(8,128)} fusion(s32[1024]{0:T(1024)S(1)} %convert_element_type.50, f32[1024,384]{1,0:T(8,128)S(1)} %copy-done.2, f32[1024,640]{1,0:T(8,128)} %bitcast.9, f32[1024,128]{1,0:T(8,128)S(1)} %fusion.26, f32[384]{0:T(512)S(1)} %fusion.42), kind=kOutput, calls=%fused_computation.3 | convolution fusion | flops 4079714304 | bytes 5002752 | tf_op jit(solution)/shard_map/dot_general | solution.py:294
  89.1 22.5 %shard_map.96 = f32[3,864,128]{2,1,0:T(8,128)} custom-call(f32[6,864,128]{2,1,0:T(8,128)} %pad_maximum_fusion.both_ref, f32[864,384]{1,0:T(8,128)} %fusion.1.sum_ref), custom_call_target="tpu_custom_call" | custom-call | tf_op jit(solution)/shard_map/pallas_call | solution.py:209
  111.6 0.5 fusion.15
  112.1 0.5 convolution_add_fusion.1
  112.6 0.5 convolution_add_fusion
  113.1 0.2 copy.17
  113.2 0.9 copy.18
  114.1 0.3 copy-done.3
  114.5 1.1 copy.20
  (26 shorter events, 0.2 us)
Async XLA Ops:
  0.6 3.0 %copy-start = (f32[512,128]{1,0:T(8,128)S(1)}, f32[512,128]{1,0:T(8,128)}, u32[]{:S(2)}) copy-start(f32[512,128]{1,0:T(8,128)} %param.12) | copy-start | bytes 786436
  0.6 2.8 %copy-start.6 = (s32[512,1]{0,1:T(1,128)S(1)}, s32[512,1]{0,1:T(1,128)}, u32[]{:S(2)}) copy-start(s32[512,1]{0,1:T(1,128)} %param.14) | copy-start | bytes 6148
  0.7 2.8 %copy-start.4 = (f32[256,3,128]{2,0,1:T(8,128)S(1)}, f32[256,3,128]{2,0,1:T(8,128)}, u32[]{:S(2)}) copy-start(f32[256,3,128]{2,0,1:T(8,128)} %param.10) | copy-start | bytes 1179652
  5.2 0.7 copy-start.7
  6.5 1.5 %copy-start.5 = (s32[256,128]{1,0:T(8,128)S(1)}, s32[256,128]{1,0:T(8,128)}, u32[]{:S(2)}) copy-start(s32[256,128]{1,0:T(8,128)} %param.11) | copy-start | bytes 393220
  13.4 50.2 %all-to-all-start = ((f32[128,8,640]{2,1,0:T(8,128)}), f32[128,8,640]{2,1,0:T(8,128)}, u32[]{:S(2)}, u32[]{:S(2)}) async-start(f32[128,8,640]{2,1,0:T(8,128)} %bitcast.33), calls=%async_computation | async-start | bytes 5242880 | tf_op jit(solution)/shard_map/all_to_all | solution.py:264
  69.6 2.5 %copy-start.1 = (f32[1024,384]{1,0:T(8,128)}, f32[1024,384]{1,0:T(8,128)S(1)}, u32[]{:S(2)}) copy-start(f32[1024,384]{1,0:T(8,128)S(1)} %fusion) | copy-start | bytes 4718596
  75.1 36.5 %all-to-all-start.1 = ((f32[128,8,384]{2,1,0:T(8,128)}), f32[128,8,384]{2,1,0:T(8,128)S(1)}, u32[]{:S(2)}, u32[]{:S(2)}) async-start(f32[128,8,384]{2,1,0:T(8,128)} %fusion.49), calls=%async_computation.1 | async-start | bytes 3145728 | tf_op jit(solution)/shard_map/all_to_all | solution.py:293
  80.0 3.5 %copy-start.2 = (f32[1024,384]{1,0:T(8,128)S(1)}, f32[1024,384]{1,0:T(8,128)}, u32[]{:S(2)}) copy-start(f32[1024,384]{1,0:T(8,128)} %copy-done.1) | copy-start | bytes 4718596
  113.1 1.4 %copy-start.3 = (f32[3,864,128]{2,1,0:T(8,128)S(1)}, f32[3,864,128]{2,1,0:T(8,128)}, u32[]{:S(2)}) copy-start(f32[3,864,128]{2,1,0:T(8,128)} %shard_map.96) | copy-start | bytes 3981316
